TPU v7x, 128 devices: a whole 4x4x4 slice. The times are simulated.
128 devices in a mesh: dp: 32 (over z, y, core), section: 4 (over x).
Axes of the slice: x: 4, y: 4, z: 4, core: 2. Of those that a mesh axis runs over, the one named last changes fastest.
Arguments:
- real_in: bfloat16 [256, 144, 512], P('dp'), may hold values from -48 to 48
- fake_in: bfloat16 [256, 144, 512], P('dp'), may hold values from -48 to 48
- kernel_first: bfloat16 [5, 512, 1024], P(None, None, 'section'), may hold values from -0.15625 to 0.15625
- kernel_second: bfloat16 [5, 1024, 1024], P(None, None, 'section'), may hold values from -0.125 to 0.125
Outputs:
- layer_loss: float32 [2], replicated
- grad_first: float32 [512, 5, 1024], P('dp', None, 'section')
- grad_second: float32 [1024, 5, 1024], P('dp', None, 'section')
All inputs are finite; a program needn't handle non-finite values.
Results may differ from a plain program's by a relative error of at most 0.012.
The roundings to bfloat16 on the way count: a program that leaves them out, or rounds other values in their place, can miss the bound.
Values may be sent and summed in bfloat16 or wider, within the bound.
No kernel may reach another device: no remote copies, remote signals or barrier semaphores. Data moves between devices by JAX's collectives and lax.ppermute only.
A program may use at most 128 MiB of HBM per device.

v0:
```python
import jax
import jax.numpy as jnp
from jax import lax
from jax.sharding import Mesh
from jax.sharding import PartitionSpec as P

K = 5
DP = ("dp_0", "dp_1", "dp_2")
DP_SECTION = ("dp_0", "dp_1", "dp_2", "section")


smooth_width = 0.1
leak_slope = 0.1


def copy_for_each(x, axis):
    count = lax.axis_size(axis)
    return lax.all_to_all(jnp.broadcast_to(x[None], (count, *x.shape)), axis, 0, 0, tiled=True)


def in_order(blocks, dim):
    shape = list(blocks.shape[1:])
    shape[dim] *= blocks.shape[0]
    return jnp.moveaxis(blocks, 0, dim).reshape(shape)


def gathered_copies(x, axis, dim):
    blocks = copy_for_each(x, axis)
    return in_order(blocks, dim)


def one_axis_at_a_time(x, axes):
    for axis in axes:
        x = lax.psum(x, axis)
    return x


def in_blocks(x, dim, count):
    shape = x.shape
    blocks = x.reshape(*shape[:dim], count, shape[dim] // count, *shape[dim + 1 :])
    return jnp.moveaxis(blocks, dim, 0)


def sum_packed(arrays, axis, dims):
    count = lax.axis_size(axis)
    blocks = [in_blocks(a, dim, count) for a, dim in zip(arrays, dims)]
    lines = jnp.concatenate([b.reshape(count, -1) for b in blocks], axis=1)
    span = max(16, -(-lines.shape[1] // 1024) * 8)
    lines = jnp.pad(lines, ((0, 0), (0, span * 128 - lines.shape[1]))).reshape(-1, 128)
    vector, at, finished = (lax.psum_scatter(lines, axis, tiled=True).reshape(-1), 0, [])
    for b in blocks:
        part = b[0]
        finished.append(vector[at : at + part.size].reshape(part.shape))
        at += part.size
    return tuple(finished)


def conv_strided(values, kernel, frames):
    padded = jnp.pad(values, ((0, 0), (2, 2), (0, 0)))
    summed = jnp.zeros((values.shape[0] * frames, kernel.shape[2]), jnp.float32)
    for tap in range(kernel.shape[0]):
        window = padded[:, tap : tap + 3 * frames - 2 : 3].reshape(-1, values.shape[2])
        summed = summed + jnp.dot(window, kernel[tap], preferred_element_type=jnp.float32)
    return summed.reshape(values.shape[0], frames, -1)


def conv_forward(values, kernel):
    frames = values.shape[1]
    padded = jnp.pad(values, ((0, 0), (2, 2), (0, 0)))
    summed = jnp.zeros((values.shape[0] * frames, kernel.shape[2]), jnp.float32)
    for tap in range(kernel.shape[0]):
        window = padded[:, tap : tap + frames].reshape(-1, values.shape[2])
        summed = summed + jnp.dot(window, kernel[tap], preferred_element_type=jnp.float32)
    return summed.reshape(values.shape[0], frames, -1)


def conv_backward(delta, kernel):
    frames = delta.shape[1]
    padded = jnp.pad(delta, ((0, 0), (2, 2), (0, 0)))
    summed = jnp.zeros((delta.shape[0] * frames, kernel.shape[1]), jnp.float32)
    for tap in range(kernel.shape[0]):
        window = padded[:, 4 - tap : 4 - tap + frames].reshape(-1, delta.shape[2])
        summed = summed + lax.dot_general(
            window, kernel[tap], (((1,), (1,)), ((), ())), preferred_element_type=jnp.float32
        )
    return summed.reshape(delta.shape[0], frames, -1)


def weight_term(values, delta, amount, stride):
    frames = delta.shape[1]
    padded = jnp.pad(values, ((0, 0), (2, 2), (0, 0)))
    flat_delta = delta.reshape(-1, delta.shape[2])
    pieces = []
    for tap in range(K):
        window = padded[:, tap : tap + stride * (frames - 1) + 1 : stride].reshape(-1, amount)
        pieces.append(
            lax.dot_general(
                window, flat_delta, (((0,), (0,)), ((), ())), preferred_element_type=jnp.float32
            )
        )
    return jnp.stack(pieces, axis=1)


def activate(pre):
    return jnp.where(pre > 0, pre, leak_slope * pre).astype(jnp.bfloat16)


def local_grad(feature, normaliser):
    half = feature.shape[0] // 2
    difference = feature[:half].astype(jnp.float32) - feature[half:].astype(jnp.float32)
    slope = (
        difference / jnp.sqrt(difference * difference + smooth_width * smooth_width) / normaliser
    )
    return jnp.concatenate([slope, -slope], axis=0)


def smooth_total(feature):
    half = feature.shape[0] // 2
    difference = feature[:half].astype(jnp.float32) - feature[half:].astype(jnp.float32)
    return jnp.sum(jnp.sqrt(difference * difference + smooth_width * smooth_width) - smooth_width)


def shards(real_in, fake_in, kernel_first, kernel_second):
    replicas = lax.axis_size(DP)
    frames = real_in.shape[1] // 3
    in_width = real_in.shape[2]
    width = kernel_second.shape[1]
    normaliser = float(real_in.shape[0] * frames)
    count_all = float(real_in.shape[0] * replicas * frames * width)
    values = jnp.concatenate([real_in, fake_in], axis=0)
    first = activate(conv_strided(values, kernel_first, frames))
    partial_first = smooth_total(first)
    whole_first = gathered_copies(first, "section", 2)
    second = activate(conv_forward(whole_first, kernel_second))
    partial_second = smooth_total(second)
    total_first, total_second = (
        one_axis_at_a_time(partial_first, DP_SECTION),
        one_axis_at_a_time(partial_second, DP_SECTION),
    )
    layer_loss = jnp.stack([total_first, total_second]) / count_all
    delta_second = (local_grad(second, normaliser) * jnp.where(second > 0, 1.0, leak_slope)).astype(
        jnp.bfloat16
    )
    upstream_terms = conv_backward(delta_second, kernel_second)
    upstream = lax.psum_scatter(
        upstream_terms.astype(jnp.bfloat16), "section", scatter_dimension=2, tiled=True
    )
    delta_first = (
        (local_grad(first, normaliser) + upstream.astype(jnp.float32))
        * jnp.where(first > 0, 1.0, leak_slope)
    ).astype(jnp.bfloat16)
    term_first = weight_term(values, delta_first, in_width, 3)
    term_second = weight_term(whole_first, delta_second, width, 1)
    grad_first, grad_second = tuple(
        (
            part.astype(jnp.float32)
            for part in sum_packed(
                (term_first.astype(jnp.bfloat16), term_second.astype(jnp.bfloat16)), DP, (0, 0)
            )
        )
    )
    return (layer_loss, grad_first, grad_second)


def solution(mesh):
    finer = Mesh(
        mesh.devices.reshape(4, 4, 2, mesh.shape["section"]), ("dp_0", "dp_1", "dp_2", "section")
    )
    return jax.shard_map(
        shards,
        mesh=finer,
        in_specs=(
            P(DP, None, None),
            P(DP, None, None),
            P(None, None, "section"),
            P(None, None, "section"),
        ),
        out_specs=(P(), P(DP, None, "section"), P(DP, None, "section")),
        check_vma=False,
    )
```

profile of v0, /device:TPU:0, one launch (start us, length us, event | category | flops | bytes accessed | tf_op | source)
XLA Modules:
  0.0 208.0 jit_solution(5430325532296938739)
XLA Ops:
  7.2 2.6 %fusion.3 = bf16[16,148,512]{2,1,0:T(8,128)(2,1)S(1)} fusion(bf16[8,144,512]{2,1,0:T(8,128)(2,1)} %param.5, bf16[8,144,512]{2,1,0:T(8,128)(2,1)} %param.4), kind=kLoop, calls=%fused_computation.7 | loop fusion | flops 10911744 | bytes 4784128 | tf_op jit(solution)/shard_map/concatenate | solution.py:130
  9.9 3.4 %slice.116 = bf16[16,48,512]{2,1,0:T(8,128)(2,1)} slice(bf16[16,148,512]{2,1,0:T(8,128)(2,1)S(1)} %fusion.3), slice={[0:16:1], [3:145:3], [0:512:1]} | slice | bytes 1572864 | tf_op jit(solution)/shard_map/slice | solution.py:62
  13.2 3.2 %slice.114 = bf16[16,48,512]{2,1,0:T(8,128)(2,1)} slice(bf16[16,148,512]{2,1,0:T(8,128)(2,1)S(1)} %fusion.3), slice={[0:16:1], [2:144:3], [0:512:1]} | slice | bytes 1572864 | tf_op jit(solution)/shard_map/slice | solution.py:62
  16.5 3.3 %slice.112 = bf16[16,48,512]{2,1,0:T(8,128)(2,1)} slice(bf16[16,148,512]{2,1,0:T(8,128)(2,1)S(1)} %fusion.3), slice={[0:16:1], [1:143:3], [0:512:1]} | slice | bytes 1572864 | tf_op jit(solution)/shard_map/slice | solution.py:62
  19.7 1.2 slice.110
  20.9 3.5 %slice.118 = bf16[16,48,512]{2,1,0:T(8,128)(2,1)} slice(bf16[16,148,512]{2,1,0:T(8,128)(2,1)S(1)} %fusion.3), slice={[0:16:1], [4:146:3], [0:512:1]} | slice | bytes 1572864 | tf_op jit(solution)/shard_map/slice | solution.py:62
  24.4 1.5 fusion.68
  25.9 1.3 convolution_add_fusion.7
  30.1 24.9 %all_to_all.5 = bf16[4,16,48,256]{3,2,1,0:T(8,128)(2,1)S(1)} all-to-all(bf16[4,16,48,256]{3,2,1,0:T(8,128)(2,1)S(1)} %broadcast_in_dim.16), channel_id=1, replica_groups=mesh['dp_0'=4,'dp_1'=4,'dp_2'=2,'section'=4] {'section'}, dimensions={0} | all-to-all | bytes 3145728 | tf_op jit(solution)/shard_map/all_to_all | solution.py:18
  55.0 1.2 copy.16
  56.8 1.5 pad_slice_fusion
  58.4 1.1 copy-done
  62.5 0.8 fusion.76
  66.8 2.0 add_convert_fusion
  69.1 2.9 %fusion.75 = (f32[8,48,256]{2,1,0:T(8,128)}, f32[8,48,256]{2,1,0:T(8,128)}, f32[]{:T(128)}) fusion(bf16[16,48,256]{2,1,0:T(8,128)(2,1)} %copy-done.6), kind=kLoop, calls=%fused_computation.123 | loop fusion | flops 983039 | bytes 1179652 | tf_op jit(solution)/shard_map/neg | solution.py:114
  72.7 0.8 copy-done.5
  76.8 3.7 %copy.19 = bf16[1024,5,256]{2,1,0:T(8,128)(2,1)} copy(bf16[1024,5,256]{2,0,1:T(8,128)(2,1)S(1)} %fusion.11) | data formatting | bytes 5242880 | tf_op jit(solution)/shard_map/stack | solution.py:101
  80.5 4.7 %convert_element_type.93 = bf16[32,40960]{1,0:T(8,128)(2,1)S(1)} reshape(bf16[1024,5,256]{2,1,0:T(8,128)(2,1)} %copy.19) | data formatting | bytes 5242880 | tf_op jit(solution)/shard_map/convert_element_type | solution.py:158
  85.2 10.0 %reduce-scatter.3.cloned.1.call-done = bf16[16,48,256]{2,1,0:T(8,128)(2,1)} async-done(((bf16[16,48,1024]{2,1,0:T(8,128)(2,1)}), bf16[16,48,256]{2,1,0:T(8,128)(2,1)}) %reduce-scatter.3.cloned.1.call-update) | async-done | bytes 393232 | tf_op jit(solution)/shard_map/reduce_scatter | solution.py:145
  95.2 1.5 fusion.37
  101.7 2.2 %copy.18 = bf16[512,5,256]{2,1,0:T(8,128)(2,1)} copy(bf16[512,5,256]{2,0,1:T(8,128)(2,1)S(1)} %fusion.24) | data formatting | bytes 2621440 | tf_op jit(solution)/shard_map/stack | solution.py:101
  103.8 3.5 %convert_element_type.92 = bf16[32,20480]{1,0:T(8,128)(2,1)} reshape(bf16[512,5,256]{2,1,0:T(8,128)(2,1)} %copy.18) | data formatting | bytes 2621440 | tf_op jit(solution)/shard_map/convert_element_type | solution.py:158
  107.4 3.4 %pad_maximum_fusion = bf16[32,61440]{1,0:T(8,128)(2,1)} fusion(bf16[32,40960]{1,0:T(8,128)(2,1)S(1)} %convert_element_type.93, bf16[32,20480]{1,0:T(8,128)(2,1)} %convert_element_type.92), kind=kLoop, calls=%fused_computation.5 | loop fusion | flops 7864320 | bytes 7864320 | tf_op jit(solution)/shard_map/concatenate | solution.py:47
  110.8 5.4 %reshape.124 = bf16[15360,128]{1,0:T(8,128)(2,1)} reshape(bf16[32,61440]{1,0:T(8,128)(2,1)} %pad_maximum_fusion) | data formatting | bytes 7864320 | tf_op jit(solution)/shard_map/reshape | solution.py:49
  116.2 11.3 %all-reduce.5 = (f32[]{:T(128)}, f32[]{:T(128)}) all-reduce(f32[]{:T(128)} %get-tuple-element.35, f32[]{:T(128)} %get-tuple-element.34), channel_id=1, replica_groups=mesh['dp_0'=4,'dp_1'=4,'dp_2'=2,'section'=4] {'dp_0'}, use_global_device_ids=true, to_apply=%region_6.7 | all-reduce | flops 2 | bytes 16 | tf_op jit(solution)/shard_map/psum | solution.py:34
  127.6 11.1 %all-reduce.4 = (f32[]{:T(128)}, f32[]{:T(128)}) all-reduce(f32[]{:T(128)} %get-tuple-element.16, f32[]{:T(128)} %get-tuple-element.17), channel_id=1, replica_groups=mesh['dp_0'=4,'dp_1'=4,'dp_2'=2,'section'=4] {'dp_1'}, use_global_device_ids=true, to_apply=%region_7.8 | all-reduce | flops 2 | bytes 16 | tf_op jit(solution)/shard_map/psum | solution.py:34
  138.7 3.1 %all-reduce.6 = (f32[]{:T(128)}, f32[]{:T(128)}) all-reduce(f32[]{:T(128)} %get-tuple-element.14, f32[]{:T(128)} %get-tuple-element.15), channel_id=1, replica_groups=mesh['dp_0'=4,'dp_1'=4,'dp_2'=2,'section'=4] {'dp_2'}, use_global_device_ids=true, to_apply=%region_8.9 | all-reduce | flops 2 | bytes 16 | tf_op jit(solution)/shard_map/psum | solution.py:34
  141.7 9.6 %all-reduce.3 = (f32[1]{0:T(128)}, f32[1]{0:T(128)}) all-reduce(f32[1]{0:T(128)} %bitcast.23, f32[1]{0:T(128)} %bitcast.11), channel_id=1, replica_groups=mesh['dp_0'=4,'dp_1'=4,'dp_2'=2,'section'=4] {'section'}, use_global_device_ids=true, to_apply=%region_9.10 | all-reduce | flops 2 | bytes 16 | tf_op jit(solution)/shard_map/psum | solution.py:34
  151.4 1.9 maximum_multiply_fusion
  153.3 44.7 %reduce-scatter.5.cloned.1.call-done = bf16[480,128]{1,0:T(8,128)(2,1)} async-done(((bf16[15360,128]{1,0:T(8,128)(2,1)}), bf16[480,128]{1,0:T(8,128)(2,1)}) %reduce-scatter.5.cloned.1.call-update) | async-done | bytes 122896 | tf_op jit(solution)/shard_map/reduce_scatter | solution.py:50
  198.0 0.8 slice_convert_fusion.1
  199.5 0.9 slice_convert_fusion
  (80 shorter events, 20.5 us)
Async XLA Ops:
  7.2 88.0 %reduce-scatter.3.cloned.1.call-start = ((), (), s32[]{:S(2)}) async-start(), calls=%async_computation.3 | async-start | bytes 1966080 | tf_op jit(solution)/shard_map/reduce_scatter | solution.py:145
  20.9 6.3 %copy-start.7 = (bf16[16,48,512]{2,1,0:T(8,128)(2,1)}, bf16[16,48,512]{2,1,0:T(8,128)(2,1)S(1)}, u32[]{:S(2)}) copy-start(bf16[16,48,512]{2,1,0:T(8,128)(2,1)S(1)} %slice.110) | copy-start | bytes 2359300
  24.4 1.5 copy-start.15
  24.4 2.8 %copy-start.13 = (bf16[16,48,512]{2,1,0:T(8,128)(2,1)S(1)}, bf16[16,48,512]{2,1,0:T(8,128)(2,1)}, u32[]{:S(2)}) copy-start(bf16[16,48,512]{2,1,0:T(8,128)(2,1)} %slice.114) | copy-start | bytes 2359300
  24.4 2.8 %copy-start.21 = (bf16[5,512,256]{2,1,0:T(8,128)(2,1)S(1)}, bf16[5,512,256]{2,1,0:T(8,128)(2,1)}, u32[]{:S(2)}) copy-start(bf16[5,512,256]{2,1,0:T(8,128)(2,1)} %param.6) | copy-start | bytes 3932164
  27.2 1.1 copy-start.9
  27.6 1.2 copy-start.11
  29.3 0.8 copy-start.6
  56.6 4.1 %copy-start.1 = (bf16[96,8,4,256]{3,1,2,0:T(8,128)(2,1)}, bf16[96,8,4,256]{3,1,2,0:T(8,128)(2,1)S(1)}, u32[]{:S(2)}) copy-start(bf16[96,8,4,256]{3,1,2,0:T(8,128)(2,1)S(1)} %copy.23) | copy-start | bytes 4718596
  56.8 1.6 copy-start.3
  56.8 2.7 %copy-start = (bf16[5,1024,256]{2,1,0:T(8,128)(2,1)S(1)}, bf16[5,1024,256]{2,1,0:T(8,128)(2,1)}, u32[]{:S(2)}) copy-start(bf16[5,1024,256]{2,1,0:T(8,128)(2,1)} %param.7) | copy-start | bytes 7864324
  63.6 0.8 copy-start.17
  63.8 1.2 copy-start.19
  68.8 3.2 %copy-start.4 = (bf16[4,16,6,8,256]{4,3,0,2,1:T(8,128)(2,1)S(1)}, bf16[4,16,6,8,256]{4,3,0,2,1:T(8,128)(2,1)}, u32[]{:S(2)}) copy-start(bf16[4,16,6,8,256]{4,3,0,2,1:T(8,128)(2,1)} %copy-done.3) | copy-start | bytes 4718596
  68.8 3.2 %copy-start.18 = (bf16[16,48,256]{2,1,0:T(8,128)(2,1)S(1)}, bf16[16,48,256]{2,1,0:T(8,128)(2,1)}, u32[]{:S(2)}) copy-start(bf16[16,48,256]{2,1,0:T(8,128)(2,1)} %copy-done.17) | copy-start | bytes 1179652
  68.9 129.1 %reduce-scatter.5.cloned.1.call-start = ((), (), s32[]{:S(2)}) async-start(), calls=%async_computation.4 | async-start | bytes 4055040 | tf_op jit(solution)/shard_map/reduce_scatter | solution.py:50
  72.0 1.4 copy-start.5
  73.5 1.4 copy-start.2
  73.5 1.5 copy-start.20
  95.2 1.5 copy-start.8
  96.7 1.1 copy-start.16
  97.9 1.1 copy-start.14
  99.0 1.1 copy-start.10
  100.1 1.1 copy-start.12
Sparse Core Ops, SparseCore 0:
  69.0 26.1 reduce-scatter.2
  116.3 81.5 reduce-scatter.4
where the time goes:
time: 209 us; the launch traced here: 208 us
  blocking collectives  60 us (29%)
  waiting for transfers between devices  54.7 us (26%)
  local copies, waits for them, and re-layouts  46.6 us (22%)
  matrix products  16.4 us (8%)
  other arithmetic  15.4 us (7%)
  between operations  14.5 us (7%)
    reduce_scatter x1, waiting for transfers between devices, sum_packed(): lax.psum_scatter(lines, axis, tiled=True).reshape(-1)  44.7 us
    psum x4, blocking collectives, one_axis_at_a_time(): x = lax.psum(x, axis)  35.2 us
    all_to_all x1, blocking collectives, copy_for_each(): lax.all_to_all(jnp.broadcast_to(x[None], (count, *x.shape)), axis, 0, 0,...  24.9 us
    slice x5, local copies, waits for them, and re-layouts, conv_strided(): window = padded[:, tap:tap + 3 * frames - 2:3].reshape(-1, values.shape[2])  14.5 us
    reduce_scatter x1, waiting for transfers between devices, shards(): lax.psum_scatter(upstream_terms.astype(jnp.bfloat16), 'section', scatter_...  9.96 us
    unnamed x47, local copies, waits for them, and re-layouts  8.98 us
    another operation x2, local copies, waits for them, and re-layouts, weight_term(): return jnp.stack(pieces, axis=1)  5.81 us
    reshape x1, local copies, waits for them, and re-layouts, sum_packed(): jnp.pad(lines, ((0, 0), (0, span * 128 - lines.shape[1]))).reshape(-1, 128)  5.43 us
  transfers between devices with their start and end apart: 2, of which 2 were waited for; matrix products, arithmetic and copies ran while one was open for 8% of the time, Pallas kernels for 0%

commit v1 on v0

v1 whole, which is shorter than its diff:
```python
import functools

import jax
import jax.numpy as jnp
from jax import lax
from jax.experimental import pallas as pl
from jax.experimental.pallas import tpu as pltpu
from jax.sharding import Mesh
from jax.sharding import PartitionSpec as P

DP = ("dp_0", "dp_1", "dp_2")
ZY = ("dp_0", "dp_1")
F32 = jnp.float32
BF16 = jnp.bfloat16

smooth_width = 0.1
leak_slope = 0.1


def leaky(pre):
    return jnp.where(pre > 0, pre, leak_slope * pre).astype(BF16)


def fold_rows(x):
    x = jnp.sum(x.reshape(-1, 8, x.shape[1]), axis=0)
    return sum(x[:, at : at + 128] for at in range(0, x.shape[1], 128))


def difference_terms(real, fake):
    difference = real.astype(F32) - fake.astype(F32)
    root = jnp.sqrt(difference * difference + smooth_width * smooth_width)
    return difference, root


def dot(a, b):
    return jnp.dot(a, b, preferred_element_type=F32)


def dot_rows(a, b):
    return lax.dot_general(a, b, (((0,), (0,)), ((), ())), preferred_element_type=F32)


def dot_lanes(a, b):
    return lax.dot_general(a, b, (((1,), (1,)), ((), ())), preferred_element_type=F32)


def first_kernel(real, fake, w, h_real, h_fake, phases, loss, padded):
    cols, span, _ = real.shape
    frames = span // 3
    half = cols * frames
    width = w.shape[2]
    row = lax.broadcasted_iota(jnp.int32, (span, span), 0)
    col = lax.broadcasted_iota(jnp.int32, (span, span), 1)
    phase = jnp.where(row >= 2 * frames, 2, jnp.where(row >= frames, 1, 0))
    select = (col == 3 * (row - frames * phase) + phase).astype(F32).astype(BF16)
    for source, base in ((real, 0), (fake, half)):

        def split(r, carry, source=source, base=base):
            parts = dot(select, source[r]).astype(BF16)
            at = pl.multiple_of(base + r * frames, 16)
            for p in range(3):
                phases[p, pl.ds(at, frames), :] = parts[p * frames : (p + 1) * frames]
            return carry

        lax.fori_loop(0, cols, split, 0)
    padded[:, :8, :] = jnp.zeros((2 * cols, 8, width), F32)
    earlier = dot(phases[1], w[0]) + dot(phases[2], w[1])
    padded[:, 8 : 8 + frames, :] = earlier.reshape(2 * cols, frames, width)
    same = dot(phases[0], w[2]) + dot(phases[1], w[3]) + dot(phases[2], w[4])
    pre = same + padded[:, 7 : 7 + frames, :].reshape(2 * half, width)
    h = leaky(pre)
    h_real[...] = h[:half]
    h_fake[...] = h[half:]
    _, root = difference_terms(h[:half], h[half:])
    loss[...] = fold_rows(root - smooth_width)


def second_kernel(
    normaliser, s_ref, own_r, own_f, prev_r, prev_f, next_r, next_f, far_r, far_f, w,
    h_all, shifted, t_r, t_f, loss, padded,
):
    half, width = own_r.shape
    taps = w.shape[0]
    frames = padded.shape[1] - 16
    s = s_ref[0]
    for (r, f), away in (
        ((own_r, own_f), 0), ((next_r, next_f), 1), ((far_r, far_f), 2), ((prev_r, prev_f), 3)
    ):
        at = pl.multiple_of(lax.rem(s + away, 4) * width, 256)
        h_all[:half, pl.ds(at, width)] = r[...]
        h_all[half:, pl.ds(at, width)] = f[...]
    zeros = jnp.zeros((padded.shape[0], 8, width), F32)
    padded[:, :8, :] = zeros
    padded[:, 8 + frames :, :] = zeros
    pre = dot(h_all[...], w[2])
    for k in (0, 1, 3, 4):
        padded[:, 8 : 8 + frames, :] = dot(h_all[...], w[k]).reshape(-1, frames, width)
        pre = pre + padded[:, 6 + k : 6 + k + frames, :].reshape(2 * half, width)
    h = leaky(pre)
    difference, root = difference_terms(h[:half], h[half:])
    loss[...] = fold_rows(root - smooth_width)
    slope = difference / root / normaliser
    for value, sign, at in ((h[:half], 1.0, 0), (h[half:], -1.0, half // frames)):
        gate = jnp.where(value.astype(F32) > 0, 1.0, leak_slope)
        delta = (sign * slope * gate).astype(BF16).astype(F32)
        padded[at : at + half // frames, 8 : 8 + frames, :] = delta.reshape(-1, frames, width)
    for k in range(taps):
        moved = padded[:, 10 - k : 10 - k + frames, :].reshape(2 * half, width)
        shifted[:, k * width : (k + 1) * width] = moved.astype(BF16)
    at = pl.multiple_of(lax.rem(s + 2, 4) * width, 256)
    term = back_term(shifted, w, at, width)
    t_r[...] = term[:half].astype(BF16)
    t_f[...] = term[half:].astype(BF16)


def back_term(shifted, w, at, width):
    term = None
    for k in range(w.shape[0]):
        part = dot_lanes(shifted[:, k * width : (k + 1) * width], w[k, pl.ds(at, width), :])
        term = part if term is None else term + part
    return term


def back_kernel(s_ref, shifted, w, own, next_r, next_f, prev_r, prev_f):
    width = w.shape[2]
    half = next_r.shape[0]
    s = s_ref[0]
    for away in (1, 3, 0):
        at = pl.multiple_of(lax.rem(s + away, 4) * width, 256)
        term = back_term(shifted, w, at, width).astype(BF16)
        if away == 0:
            own[...] = term
        else:
            r, f = (next_r, next_f) if away == 1 else (prev_r, prev_f)
            r[...] = term[:half]
            f[...] = term[half:]


def put(g, c, mine, theirs, at, k):
    rows = mine.shape[2]
    count = g.shape[0] // (2 * rows)
    g = g.astype(BF16).reshape(count, 2, rows, g.shape[1])
    even, odd = g[:, 0], g[:, 1]
    mine[at : at + count, k] = jnp.where(c == 0, even, odd)
    theirs[at : at + count, k] = jnp.where(c == 0, odd, even)


def weight_second_kernel(c_ref, h_all, shifted, mine, theirs):
    width = mine.shape[3]
    c = c_ref[0]
    step = 256
    for q in range(h_all.shape[1] // step):
        g = dot_rows(h_all[:, q * step : (q + 1) * step], shifted[...])
        for k in range(mine.shape[1]):
            put(g[:, k * width : (k + 1) * width], c, mine, theirs,
                q * step // (2 * mine.shape[2]), k)


def weight_first_kernel(
    normaliser, c_ref, h_real, h_fake, own, from_prev_r, from_prev_f, from_next_r, from_next_f,
    phases, mine, theirs, padded, moved,
):
    half, width = h_real.shape
    frames = padded.shape[1] - 8
    c = c_ref[0]
    difference, root = difference_terms(h_real[...], h_fake[...])
    slope = difference / root / normaliser
    padded[:, frames:, :] = jnp.zeros((padded.shape[0], 8, width), F32)
    for h, a, b, sign, at in (
        (h_real, from_prev_r, from_next_r, 1.0, 0), (h_fake, from_prev_f, from_next_f, -1.0, half)
    ):
        up = own[at : at + half, :].astype(F32) + a[...].astype(F32) + b[...].astype(F32)
        up = up.astype(BF16).astype(F32)
        gate = jnp.where(h[...].astype(F32) > 0, 1.0, leak_slope)
        delta = ((sign * slope + up) * gate).astype(BF16)
        moved[at : at + half, :width] = delta
        cols = half // frames
        lead = at // frames
        padded[lead : lead + cols, :frames, :] = delta.astype(F32).reshape(cols, frames, width)
    moved[:, width:] = padded[:, 1 : 1 + frames, :].reshape(2 * half, width).astype(BF16)
    for p in range(3):
        if p == 0:
            put(dot_rows(phases[p], moved[:, :width]), c, mine, theirs, 0, 2)
        else:
            g = dot_rows(phases[p], moved[...])
            put(g[:, :width], c, mine, theirs, 0, 2 + p)
            put(g[:, width:], c, mine, theirs, 0, p - 1)


def total_kernel(blocks, out):
    total = jnp.sum(blocks[...].astype(F32), axis=0)
    for k in range(total.shape[0]):
        out[:, k, :] = total[k]


def call(kernel, operands, outs, scratch=(), smem=0, flops=0, name=None):
    moved = sum(x.size * x.dtype.itemsize for x in operands)
    moved += sum(x.size * x.dtype.itemsize for x in outs)
    vmem, small = pl.BlockSpec(memory_space=pltpu.VMEM), pl.BlockSpec(memory_space=pltpu.SMEM)
    return pl.pallas_call(
        kernel,
        out_shape=outs,
        in_specs=[small if at < smem else vmem for at in range(len(operands))],
        out_specs=[vmem] * len(outs),
        scratch_shapes=list(scratch),
        compiler_params=pltpu.CompilerParams(vmem_limit_bytes=40 << 20),
        cost_estimate=pl.CostEstimate(flops=flops, bytes_accessed=moved, transcendentals=0),
        name=name,
    )(*operands)


def like(shape, dtype=BF16):
    return jax.ShapeDtypeStruct(shape, dtype)


def turn(x, step):
    count = lax.axis_size("section")
    return lax.ppermute(x, "section", [(i, (i + step) % count) for i in range(count)])


def across(x, axis, mask):
    return lax.ppermute(x, axis, [(i, i ^ mask) for i in range(lax.axis_size(axis))])


def add(*terms):
    return sum(t.astype(F32) for t in terms).astype(BF16)


def over_dp(mine, theirs, rows, taps, width):
    half = add(mine, across(theirs, "dp_2", 1))
    blocks = lax.all_to_all(half, ZY, 0, 0)
    return call(total_kernel, (blocks,), [like((rows, taps, width), F32)], name="total")[0]


def shards(real_in, fake_in, kernel_first, kernel_second):
    replicas = lax.axis_size(DP)
    cols, span, in_width = real_in.shape
    frames = span // 3
    taps, width_all, width = kernel_second.shape
    half = cols * frames
    rows = 2 * half
    normaliser = float(cols * frames)
    count_all = float(cols * replicas * frames * width_all)
    groups = replicas // 2
    s = lax.axis_index("section").reshape(1).astype(jnp.int32)
    c = lax.axis_index("dp_2").reshape(1).astype(jnp.int32)

    h_real, h_fake, phases, loss_first = call(
        first_kernel,
        (real_in, fake_in, kernel_first),
        [like((half, width)), like((half, width)), like((3, rows, in_width)), like((8, 128), F32)],
        [pltpu.VMEM((2 * cols, frames + 8, width), F32)],
        flops=2 * rows * taps * in_width * width,
        name="first",
    )
    prev_r = turn(h_real, 1)
    next_f = turn(h_fake, -1)
    prev_f = turn(h_fake, 1)
    next_r = turn(h_real, -1)
    far_r = turn(prev_r, 1)
    far_f = turn(next_f, -1)
    h_all, shifted, far_t_r, far_t_f, loss_second = call(
        functools.partial(second_kernel, normaliser),
        (s, h_real, h_fake, prev_r, prev_f, next_r, next_f, far_r, far_f, kernel_second),
        [like((rows, width_all)), like((rows, taps * width)), like((half, width)),
         like((half, width)), like((8, 128), F32)],
        [pltpu.VMEM((2 * cols, frames + 16, width), F32)],
        smem=1,
        flops=2 * rows * taps * (width_all + width) * width,
        name="second",
    )
    pass_r = turn(far_t_r, 1)
    pass_f = turn(far_t_f, -1)
    own_t, next_t_r, next_t_f, prev_t_r, prev_t_f = call(
        back_kernel,
        (s, shifted, kernel_second),
        [like((rows, width))] + [like((half, width))] * 4,
        smem=1,
        flops=2 * rows * taps * width * width * 3,
        name="back",
    )
    from_prev_f = turn(next_t_f, 1)
    from_next_r = turn(prev_t_r, -1)
    from_prev_r = turn(add(next_t_r, pass_r), 1)
    from_next_f = turn(add(prev_t_f, pass_f), -1)

    own_rows = width_all // replicas
    mine, theirs = call(
        weight_second_kernel,
        (c, h_all, shifted),
        [like((groups, taps, own_rows, width))] * 2,
        smem=1,
        flops=2 * rows * taps * width * width_all,
        name="weight_second",
    )
    grad_second = over_dp(mine, theirs, own_rows, taps, width)

    own_rows = in_width // replicas
    mine, theirs = call(
        functools.partial(weight_first_kernel, normaliser),
        (c, h_real, h_fake, own_t, from_prev_r, from_prev_f, from_next_r, from_next_f, phases),
        [like((groups, taps, own_rows, width))] * 2,
        [pltpu.VMEM((2 * cols, frames + 8, width), F32), pltpu.VMEM((rows, 2 * width), BF16)],
        smem=1,
        flops=2 * rows * taps * width * in_width,
        name="weight_first",
    )
    grad_first = over_dp(mine, theirs, own_rows, taps, width)

    losses = jnp.concatenate([loss_first, loss_second], axis=0)
    for axis, mask in (
        ("dp_2", 1), ("section", 1), ("section", 3), ("dp_1", 1), ("dp_1", 3), ("dp_0", 1),
        ("dp_0", 3),
    ):
        losses = losses + across(losses, axis, mask)
    layer_loss = jnp.sum(losses.reshape(2, 8 * 128), axis=1) / count_all
    return (layer_loss, grad_first, grad_second)


def solution(mesh):
    finer = Mesh(
        mesh.devices.reshape(4, 4, 2, mesh.shape["section"]), ("dp_0", "dp_1", "dp_2", "section")
    )
    return jax.shard_map(
        shards,
        mesh=finer,
        in_specs=(
            P(DP, None, None),
            P(DP, None, None),
            P(None, None, "section"),
            P(None, None, "section"),
        ),
        out_specs=(P(), P(DP, None, "section"), P(DP, None, "section")),
        check_vma=False,
    )
```

time: 209 us -> 123 us (0.59)
  blocking collectives: 60 us -> 0 us
  starting transfers between devices: 0.3 us -> 40.3 us
  local copies, waits for them, and re-layouts: 46.6 us -> 12.2 us
  Pallas kernels: 0 us -> 18.6 us
  matrix products: 16.4 us -> 0 us
  between operations: 14.5 us -> 0.78 us
  waiting for transfers between devices: 54.7 us -> 44.4 us
  other arithmetic: 15.4 us -> 6.19 us
    reduce_scatter x2 -> x0, waiting for transfers between devices: 54.7 us -> none  [the longest x1 44.7 us: sum_packed(): lax.psum_scatter(lines, axis, tiled=True).reshape(-1)]
    psum x4 -> x0, blocking collectives: 35.2 us -> none  [one_axis_at_a_time(): x = lax.psum(x, axis)]
    ppermute x0 -> x21, waiting for transfers between devices: none -> 33.9 us  [the longest x9 22.6 us: across(): lax.ppermute(x, axis, [(i, i ^ mask) for i in range(lax.axis_size(axis))])]
    ppermute x0 -> x21, starting transfers between devices: none -> 28.6 us  [the longest x12 19.8 us: turn(): lax.ppermute(x, 'section', [(i, (i + step) % count) for i in range(count)])]
    all_to_all x1 -> x0, blocking collectives: 24.9 us -> none  [copy_for_each(): lax.all_to_all(jnp.broadcast_to(x[None], (count, *x.shape)), axis, 0, 0,...]
    pallas_call x0 -> x7, Pallas kernels: none -> 18.6 us  [call(): pl.pallas_call(kernel, out_shape=outs, in_specs=[small if at < smem else...]
    slice x7 -> x0, local copies, waits for them, and re-layouts: 16.5 us -> none  [the longest x5 14.5 us: conv_strided(): window = padded[:, tap:tap + 3 * frames - 2:3].reshape(-1, values.shape[2])]
    dot_general x25 -> x0, matrix products: 16.4 us -> none  [the longest x10 5.22 us: weight_term(): lax.dot_general(window, flat_delta, (((0,), (0,)), ((), ())), preferred_e...]
  transfers between devices with their start and end apart: 2 -> 23, of which waited for: 2 -> 15; matrix products, arithmetic and copies ran while one was open for 8% -> 6% of each run, Pallas kernels for 0% -> 7%
where the time goes in v1:
time: 123 us
  waiting for transfers between devices  44.4 us (36%)
  starting transfers between devices  40.3 us (33%)
  Pallas kernels  18.6 us (15%)
  local copies, waits for them, and re-layouts  12.2 us (10%)
  other arithmetic  6.19 us (5%)
    ppermute x9, waiting for transfers between devices, across(): lax.ppermute(x, axis, [(i, i ^ mask) for i in range(lax.axis_size(axis))])  22.6 us
    ppermute x12, starting transfers between devices, turn(): lax.ppermute(x, 'section', [(i, (i + step) % count) for i in range(count)])  19.8 us
    pallas_call x7, Pallas kernels, call(): pl.pallas_call(kernel, out_shape=outs, in_specs=[small if at < smem else...  18.6 us
    unnamed x25, local copies, waits for them, and re-layouts  12.1 us
    all_to_all x2, starting transfers between devices, over_dp(): blocks = lax.all_to_all(half, ZY, 0, 0)  11.8 us
    ppermute x12, waiting for transfers between devices, turn(): lax.ppermute(x, 'section', [(i, (i + step) % count) for i in range(count)])  11.3 us
    all_to_all x2, waiting for transfers between devices, over_dp(): blocks = lax.all_to_all(half, ZY, 0, 0)  10.5 us
    ppermute x9, starting transfers between devices, across(): lax.ppermute(x, axis, [(i, i ^ mask) for i in range(lax.axis_size(axis))])  8.79 us
  transfers between devices with their start and end apart: 23, of which 15 were waited for; matrix products, arithmetic and copies ran while one was open for 6% of the time, Pallas kernels for 7%

profile of v1, /device:TPU:0, one launch (start us, length us, event | category | flops | bytes accessed | tf_op | source)
XLA Modules:
  0.0 122.5 jit_solution(10764458682191885343)
XLA Ops:
  4.5 4.3 %first.1 = (bf16[384,256]{1,0:T(8,128)(2,1)S(1)}, bf16[384,256]{1,0:T(8,128)(2,1)S(1)}, bf16[3,768,512]{2,1,0:T(8,128)(2,1)S(1)}, f32[8,128]{1,0:T(8,128)S(1)}) custom-call(bf16[8,144,512]{2,1,0:T(8,128)(2,1)S(1)} %copy-done.5, bf16[8,144,512]{2,1,0:T(8,128)(2,1)S(1)} %copy-done.6, bf16[5,512,256]{2,1,0:T(8,128)(2,1)S(1)} %copy-done.4), custom_call_target="tpu_custom_call" | custom-call | flops 1006632960 | bytes 6426624 | tf_op jit(solution)/shard_map/first/pallas_call | solution.py:200
  8.8 1.6 %collective-permute-start = (bf16[384,256]{1,0:T(8,128)(2,1)S(1)}, bf16[384,256]{1,0:T(8,128)(2,1)S(1)}, u32[]{:S(2)}, u32[]{:S(2)}) collective-permute-start(bf16[384,256]{1,0:T(8,128)(2,1)S(1)} %get-tuple-element.22.own_r.h_real), channel_id=1, source_target_pairs={{0,1},{1,2},{2,3},{3,0},{4,5},{5,6},{6,7},{7,4},{8,9},{9,10},{10,1... | collective-permute-start | bytes 589832 | tf_op jit(solution)/shard_map/ppermute | solution.py:218
  10.4 1.7 %collective-permute-start.3 = (bf16[384,256]{1,0:T(8,128)(2,1)S(1)}, bf16[384,256]{1,0:T(8,128)(2,1)S(1)}, u32[]{:S(2)}, u32[]{:S(2)}) collective-permute-start(bf16[384,256]{1,0:T(8,128)(2,1)S(1)} %get-tuple-element.23.own_f.h_fake), channel_id=1, source_target_pairs={{0,3},{1,0},{2,1},{3,2},{4,7},{5,4},{6,5},{7,6},{8,11},{9,8},{10,9... | collective-permute-start | bytes 589832 | tf_op jit(solution)/shard_map/ppermute | solution.py:218
  12.4 2.9 %collective-permute-start.2 = (bf16[384,256]{1,0:T(8,128)(2,1)S(1)}, bf16[384,256]{1,0:T(8,128)(2,1)S(1)}, u32[]{:S(2)}, u32[]{:S(2)}) collective-permute-start(bf16[384,256]{1,0:T(8,128)(2,1)S(1)} %get-tuple-element.22.own_r.h_real), channel_id=1, source_target_pairs={{0,3},{1,0},{2,1},{3,2},{4,7},{5,4},{6,5},{7,6},{8,11},{9,8},{10,9... | collective-permute-start | bytes 589832 | tf_op jit(solution)/shard_map/ppermute | solution.py:218
  15.3 2.5 %collective-permute-done.prev_r = bf16[384,256]{1,0:T(8,128)(2,1)S(1)} collective-permute-done((bf16[384,256]{1,0:T(8,128)(2,1)S(1)}, bf16[384,256]{1,0:T(8,128)(2,1)S(1)}, u32[]{:S(2)}, u32[]{:S(2)}) %collective-permute-start) | collective-permute-done | bytes 196640 | tf_op jit(solution)/shard_map/ppermute | solution.py:218
  18.2 2.9 %collective-permute-start.5 = (bf16[384,256]{1,0:T(8,128)(2,1)S(1)}, bf16[384,256]{1,0:T(8,128)(2,1)}, u32[]{:S(2)}, u32[]{:S(2)}) collective-permute-start(bf16[384,256]{1,0:T(8,128)(2,1)S(1)} %collective-permute-done.3.next_f), channel_id=1, source_target_pairs={{0,3},{1,0},{2,1},{3,2},{4,7},{5,4},{6,5},{7,6},{8,11},{9,8},{10,9... | collective-permute-start | bytes 589832 | tf_op jit(solution)/shard_map/ppermute | solution.py:218
  22.5 2.7 %collective-permute-done.4.far_r = bf16[384,256]{1,0:T(8,128)(2,1)} collective-permute-done((bf16[384,256]{1,0:T(8,128)(2,1)S(1)}, bf16[384,256]{1,0:T(8,128)(2,1)}, u32[]{:S(2)}, u32[]{:S(2)}) %collective-permute-start.4) | collective-permute-done | bytes 196640 | tf_op jit(solution)/shard_map/ppermute | solution.py:218
  25.3 1.7 %copy-done.2 = bf16[5,1024,256]{2,1,0:T(8,128)(2,1)S(1)} copy-done((bf16[5,1024,256]{2,1,0:T(8,128)(2,1)S(1)}, bf16[5,1024,256]{2,1,0:T(8,128)(2,1)}, u32[]{:S(2)}) %copy-start.2) | copy-done | bytes 2621464
  27.0 5.6 %second.1 = (bf16[768,1024]{1,0:T(8,128)(2,1)S(1)}, bf16[768,1280]{1,0:T(8,128)(2,1)S(1)}, bf16[384,256]{1,0:T(8,128)(2,1)S(1)}, bf16[384,256]{1,0:T(8,128)(2,1)S(1)}, f32[8,128]{1,0:T(8,128)S(1)}) custom-call(s32[1]{0:T(128)} %bitcast.s_ref, bf16[384,256]{1,0:T(8,128)(2,1)S(1)} %get-tuple-element.22.own_r.h_real, ...), custom_call_target="tpu_custom_call" | custom-call | flops 2516582400 | bytes 8130564 | tf_op jit(solution)/shard_map/second/pallas_call | solution.py:200
  35.3 2.4 %back.1 = (bf16[768,256]{1,0:T(8,128)(2,1)S(1)}, bf16[384,256]{1,0:T(8,128)(2,1)S(1)}, bf16[384,256]{1,0:T(8,128)(2,1)}, bf16[384,256]{1,0:T(8,128)(2,1)}, bf16[384,256]{1,0:T(8,128)(2,1)S(1)}) custom-call(s32[1]{0:T(128)} %bitcast.s_ref, bf16[768,1280]{1,0:T(8,128)(2,1)S(1)} %get-tuple-element.25.shifted, bf16[5,1024,256]{2,1,0:T(8,128)(2,1)S(1)} %copy-done.3), custom_call_target="tpu_custom_call" | custom-call | flops 1509949440 | bytes 5767172 | tf_op jit(solution)/shard_map/back/pallas_call | solution.py:200
  38.8 2.0 %collective-permute-start.16 = (bf16[384,256]{1,0:T(8,128)(2,1)}, bf16[384,256]{1,0:T(8,128)(2,1)S(1)}, u32[]{:S(2)}, u32[]{:S(2)}) collective-permute-start(bf16[384,256]{1,0:T(8,128)(2,1)} %get-tuple-element.30), channel_id=1, source_target_pairs={{0,3},{1,0},{2,1},{3,2},{4,7},{5,4},{6,5},{7,6},{8,11},{9,8},{10,9... | collective-permute-start | bytes 589832 | tf_op jit(solution)/shard_map/ppermute | solution.py:218
  42.2 1.5 %collective-permute-start.14 = (bf16[384,256]{1,0:T(8,128)(2,1)}, bf16[384,256]{1,0:T(8,128)(2,1)}, u32[]{:S(2)}, u32[]{:S(2)}) collective-permute-start(bf16[384,256]{1,0:T(8,128)(2,1)} %add_convert_fusion.3), channel_id=1, source_target_pairs={{0,1},{1,2},{2,3},{3,0},{4,5},{5,6},{6,7},{7,4},{8,9},{9,10},{10,1... | collective-permute-start | bytes 589832 | tf_op jit(solution)/shard_map/ppermute | solution.py:218
  43.6 4.5 %collective-permute-done.17 = bf16[384,256]{1,0:T(8,128)(2,1)S(1)} collective-permute-done((bf16[384,256]{1,0:T(8,128)(2,1)S(1)}, bf16[384,256]{1,0:T(8,128)(2,1)S(1)}, u32[]{:S(2)}, u32[]{:S(2)}) %collective-permute-start.17) | collective-permute-done | bytes 196640 | tf_op jit(solution)/shard_map/ppermute | solution.py:218
  48.9 3.2 %collective-permute-start.18 = (bf16[384,256]{1,0:T(8,128)(2,1)}, bf16[384,256]{1,0:T(8,128)(2,1)}, u32[]{:S(2)}, u32[]{:S(2)}) collective-permute-start(bf16[384,256]{1,0:T(8,128)(2,1)} %add_convert_fusion.2), channel_id=1, source_target_pairs={{0,3},{1,0},{2,1},{3,2},{4,7},{5,4},{6,5},{7,6},{8,11},{9,8},{10,9... | collective-permute-start | bytes 589832 | tf_op jit(solution)/shard_map/ppermute | solution.py:218
  52.1 1.5 %copy-done.8 = bf16[768,1280]{1,0:T(8,128)(2,1)S(1)} copy-done((bf16[768,1280]{1,0:T(8,128)(2,1)S(1)}, bf16[768,1280]{1,0:T(8,128)(2,1)}, u32[]{:S(2)}) %copy-start.8) | copy-done | bytes 1966104
  55.1 3.3 %weight_second.1 = (bf16[16,5,32,256]{3,2,1,0:T(8,128)(2,1)S(1)}, bf16[16,5,32,256]{3,2,1,0:T(8,128)(2,1)}) custom-call(s32[1]{0:T(128)} %bitcast.1.c_ref, bf16[768,1024]{1,0:T(8,128)(2,1)S(1)} %copy-done.10, bf16[768,1280]{1,0:T(8,128)(2,1)S(1)} %copy-done.8), custom_call_target="tpu_custom_call" | custom-call | flops 2013265920 | bytes 6160388 | tf_op jit(solution)/shard_map/weight_second/pallas_call | solution.py:200
  59.5 2.7 %weight_first.1 = (bf16[16,5,16,256]{3,2,1,0:T(8,128)(2,1)S(1)}, bf16[16,5,16,256]{3,2,1,0:T(8,128)(2,1)S(1)}) custom-call(s32[1]{0:T(128)} %bitcast.1.c_ref, bf16[384,256]{1,0:T(8,128)(2,1)S(1)} %get-tuple-element.22.own_r.h_real, bf16[384,256]{1,0:T(8,128)(2,1)S(1)} %get-tuple-element.23.own_f.h_fake, bf16[768,256]{1,0:T(8,128)(2,1)S(1)} %get-tuple-element.26.own, ...), custom_call_target="tpu_custom_call" | custom-call | flops 1006632960 | bytes 5242884 | tf_op jit(solution)/shard_map/weight_first/pallas_call | solution.py:200
  62.8 1.7 %collective-permute-done.19 = bf16[16,5,16,256]{3,2,1,0:T(8,128)(2,1)S(1)} collective-permute-done((bf16[16,5,16,256]{3,2,1,0:T(8,128)(2,1)S(1)}, bf16[16,5,16,256]{3,2,1,0:T(8,128)(2,1)S(1)}, u32[]{:S(2)}, u32[]{:S(2)}) %collective-permute-start.19) | collective-permute-done | bytes 655392 | tf_op jit(solution)/shard_map/ppermute | solution.py:222
  65.6 8.1 %all-to-all-start = ((bf16[16,5,16,256]{3,2,1,0:T(8,128)(2,1)}), bf16[16,5,16,256]{3,2,1,0:T(8,128)(2,1)S(1)}, u32[]{:S(2)}, u32[]{:S(2)}) async-start(bf16[16,5,16,256]{3,2,1,0:T(8,128)(2,1)} %add_convert_fusion.1), calls=%async_computation | async-start | bytes 1310720 | tf_op jit(solution)/shard_map/all_to_all | solution.py:231
  73.7 2.9 %add_convert_fusion = bf16[16,5,32,256]{3,2,1,0:T(8,128)(2,1)} fusion(bf16[16,5,32,256]{3,2,1,0:T(8,128)(2,1)} %collective-permute-done.20, bf16[16,5,32,256]{3,2,1,0:T(8,128)(2,1)S(1)} %copy-done.1), kind=kLoop, calls=%fused_computation | loop fusion | flops 2621440 | bytes 3932160 | tf_op jit(solution)/shard_map/convert_element_type | solution.py:226
  76.6 10.5 %all-to-all-done.blocks = bf16[16,5,16,256]{3,2,1,0:T(8,128)(2,1)S(1)} async-done(((bf16[16,5,16,256]{3,2,1,0:T(8,128)(2,1)}), bf16[16,5,16,256]{3,2,1,0:T(8,128)(2,1)S(1)}, u32[]{:S(2)}, u32[]{:S(2)}) %all-to-all-start) | async-done | bytes 655392 | tf_op jit(solution)/shard_map/all_to_all | solution.py:231
  87.1 3.7 %all-to-all-start.1 = ((bf16[16,5,32,256]{3,2,1,0:T(8,128)(2,1)}), bf16[16,5,32,256]{3,2,1,0:T(8,128)(2,1)S(1)}, u32[]{:S(2)}, u32[]{:S(2)}) async-start(bf16[16,5,32,256]{3,2,1,0:T(8,128)(2,1)} %add_convert_fusion), calls=%async_computation.1 | async-start | bytes 2621440 | tf_op jit(solution)/shard_map/all_to_all | solution.py:231
  92.1 3.6 %collective-permute-done.7 = f32[16,128]{1,0:T(8,128)S(1)} collective-permute-done((f32[16,128]{1,0:T(8,128)S(1)}, f32[16,128]{1,0:T(8,128)S(1)}, u32[]{:S(2)}, u32[]{:S(2)}) %collective-permute-start.7) | collective-permute-done | bytes 8224 | tf_op jit(solution)/shard_map/ppermute | solution.py:222
  95.7 4.9 %collective-permute-done.8 = f32[16,128]{1,0:T(8,128)S(1)} collective-permute-done((f32[16,128]{1,0:T(8,128)S(1)}, f32[16,128]{1,0:T(8,128)S(1)}, u32[]{:S(2)}, u32[]{:S(2)}) %collective-permute-start.8) | collective-permute-done | bytes 8224 | tf_op jit(solution)/shard_map/ppermute | solution.py:222
  100.6 1.8 %collective-permute-start.9 = (f32[16,128]{1,0:T(8,128)S(1)}, f32[16,128]{1,0:T(8,128)S(1)}, u32[]{:S(2)}, u32[]{:S(2)}) collective-permute-start(f32[16,128]{1,0:T(8,128)S(1)} %add.35), channel_id=1, source_target_pairs={{0,8},{8,0},{16,24},{24,16},{1,9},{9,1},{17,25},{25,17},{2,10},{10... | collective-permute-start | bytes 24584 | tf_op jit(solution)/shard_map/ppermute | solution.py:222
  102.4 4.2 %collective-permute-done.9 = f32[16,128]{1,0:T(8,128)S(1)} collective-permute-done((f32[16,128]{1,0:T(8,128)S(1)}, f32[16,128]{1,0:T(8,128)S(1)}, u32[]{:S(2)}, u32[]{:S(2)}) %collective-permute-start.9) | collective-permute-done | bytes 8224 | tf_op jit(solution)/shard_map/ppermute | solution.py:222
  106.6 2.1 %collective-permute-start.10 = (f32[16,128]{1,0:T(8,128)S(1)}, f32[16,128]{1,0:T(8,128)S(1)}, u32[]{:S(2)}, u32[]{:S(2)}) collective-permute-start(f32[16,128]{1,0:T(8,128)S(1)} %add.36), channel_id=1, source_target_pairs={{0,24},{8,16},{16,8},{24,0},{1,25},{9,17},{17,9},{25,1},{2,26},{10... | collective-permute-start | bytes 24584 | tf_op jit(solution)/shard_map/ppermute | solution.py:222
  108.7 2.8 %collective-permute-done.10 = f32[16,128]{1,0:T(8,128)S(1)} collective-permute-done((f32[16,128]{1,0:T(8,128)S(1)}, f32[16,128]{1,0:T(8,128)S(1)}, u32[]{:S(2)}, u32[]{:S(2)}) %collective-permute-start.10) | collective-permute-done | bytes 8224 | tf_op jit(solution)/shard_map/ppermute | solution.py:222
  111.5 1.5 %collective-permute-start.11 = (f32[16,128]{1,0:T(8,128)S(1)}, f32[16,128]{1,0:T(8,128)S(1)}, u32[]{:S(2)}, u32[]{:S(2)}) collective-permute-start(f32[16,128]{1,0:T(8,128)S(1)} %add.37), channel_id=1, source_target_pairs={{0,32},{32,0},{64,96},{96,64},{1,33},{33,1},{65,97},{97,65},{2,34}... | collective-permute-start | bytes 24584 | tf_op jit(solution)/shard_map/ppermute | solution.py:222
  113.0 2.2 %collective-permute-done.11 = f32[16,128]{1,0:T(8,128)S(1)} collective-permute-done((f32[16,128]{1,0:T(8,128)S(1)}, f32[16,128]{1,0:T(8,128)S(1)}, u32[]{:S(2)}, u32[]{:S(2)}) %collective-permute-start.11) | collective-permute-done | bytes 8224 | tf_op jit(solution)/shard_map/ppermute | solution.py:222
  115.1 2.8 %collective-permute-start.12 = (f32[16,128]{1,0:T(8,128)S(1)}, f32[16,128]{1,0:T(8,128)S(1)}, u32[]{:S(2)}, u32[]{:S(2)}) collective-permute-start(f32[16,128]{1,0:T(8,128)S(1)} %add.38), channel_id=1, source_target_pairs={{0,96},{32,64},{64,32},{96,0},{1,97},{33,65},{65,33},{97,1},{2,98}... | collective-permute-start | bytes 24584 | tf_op jit(solution)/shard_map/ppermute | solution.py:222
  117.9 2.1 %collective-permute-done.12 = f32[16,128]{1,0:T(8,128)S(1)} collective-permute-done((f32[16,128]{1,0:T(8,128)S(1)}, f32[16,128]{1,0:T(8,128)S(1)}, u32[]{:S(2)}, u32[]{:S(2)}) %collective-permute-start.12) | collective-permute-done | bytes 8224 | tf_op jit(solution)/shard_map/ppermute | solution.py:222
  (61 shorter events, 19.9 us)
Async XLA Ops:
  0.6 1.3 %copy-start.4 = (bf16[5,512,256]{2,1,0:T(8,128)(2,1)S(1)}, bf16[5,512,256]{2,1,0:T(8,128)(2,1)}, u32[]{:S(2)}) copy-start(bf16[5,512,256]{2,1,0:T(8,128)(2,1)} %w.3) | copy-start | bytes 3932164
  1.9 1.3 %copy-start.5 = (bf16[8,144,512]{2,1,0:T(8,128)(2,1)S(1)}, bf16[8,144,512]{2,1,0:T(8,128)(2,1)}, u32[]{:S(2)}) copy-start(bf16[8,144,512]{2,1,0:T(8,128)(2,1)} %real.1) | copy-start | bytes 3538948
  3.2 1.3 %copy-start.6 = (bf16[8,144,512]{2,1,0:T(8,128)(2,1)S(1)}, bf16[8,144,512]{2,1,0:T(8,128)(2,1)}, u32[]{:S(2)}) copy-start(bf16[8,144,512]{2,1,0:T(8,128)(2,1)} %fake.1) | copy-start | bytes 3538948
  8.8 9.1 %collective-permute-start = (bf16[384,256]{1,0:T(8,128)(2,1)S(1)}, bf16[384,256]{1,0:T(8,128)(2,1)S(1)}, u32[]{:S(2)}, u32[]{:S(2)}) collective-permute-start(bf16[384,256]{1,0:T(8,128)(2,1)S(1)} %get-tuple-element.22.own_r.h_real), channel_id=1, source_target_pairs={{0,1},{1,2},{2,3},{3,0},{4,5},{5,6},{6,7},{7,4},{8,9},{9,10},{10,1... | collective-permute-start | bytes 589832 | tf_op jit(solution)/shard_map/ppermute | solution.py:218
  10.4 7.8 %collective-permute-start.3 = (bf16[384,256]{1,0:T(8,128)(2,1)S(1)}, bf16[384,256]{1,0:T(8,128)(2,1)S(1)}, u32[]{:S(2)}, u32[]{:S(2)}) collective-permute-start(bf16[384,256]{1,0:T(8,128)(2,1)S(1)} %get-tuple-element.23.own_f.h_fake), channel_id=1, source_target_pairs={{0,3},{1,0},{2,1},{3,2},{4,7},{5,4},{6,5},{7,6},{8,11},{9,8},{10,9... | collective-permute-start | bytes 589832 | tf_op jit(solution)/shard_map/ppermute | solution.py:218
  12.1 10.0 %collective-permute-start.1 = (bf16[384,256]{1,0:T(8,128)(2,1)S(1)}, bf16[384,256]{1,0:T(8,128)(2,1)S(1)}, u32[]{:S(2)}, u32[]{:S(2)}) collective-permute-start(bf16[384,256]{1,0:T(8,128)(2,1)S(1)} %get-tuple-element.23.own_f.h_fake), channel_id=1, source_target_pairs={{0,1},{1,2},{2,3},{3,0},{4,5},{5,6},{6,7},{7,4},{8,9},{9,10},{10,1... | collective-permute-start | bytes 589832 | tf_op jit(solution)/shard_map/ppermute | solution.py:218
  12.4 10.0 %collective-permute-start.2 = (bf16[384,256]{1,0:T(8,128)(2,1)S(1)}, bf16[384,256]{1,0:T(8,128)(2,1)S(1)}, u32[]{:S(2)}, u32[]{:S(2)}) collective-permute-start(bf16[384,256]{1,0:T(8,128)(2,1)S(1)} %get-tuple-element.22.own_r.h_real), channel_id=1, source_target_pairs={{0,3},{1,0},{2,1},{3,2},{4,7},{5,4},{6,5},{7,6},{8,11},{9,8},{10,9... | collective-permute-start | bytes 589832 | tf_op jit(solution)/shard_map/ppermute | solution.py:218
  17.9 7.3 %collective-permute-start.4 = (bf16[384,256]{1,0:T(8,128)(2,1)S(1)}, bf16[384,256]{1,0:T(8,128)(2,1)}, u32[]{:S(2)}, u32[]{:S(2)}) collective-permute-start(bf16[384,256]{1,0:T(8,128)(2,1)S(1)} %collective-permute-done.prev_r), channel_id=1, source_target_pairs={{0,1},{1,2},{2,3},{3,0},{4,5},{5,6},{6,7},{7,4},{8,9},{9,10},{10,1... | collective-permute-start | bytes 589832 | tf_op jit(solution)/shard_map/ppermute | solution.py:218
  18.2 7.1 %collective-permute-start.5 = (bf16[384,256]{1,0:T(8,128)(2,1)S(1)}, bf16[384,256]{1,0:T(8,128)(2,1)}, u32[]{:S(2)}, u32[]{:S(2)}) collective-permute-start(bf16[384,256]{1,0:T(8,128)(2,1)S(1)} %collective-permute-done.3.next_f), channel_id=1, source_target_pairs={{0,3},{1,0},{2,1},{3,2},{4,7},{5,4},{6,5},{7,6},{8,11},{9,8},{10,9... | collective-permute-start | bytes 589832 | tf_op jit(solution)/shard_map/ppermute | solution.py:218
  25.3 1.7 %copy-start.2 = (bf16[5,1024,256]{2,1,0:T(8,128)(2,1)S(1)}, bf16[5,1024,256]{2,1,0:T(8,128)(2,1)}, u32[]{:S(2)}) copy-start(bf16[5,1024,256]{2,1,0:T(8,128)(2,1)} %w.5) | copy-start | bytes 7864324
  27.0 8.2 %copy-start.3 = (bf16[5,1024,256]{2,1,0:T(8,128)(2,1)S(1)}, bf16[5,1024,256]{2,1,0:T(8,128)(2,1)}, u32[]{:S(2)}) copy-start(bf16[5,1024,256]{2,1,0:T(8,128)(2,1)} %w.5) | copy-start | bytes 7864324
  33.8 3.9 %copy-start.7 = (bf16[768,1280]{1,0:T(8,128)(2,1)}, bf16[768,1280]{1,0:T(8,128)(2,1)S(1)}, u32[]{:S(2)}) copy-start(bf16[768,1280]{1,0:T(8,128)(2,1)S(1)} %get-tuple-element.25.shifted) | copy-start | bytes 5898244
  33.8 7.6 %collective-permute-start.13 = (bf16[384,256]{1,0:T(8,128)(2,1)S(1)}, bf16[384,256]{1,0:T(8,128)(2,1)S(1)}, u32[]{:S(2)}, u32[]{:S(2)}) collective-permute-start(bf16[384,256]{1,0:T(8,128)(2,1)S(1)} %get-tuple-element.28), channel_id=1, source_target_pairs={{0,1},{1,2},{2,3},{3,0},{4,5},{5,6},{6,7},{7,4},{8,9},{9,10},{10,1... | collective-permute-start | bytes 589832 | tf_op jit(solution)/shard_map/ppermute | solution.py:218
  37.6 21.9 %collective-permute-start.15 = (bf16[384,256]{1,0:T(8,128)(2,1)}, bf16[384,256]{1,0:T(8,128)(2,1)S(1)}, u32[]{:S(2)}, u32[]{:S(2)}) collective-permute-start(bf16[384,256]{1,0:T(8,128)(2,1)} %get-tuple-element.29), channel_id=1, source_target_pairs={{0,1},{1,2},{2,3},{3,0},{4,5},{5,6},{6,7},{7,4},{8,9},{9,10},{10,1... | collective-permute-start | bytes 589832 | tf_op jit(solution)/shard_map/ppermute | solution.py:218
  38.8 20.7 %collective-permute-start.16 = (bf16[384,256]{1,0:T(8,128)(2,1)}, bf16[384,256]{1,0:T(8,128)(2,1)S(1)}, u32[]{:S(2)}, u32[]{:S(2)}) collective-permute-start(bf16[384,256]{1,0:T(8,128)(2,1)} %get-tuple-element.30), channel_id=1, source_target_pairs={{0,3},{1,0},{2,1},{3,2},{4,7},{5,4},{6,5},{7,6},{8,11},{9,8},{10,9... | collective-permute-start | bytes 589832 | tf_op jit(solution)/shard_map/ppermute | solution.py:218
  40.9 7.3 %collective-permute-start.17 = (bf16[384,256]{1,0:T(8,128)(2,1)S(1)}, bf16[384,256]{1,0:T(8,128)(2,1)S(1)}, u32[]{:S(2)}, u32[]{:S(2)}) collective-permute-start(bf16[384,256]{1,0:T(8,128)(2,1)S(1)} %get-tuple-element.32), channel_id=1, source_target_pairs={{0,3},{1,0},{2,1},{3,2},{4,7},{5,4},{6,5},{7,6},{8,11},{9,8},{10,9... | collective-permute-start | bytes 589832 | tf_op jit(solution)/shard_map/ppermute | solution.py:218
  42.2 17.4 %collective-permute-start.14 = (bf16[384,256]{1,0:T(8,128)(2,1)}, bf16[384,256]{1,0:T(8,128)(2,1)}, u32[]{:S(2)}, u32[]{:S(2)}) collective-permute-start(bf16[384,256]{1,0:T(8,128)(2,1)} %add_convert_fusion.3), channel_id=1, source_target_pairs={{0,1},{1,2},{2,3},{3,0},{4,5},{5,6},{6,7},{7,4},{8,9},{9,10},{10,1... | collective-permute-start | bytes 589832 | tf_op jit(solution)/shard_map/ppermute | solution.py:218
  48.9 10.6 %collective-permute-start.18 = (bf16[384,256]{1,0:T(8,128)(2,1)}, bf16[384,256]{1,0:T(8,128)(2,1)}, u32[]{:S(2)}, u32[]{:S(2)}) collective-permute-start(bf16[384,256]{1,0:T(8,128)(2,1)} %add_convert_fusion.2), channel_id=1, source_target_pairs={{0,3},{1,0},{2,1},{3,2},{4,7},{5,4},{6,5},{7,6},{8,11},{9,8},{10,9... | collective-permute-start | bytes 589832 | tf_op jit(solution)/shard_map/ppermute | solution.py:218
  52.1 1.5 %copy-start.8 = (bf16[768,1280]{1,0:T(8,128)(2,1)S(1)}, bf16[768,1280]{1,0:T(8,128)(2,1)}, u32[]{:S(2)}) copy-start(bf16[768,1280]{1,0:T(8,128)(2,1)} %copy-done.7) | copy-start | bytes 5898244
  53.7 1.4 %copy-start.10 = (bf16[768,1024]{1,0:T(8,128)(2,1)S(1)}, bf16[768,1024]{1,0:T(8,128)(2,1)}, u32[]{:S(2)}) copy-start(bf16[768,1024]{1,0:T(8,128)(2,1)} %copy-done.9) | copy-start | bytes 4718596
  59.5 14.1 %collective-permute-start.20 = (bf16[16,5,32,256]{3,2,1,0:T(8,128)(2,1)}, bf16[16,5,32,256]{3,2,1,0:T(8,128)(2,1)}, u32[]{:S(2)}, u32[]{:S(2)}) collective-permute-start(bf16[16,5,32,256]{3,2,1,0:T(8,128)(2,1)} %get-tuple-element.38), channel_id=1, source_target_pairs={{0,4},{4,0},{1,5},{5,1},{2,6},{6,2},{3,7},{7,3},{8,12},{12,8},{9,1... | collective-permute-start | bytes 3932168 | tf_op jit(solution)/shard_map/ppermute | solution.py:222
  62.2 2.3 %collective-permute-start.19 = (bf16[16,5,16,256]{3,2,1,0:T(8,128)(2,1)S(1)}, bf16[16,5,16,256]{3,2,1,0:T(8,128)(2,1)S(1)}, u32[]{:S(2)}, u32[]{:S(2)}) collective-permute-start(bf16[16,5,16,256]{3,2,1,0:T(8,128)(2,1)S(1)} %get-tuple-element.35), channel_id=1, source_target_pairs={{0,4},{4,0},{1,5},{5,1},{2,6},{6,2},{3,7},{7,3},{8,12},{12,8},{9,1... | collective-permute-start | bytes 1966088 | tf_op jit(solution)/shard_map/ppermute | solution.py:222
  64.5 9.1 %copy-start.1 = (bf16[16,5,32,256]{3,2,1,0:T(8,128)(2,1)S(1)}, bf16[16,5,32,256]{3,2,1,0:T(8,128)(2,1)}, u32[]{:S(2)}) copy-start(bf16[16,5,32,256]{3,2,1,0:T(8,128)(2,1)} %copy-done) | copy-start | bytes 3932164
  65.6 21.5 %all-to-all-start = ((bf16[16,5,16,256]{3,2,1,0:T(8,128)(2,1)}), bf16[16,5,16,256]{3,2,1,0:T(8,128)(2,1)S(1)}, u32[]{:S(2)}, u32[]{:S(2)}) async-start(bf16[16,5,16,256]{3,2,1,0:T(8,128)(2,1)} %add_convert_fusion.1), calls=%async_computation | async-start | bytes 1310720 | tf_op jit(solution)/shard_map/all_to_all | solution.py:231
  87.1 34.5 %all-to-all-start.1 = ((bf16[16,5,32,256]{3,2,1,0:T(8,128)(2,1)}), bf16[16,5,32,256]{3,2,1,0:T(8,128)(2,1)S(1)}, u32[]{:S(2)}, u32[]{:S(2)}) async-start(bf16[16,5,32,256]{3,2,1,0:T(8,128)(2,1)} %add_convert_fusion), calls=%async_computation.1 | async-start | bytes 2621440 | tf_op jit(solution)/shard_map/all_to_all | solution.py:231
  90.8 1.3 %collective-permute-start.6 = (f32[16,128]{1,0:T(8,128)S(1)}, f32[16,128]{1,0:T(8,128)S(1)}, u32[]{:S(2)}, u32[]{:S(2)}) collective-permute-start(f32[16,128]{1,0:T(8,128)S(1)} %constant_dynamic-update-slice_fusion), channel_id=1, source_target_pairs={{0,4},{4,0},{1,5},{5,1},{2,6},{6,2},{3,7},{7,3},{8,12},{12,8},{9,1... | collective-permute-start | bytes 24584 | tf_op jit(solution)/shard_map/ppermute | solution.py:222
  92.1 3.7 %collective-permute-start.7 = (f32[16,128]{1,0:T(8,128)S(1)}, f32[16,128]{1,0:T(8,128)S(1)}, u32[]{:S(2)}, u32[]{:S(2)}) collective-permute-start(f32[16,128]{1,0:T(8,128)S(1)} %add.33), channel_id=1, source_target_pairs={{0,1},{1,0},{2,3},{3,2},{4,5},{5,4},{6,7},{7,6},{8,9},{9,8},{10,11... | collective-permute-start | bytes 24584 | tf_op jit(solution)/shard_map/ppermute | solution.py:222
  95.7 4.9 %collective-permute-start.8 = (f32[16,128]{1,0:T(8,128)S(1)}, f32[16,128]{1,0:T(8,128)S(1)}, u32[]{:S(2)}, u32[]{:S(2)}) collective-permute-start(f32[16,128]{1,0:T(8,128)S(1)} %add.34), channel_id=1, source_target_pairs={{0,3},{1,2},{2,1},{3,0},{4,7},{5,6},{6,5},{7,4},{8,11},{9,10},{10,... | collective-permute-start | bytes 24584 | tf_op jit(solution)/shard_map/ppermute | solution.py:222
  100.6 6.0 %collective-permute-start.9 = (f32[16,128]{1,0:T(8,128)S(1)}, f32[16,128]{1,0:T(8,128)S(1)}, u32[]{:S(2)}, u32[]{:S(2)}) collective-permute-start(f32[16,128]{1,0:T(8,128)S(1)} %add.35), channel_id=1, source_target_pairs={{0,8},{8,0},{16,24},{24,16},{1,9},{9,1},{17,25},{25,17},{2,10},{10... | collective-permute-start | bytes 24584 | tf_op jit(solution)/shard_map/ppermute | solution.py:222
  106.6 4.9 %collective-permute-start.10 = (f32[16,128]{1,0:T(8,128)S(1)}, f32[16,128]{1,0:T(8,128)S(1)}, u32[]{:S(2)}, u32[]{:S(2)}) collective-permute-start(f32[16,128]{1,0:T(8,128)S(1)} %add.36), channel_id=1, source_target_pairs={{0,24},{8,16},{16,8},{24,0},{1,25},{9,17},{17,9},{25,1},{2,26},{10... | collective-permute-start | bytes 24584 | tf_op jit(solution)/shard_map/ppermute | solution.py:222
  111.5 3.7 %collective-permute-start.11 = (f32[16,128]{1,0:T(8,128)S(1)}, f32[16,128]{1,0:T(8,128)S(1)}, u32[]{:S(2)}, u32[]{:S(2)}) collective-permute-start(f32[16,128]{1,0:T(8,128)S(1)} %add.37), channel_id=1, source_target_pairs={{0,32},{32,0},{64,96},{96,64},{1,33},{33,1},{65,97},{97,65},{2,34}... | collective-permute-start | bytes 24584 | tf_op jit(solution)/shard_map/ppermute | solution.py:222
  115.1 4.9 %collective-permute-start.12 = (f32[16,128]{1,0:T(8,128)S(1)}, f32[16,128]{1,0:T(8,128)S(1)}, u32[]{:S(2)}, u32[]{:S(2)}) collective-permute-start(f32[16,128]{1,0:T(8,128)S(1)} %add.38), channel_id=1, source_target_pairs={{0,96},{32,64},{64,32},{96,0},{1,97},{33,65},{65,33},{97,1},{2,98}... | collective-permute-start | bytes 24584 | tf_op jit(solution)/shard_map/ppermute | solution.py:222
  (2 other events, 2.2 us)

commit v2 on v1

v2 whole, which is shorter than its diff:
```python
import functools

import jax
import jax.numpy as jnp
from jax import lax
from jax.experimental import pallas as pl
from jax.experimental.pallas import tpu as pltpu
from jax.sharding import Mesh
from jax.sharding import PartitionSpec as P

DP = ("dp_0", "dp_1", "dp_2")
ZY = ("dp_0", "dp_1")
F32 = jnp.float32
BF16 = jnp.bfloat16
VMEM_LIMIT = 16 << 20

smooth_width = 0.1
leak_slope = 0.1


def leaky(pre):
    return jnp.where(pre > 0, pre, leak_slope * pre).astype(BF16)


def fold_rows(x):
    x = jnp.sum(x.reshape(-1, 8, x.shape[1]), axis=0)
    return sum(x[:, at : at + 128] for at in range(0, x.shape[1], 128))


def difference_terms(real, fake):
    difference = real.astype(F32) - fake.astype(F32)
    root = jnp.sqrt(difference * difference + smooth_width * smooth_width)
    return difference, root


def dot(a, b):
    return jnp.dot(a, b, preferred_element_type=F32)


def dot_rows(a, b):
    return lax.dot_general(a, b, (((0,), (0,)), ((), ())), preferred_element_type=F32)


def dot_lanes(a, b):
    return lax.dot_general(a, b, (((1,), (1,)), ((), ())), preferred_element_type=F32)


def losses_split(first, second):
    value = jnp.sum(jnp.concatenate([first, second], axis=1), axis=0, keepdims=True)
    return split_rows(value, 0)


def split_rows(value, base):
    row = lax.broadcasted_iota(jnp.int32, (8, value.shape[1]), 0) - base
    high = value.astype(BF16).astype(F32)
    middle = (value - high).astype(BF16).astype(F32)
    low = value - high - middle
    out = jnp.where(row == 0, high, jnp.where(row == 1, middle, jnp.where(row == 2, low, 0.0)))
    return out.astype(BF16)


def strided_conv(take, cols, span, w, h_out, phases_out, loss, padded, phases, out_sem):
    frames = span // 3
    rows = 2 * cols * frames
    width = w.shape[2]
    row = lax.broadcasted_iota(jnp.int32, (span, span), 0)
    col = lax.broadcasted_iota(jnp.int32, (span, span), 1)
    phase = jnp.where(row >= 2 * frames, 2, jnp.where(row >= frames, 1, 0))
    select = (col == 3 * (row - frames * phase) + phase).astype(F32).astype(BF16)
    for n in range(2 * cols):
        parts = dot(select, take(n)).astype(BF16)
        for p in range(3):
            phases[p, n * frames : (n + 1) * frames, :] = parts[p * frames : (p + 1) * frames]
    copy_out = pltpu.make_async_copy(phases, phases_out, out_sem)
    copy_out.start()
    padded[:, :8, :] = jnp.zeros((2 * cols, 8, width), F32)
    earlier = dot(phases[1], w[0]) + dot(phases[2], w[1])
    padded[:, 8 : 8 + frames, :] = earlier.reshape(2 * cols, frames, width)
    same = dot(phases[0], w[2]) + dot(phases[1], w[3]) + dot(phases[2], w[4])
    h = leaky(same + padded[:, 7 : 7 + frames, :].reshape(rows, width))
    h_out[...] = h
    _, root = difference_terms(h[: rows // 2], h[rows // 2 :])
    loss[...] = fold_rows(root - smooth_width)
    copy_out.wait()


def first_early_kernel(
    real, fake, w_hbm, h_out, phases_out, loss, w, rest,
    padded, phases, out_sem, held, held_sem, rest_sem, w_sem,
):
    cols = held.shape[0] // 2
    span = held.shape[1]
    for n in range(2 * cols):
        source = real if n < cols else fake
        pltpu.make_async_copy(source.at[n % cols], held.at[n], held_sem.at[n]).start()
    w_copy = pltpu.make_async_copy(w_hbm, w, w_sem)
    w_copy.start()
    rest_copies = [
        pltpu.make_async_copy(x.at[cols:], rest.at[at * cols : (at + 1) * cols], rest_sem.at[at])
        for at, x in enumerate((real, fake))
    ]
    for copy in rest_copies:
        copy.start()

    def take(n):
        source = real if n < cols else fake
        pltpu.make_async_copy(source.at[n % cols], held.at[n], held_sem.at[n]).wait()
        if n == 2 * cols - 1:
            w_copy.wait()
        return held[n]

    strided_conv(take, cols, span, w, h_out, phases_out, loss, padded, phases, out_sem)
    for copy in rest_copies:
        copy.wait()


def first_late_kernel(
    rest, w, w_next_hbm, h_out, phases_out, loss, w_next, padded, phases, out_sem, sem
):
    copy = pltpu.make_async_copy(w_next_hbm, w_next, sem)
    copy.start()
    cols, span = rest.shape[0] // 2, rest.shape[1]
    strided_conv(
        lambda n: rest[n], cols, span, w, h_out, phases_out, loss, padded, phases, out_sem
    )
    copy.wait()


def second_kernel(
    normaliser, whole, s_ref, own, prev, following, far, w, loss_first,
    all_out, shifted_out, far_t, loss, *rest,
):
    *backs, h_all, shifted, padded, in_sems, all_sem, shifted_sem = rest
    rows, width = own.shape
    half = rows // 2
    taps = w.shape[0]
    frames = padded.shape[1] - 16
    s = s_ref[0]
    copies = []
    for away, x in enumerate((own, following, far, prev)):
        at = pl.multiple_of(lax.rem(s + away, 4) * width, 256)
        copies.append(
            pltpu.make_async_copy(x, h_all.at[:, pl.ds(at, width)], in_sems.at[away])
        )
        copies[-1].start()
    for copy in copies:
        copy.wait()
    copy_all = pltpu.make_async_copy(h_all, all_out, all_sem)
    copy_all.start()
    zeros = jnp.zeros((padded.shape[0], 8, width), F32)
    padded[:, :8, :] = zeros
    padded[:, 8 + frames :, :] = zeros
    pre = dot(h_all[...], w[2])
    for k in (0, 1, 3, 4):
        padded[:, 8 : 8 + frames, :] = dot(h_all[...], w[k]).reshape(-1, frames, width)
        pre = pre + padded[:, 6 + k : 6 + k + frames, :].reshape(rows, width)
    h = leaky(pre)
    difference, root = difference_terms(h[:half], h[half:])
    loss_rows = losses_split(loss_first[...], fold_rows(root - smooth_width))
    loss[...] = loss_rows
    slope = difference / root / normaliser
    for value, sign, at in ((h[:half], 1.0, 0), (h[half:], -1.0, half // frames)):
        gate = jnp.where(value.astype(F32) > 0, 1.0, leak_slope)
        delta = (sign * slope * gate).astype(BF16).astype(F32)
        padded[at : at + half // frames, 8 : 8 + frames, :] = delta.reshape(-1, frames, width)
    for k in range(taps):
        moved = padded[:, 10 - k : 10 - k + frames, :].reshape(rows, width)
        shifted[:, k * width : (k + 1) * width] = moved.astype(BF16)
    copy_shifted = pltpu.make_async_copy(shifted, shifted_out, shifted_sem)
    copy_shifted.start()
    far_t[:rows] = back_term(s, 2, shifted, w)
    far_t[rows:] = loss_rows
    if whole:
        back_rest(s, shifted, w, loss_rows, 3, *backs)
    copy_all.wait()
    copy_shifted.wait()


def back_term(s, away, shifted, w):
    width = w.shape[2]
    at = pl.multiple_of(lax.rem(s + away, 4) * width, 256)
    term = None
    for k in range(w.shape[0]):
        part = dot_lanes(shifted[:, k * width : (k + 1) * width], w[k, pl.ds(at, width), :])
        term = part if term is None else term + part
    return term.astype(BF16)


def back_rest(s, shifted, w, loss_rows, with_loss, following, prev, own):
    rows = own.shape[0]
    for away, out in ((1, following), (3, prev)) if with_loss == 1 else ((3, prev), (1, following)):
        out[:rows] = back_term(s, away, shifted, w)
        out[rows:] = loss_rows if away == with_loss else jnp.zeros_like(loss_rows)
    own[...] = back_term(s, 0, shifted, w)


def back_kernel(s_ref, shifted_hbm, w, loss, following, prev, own, shifted, sem):
    copy = pltpu.make_async_copy(shifted_hbm, shifted, sem)
    copy.start()
    copy.wait()
    back_rest(s_ref[0], shifted, w, loss[...], 1, following, prev, own)


def add_kernel(a, b, out):
    out[...] = (a[...].astype(F32) + b[...].astype(F32)).astype(BF16)


def put(g, c, outs, at, rows, k):
    count = g.shape[0] // (2 * rows)
    g = g.astype(BF16).reshape(count, 2, rows, g.shape[1])
    even, odd = g[:, 0], g[:, 1]
    mine, theirs = outs
    mine[at : at + count, k * rows : (k + 1) * rows] = jnp.where(c == 0, even, odd)
    theirs[at : at + count, k * rows : (k + 1) * rows] = jnp.where(c == 0, odd, even)


def weight_second_kernel(
    taps, c_ref, h_a, h_b, shifted_a, shifted_b, mine, theirs, h_all, shifted, h_sem, shifted_sem
):
    own_rows, width = mine.shape[1] // taps, mine.shape[2]
    rows = h_a.shape[0]
    c = c_ref[0]
    step = 256
    count = h_all.shape[1] // step
    moves = []
    for n, x in enumerate((shifted_a, shifted_b)):
        moves.append(
            pltpu.make_async_copy(x, shifted.at[n * rows : (n + 1) * rows], shifted_sem.at[n])
        )
    parts = []
    for q in range(count):
        for n, x in enumerate((h_a, h_b)):
            cut = slice(q * step, (q + 1) * step)
            parts.append(
                pltpu.make_async_copy(
                    x.at[:, cut], h_all.at[n * rows : (n + 1) * rows, cut], h_sem.at[2 * q + n]
                )
            )
    for copy in moves + parts:
        copy.start()
    for copy in moves:
        copy.wait()
    for q in range(count):
        parts[2 * q].wait()
        parts[2 * q + 1].wait()
        g = dot_rows(h_all[:, q * step : (q + 1) * step], shifted[...])
        for k in range(taps):
            put(g[:, k * width : (k + 1) * width], c, (mine, theirs),
                q * step // (2 * own_rows), own_rows, k)


def weight_first_kernel(
    normaliser, taps, c_ref, loss_a, loss_b, *refs,
):
    *sources, phases_a, phases_b, mine, theirs, padded, moved, got, phases, sems, phase_sems = refs
    rows, width = sources[0].shape
    half = rows // 2
    frames = padded.shape[1] - 8
    c = c_ref[0]
    copies = []
    for n, x in enumerate(sources):
        copies.append(pltpu.make_async_copy(x, got.at[n, : x.shape[0]], sems.at[n]))
    phase_copies = []
    for p in range(3):
        for n, x in enumerate((phases_a, phases_b)):
            phase_copies.append(
                pltpu.make_async_copy(
                    x.at[p], phases.at[p, n * rows : (n + 1) * rows], phase_sems.at[2 * p + n]
                )
            )
    for copy in copies + phase_copies:
        copy.start()
    for copy in copies:
        copy.wait()
    padded[:, frames:, :] = jnp.zeros((padded.shape[0], 8, width), F32)
    for n in range(2):
        h, own, a, b = (got.at[2 * at + n] for at in range(4))
        difference, root = difference_terms(h[:half], h[half:rows])
        slope = difference / root / normaliser
        for at, sign in ((0, 1.0), (half, -1.0)):
            cut = slice(at, at + half)
            up = own[cut].astype(F32) + a[cut].astype(F32) + b[cut].astype(F32)
            up = up.astype(BF16).astype(F32)
            gate = jnp.where(h[cut].astype(F32) > 0, 1.0, leak_slope)
            delta = ((sign * slope + up) * gate).astype(BF16)
            base = n * rows + at
            moved[base : base + half, :width] = delta
            cols, lead = half // frames, base // frames
            padded[lead : lead + cols, :frames, :] = delta.astype(F32).reshape(cols, frames, width)
    moved[:, width:] = padded[:, 1 : 1 + frames, :].reshape(2 * rows, width).astype(BF16)
    groups = mine.shape[0]
    own_rows = (mine.shape[1] - 8) // taps
    outs = (mine, theirs)
    for p in range(3):
        phase_copies[2 * p].wait()
        phase_copies[2 * p + 1].wait()
        if p == 0:
            put(dot_rows(phases[p], moved[:, :width]), c, outs, 0, own_rows, 2)
        else:
            g = dot_rows(phases[p], moved[...])
            put(g[:, :width], c, outs, 0, own_rows, 2 + p)
            put(g[:, width:], c, outs, 0, own_rows, p - 1)
    total = loss_a[...].astype(F32) + loss_b[...].astype(F32)
    for at in range(4, 10):
        total = total + got[at, rows:].astype(F32)
    lines = split_rows(jnp.sum(total, axis=0, keepdims=True), 3 * c)
    for x in outs:
        x[:, taps * own_rows :, :] = jnp.broadcast_to(lines[None], (groups, 8, width))


def total_kernel(taps, blocks, out):
    total = jnp.sum(blocks[...].astype(F32), axis=0)
    out[...] = total.reshape(taps, -1, total.shape[1])


def total_loss_kernel(taps, count_all, blocks, out, loss):
    rows = out.shape[1]
    total = jnp.sum(blocks[...].astype(F32), axis=0)
    out[...] = total[: taps * rows].reshape(taps, rows, -1)
    lines = total[taps * rows :]
    loss[0] = jnp.sum(lines[:, :128]) / count_all
    loss[1] = jnp.sum(lines[:, 128:]) / count_all


def call(
    kernel, operands, outs, scratch=(), smem=0, hbm=(), loose=(), after=(), smem_outs=(),
    hbm_outs=(), flops=0, cost=1, name=None,
):
    moved = sum(x.size * x.dtype.itemsize for x in operands)
    moved += sum(x.size * x.dtype.itemsize for x in outs)
    vmem, small = pl.BlockSpec(memory_space=pltpu.VMEM), pl.BlockSpec(memory_space=pltpu.SMEM)
    far, anywhere = pl.BlockSpec(memory_space=pltpu.HBM), pl.BlockSpec(memory_space=pl.ANY)
    count = len(operands)
    operands = tuple(
        pltpu.with_memory_space_constraint(x, pltpu.HBM) if at in hbm else x
        for at, x in enumerate(operands)
    )

    def body(*refs):
        kernel(*refs[:count], *refs[count + len(after) :])

    return pl.pallas_call(
        body,
        out_shape=[
            pltpu.HBM(x.shape, x.dtype) if at in hbm_outs else x for at, x in enumerate(outs)
        ],
        in_specs=[
            small if at < smem else far if at in hbm else anywhere if at in loose else vmem
            for at in range(count)
        ]
        + [anywhere] * len(after),
        out_specs=[
            small if at in smem_outs else far if at in hbm_outs else vmem
            for at in range(len(outs))
        ],
        scratch_shapes=list(scratch),
        compiler_params=pltpu.CompilerParams(vmem_limit_bytes=VMEM_LIMIT),
        cost_estimate=pl.CostEstimate(
            flops=int(flops * cost), bytes_accessed=int(moved * cost), transcendentals=0
        ),
        name=name,
    )(*operands, *after)


def like(shape, dtype=BF16):
    return jax.ShapeDtypeStruct(shape, dtype)


def turn(x, step):
    count = lax.axis_size("section")
    return lax.ppermute(x, "section", [(i, (i + step) % count) for i in range(count)])


def added(a, b, name, after=()):
    return call(add_kernel, (a, b), [like(a.shape)], after=after, name=name)[0]


def other_core(x):
    return lax.ppermute(x, "dp_2", [(0, 1), (1, 0)])


def shards(real_in, fake_in, kernel_first, kernel_second):
    replicas = lax.axis_size(DP)
    cols, span, in_width = real_in.shape
    frames = span // 3
    taps, width_all, width = kernel_second.shape
    normaliser = float(cols * frames)
    count_all = float(cols * replicas * frames * width_all)
    groups = replicas // 2
    part = cols // 2
    rows = cols * frames
    s = lax.axis_index("section").reshape(1).astype(jnp.int32)
    c = lax.axis_index("dp_2").reshape(1).astype(jnp.int32)
    dma = pltpu.SemaphoreType.DMA
    chunk_outs = [like((rows, width)), like((3, rows, in_width)), like((8, 128), F32)]
    conv_scratch = [
        pltpu.VMEM((cols, frames + 8, width), F32), pltpu.VMEM((3, rows, in_width), BF16), dma
    ]
    flops = 2 * rows * taps * in_width * width

    h_a, phases_a, loss_a, w_first, rest = call(
        first_early_kernel,
        (real_in, fake_in, kernel_first),
        chunk_outs + [like(kernel_first.shape), like((cols, span, in_width))],
        conv_scratch
        + [pltpu.VMEM((cols, span, in_width), BF16), dma((cols,)), dma((2,)), dma],
        hbm=(0, 1, 2),
        hbm_outs=(1,),
        flops=flops,
        name="first_a",
    )
    prev_a = turn(h_a, 1)
    following_a = turn(h_a, -1)
    h_b, phases_b, loss_b, w_second = call(
        first_late_kernel,
        (rest, w_first, kernel_second),
        chunk_outs + [like(kernel_second.shape)],
        conv_scratch + [dma],
        hbm=(2,),
        hbm_outs=(1,),
        flops=flops,
        cost=1,
        name="first_b",
    )
    far_a = turn(prev_a, 1)
    following_b = turn(h_b, -1)
    prev_b = turn(h_b, 1)
    far_b = turn(following_b, -1)

    second_outs = [like((rows, width_all)), like((rows, taps * width)), like((rows + 8, width)),
                   like((8, width))]
    back_outs = [like((rows + 8, width)), like((rows + 8, width)), like((rows, width))]
    second_scratch = [
        pltpu.VMEM((rows, width_all), BF16), pltpu.VMEM((rows, taps * width), BF16),
        pltpu.VMEM((cols, frames + 16, width), F32), dma((4,)), dma, dma,
    ]
    flops = 2 * rows * taps * (width_all + width) * width
    all_a, shifted_a, far_t, loss_a, next_t, prev_t, own_a = call(
        functools.partial(second_kernel, normaliser, True),
        (s, h_a, prev_a, following_a, far_a, w_second, loss_a),
        second_outs + back_outs,
        second_scratch,
        smem=1,
        loose=(1, 2, 3, 4),
        hbm_outs=(0, 1),
        cost=1,
        flops=flops,
        name="second_a",
    )
    pass_a = turn(far_t, 1)
    from_following_a = turn(prev_t, -1)
    relayed_a = added(next_t, pass_a, "relay_a")
    from_prev_a = turn(relayed_a, 1)

    all_b, shifted_b, far_t, loss_b = call(
        functools.partial(second_kernel, normaliser, False),
        (s, h_b, prev_b, following_b, far_b, w_second, loss_b),
        second_outs,
        second_scratch,
        smem=1,
        loose=(1, 2, 3, 4),
        hbm_outs=(0, 1),
        cost=1,
        after=(own_a,),
        flops=flops,
        name="second_b",
    )
    pass_b = turn(far_t, -1)
    next_t, prev_t, own_b = call(
        back_kernel,
        (s, shifted_b, w_second, loss_b),
        back_outs,
        [pltpu.VMEM((rows, taps * width), BF16), dma],
        smem=1,
        hbm=(1,),
        cost=4,
        flops=2 * rows * taps * width * width * 3,
        name="back_b",
    )
    from_prev_b = turn(next_t, 1)
    relayed_b = added(prev_t, pass_b, "relay_b")
    from_following_b = turn(relayed_b, -1)

    own_rows = width_all // replicas
    mine_second, theirs = call(
        functools.partial(weight_second_kernel, taps),
        (c, all_a, all_b, shifted_a, shifted_b),
        [like((groups, taps * own_rows, width))] * 2,
        [pltpu.VMEM((2 * rows, width_all), BF16), pltpu.VMEM((2 * rows, taps * width), BF16),
         dma((2 * width_all // 256,)), dma((2,))],
        smem=1,
        hbm=(1, 2, 3, 4),
        cost=4,
        after=(relayed_a, relayed_b),
        flops=4 * rows * taps * width * width_all,
        name="weight_second",
    )
    theirs_second = other_core(theirs)

    first_rows = in_width // replicas
    mine_first, theirs = call(
        functools.partial(weight_first_kernel, normaliser, taps),
        (c, loss_a, loss_b, h_a, h_b, own_a, own_b, from_prev_a, from_prev_b, from_following_a,
         from_following_b, pass_a, pass_b, phases_a, phases_b),
        [like((groups, taps * first_rows + 8, width))] * 2,
        [pltpu.VMEM((2 * cols, frames + 8, width), F32), pltpu.VMEM((2 * rows, 2 * width), BF16),
         pltpu.VMEM((10, rows + 8, width), BF16), pltpu.VMEM((3, 2 * rows, in_width), BF16),
         dma((10,)), dma((6,))],
        smem=1,
        hbm=(13, 14),
        loose=tuple(range(3, 13)),
        cost=20,
        after=(mine_second,),
        flops=4 * rows * taps * width * in_width,
        name="weight_first",
    )
    theirs_first = other_core(theirs)
    summed_second = added(mine_second, theirs_second, "core_second", (mine_first,))
    blocks_second = lax.all_to_all(summed_second, ZY, 0, 0)
    summed_first = added(mine_first, theirs_first, "core_first", (summed_second,))
    blocks_first = lax.all_to_all(summed_first, ZY, 0, 0)

    (grad_second,) = call(
        functools.partial(total_kernel, taps),
        (blocks_second,),
        [like((taps, own_rows, width), F32)],
        name="total_second",
    )
    grad_first, layer_loss = call(
        functools.partial(total_loss_kernel, taps, count_all),
        (blocks_first,),
        [like((taps, first_rows, width), F32), like((2,), F32)],
        smem_outs=(1,),
        name="total_first",
    )
    return (layer_loss, jnp.transpose(grad_first, (1, 0, 2)), jnp.transpose(grad_second, (1, 0, 2)))


def solution(mesh):
    finer = Mesh(
        mesh.devices.reshape(4, 4, 2, mesh.shape["section"]), ("dp_0", "dp_1", "dp_2", "section")
    )
    return jax.shard_map(
        shards,
        mesh=finer,
        in_specs=(
            P(DP, None, None),
            P(DP, None, None),
            P(None, None, "section"),
            P(None, None, "section"),
        ),
        out_specs=(P(), P(DP, None, "section"), P(DP, None, "section")),
        check_vma=False,
    )
```

time: 123 us -> 101 us (0.82)
  blocking collectives: 0 us -> 21.6 us
  waiting for transfers between devices: 44.4 us -> 25.9 us
  starting transfers between devices: 40.3 us -> 22.5 us
  local copies, waits for them, and re-layouts: 12.2 us -> 0 us
  Pallas kernels: 18.6 us -> 30.1 us
  other arithmetic: 6.19 us -> 0 us
    ppermute x9 -> x2, waiting for transfers between devices: 22.6 us -> 0.8 us  [other_core(): return lax.ppermute(x, 'dp_2', [(0, 1), (1, 0)])]
    all_to_all x0 -> x1, blocking collectives: none -> 21.6 us  [shards(): blocks_first = lax.all_to_all(summed_first, ZY, 0, 0)]
    unnamed x25 -> x0, local copies, waits for them, and re-layouts: 12.1 us -> none
    pallas_call x7 -> x13, Pallas kernels: 18.6 us -> 30.1 us  [call(): pl.pallas_call(body, out_shape=[pltpu.HBM(x.shape, x.dtype) if at in hbm_...]
    all_to_all x2 -> x1, waiting for transfers between devices: 10.5 us -> 19.4 us  [shards(): blocks_second = lax.all_to_all(summed_second, ZY, 0, 0)]
    ppermute x9 -> x2, starting transfers between devices: 8.79 us -> 0.17 us  [other_core(): return lax.ppermute(x, 'dp_2', [(0, 1), (1, 0)])]
    all_to_all x2 -> x1, starting transfers between devices: 11.8 us -> 3.7 us  [shards(): blocks_second = lax.all_to_all(summed_second, ZY, 0, 0)]
    ppermute x12, waiting for transfers between devices: 11.3 us -> 5.76 us  [turn(): lax.ppermute(x, 'section', [(i, (i + step) % count) for i in range(count)])]
  transfers between devices with their start and end apart: 23 -> 15, of which waited for: 15 -> 7; matrix products, arithmetic and copies ran while one was open for 6% -> 0% of each run, Pallas kernels for 7% -> 21%
where the time goes in v2:
time: 101 us
  Pallas kernels  30.1 us (30%)
  waiting for transfers between devices  25.9 us (26%)
  starting transfers between devices  22.5 us (22%)
  blocking collectives  21.6 us (21%)
    pallas_call x13, Pallas kernels, call(): pl.pallas_call(body, out_shape=[pltpu.HBM(x.shape, x.dtype) if at in hbm_...  30.1 us
    all_to_all x1, blocking collectives, shards(): blocks_first = lax.all_to_all(summed_first, ZY, 0, 0)  21.6 us
    all_to_all x1, waiting for transfers between devices, shards(): blocks_second = lax.all_to_all(summed_second, ZY, 0, 0)  19.4 us
    ppermute x12, starting transfers between devices, turn(): lax.ppermute(x, 'section', [(i, (i + step) % count) for i in range(count)])  18.7 us
    ppermute x12, waiting for transfers between devices, turn(): lax.ppermute(x, 'section', [(i, (i + step) % count) for i in range(count)])  5.76 us
    all_to_all x1, starting transfers between devices, shards(): blocks_second = lax.all_to_all(summed_second, ZY, 0, 0)  3.7 us
  transfers between devices with their start and end apart: 15, of which 7 were waited for; matrix products, arithmetic and copies ran while one was open for 0% of the time, Pallas kernels for 21%

profile of v2, /device:TPU:0, one launch (start us, length us, event | category | flops | bytes accessed | tf_op | source)
XLA Modules:
  0.0 101.0 jit_solution(5110440105063671414)
XLA Ops:
  0.6 3.5 %first_a.1 = (bf16[384,256]{1,0:T(8,128)(2,1)S(1)}, bf16[3,384,512]{2,1,0:T(8,128)(2,1)}, f32[8,128]{1,0:T(8,128)S(1)}, bf16[5,512,256]{2,1,0:T(8,128)(2,1)S(1)}, bf16[8,144,512]{2,1,0:T(8,128)(2,1)S(1)}) custom-call(bf16[8,144,512]{2,1,0:T(8,128)(2,1)} %refs_0_.1, bf16[8,144,512]{2,1,0:T(8,128)(2,1)} %refs_1_.1, bf16[5,512,256]{2,1,0:T(8,128)(2,1)} %refs_2_.2), custom_call_target="tpu_custom_call" | custom-call | flops 503316480 | bytes 7540736 | tf_op jit(solution)/shard_map/first_a/pallas_call | solution.py:342
  4.2 1.6 %collective-permute-start = (bf16[384,256]{1,0:T(8,128)(2,1)S(1)}, bf16[384,256]{1,0:T(8,128)(2,1)S(1)}, u32[]{:S(2)}, u32[]{:S(2)}) collective-permute-start(bf16[384,256]{1,0:T(8,128)(2,1)S(1)} %get-tuple-element.32.refs_1_.refs_3_), channel_id=1, source_target_pairs={{0,1},{1,2},{2,3},{3,0},{4,5},{5,6},{6,7},{7,4},{8,9},{9,10},{10,1... | collective-permute-start | bytes 589832 | tf_op jit(solution)/shard_map/ppermute | solution.py:371
  5.8 2.6 %first_b.1 = (bf16[384,256]{1,0:T(8,128)(2,1)S(1)}, bf16[3,384,512]{2,1,0:T(8,128)(2,1)}, f32[8,128]{1,0:T(8,128)S(1)}, bf16[5,1024,256]{2,1,0:T(8,128)(2,1)S(1)}) custom-call(bf16[8,144,512]{2,1,0:T(8,128)(2,1)S(1)} %get-tuple-element.33.refs_0_, bf16[5,512,256]{2,1,0:T(8,128)(2,1)S(1)} %get-tuple-element.34.refs_1_, bf16[5,1024,256]{2,1,0:T(8,128)(2,1)} %refs_2_.3), custom_call_target="tpu_custom_call" | custom-call | flops 503316480 | bytes 9113600 | tf_op jit(solution)/shard_map/first_b/pallas_call | solution.py:342
  8.5 1.7 %collective-permute-start.4 = (bf16[384,256]{1,0:T(8,128)(2,1)S(1)}, bf16[384,256]{1,0:T(8,128)(2,1)S(1)}, u32[]{:S(2)}, u32[]{:S(2)}) collective-permute-start(bf16[384,256]{1,0:T(8,128)(2,1)S(1)} %get-tuple-element.38.refs_1_.refs_4_), channel_id=1, source_target_pairs={{0,3},{1,0},{2,1},{3,2},{4,7},{5,4},{6,5},{7,6},{8,11},{9,8},{10,9... | collective-permute-start | bytes 589832 | tf_op jit(solution)/shard_map/ppermute | solution.py:371
  10.2 1.6 %collective-permute-start.1 = (bf16[384,256]{1,0:T(8,128)(2,1)S(1)}, bf16[384,256]{1,0:T(8,128)(2,1)}, u32[]{:S(2)}, u32[]{:S(2)}) collective-permute-start(bf16[384,256]{1,0:T(8,128)(2,1)S(1)} %get-tuple-element.32.refs_1_.refs_3_), channel_id=1, source_target_pairs={{0,3},{1,0},{2,1},{3,2},{4,7},{5,4},{6,5},{7,6},{8,11},{9,8},{10,9... | collective-permute-start | bytes 589832 | tf_op jit(solution)/shard_map/ppermute | solution.py:371
  11.8 0.1 collective-permute-done.refs_2_
  12.0 0.5 collective-permute-start.2
  12.4 1.5 %collective-permute-start.3 = (bf16[384,256]{1,0:T(8,128)(2,1)S(1)}, bf16[384,256]{1,0:T(8,128)(2,1)}, u32[]{:S(2)}, u32[]{:S(2)}) collective-permute-start(bf16[384,256]{1,0:T(8,128)(2,1)S(1)} %get-tuple-element.38.refs_1_.refs_4_), channel_id=1, source_target_pairs={{0,1},{1,2},{2,3},{3,0},{4,5},{5,6},{6,7},{7,4},{8,9},{9,10},{10,1... | collective-permute-start | bytes 589832 | tf_op jit(solution)/shard_map/ppermute | solution.py:371
  13.9 2.4 %collective-permute-done.4.refs_3_ = bf16[384,256]{1,0:T(8,128)(2,1)S(1)} collective-permute-done((bf16[384,256]{1,0:T(8,128)(2,1)S(1)}, bf16[384,256]{1,0:T(8,128)(2,1)S(1)}, u32[]{:S(2)}, u32[]{:S(2)}) %collective-permute-start.4) | collective-permute-done | bytes 196640 | tf_op jit(solution)/shard_map/ppermute | solution.py:371
  16.4 2.9 %collective-permute-start.5 = (bf16[384,256]{1,0:T(8,128)(2,1)S(1)}, bf16[384,256]{1,0:T(8,128)(2,1)}, u32[]{:S(2)}, u32[]{:S(2)}) collective-permute-start(bf16[384,256]{1,0:T(8,128)(2,1)S(1)} %collective-permute-done.4.refs_3_), channel_id=1, source_target_pairs={{0,3},{1,0},{2,1},{3,2},{4,7},{5,4},{6,5},{7,6},{8,11},{9,8},{10,9... | collective-permute-start | bytes 589832 | tf_op jit(solution)/shard_map/ppermute | solution.py:371
  19.2 1.4 %collective-permute-done.1.refs_3_ = bf16[384,256]{1,0:T(8,128)(2,1)} collective-permute-done((bf16[384,256]{1,0:T(8,128)(2,1)S(1)}, bf16[384,256]{1,0:T(8,128)(2,1)}, u32[]{:S(2)}, u32[]{:S(2)}) %collective-permute-start.1) | collective-permute-done | bytes 196640 | tf_op jit(solution)/shard_map/ppermute | solution.py:371
  20.7 0.4 collective-permute-done.2.refs_4_
  21.0 3.8 %second_a.1 = (bf16[384,1024]{1,0:T(8,128)(2,1)}, bf16[384,1280]{1,0:T(8,128)(2,1)}, bf16[392,256]{1,0:T(8,128)(2,1)S(1)}, bf16[8,256]{1,0:T(8,128)(2,1)S(1)}, b...) custom-call(s32[1]{0:T(128)} %bitcast.1.refs_0_, ...), custom_call_target="tpu_custom_call" | custom-call | flops 1258291200 | bytes 5984260 | tf_op jit(solution)/shard_map/second_a/pallas_call | solution.py:342
  24.8 4.0 %second_b.1 = (bf16[384,1024]{1,0:T(8,128)(2,1)}, bf16[384,1280]{1,0:T(8,128)(2,1)}, bf16[392,256]{1,0:T(8,128)(2,1)S(1)}, bf16[8,256]{1,0:T(8,128)(2,1)S(1)}) custom-call(s32[1]{0:T(128)} %bitcast.1.refs_0_, bf16[384,256]{1,0:T(8,128)(2,1)S(1)} %get-tuple-element.38.refs_1_.refs_4_, bf16[384,256]{1,0:T(8,128)(2,1)} %collective-permute-done.3.refs_2_, ...), custom_call_target="tpu_custom_call" | custom-call | flops 1258291200 | bytes 5386244 | tf_op jit(solution)/shard_map/second_b/pallas_call | solution.py:342
  28.8 2.6 %collective-permute-start.10 = (bf16[392,256]{1,0:T(8,128)(2,1)S(1)}, bf16[392,256]{1,0:T(8,128)(2,1)S(1)}, u32[]{:S(2)}, u32[]{:S(2)}) collective-permute-start(bf16[392,256]{1,0:T(8,128)(2,1)S(1)} %get-tuple-element.49), channel_id=1, source_target_pairs={{0,3},{1,0},{2,1},{3,2},{4,7},{5,4},{6,5},{7,6},{8,11},{9,8},{10,9... | collective-permute-start | bytes 602120 | tf_op jit(solution)/shard_map/ppermute | solution.py:371
  31.4 2.2 %back_b.1 = (bf16[392,256]{1,0:T(8,128)(2,1)S(1)}, bf16[392,256]{1,0:T(8,128)(2,1)S(1)}, bf16[384,256]{1,0:T(8,128)(2,1)S(1)}) custom-call(s32[1]{0:T(128)} %bitcast.1.refs_0_, bf16[384,1280]{1,0:T(8,128)(2,1)} %get-tuple-element.42.refs_1_.refs_4_, bf16[5,1024,256]{2,1,0:T(8,128)(2,1)S(1)} %get-tuple-element.35.refs_5_.refs_2_, ...), custom_call_target="tpu_custom_call" | custom-call | flops 3019898880 | bytes 16826384 | tf_op jit(solution)/shard_map/back_b/pallas_call | solution.py:342
  33.6 0.7 collective-permute-start.8
  34.3 2.7 %collective-permute-start.9 = (bf16[392,256]{1,0:T(8,128)(2,1)S(1)}, bf16[392,256]{1,0:T(8,128)(2,1)S(1)}, u32[]{:S(2)}, u32[]{:S(2)}) collective-permute-start(bf16[392,256]{1,0:T(8,128)(2,1)S(1)} %get-tuple-element.47), channel_id=1, source_target_pairs={{0,3},{1,0},{2,1},{3,2},{4,7},{5,4},{6,5},{7,6},{8,11},{9,8},{10,9... | collective-permute-start | bytes 602120 | tf_op jit(solution)/shard_map/ppermute | solution.py:371
  37.0 2.6 %collective-permute-start.11 = (bf16[392,256]{1,0:T(8,128)(2,1)S(1)}, bf16[392,256]{1,0:T(8,128)(2,1)S(1)}, u32[]{:S(2)}, u32[]{:S(2)}) collective-permute-start(bf16[392,256]{1,0:T(8,128)(2,1)S(1)} %relay_b.1.refs_6_), channel_id=1, source_target_pairs={{0,3},{1,0},{2,1},{3,2},{4,7},{5,4},{6,5},{7,6},{8,11},{9,8},{10,9... | collective-permute-start | bytes 602120 | tf_op jit(solution)/shard_map/ppermute | solution.py:371
  39.6 0.3 collective-permute-start.7
  39.9 5.4 %weight_second.1 = (bf16[16,160,256]{2,1,0:T(8,128)(2,1)S(1)}, bf16[16,160,256]{2,1,0:T(8,128)(2,1)S(1)}) custom-call(s32[1]{0:T(128)} %bitcast.refs_0_, bf16[384,1024]{1,0:T(8,128)(2,1)} %get-tuple-element.52.refs_1_, bf16[384,1024]{1,0:T(8,128)(2,1)} %get-tuple-element.53.refs_2_, bf16[384,1280]{1,0:T(8,128)(2,1)} %get-tuple-element.54.refs_3_, ...), custom_call_target="tpu_custom_call" | custom-call | flops 8053063680 | bytes 24641552 | tf_op jit(solution)/shard_map/weight_second/pallas_call | solution.py:342
  45.3 0.1 collective-permute-start.13
  45.4 1.4 %collective-permute-done.7.refs_7_ = bf16[392,256]{1,0:T(8,128)(2,1)S(1)} collective-permute-done((bf16[392,256]{1,0:T(8,128)(2,1)S(1)}, bf16[392,256]{1,0:T(8,128)(2,1)S(1)}, u32[]{:S(2)}, u32[]{:S(2)}) %collective-permute-start.7) | collective-permute-done | bytes 200736 | tf_op jit(solution)/shard_map/ppermute | solution.py:371
  46.8 5.4 %weight_first.1 = (bf16[16,88,256]{2,1,0:T(8,128)(2,1)S(1)}, bf16[16,88,256]{2,1,0:T(8,128)(2,1)S(1)}) custom-call(s32[1]{0:T(128)} %bitcast.refs_0_, bf16[8,256]{1,0:T(8,128)(2,1)S(1)} %get-tuple-element.37.refs_1_, bf16[8,256]{1,0:T(8,128)(2,1)S(1)} %get-tuple-element.41.refs_3_.refs_2_, bf16[384,256]{1,0:T(8,128)(2,1)S(1)} %get-tuple-element.32.refs_1_.refs_3_, ...), custom_call_target="tpu_custom_call" | custom-call | flops 20132659200 | bytes 115998800 | tf_op jit(solution)/shard_map/weight_first/pallas_call | solution.py:342
  52.4 1.4 %core_second.1.refs_2_ = bf16[16,160,256]{2,1,0:T(8,128)(2,1)} custom-call(bf16[16,160,256]{2,1,0:T(8,128)(2,1)S(1)} %get-tuple-element.55.refs_15_.refs_0_, bf16[16,160,256]{2,1,0:T(8,128)(2,1)S(1)} %collective-permute-done.13.refs_1_, bf16[16,88,256]{2,1,0:T(8,128)(2,1)S(1)} %get-tuple-element.56.refs_2_.refs_0_), custom_call_target="tpu_custom_call" | custom-call | bytes 3932160 | tf_op jit(solution)/shard_map/core_second/pallas_call | solution.py:342
  53.7 0.8 collective-permute-done.12.refs_1_
  54.5 0.2 core_first.1
  54.7 21.6 %all_to_all.10.refs_0_ = bf16[16,88,256]{2,1,0:T(8,128)(2,1)S(1)} all-to-all(bf16[16,88,256]{2,1,0:T(8,128)(2,1)S(1)} %core_first.1), channel_id=1, replica_groups=mesh['dp_0'=4,'dp_1'=4,'dp_2'=2,'section'=4] {'dp_0','dp_1'}, dimensions={0} | all-to-all | bytes 1441792 | tf_op jit(solution)/shard_map/all_to_all | solution.py:521
  76.3 3.7 %all-to-all-start.1 = ((bf16[16,160,256]{2,1,0:T(8,128)(2,1)}), bf16[16,160,256]{2,1,0:T(8,128)(2,1)S(1)}, u32[]{:S(2)}, u32[]{:S(2)}) async-start(bf16[16,160,256]{2,1,0:T(8,128)(2,1)} %core_second.1.refs_2_), calls=%async_computation.1 | async-start | bytes 2621440 | tf_op jit(solution)/shard_map/all_to_all | solution.py:519
  80.0 0.8 total_first.1
  80.8 19.4 %all-to-all-done.1.refs_0_ = bf16[16,160,256]{2,1,0:T(8,128)(2,1)S(1)} async-done(((bf16[16,160,256]{2,1,0:T(8,128)(2,1)}), bf16[16,160,256]{2,1,0:T(8,128)(2,1)S(1)}, u32[]{:S(2)}, u32[]{:S(2)}) %all-to-all-start.1) | async-done | bytes 1310752 | tf_op jit(solution)/shard_map/all_to_all | solution.py:519
  100.2 0.8 total_second.1
  (12 shorter events, 0.2 us)
Async XLA Ops:
  4.2 7.8 %collective-permute-start = (bf16[384,256]{1,0:T(8,128)(2,1)S(1)}, bf16[384,256]{1,0:T(8,128)(2,1)S(1)}, u32[]{:S(2)}, u32[]{:S(2)}) collective-permute-start(bf16[384,256]{1,0:T(8,128)(2,1)S(1)} %get-tuple-element.32.refs_1_.refs_3_), channel_id=1, source_target_pairs={{0,1},{1,2},{2,3},{3,0},{4,5},{5,6},{6,7},{7,4},{8,9},{9,10},{10,1... | collective-permute-start | bytes 589832 | tf_op jit(solution)/shard_map/ppermute | solution.py:371
  8.5 7.9 %collective-permute-start.4 = (bf16[384,256]{1,0:T(8,128)(2,1)S(1)}, bf16[384,256]{1,0:T(8,128)(2,1)S(1)}, u32[]{:S(2)}, u32[]{:S(2)}) collective-permute-start(bf16[384,256]{1,0:T(8,128)(2,1)S(1)} %get-tuple-element.38.refs_1_.refs_4_), channel_id=1, source_target_pairs={{0,3},{1,0},{2,1},{3,2},{4,7},{5,4},{6,5},{7,6},{8,11},{9,8},{10,9... | collective-permute-start | bytes 589832 | tf_op jit(solution)/shard_map/ppermute | solution.py:371
  10.2 10.5 %collective-permute-start.1 = (bf16[384,256]{1,0:T(8,128)(2,1)S(1)}, bf16[384,256]{1,0:T(8,128)(2,1)}, u32[]{:S(2)}, u32[]{:S(2)}) collective-permute-start(bf16[384,256]{1,0:T(8,128)(2,1)S(1)} %get-tuple-element.32.refs_1_.refs_3_), channel_id=1, source_target_pairs={{0,3},{1,0},{2,1},{3,2},{4,7},{5,4},{6,5},{7,6},{8,11},{9,8},{10,9... | collective-permute-start | bytes 589832 | tf_op jit(solution)/shard_map/ppermute | solution.py:371
  12.0 9.1 %collective-permute-start.2 = (bf16[384,256]{1,0:T(8,128)(2,1)S(1)}, bf16[384,256]{1,0:T(8,128)(2,1)}, u32[]{:S(2)}, u32[]{:S(2)}) collective-permute-start(bf16[384,256]{1,0:T(8,128)(2,1)S(1)} %collective-permute-done.refs_2_), channel_id=1, source_target_pairs={{0,1},{1,2},{2,3},{3,0},{4,5},{5,6},{6,7},{7,4},{8,9},{9,10},{10,1... | collective-permute-start | bytes 589832 | tf_op jit(solution)/shard_map/ppermute | solution.py:371
  12.4 12.4 %collective-permute-start.3 = (bf16[384,256]{1,0:T(8,128)(2,1)S(1)}, bf16[384,256]{1,0:T(8,128)(2,1)}, u32[]{:S(2)}, u32[]{:S(2)}) collective-permute-start(bf16[384,256]{1,0:T(8,128)(2,1)S(1)} %get-tuple-element.38.refs_1_.refs_4_), channel_id=1, source_target_pairs={{0,1},{1,2},{2,3},{3,0},{4,5},{5,6},{6,7},{7,4},{8,9},{9,10},{10,1... | collective-permute-start | bytes 589832 | tf_op jit(solution)/shard_map/ppermute | solution.py:371
  16.4 8.5 %collective-permute-start.5 = (bf16[384,256]{1,0:T(8,128)(2,1)S(1)}, bf16[384,256]{1,0:T(8,128)(2,1)}, u32[]{:S(2)}, u32[]{:S(2)}) collective-permute-start(bf16[384,256]{1,0:T(8,128)(2,1)S(1)} %collective-permute-done.4.refs_3_), channel_id=1, source_target_pairs={{0,3},{1,0},{2,1},{3,2},{4,7},{5,4},{6,5},{7,6},{8,11},{9,8},{10,9... | collective-permute-start | bytes 589832 | tf_op jit(solution)/shard_map/ppermute | solution.py:371
  28.8 8.2 %collective-permute-start.10 = (bf16[392,256]{1,0:T(8,128)(2,1)S(1)}, bf16[392,256]{1,0:T(8,128)(2,1)S(1)}, u32[]{:S(2)}, u32[]{:S(2)}) collective-permute-start(bf16[392,256]{1,0:T(8,128)(2,1)S(1)} %get-tuple-element.49), channel_id=1, source_target_pairs={{0,3},{1,0},{2,1},{3,2},{4,7},{5,4},{6,5},{7,6},{8,11},{9,8},{10,9... | collective-permute-start | bytes 602120 | tf_op jit(solution)/shard_map/ppermute | solution.py:371
  31.4 8.2 %collective-permute-start.6 = (bf16[392,256]{1,0:T(8,128)(2,1)S(1)}, bf16[392,256]{1,0:T(8,128)(2,1)S(1)}, u32[]{:S(2)}, u32[]{:S(2)}) collective-permute-start(bf16[392,256]{1,0:T(8,128)(2,1)S(1)} %get-tuple-element.45), channel_id=1, source_target_pairs={{0,1},{1,2},{2,3},{3,0},{4,5},{5,6},{6,7},{7,4},{8,9},{9,10},{10,1... | collective-permute-start | bytes 602120 | tf_op jit(solution)/shard_map/ppermute | solution.py:371
  33.6 11.8 %collective-permute-start.8 = (bf16[392,256]{1,0:T(8,128)(2,1)S(1)}, bf16[392,256]{1,0:T(8,128)(2,1)S(1)}, u32[]{:S(2)}, u32[]{:S(2)}) collective-permute-start(bf16[392,256]{1,0:T(8,128)(2,1)S(1)} %get-tuple-element.46), channel_id=1, source_target_pairs={{0,1},{1,2},{2,3},{3,0},{4,5},{5,6},{6,7},{7,4},{8,9},{9,10},{10,1... | collective-permute-start | bytes 602120 | tf_op jit(solution)/shard_map/ppermute | solution.py:371
  34.3 11.2 %collective-permute-start.9 = (bf16[392,256]{1,0:T(8,128)(2,1)S(1)}, bf16[392,256]{1,0:T(8,128)(2,1)S(1)}, u32[]{:S(2)}, u32[]{:S(2)}) collective-permute-start(bf16[392,256]{1,0:T(8,128)(2,1)S(1)} %get-tuple-element.47), channel_id=1, source_target_pairs={{0,3},{1,0},{2,1},{3,2},{4,7},{5,4},{6,5},{7,6},{8,11},{9,8},{10,9... | collective-permute-start | bytes 602120 | tf_op jit(solution)/shard_map/ppermute | solution.py:371
  37.0 8.4 %collective-permute-start.11 = (bf16[392,256]{1,0:T(8,128)(2,1)S(1)}, bf16[392,256]{1,0:T(8,128)(2,1)S(1)}, u32[]{:S(2)}, u32[]{:S(2)}) collective-permute-start(bf16[392,256]{1,0:T(8,128)(2,1)S(1)} %relay_b.1.refs_6_), channel_id=1, source_target_pairs={{0,3},{1,0},{2,1},{3,2},{4,7},{5,4},{6,5},{7,6},{8,11},{9,8},{10,9... | collective-permute-start | bytes 602120 | tf_op jit(solution)/shard_map/ppermute | solution.py:371
  39.6 7.2 %collective-permute-start.7 = (bf16[392,256]{1,0:T(8,128)(2,1)S(1)}, bf16[392,256]{1,0:T(8,128)(2,1)S(1)}, u32[]{:S(2)}, u32[]{:S(2)}) collective-permute-start(bf16[392,256]{1,0:T(8,128)(2,1)S(1)} %relay_a.1.refs_5_), channel_id=1, source_target_pairs={{0,1},{1,2},{2,3},{3,0},{4,5},{5,6},{6,7},{7,4},{8,9},{9,10},{10,1... | collective-permute-start | bytes 602120 | tf_op jit(solution)/shard_map/ppermute | solution.py:371
  45.3 7.0 %collective-permute-start.13 = (bf16[16,160,256]{2,1,0:T(8,128)(2,1)S(1)}, bf16[16,160,256]{2,1,0:T(8,128)(2,1)S(1)}, u32[]{:S(2)}, u32[]{:S(2)}) collective-permute-start(bf16[16,160,256]{2,1,0:T(8,128)(2,1)S(1)} %get-tuple-element.58), channel_id=1, source_target_pairs={{0,4},{4,0},{1,5},{5,1},{2,6},{6,2},{3,7},{7,3},{8,12},{12,8},{9,1... | collective-permute-start | bytes 3932168 | tf_op jit(solution)/shard_map/ppermute | solution.py:379
  52.3 2.3 %collective-permute-start.12 = (bf16[16,88,256]{2,1,0:T(8,128)(2,1)S(1)}, bf16[16,88,256]{2,1,0:T(8,128)(2,1)S(1)}, u32[]{:S(2)}, u32[]{:S(2)}) collective-permute-start(bf16[16,88,256]{2,1,0:T(8,128)(2,1)S(1)} %get-tuple-element.57), channel_id=1, source_target_pairs={{0,4},{4,0},{1,5},{5,1},{2,6},{6,2},{3,7},{7,3},{8,12},{12,8},{9,1... | collective-permute-start | bytes 2162696 | tf_op jit(solution)/shard_map/ppermute | solution.py:379
  76.3 23.9 %all-to-all-start.1 = ((bf16[16,160,256]{2,1,0:T(8,128)(2,1)}), bf16[16,160,256]{2,1,0:T(8,128)(2,1)S(1)}, u32[]{:S(2)}, u32[]{:S(2)}) async-start(bf16[16,160,256]{2,1,0:T(8,128)(2,1)} %core_second.1.refs_2_), calls=%async_computation.1 | async-start | bytes 2621440 | tf_op jit(solution)/shard_map/all_to_all | solution.py:519

commit v3 on v2

--- a/solution.py
+++ b/solution.py
@@ -308,23 +308,33 @@
         x[:, taps * own_rows :, :] = jnp.broadcast_to(lines[None], (groups, 8, width))
 
 
-def total_kernel(taps, blocks, out):
+def join_kernel(at, a, b, joint, summed, sem):
+    summed[...] = (a[...].astype(F32) + b[...].astype(F32)).astype(BF16)
+    copy = pltpu.make_async_copy(summed, joint.at[:, at : at + summed.shape[1]], sem)
+    copy.start()
+    copy.wait()
+
+
+def join_late_kernel(at, a, b, held, joint, summed, sem):
+    del held
+    join_kernel(at, a, b, joint, summed, sem)
+
+
+def total_kernel(taps, count_all, blocks, second, first, loss):
     total = jnp.sum(blocks[...].astype(F32), axis=0)
-    out[...] = total.reshape(taps, -1, total.shape[1])
-
-
-def total_loss_kernel(taps, count_all, blocks, out, loss):
-    rows = out.shape[1]
-    total = jnp.sum(blocks[...].astype(F32), axis=0)
-    out[...] = total[: taps * rows].reshape(taps, rows, -1)
-    lines = total[taps * rows :]
+    at = 0
+    for out in (second, first):
+        rows = taps * out.shape[1]
+        out[...] = total[at : at + rows].reshape(out.shape)
+        at += rows
+    lines = total[at:]
     loss[0] = jnp.sum(lines[:, :128]) / count_all
     loss[1] = jnp.sum(lines[:, 128:]) / count_all
 
 
 def call(
     kernel, operands, outs, scratch=(), smem=0, hbm=(), loose=(), after=(), smem_outs=(),
-    hbm_outs=(), flops=0, cost=1, name=None,
+    hbm_outs=(), aliases={}, flops=0, cost=1, name=None,
 ):
     moved = sum(x.size * x.dtype.itemsize for x in operands)
     moved += sum(x.size * x.dtype.itemsize for x in outs)
@@ -354,6 +364,7 @@
             for at in range(len(outs))
         ],
         scratch_shapes=list(scratch),
+        input_output_aliases=aliases,
         compiler_params=pltpu.CompilerParams(vmem_limit_bytes=VMEM_LIMIT),
         cost_estimate=pl.CostEstimate(
             flops=int(flops * cost), bytes_accessed=int(moved * cost), transcendentals=0
@@ -495,9 +506,18 @@
         flops=4 * rows * taps * width * width_all,
         name="weight_second",
     )
-    theirs_second = other_core(theirs)
-
     first_rows = in_width // replicas
+    size_second, size_first = taps * own_rows, taps * first_rows + 8
+    joint_like = like((groups, size_second + size_first, width))
+    (joint,) = call(
+        functools.partial(join_kernel, 0),
+        (mine_second, other_core(theirs)),
+        [joint_like],
+        [pltpu.VMEM((groups, size_second, width), BF16), dma],
+        hbm_outs=(0,),
+        name="join_second",
+    )
+
     mine_first, theirs = call(
         functools.partial(weight_first_kernel, normaliser, taps),
         (c, loss_a, loss_b, h_a, h_b, own_a, own_b, from_prev_a, from_prev_b, from_following_a,
@@ -514,24 +534,24 @@
         flops=4 * rows * taps * width * in_width,
         name="weight_first",
     )
-    theirs_first = other_core(theirs)
-    summed_second = added(mine_second, theirs_second, "core_second", (mine_first,))
-    blocks_second = lax.all_to_all(summed_second, ZY, 0, 0)
-    summed_first = added(mine_first, theirs_first, "core_first", (summed_second,))
-    blocks_first = lax.all_to_all(summed_first, ZY, 0, 0)
-
-    (grad_second,) = call(
-        functools.partial(total_kernel, taps),
-        (blocks_second,),
-        [like((taps, own_rows, width), F32)],
-        name="total_second",
-    )
-    grad_first, layer_loss = call(
-        functools.partial(total_loss_kernel, taps, count_all),
-        (blocks_first,),
-        [like((taps, first_rows, width), F32), like((2,), F32)],
-        smem_outs=(1,),
-        name="total_first",
+    (joint,) = call(
+        functools.partial(join_late_kernel, size_second),
+        (mine_first, other_core(theirs), joint),
+        [joint_like],
+        [pltpu.VMEM((groups, size_first, width), BF16), dma],
+        hbm=(2,),
+        hbm_outs=(0,),
+        aliases={2: 0},
+        name="join_first",
+    )
+    blocks = lax.all_to_all(joint, ZY, 0, 0)
+    grad_second, grad_first, layer_loss = call(
+        functools.partial(total_kernel, taps, count_all),
+        (blocks,),
+        [like((taps, own_rows, width), F32), like((taps, first_rows, width), F32),
+         like((2,), F32)],
+        smem_outs=(2,),
+        name="total",
     )
     return (layer_loss, jnp.transpose(grad_first, (1, 0, 2)), jnp.transpose(grad_second, (1, 0, 2)))
 

time: 101 us -> 93 us (0.921)
  waiting for transfers between devices: 25.9 us -> 6.51 us
  blocking collectives: 21.6 us -> 35.9 us
  starting transfers between devices: 22.5 us -> 18.8 us
    all_to_all x1 -> x0, waiting for transfers between devices: 19.4 us -> none  [shards(): blocks_second = lax.all_to_all(summed_second, ZY, 0, 0)]
    all_to_all x1, blocking collectives: 21.6 us -> 35.9 us  [shards(): blocks = lax.all_to_all(joint, ZY, 0, 0)]
    all_to_all x1 -> x0, starting transfers between devices: 3.7 us -> none  [shards(): blocks_second = lax.all_to_all(summed_second, ZY, 0, 0)]
    pallas_call x13 -> x12, Pallas kernels: 30.1 us -> 30.5 us  [call(): pl.pallas_call(body, out_shape=[pltpu.HBM(x.shape, x.dtype) if at in hbm_...]
  transfers between devices with their start and end apart: 15 -> 14, of which waited for: 7 -> 6; matrix products, arithmetic and copies ran while one was open for 0% -> 0% of each run, Pallas kernels for 21% -> 23%
where the time goes in v3:
time: 93 us; the launch traced here: 92.6 us
  blocking collectives  35.9 us (39%)
  Pallas kernels  30.5 us (33%)
  starting transfers between devices  18.8 us (20%)
  waiting for transfers between devices  6.51 us (7%)
  between operations  0.95 us (1%)
    all_to_all x1, blocking collectives, shards(): blocks = lax.all_to_all(joint, ZY, 0, 0)  35.9 us
    pallas_call x12, Pallas kernels, call(): pl.pallas_call(body, out_shape=[pltpu.HBM(x.shape, x.dtype) if at in hbm_...  30.5 us
    ppermute x12, starting transfers between devices, turn(): lax.ppermute(x, 'section', [(i, (i + step) % count) for i in range(count)])  18.7 us
    ppermute x12, waiting for transfers between devices, turn(): lax.ppermute(x, 'section', [(i, (i + step) % count) for i in range(count)])  5.76 us
  transfers between devices with their start and end apart: 14, of which 6 were waited for; matrix products, arithmetic and copies ran while one was open for 0% of the time, Pallas kernels for 23%

profile of v3, /device:TPU:0, one launch (start us, length us, event | category | flops | bytes accessed | tf_op | source)
XLA Modules:
  0.0 92.6 jit_solution(15513886840817588175)
XLA Ops:
  0.6 3.5 %first_a.1 = (bf16[384,256]{1,0:T(8,128)(2,1)S(1)}, bf16[3,384,512]{2,1,0:T(8,128)(2,1)}, f32[8,128]{1,0:T(8,128)S(1)}, bf16[5,512,256]{2,1,0:T(8,128)(2,1)S(1)}, bf16[8,144,512]{2,1,0:T(8,128)(2,1)S(1)}) custom-call(bf16[8,144,512]{2,1,0:T(8,128)(2,1)} %refs_0_.1, bf16[8,144,512]{2,1,0:T(8,128)(2,1)} %refs_1_.1, bf16[5,512,256]{2,1,0:T(8,128)(2,1)} %refs_2_.2), custom_call_target="tpu_custom_call" | custom-call | flops 503316480 | bytes 7540736 | tf_op jit(solution)/shard_map/first_a/pallas_call | solution.py:352
  4.2 1.6 %collective-permute-start = (bf16[384,256]{1,0:T(8,128)(2,1)S(1)}, bf16[384,256]{1,0:T(8,128)(2,1)S(1)}, u32[]{:S(2)}, u32[]{:S(2)}) collective-permute-start(bf16[384,256]{1,0:T(8,128)(2,1)S(1)} %get-tuple-element.33.refs_1_.refs_3_), channel_id=1, source_target_pairs={{0,1},{1,2},{2,3},{3,0},{4,5},{5,6},{6,7},{7,4},{8,9},{9,10},{10,1... | collective-permute-start | bytes 589832 | tf_op jit(solution)/shard_map/ppermute | solution.py:382
  5.8 2.6 %first_b.1 = (bf16[384,256]{1,0:T(8,128)(2,1)S(1)}, bf16[3,384,512]{2,1,0:T(8,128)(2,1)}, f32[8,128]{1,0:T(8,128)S(1)}, bf16[5,1024,256]{2,1,0:T(8,128)(2,1)S(1)}) custom-call(bf16[8,144,512]{2,1,0:T(8,128)(2,1)S(1)} %get-tuple-element.34.refs_0_, bf16[5,512,256]{2,1,0:T(8,128)(2,1)S(1)} %get-tuple-element.35.refs_1_, bf16[5,1024,256]{2,1,0:T(8,128)(2,1)} %refs_2_.3), custom_call_target="tpu_custom_call" | custom-call | flops 503316480 | bytes 9113600 | tf_op jit(solution)/shard_map/first_b/pallas_call | solution.py:352
  8.5 1.7 %collective-permute-start.4 = (bf16[384,256]{1,0:T(8,128)(2,1)S(1)}, bf16[384,256]{1,0:T(8,128)(2,1)S(1)}, u32[]{:S(2)}, u32[]{:S(2)}) collective-permute-start(bf16[384,256]{1,0:T(8,128)(2,1)S(1)} %get-tuple-element.39.refs_1_.refs_4_), channel_id=1, source_target_pairs={{0,3},{1,0},{2,1},{3,2},{4,7},{5,4},{6,5},{7,6},{8,11},{9,8},{10,9... | collective-permute-start | bytes 589832 | tf_op jit(solution)/shard_map/ppermute | solution.py:382
  10.2 1.6 %collective-permute-start.1 = (bf16[384,256]{1,0:T(8,128)(2,1)S(1)}, bf16[384,256]{1,0:T(8,128)(2,1)}, u32[]{:S(2)}, u32[]{:S(2)}) collective-permute-start(bf16[384,256]{1,0:T(8,128)(2,1)S(1)} %get-tuple-element.33.refs_1_.refs_3_), channel_id=1, source_target_pairs={{0,3},{1,0},{2,1},{3,2},{4,7},{5,4},{6,5},{7,6},{8,11},{9,8},{10,9... | collective-permute-start | bytes 589832 | tf_op jit(solution)/shard_map/ppermute | solution.py:382
  11.8 0.1 collective-permute-done.refs_2_
  12.0 0.5 collective-permute-start.2
  12.5 1.5 %collective-permute-start.3 = (bf16[384,256]{1,0:T(8,128)(2,1)S(1)}, bf16[384,256]{1,0:T(8,128)(2,1)}, u32[]{:S(2)}, u32[]{:S(2)}) collective-permute-start(bf16[384,256]{1,0:T(8,128)(2,1)S(1)} %get-tuple-element.39.refs_1_.refs_4_), channel_id=1, source_target_pairs={{0,1},{1,2},{2,3},{3,0},{4,5},{5,6},{6,7},{7,4},{8,9},{9,10},{10,1... | collective-permute-start | bytes 589832 | tf_op jit(solution)/shard_map/ppermute | solution.py:382
  13.9 2.4 %collective-permute-done.4.refs_3_ = bf16[384,256]{1,0:T(8,128)(2,1)S(1)} collective-permute-done((bf16[384,256]{1,0:T(8,128)(2,1)S(1)}, bf16[384,256]{1,0:T(8,128)(2,1)S(1)}, u32[]{:S(2)}, u32[]{:S(2)}) %collective-permute-start.4) | collective-permute-done | bytes 196640 | tf_op jit(solution)/shard_map/ppermute | solution.py:382
  16.4 2.9 %collective-permute-start.5 = (bf16[384,256]{1,0:T(8,128)(2,1)S(1)}, bf16[384,256]{1,0:T(8,128)(2,1)}, u32[]{:S(2)}, u32[]{:S(2)}) collective-permute-start(bf16[384,256]{1,0:T(8,128)(2,1)S(1)} %collective-permute-done.4.refs_3_), channel_id=1, source_target_pairs={{0,3},{1,0},{2,1},{3,2},{4,7},{5,4},{6,5},{7,6},{8,11},{9,8},{10,9... | collective-permute-start | bytes 589832 | tf_op jit(solution)/shard_map/ppermute | solution.py:382
  19.3 1.4 %collective-permute-done.1.refs_3_ = bf16[384,256]{1,0:T(8,128)(2,1)} collective-permute-done((bf16[384,256]{1,0:T(8,128)(2,1)S(1)}, bf16[384,256]{1,0:T(8,128)(2,1)}, u32[]{:S(2)}, u32[]{:S(2)}) %collective-permute-start.1) | collective-permute-done | bytes 196640 | tf_op jit(solution)/shard_map/ppermute | solution.py:382
  20.7 0.4 collective-permute-done.2.refs_4_
  21.1 3.8 %second_a.1 = (bf16[384,1024]{1,0:T(8,128)(2,1)}, bf16[384,1280]{1,0:T(8,128)(2,1)}, bf16[392,256]{1,0:T(8,128)(2,1)S(1)}, bf16[8,256]{1,0:T(8,128)(2,1)S(1)}, b...) custom-call(s32[1]{0:T(128)} %bitcast.1.refs_0_, ...), custom_call_target="tpu_custom_call" | custom-call | flops 1258291200 | bytes 5984260 | tf_op jit(solution)/shard_map/second_a/pallas_call | solution.py:352
  24.8 0.0 collective-permute-done.5.refs_4_
  24.8 3.9 %second_b.1 = (bf16[384,1024]{1,0:T(8,128)(2,1)}, bf16[384,1280]{1,0:T(8,128)(2,1)}, bf16[392,256]{1,0:T(8,128)(2,1)S(1)}, bf16[8,256]{1,0:T(8,128)(2,1)S(1)}) custom-call(s32[1]{0:T(128)} %bitcast.1.refs_0_, bf16[384,256]{1,0:T(8,128)(2,1)S(1)} %get-tuple-element.39.refs_1_.refs_4_, bf16[384,256]{1,0:T(8,128)(2,1)} %collective-permute-done.3.refs_2_, ...), custom_call_target="tpu_custom_call" | custom-call | flops 1258291200 | bytes 5386244 | tf_op jit(solution)/shard_map/second_b/pallas_call | solution.py:352
  28.8 2.6 %collective-permute-start.10 = (bf16[392,256]{1,0:T(8,128)(2,1)S(1)}, bf16[392,256]{1,0:T(8,128)(2,1)S(1)}, u32[]{:S(2)}, u32[]{:S(2)}) collective-permute-start(bf16[392,256]{1,0:T(8,128)(2,1)S(1)} %get-tuple-element.50), channel_id=1, source_target_pairs={{0,3},{1,0},{2,1},{3,2},{4,7},{5,4},{6,5},{7,6},{8,11},{9,8},{10,9... | collective-permute-start | bytes 602120 | tf_op jit(solution)/shard_map/ppermute | solution.py:382
  31.4 0.0 collective-permute-start.6
  31.4 2.2 %back_b.1 = (bf16[392,256]{1,0:T(8,128)(2,1)S(1)}, bf16[392,256]{1,0:T(8,128)(2,1)S(1)}, bf16[384,256]{1,0:T(8,128)(2,1)S(1)}) custom-call(s32[1]{0:T(128)} %bitcast.1.refs_0_, bf16[384,1280]{1,0:T(8,128)(2,1)} %get-tuple-element.43.refs_1_.refs_4_, bf16[5,1024,256]{2,1,0:T(8,128)(2,1)S(1)} %get-tuple-element.36.refs_5_.refs_2_, ...), custom_call_target="tpu_custom_call" | custom-call | flops 3019898880 | bytes 16826384 | tf_op jit(solution)/shard_map/back_b/pallas_call | solution.py:352
  33.6 0.7 collective-permute-start.8
  34.3 2.7 %collective-permute-start.9 = (bf16[392,256]{1,0:T(8,128)(2,1)S(1)}, bf16[392,256]{1,0:T(8,128)(2,1)S(1)}, u32[]{:S(2)}, u32[]{:S(2)}) collective-permute-start(bf16[392,256]{1,0:T(8,128)(2,1)S(1)} %get-tuple-element.48), channel_id=1, source_target_pairs={{0,3},{1,0},{2,1},{3,2},{4,7},{5,4},{6,5},{7,6},{8,11},{9,8},{10,9... | collective-permute-start | bytes 602120 | tf_op jit(solution)/shard_map/ppermute | solution.py:382
  37.0 2.6 %collective-permute-start.11 = (bf16[392,256]{1,0:T(8,128)(2,1)S(1)}, bf16[392,256]{1,0:T(8,128)(2,1)S(1)}, u32[]{:S(2)}, u32[]{:S(2)}) collective-permute-start(bf16[392,256]{1,0:T(8,128)(2,1)S(1)} %relay_b.1.refs_6_), channel_id=1, source_target_pairs={{0,3},{1,0},{2,1},{3,2},{4,7},{5,4},{6,5},{7,6},{8,11},{9,8},{10,9... | collective-permute-start | bytes 602120 | tf_op jit(solution)/shard_map/ppermute | solution.py:382
  39.6 0.3 collective-permute-start.7
  39.9 5.4 %weight_second.1 = (bf16[16,160,256]{2,1,0:T(8,128)(2,1)S(1)}, bf16[16,160,256]{2,1,0:T(8,128)(2,1)S(1)}) custom-call(s32[1]{0:T(128)} %bitcast.refs_0_, bf16[384,1024]{1,0:T(8,128)(2,1)} %get-tuple-element.53.refs_1_, bf16[384,1024]{1,0:T(8,128)(2,1)} %get-tuple-element.54.refs_2_, bf16[384,1280]{1,0:T(8,128)(2,1)} %get-tuple-element.55.refs_3_, ...), custom_call_target="tpu_custom_call" | custom-call | flops 8053063680 | bytes 24641552 | tf_op jit(solution)/shard_map/weight_second/pallas_call | solution.py:352
  45.3 0.1 collective-permute-start.13
  45.4 1.4 %collective-permute-done.7.refs_7_ = bf16[392,256]{1,0:T(8,128)(2,1)S(1)} collective-permute-done((bf16[392,256]{1,0:T(8,128)(2,1)S(1)}, bf16[392,256]{1,0:T(8,128)(2,1)S(1)}, u32[]{:S(2)}, u32[]{:S(2)}) %collective-permute-start.7) | collective-permute-done | bytes 200736 | tf_op jit(solution)/shard_map/ppermute | solution.py:382
  46.8 5.4 %weight_first.1 = (bf16[16,88,256]{2,1,0:T(8,128)(2,1)S(1)}, bf16[16,88,256]{2,1,0:T(8,128)(2,1)S(1)}) custom-call(s32[1]{0:T(128)} %bitcast.refs_0_, bf16[8,256]{1,0:T(8,128)(2,1)S(1)} %get-tuple-element.38.refs_1_, bf16[8,256]{1,0:T(8,128)(2,1)S(1)} %get-tuple-element.42.refs_3_.refs_2_, bf16[384,256]{1,0:T(8,128)(2,1)S(1)} %get-tuple-element.33.refs_1_.refs_3_, ...), custom_call_target="tpu_custom_call" | custom-call | flops 20132659200 | bytes 115998800 | tf_op jit(solution)/shard_map/weight_first/pallas_call | solution.py:352
  52.3 0.1 collective-permute-start.12
  52.4 1.4 %join_second.1.refs_2_ = bf16[16,248,256]{2,1,0:T(8,128)(2,1)} custom-call(bf16[16,160,256]{2,1,0:T(8,128)(2,1)S(1)} %get-tuple-element.56.refs_15_.refs_0_, bf16[16,160,256]{2,1,0:T(8,128)(2,1)S(1)} %collective-permute-done.13.refs_1_), custom_call_target="tpu_custom_call" | custom-call | bytes 4653056 | tf_op jit(solution)/shard_map/join_second/pallas_call | solution.py:352
  53.8 0.7 collective-permute-done.12.refs_1_
  54.5 1.1 %join_first.1 = bf16[16,248,256]{2,1,0:T(8,128)(2,1)} custom-call(bf16[16,88,256]{2,1,0:T(8,128)(2,1)S(1)} %get-tuple-element.57.refs_0_, bf16[16,88,256]{2,1,0:T(8,128)(2,1)S(1)} %collective-permute-done.12.refs_1_, bf16[16,248,256]{2,1,0:T(8,128)(2,1)} %join_second.1.refs_2_), custom_call_target="tpu_custom_call", output_to_operand_aliasing={{}: (2, {})} | custom-call | bytes 5505024 | tf_op jit(solution)/shard_map/join_first/pallas_call | solution.py:352
  55.6 35.9 %all_to_all.5.refs_0_ = bf16[16,248,256]{2,1,0:T(8,128)(2,1)S(1)} all-to-all(bf16[16,248,256]{2,1,0:T(8,128)(2,1)} %join_first.1), channel_id=1, replica_groups=mesh['dp_0'=4,'dp_1'=4,'dp_2'=2,'section'=4] {'dp_0','dp_1'}, dimensions={0} | all-to-all | bytes 4063232 | tf_op jit(solution)/shard_map/all_to_all | solution.py:547
  91.5 1.0 %total.1 = (f32[5,32,256]{2,1,0:T(8,128)}, f32[5,16,256]{2,1,0:T(8,128)}, f32[2]{0:T(128)}) custom-call(bf16[16,248,256]{2,1,0:T(8,128)(2,1)S(1)} %all_to_all.5.refs_0_), custom_call_target="tpu_custom_call" | custom-call | bytes 2277384 | tf_op jit(solution)/shard_map/total/pallas_call | solution.py:352
  (9 shorter events, 0.1 us)
Async XLA Ops:
  4.2 7.8 %collective-permute-start = (bf16[384,256]{1,0:T(8,128)(2,1)S(1)}, bf16[384,256]{1,0:T(8,128)(2,1)S(1)}, u32[]{:S(2)}, u32[]{:S(2)}) collective-permute-start(bf16[384,256]{1,0:T(8,128)(2,1)S(1)} %get-tuple-element.33.refs_1_.refs_3_), channel_id=1, source_target_pairs={{0,1},{1,2},{2,3},{3,0},{4,5},{5,6},{6,7},{7,4},{8,9},{9,10},{10,1... | collective-permute-start | bytes 589832 | tf_op jit(solution)/shard_map/ppermute | solution.py:382
  8.5 7.9 %collective-permute-start.4 = (bf16[384,256]{1,0:T(8,128)(2,1)S(1)}, bf16[384,256]{1,0:T(8,128)(2,1)S(1)}, u32[]{:S(2)}, u32[]{:S(2)}) collective-permute-start(bf16[384,256]{1,0:T(8,128)(2,1)S(1)} %get-tuple-element.39.refs_1_.refs_4_), channel_id=1, source_target_pairs={{0,3},{1,0},{2,1},{3,2},{4,7},{5,4},{6,5},{7,6},{8,11},{9,8},{10,9... | collective-permute-start | bytes 589832 | tf_op jit(solution)/shard_map/ppermute | solution.py:382
  10.2 10.5 %collective-permute-start.1 = (bf16[384,256]{1,0:T(8,128)(2,1)S(1)}, bf16[384,256]{1,0:T(8,128)(2,1)}, u32[]{:S(2)}, u32[]{:S(2)}) collective-permute-start(bf16[384,256]{1,0:T(8,128)(2,1)S(1)} %get-tuple-element.33.refs_1_.refs_3_), channel_id=1, source_target_pairs={{0,3},{1,0},{2,1},{3,2},{4,7},{5,4},{6,5},{7,6},{8,11},{9,8},{10,9... | collective-permute-start | bytes 589832 | tf_op jit(solution)/shard_map/ppermute | solution.py:382
  12.0 9.1 %collective-permute-start.2 = (bf16[384,256]{1,0:T(8,128)(2,1)S(1)}, bf16[384,256]{1,0:T(8,128)(2,1)}, u32[]{:S(2)}, u32[]{:S(2)}) collective-permute-start(bf16[384,256]{1,0:T(8,128)(2,1)S(1)} %collective-permute-done.refs_2_), channel_id=1, source_target_pairs={{0,1},{1,2},{2,3},{3,0},{4,5},{5,6},{6,7},{7,4},{8,9},{9,10},{10,1... | collective-permute-start | bytes 589832 | tf_op jit(solution)/shard_map/ppermute | solution.py:382
  12.5 12.4 %collective-permute-start.3 = (bf16[384,256]{1,0:T(8,128)(2,1)S(1)}, bf16[384,256]{1,0:T(8,128)(2,1)}, u32[]{:S(2)}, u32[]{:S(2)}) collective-permute-start(bf16[384,256]{1,0:T(8,128)(2,1)S(1)} %get-tuple-element.39.refs_1_.refs_4_), channel_id=1, source_target_pairs={{0,1},{1,2},{2,3},{3,0},{4,5},{5,6},{6,7},{7,4},{8,9},{9,10},{10,1... | collective-permute-start | bytes 589832 | tf_op jit(solution)/shard_map/ppermute | solution.py:382
  16.4 8.5 %collective-permute-start.5 = (bf16[384,256]{1,0:T(8,128)(2,1)S(1)}, bf16[384,256]{1,0:T(8,128)(2,1)}, u32[]{:S(2)}, u32[]{:S(2)}) collective-permute-start(bf16[384,256]{1,0:T(8,128)(2,1)S(1)} %collective-permute-done.4.refs_3_), channel_id=1, source_target_pairs={{0,3},{1,0},{2,1},{3,2},{4,7},{5,4},{6,5},{7,6},{8,11},{9,8},{10,9... | collective-permute-start | bytes 589832 | tf_op jit(solution)/shard_map/ppermute | solution.py:382
  28.8 8.2 %collective-permute-start.10 = (bf16[392,256]{1,0:T(8,128)(2,1)S(1)}, bf16[392,256]{1,0:T(8,128)(2,1)S(1)}, u32[]{:S(2)}, u32[]{:S(2)}) collective-permute-start(bf16[392,256]{1,0:T(8,128)(2,1)S(1)} %get-tuple-element.50), channel_id=1, source_target_pairs={{0,3},{1,0},{2,1},{3,2},{4,7},{5,4},{6,5},{7,6},{8,11},{9,8},{10,9... | collective-permute-start | bytes 602120 | tf_op jit(solution)/shard_map/ppermute | solution.py:382
  31.4 8.2 %collective-permute-start.6 = (bf16[392,256]{1,0:T(8,128)(2,1)S(1)}, bf16[392,256]{1,0:T(8,128)(2,1)S(1)}, u32[]{:S(2)}, u32[]{:S(2)}) collective-permute-start(bf16[392,256]{1,0:T(8,128)(2,1)S(1)} %get-tuple-element.46), channel_id=1, source_target_pairs={{0,1},{1,2},{2,3},{3,0},{4,5},{5,6},{6,7},{7,4},{8,9},{9,10},{10,1... | collective-permute-start | bytes 602120 | tf_op jit(solution)/shard_map/ppermute | solution.py:382
  33.6 11.8 %collective-permute-start.8 = (bf16[392,256]{1,0:T(8,128)(2,1)S(1)}, bf16[392,256]{1,0:T(8,128)(2,1)S(1)}, u32[]{:S(2)}, u32[]{:S(2)}) collective-permute-start(bf16[392,256]{1,0:T(8,128)(2,1)S(1)} %get-tuple-element.47), channel_id=1, source_target_pairs={{0,1},{1,2},{2,3},{3,0},{4,5},{5,6},{6,7},{7,4},{8,9},{9,10},{10,1... | collective-permute-start | bytes 602120 | tf_op jit(solution)/shard_map/ppermute | solution.py:382
  34.3 11.2 %collective-permute-start.9 = (bf16[392,256]{1,0:T(8,128)(2,1)S(1)}, bf16[392,256]{1,0:T(8,128)(2,1)S(1)}, u32[]{:S(2)}, u32[]{:S(2)}) collective-permute-start(bf16[392,256]{1,0:T(8,128)(2,1)S(1)} %get-tuple-element.48), channel_id=1, source_target_pairs={{0,3},{1,0},{2,1},{3,2},{4,7},{5,4},{6,5},{7,6},{8,11},{9,8},{10,9... | collective-permute-start | bytes 602120 | tf_op jit(solution)/shard_map/ppermute | solution.py:382
  37.0 8.4 %collective-permute-start.11 = (bf16[392,256]{1,0:T(8,128)(2,1)S(1)}, bf16[392,256]{1,0:T(8,128)(2,1)S(1)}, u32[]{:S(2)}, u32[]{:S(2)}) collective-permute-start(bf16[392,256]{1,0:T(8,128)(2,1)S(1)} %relay_b.1.refs_6_), channel_id=1, source_target_pairs={{0,3},{1,0},{2,1},{3,2},{4,7},{5,4},{6,5},{7,6},{8,11},{9,8},{10,9... | collective-permute-start | bytes 602120 | tf_op jit(solution)/shard_map/ppermute | solution.py:382
  39.6 7.2 %collective-permute-start.7 = (bf16[392,256]{1,0:T(8,128)(2,1)S(1)}, bf16[392,256]{1,0:T(8,128)(2,1)S(1)}, u32[]{:S(2)}, u32[]{:S(2)}) collective-permute-start(bf16[392,256]{1,0:T(8,128)(2,1)S(1)} %relay_a.1.refs_5_), channel_id=1, source_target_pairs={{0,1},{1,2},{2,3},{3,0},{4,5},{5,6},{6,7},{7,4},{8,9},{9,10},{10,1... | collective-permute-start | bytes 602120 | tf_op jit(solution)/shard_map/ppermute | solution.py:382
  45.3 7.0 %collective-permute-start.13 = (bf16[16,160,256]{2,1,0:T(8,128)(2,1)S(1)}, bf16[16,160,256]{2,1,0:T(8,128)(2,1)S(1)}, u32[]{:S(2)}, u32[]{:S(2)}) collective-permute-start(bf16[16,160,256]{2,1,0:T(8,128)(2,1)S(1)} %get-tuple-element.59), channel_id=1, source_target_pairs={{0,4},{4,0},{1,5},{5,1},{2,6},{6,2},{3,7},{7,3},{8,12},{12,8},{9,1... | collective-permute-start | bytes 3932168 | tf_op jit(solution)/shard_map/ppermute | solution.py:390
  52.3 2.3 %collective-permute-start.12 = (bf16[16,88,256]{2,1,0:T(8,128)(2,1)S(1)}, bf16[16,88,256]{2,1,0:T(8,128)(2,1)S(1)}, u32[]{:S(2)}, u32[]{:S(2)}) collective-permute-start(bf16[16,88,256]{2,1,0:T(8,128)(2,1)S(1)} %get-tuple-element.58), channel_id=1, source_target_pairs={{0,4},{4,0},{1,5},{5,1},{2,6},{6,2},{3,7},{7,3},{8,12},{12,8},{9,1... | collective-permute-start | bytes 2162696 | tf_op jit(solution)/shard_map/ppermute | solution.py:390

commit v4 on v3

--- a/solution.py
+++ b/solution.py
@@ -13,6 +13,9 @@
 F32 = jnp.float32
 BF16 = jnp.bfloat16
 VMEM_LIMIT = 16 << 20
+NEAR_PHASES = (False, False)
+NEAR_ALL = (True, True)
+NEAR_SMALL = True
 
 smooth_width = 0.1
 leak_slope = 0.1
@@ -59,7 +62,8 @@
     return out.astype(BF16)
 
 
-def strided_conv(take, cols, span, w, h_out, phases_out, loss, padded, phases, out_sem):
+def strided_conv(take, cols, span, w, h_out, phases_out, loss, padded, *far):
+    phases = far[0] if far else phases_out
     frames = span // 3
     rows = 2 * cols * frames
     width = w.shape[2]
@@ -71,8 +75,9 @@
         parts = dot(select, take(n)).astype(BF16)
         for p in range(3):
             phases[p, n * frames : (n + 1) * frames, :] = parts[p * frames : (p + 1) * frames]
-    copy_out = pltpu.make_async_copy(phases, phases_out, out_sem)
-    copy_out.start()
+    if far:
+        copy_out = pltpu.make_async_copy(phases, phases_out, far[1])
+        copy_out.start()
     padded[:, :8, :] = jnp.zeros((2 * cols, 8, width), F32)
     earlier = dot(phases[1], w[0]) + dot(phases[2], w[1])
     padded[:, 8 : 8 + frames, :] = earlier.reshape(2 * cols, frames, width)
@@ -81,12 +86,13 @@
     h_out[...] = h
     _, root = difference_terms(h[: rows // 2], h[rows // 2 :])
     loss[...] = fold_rows(root - smooth_width)
-    copy_out.wait()
+    if far:
+        copy_out.wait()
 
 
 def first_early_kernel(
     real, fake, w_hbm, h_out, phases_out, loss, w, rest,
-    padded, phases, out_sem, held, held_sem, rest_sem, w_sem,
+    padded, held, held_sem, rest_sem, w_sem, *far_scratch,
 ):
     cols = held.shape[0] // 2
     span = held.shape[1]
@@ -109,28 +115,28 @@
             w_copy.wait()
         return held[n]
 
-    strided_conv(take, cols, span, w, h_out, phases_out, loss, padded, phases, out_sem)
+    strided_conv(take, cols, span, w, h_out, phases_out, loss, padded, *far_scratch)
     for copy in rest_copies:
         copy.wait()
 
 
-def first_late_kernel(
-    rest, w, w_next_hbm, h_out, phases_out, loss, w_next, padded, phases, out_sem, sem
-):
+def first_late_kernel(rest, w, w_next_hbm, h_out, phases_out, loss, w_next, padded, sem, *far):
     copy = pltpu.make_async_copy(w_next_hbm, w_next, sem)
     copy.start()
     cols, span = rest.shape[0] // 2, rest.shape[1]
-    strided_conv(
-        lambda n: rest[n], cols, span, w, h_out, phases_out, loss, padded, phases, out_sem
-    )
+    strided_conv(lambda n: rest[n], cols, span, w, h_out, phases_out, loss, padded, *far)
     copy.wait()
 
 
 def second_kernel(
-    normaliser, whole, s_ref, own, prev, following, far, w, loss_first,
+    normaliser, whole, near, s_ref, own, prev, following, far, w, loss_first,
     all_out, shifted_out, far_t, loss, *rest,
 ):
-    *backs, h_all, shifted, padded, in_sems, all_sem, shifted_sem = rest
+    if near:
+        h_all, shifted = all_out, shifted_out
+        *backs, padded, in_sems = rest
+    else:
+        *backs, padded, in_sems, h_all, shifted, all_sem, shifted_sem = rest
     rows, width = own.shape
     half = rows // 2
     taps = w.shape[0]
@@ -145,8 +151,9 @@
         copies[-1].start()
     for copy in copies:
         copy.wait()
-    copy_all = pltpu.make_async_copy(h_all, all_out, all_sem)
-    copy_all.start()
+    if not near:
+        copy_all = pltpu.make_async_copy(h_all, all_out, all_sem)
+        copy_all.start()
     zeros = jnp.zeros((padded.shape[0], 8, width), F32)
     padded[:, :8, :] = zeros
     padded[:, 8 + frames :, :] = zeros
@@ -166,14 +173,16 @@
     for k in range(taps):
         moved = padded[:, 10 - k : 10 - k + frames, :].reshape(rows, width)
         shifted[:, k * width : (k + 1) * width] = moved.astype(BF16)
-    copy_shifted = pltpu.make_async_copy(shifted, shifted_out, shifted_sem)
-    copy_shifted.start()
+    if not near:
+        copy_shifted = pltpu.make_async_copy(shifted, shifted_out, shifted_sem)
+        copy_shifted.start()
     far_t[:rows] = back_term(s, 2, shifted, w)
     far_t[rows:] = loss_rows
     if whole:
         back_rest(s, shifted, w, loss_rows, 3, *backs)
-    copy_all.wait()
-    copy_shifted.wait()
+    if not near:
+        copy_all.wait()
+        copy_shifted.wait()
 
 
 def back_term(s, away, shifted, w):
@@ -194,10 +203,13 @@
     own[...] = back_term(s, 0, shifted, w)
 
 
-def back_kernel(s_ref, shifted_hbm, w, loss, following, prev, own, shifted, sem):
-    copy = pltpu.make_async_copy(shifted_hbm, shifted, sem)
-    copy.start()
-    copy.wait()
+def back_kernel(s_ref, shifted, w, loss, following, prev, own, *rest):
+    if rest:
+        held, sem = rest
+        copy = pltpu.make_async_copy(shifted, held, sem)
+        copy.start()
+        copy.wait()
+        shifted = held
     back_rest(s_ref[0], shifted, w, loss[...], 1, following, prev, own)
 
 
@@ -214,67 +226,70 @@
     theirs[at : at + count, k * rows : (k + 1) * rows] = jnp.where(c == 0, odd, even)
 
 
-def weight_second_kernel(
-    taps, c_ref, h_a, h_b, shifted_a, shifted_b, mine, theirs, h_all, shifted, h_sem, shifted_sem
-):
+def weight_second_kernel(taps, nears, c_ref, h_a, h_b, shifted_a, shifted_b, mine, theirs, *rest):
     own_rows, width = mine.shape[1] // taps, mine.shape[2]
-    rows = h_a.shape[0]
     c = c_ref[0]
     step = 256
-    count = h_all.shape[1] // step
-    moves = []
-    for n, x in enumerate((shifted_a, shifted_b)):
-        moves.append(
-            pltpu.make_async_copy(x, shifted.at[n * rows : (n + 1) * rows], shifted_sem.at[n])
-        )
-    parts = []
-    for q in range(count):
-        for n, x in enumerate((h_a, h_b)):
-            cut = slice(q * step, (q + 1) * step)
-            parts.append(
-                pltpu.make_async_copy(
-                    x.at[:, cut], h_all.at[n * rows : (n + 1) * rows, cut], h_sem.at[2 * q + n]
+    count = h_a.shape[1] // step
+    rest = list(rest)
+    pairs, first, later = [], [], [[] for _ in range(count)]
+    for near, h, x in ((nears[0], h_a, shifted_a), (nears[1], h_b, shifted_b)):
+        if not near:
+            h_held, x_held, h_sem, x_sem = rest[:4]
+            rest = rest[4:]
+            first.append(pltpu.make_async_copy(x, x_held, x_sem))
+            for q in range(count):
+                cut = slice(q * step, (q + 1) * step)
+                later[q].append(
+                    pltpu.make_async_copy(h.at[:, cut], h_held.at[:, cut], h_sem.at[q])
                 )
-            )
-    for copy in moves + parts:
+            h, x = h_held, x_held
+        pairs.append((h, x))
+    for copy in first + sum(later, []):
         copy.start()
-    for copy in moves:
+    for copy in first:
         copy.wait()
     for q in range(count):
-        parts[2 * q].wait()
-        parts[2 * q + 1].wait()
-        g = dot_rows(h_all[:, q * step : (q + 1) * step], shifted[...])
+        for copy in later[q]:
+            copy.wait()
+        cut = slice(q * step, (q + 1) * step)
+        g = sum(dot_rows(h[:, cut], x[...]) for h, x in pairs)
         for k in range(taps):
             put(g[:, k * width : (k + 1) * width], c, (mine, theirs),
                 q * step // (2 * own_rows), own_rows, k)
 
 
 def weight_first_kernel(
-    normaliser, taps, c_ref, loss_a, loss_b, *refs,
+    normaliser, taps, nears, c_ref, loss_a, loss_b, *refs,
 ):
-    *sources, phases_a, phases_b, mine, theirs, padded, moved, got, phases, sems, phase_sems = refs
+    *sources, phases_a, phases_b, mine, theirs, padded, moved = refs[:16]
+    rest = list(refs[16:])
     rows, width = sources[0].shape
     half = rows // 2
     frames = padded.shape[1] - 8
     c = c_ref[0]
-    copies = []
-    for n, x in enumerate(sources):
-        copies.append(pltpu.make_async_copy(x, got.at[n, : x.shape[0]], sems.at[n]))
-    phase_copies = []
-    for p in range(3):
-        for n, x in enumerate((phases_a, phases_b)):
-            phase_copies.append(
-                pltpu.make_async_copy(
-                    x.at[p], phases.at[p, n * rows : (n + 1) * rows], phase_sems.at[2 * p + n]
-                )
-            )
-    for copy in copies + phase_copies:
+    small, large = [], []
+    if not nears[0]:
+        got, sems = rest[:2]
+        rest = rest[2:]
+        for n, x in enumerate(sources):
+            small.append(pltpu.make_async_copy(x, got.at[n, : x.shape[0]], sems.at[n]))
+        sources = [got.at[n, : x.shape[0]] for n, x in enumerate(sources)]
+    phases = []
+    for near, x in zip(nears[1:], (phases_a, phases_b)):
+        if not near:
+            held, sem = rest[:2]
+            rest = rest[2:]
+            large.append(pltpu.make_async_copy(x, held, sem))
+            x = held
+        phases.append(x)
+    for copy in small + large:
         copy.start()
-    for copy in copies:
+    for copy in small:
         copy.wait()
     padded[:, frames:, :] = jnp.zeros((padded.shape[0], 8, width), F32)
     for n in range(2):
-        h, own, a, b = (got.at[2 * at + n] for at in range(4))
+        h, own, a, b = (sources[2 * at + n] for at in range(4))
         difference, root = difference_terms(h[:half], h[half:rows])
         slope = difference / root / normaliser
         for at, sign in ((0, 1.0), (half, -1.0)):
@@ -291,18 +306,18 @@
     groups = mine.shape[0]
     own_rows = (mine.shape[1] - 8) // taps
     outs = (mine, theirs)
+    for copy in large:
+        copy.wait()
     for p in range(3):
-        phase_copies[2 * p].wait()
-        phase_copies[2 * p + 1].wait()
-        if p == 0:
-            put(dot_rows(phases[p], moved[:, :width]), c, outs, 0, own_rows, 2)
-        else:
-            g = dot_rows(phases[p], moved[...])
-            put(g[:, :width], c, outs, 0, own_rows, 2 + p)
+        lanes = width if p == 0 else 2 * width
+        g = dot_rows(phases[0][p], moved[:rows, :lanes])
+        g = g + dot_rows(phases[1][p], moved[rows:, :lanes])
+        put(g[:, :width], c, outs, 0, own_rows, 2 + p)
+        if p > 0:
             put(g[:, width:], c, outs, 0, own_rows, p - 1)
     total = loss_a[...].astype(F32) + loss_b[...].astype(F32)
-    for at in range(4, 10):
-        total = total + got[at, rows:].astype(F32)
+    for x in sources[4:]:
+        total = total + x[rows:].astype(F32)
     lines = split_rows(jnp.sum(total, axis=0, keepdims=True), 3 * c)
     for x in outs:
         x[:, taps * own_rows :, :] = jnp.broadcast_to(lines[None], (groups, 8, width))
@@ -404,9 +419,9 @@
     c = lax.axis_index("dp_2").reshape(1).astype(jnp.int32)
     dma = pltpu.SemaphoreType.DMA
     chunk_outs = [like((rows, width)), like((3, rows, in_width)), like((8, 128), F32)]
-    conv_scratch = [
-        pltpu.VMEM((cols, frames + 8, width), F32), pltpu.VMEM((3, rows, in_width), BF16), dma
-    ]
+    conv_scratch = [pltpu.VMEM((cols, frames + 8, width), F32)]
+    phases_far = [pltpu.VMEM((3, rows, in_width), BF16), dma]
+    all_far = [pltpu.VMEM((rows, width_all), BF16), pltpu.VMEM((rows, taps * width), BF16)]
     flops = 2 * rows * taps * in_width * width
 
     h_a, phases_a, loss_a, w_first, rest = call(
@@ -414,9 +429,10 @@
         (real_in, fake_in, kernel_first),
         chunk_outs + [like(kernel_first.shape), like((cols, span, in_width))],
         conv_scratch
-        + [pltpu.VMEM((cols, span, in_width), BF16), dma((cols,)), dma((2,)), dma],
+        + [pltpu.VMEM((cols, span, in_width), BF16), dma((cols,)), dma((2,)), dma]
+        + phases_far * (not NEAR_PHASES[0]),
         hbm=(0, 1, 2),
-        hbm_outs=(1,),
+        hbm_outs=() if NEAR_PHASES[0] else (1,),
         flops=flops,
         name="first_a",
     )
@@ -426,9 +442,9 @@
         first_late_kernel,
         (rest, w_first, kernel_second),
         chunk_outs + [like(kernel_second.shape)],
-        conv_scratch + [dma],
+        conv_scratch + [dma] + phases_far * (not NEAR_PHASES[1]),
         hbm=(2,),
-        hbm_outs=(1,),
+        hbm_outs=() if NEAR_PHASES[1] else (1,),
         flops=flops,
         cost=1,
         name="first_b",
@@ -442,18 +458,18 @@
                    like((8, width))]
     back_outs = [like((rows + 8, width)), like((rows + 8, width)), like((rows, width))]
     second_scratch = [
-        pltpu.VMEM((rows, width_all), BF16), pltpu.VMEM((rows, taps * width), BF16),
-        pltpu.VMEM((cols, frames + 16, width), F32), dma((4,)), dma, dma,
+        pltpu.VMEM((cols, frames + 16, width), F32), dma((4,)),
     ]
+    copies = all_far + [dma, dma]
     flops = 2 * rows * taps * (width_all + width) * width
     all_a, shifted_a, far_t, loss_a, next_t, prev_t, own_a = call(
-        functools.partial(second_kernel, normaliser, True),
+        functools.partial(second_kernel, normaliser, True, NEAR_ALL[0]),
         (s, h_a, prev_a, following_a, far_a, w_second, loss_a),
         second_outs + back_outs,
-        second_scratch,
+        second_scratch + copies * (not NEAR_ALL[0]),
         smem=1,
         loose=(1, 2, 3, 4),
-        hbm_outs=(0, 1),
+        hbm_outs=() if NEAR_ALL[0] else (0, 1),
         cost=1,
         flops=flops,
         name="second_a",
@@ -464,13 +480,13 @@
     from_prev_a = turn(relayed_a, 1)
 
     all_b, shifted_b, far_t, loss_b = call(
-        functools.partial(second_kernel, normaliser, False),
+        functools.partial(second_kernel, normaliser, False, NEAR_ALL[1]),
         (s, h_b, prev_b, following_b, far_b, w_second, loss_b),
         second_outs,
-        second_scratch,
+        second_scratch + copies * (not NEAR_ALL[1]),
         smem=1,
         loose=(1, 2, 3, 4),
-        hbm_outs=(0, 1),
+        hbm_outs=() if NEAR_ALL[1] else (0, 1),
         cost=1,
         after=(own_a,),
         flops=flops,
@@ -481,9 +497,9 @@
         back_kernel,
         (s, shifted_b, w_second, loss_b),
         back_outs,
-        [pltpu.VMEM((rows, taps * width), BF16), dma],
+        [] if NEAR_ALL[1] else [pltpu.VMEM((rows, taps * width), BF16), dma],
         smem=1,
-        hbm=(1,),
+        hbm=() if NEAR_ALL[1] else (1,),
         cost=4,
         flops=2 * rows * taps * width * width * 3,
         name="back_b",
@@ -494,13 +510,12 @@
 
     own_rows = width_all // replicas
     mine_second, theirs = call(
-        functools.partial(weight_second_kernel, taps),
+        functools.partial(weight_second_kernel, taps, NEAR_ALL),
         (c, all_a, all_b, shifted_a, shifted_b),
         [like((groups, taps * own_rows, width))] * 2,
-        [pltpu.VMEM((2 * rows, width_all), BF16), pltpu.VMEM((2 * rows, taps * width), BF16),
-         dma((2 * width_all // 256,)), dma((2,))],
+        (all_far + [dma((width_all // 256,)), dma]) * (2 - sum(NEAR_ALL)),
         smem=1,
-        hbm=(1, 2, 3, 4),
+        hbm=tuple(at for at in (1, 2, 3, 4) if not NEAR_ALL[(at - 1) % 2]),
         cost=4,
         after=(relayed_a, relayed_b),
         flops=4 * rows * taps * width * width_all,
@@ -519,16 +534,16 @@
     )
 
     mine_first, theirs = call(
-        functools.partial(weight_first_kernel, normaliser, taps),
+        functools.partial(weight_first_kernel, normaliser, taps, (NEAR_SMALL, *NEAR_PHASES)),
         (c, loss_a, loss_b, h_a, h_b, own_a, own_b, from_prev_a, from_prev_b, from_following_a,
          from_following_b, pass_a, pass_b, phases_a, phases_b),
         [like((groups, taps * first_rows + 8, width))] * 2,
-        [pltpu.VMEM((2 * cols, frames + 8, width), F32), pltpu.VMEM((2 * rows, 2 * width), BF16),
-         pltpu.VMEM((10, rows + 8, width), BF16), pltpu.VMEM((3, 2 * rows, in_width), BF16),
-         dma((10,)), dma((6,))],
+        [pltpu.VMEM((2 * cols, frames + 8, width), F32), pltpu.VMEM((2 * rows, 2 * width), BF16)]
+        + [pltpu.VMEM((10, rows + 8, width), BF16), dma((10,))] * (not NEAR_SMALL)
+        + phases_far * (2 - sum(NEAR_PHASES)),
         smem=1,
-        hbm=(13, 14),
-        loose=tuple(range(3, 13)),
+        hbm=tuple(at for at in (13, 14) if not NEAR_PHASES[at - 13]),
+        loose=() if NEAR_SMALL else tuple(range(3, 13)),
         cost=20,
         after=(mine_second,),
         flops=4 * rows * taps * width * in_width,

time: 93 us -> 91.4 us (0.983)
  Pallas kernels: 30.5 us -> 24 us
  waiting for transfers between devices: 6.51 us -> 9.98 us
  starting transfers between devices: 18.8 us -> 20 us
    pallas_call x12, Pallas kernels: 30.5 us -> 24 us  [call(): pl.pallas_call(body, out_shape=[pltpu.HBM(x.shape, x.dtype) if at in hbm_...]
    ppermute x12, waiting for transfers between devices: 5.76 us -> 9.23 us  [turn(): lax.ppermute(x, 'section', [(i, (i + step) % count) for i in range(count)])]
    ppermute x12, starting transfers between devices: 18.7 us -> 19.9 us  [turn(): lax.ppermute(x, 'section', [(i, (i + step) % count) for i in range(count)])]
  transfers between devices with their start and end apart: 14 -> 14, of which waited for: 6 -> 7; matrix products, arithmetic and copies ran while one was open for 0% -> 0% of each run, Pallas kernels for 23% -> 16%
where the time goes in v4:
time: 91.4 us; the launch traced here: 91.1 us
  blocking collectives  36.1 us (39%)
  Pallas kernels  24 us (26%)
  starting transfers between devices  20 us (22%)
  waiting for transfers between devices  9.98 us (11%)
  between operations  0.95 us (1%)
    all_to_all x1, blocking collectives, shards(): blocks = lax.all_to_all(joint, ZY, 0, 0)  36.1 us
    pallas_call x12, Pallas kernels, call(): pl.pallas_call(body, out_shape=[pltpu.HBM(x.shape, x.dtype) if at in hbm_...  24 us
    ppermute x12, starting transfers between devices, turn(): lax.ppermute(x, 'section', [(i, (i + step) % count) for i in range(count)])  19.9 us
    ppermute x12, waiting for transfers between devices, turn(): lax.ppermute(x, 'section', [(i, (i + step) % count) for i in range(count)])  9.23 us
  transfers between devices with their start and end apart: 14, of which 7 were waited for; matrix products, arithmetic and copies ran while one was open for 0% of the time, Pallas kernels for 16%

profile of v4, /device:TPU:0, one launch (start us, length us, event | category | flops | bytes accessed | tf_op | source)
XLA Modules:
  0.0 91.1 jit_solution(9377688840551199573)
XLA Ops:
  0.6 3.5 %first_a.1 = (bf16[384,256]{1,0:T(8,128)(2,1)S(1)}, bf16[3,384,512]{2,1,0:T(8,128)(2,1)}, f32[8,128]{1,0:T(8,128)S(1)}, bf16[5,512,256]{2,1,0:T(8,128)(2,1)S(1)}, bf16[8,144,512]{2,1,0:T(8,128)(2,1)S(1)}) custom-call(bf16[8,144,512]{2,1,0:T(8,128)(2,1)} %refs_0_.1, bf16[8,144,512]{2,1,0:T(8,128)(2,1)} %refs_1_.1, bf16[5,512,256]{2,1,0:T(8,128)(2,1)} %refs_2_.2), custom_call_target="tpu_custom_call" | custom-call | flops 503316480 | bytes 7540736 | tf_op jit(solution)/shard_map/first_a/pallas_call | solution.py:367
  4.2 1.6 %collective-permute-start = (bf16[384,256]{1,0:T(8,128)(2,1)S(1)}, bf16[384,256]{1,0:T(8,128)(2,1)S(1)}, u32[]{:S(2)}, u32[]{:S(2)}) collective-permute-start(bf16[384,256]{1,0:T(8,128)(2,1)S(1)} %get-tuple-element.33.refs_1_.refs_3_), channel_id=1, source_target_pairs={{0,1},{1,2},{2,3},{3,0},{4,5},{5,6},{6,7},{7,4},{8,9},{9,10},{10,1... | collective-permute-start | bytes 589832 | tf_op jit(solution)/shard_map/ppermute | solution.py:397
  5.8 2.6 %first_b.1 = (bf16[384,256]{1,0:T(8,128)(2,1)S(1)}, bf16[3,384,512]{2,1,0:T(8,128)(2,1)}, f32[8,128]{1,0:T(8,128)S(1)}, bf16[5,1024,256]{2,1,0:T(8,128)(2,1)S(1)}) custom-call(bf16[8,144,512]{2,1,0:T(8,128)(2,1)S(1)} %get-tuple-element.34.refs_0_, bf16[5,512,256]{2,1,0:T(8,128)(2,1)S(1)} %get-tuple-element.35.refs_1_, bf16[5,1024,256]{2,1,0:T(8,128)(2,1)} %refs_2_.3), custom_call_target="tpu_custom_call" | custom-call | flops 503316480 | bytes 9113600 | tf_op jit(solution)/shard_map/first_b/pallas_call | solution.py:367
  8.5 1.7 %collective-permute-start.4 = (bf16[384,256]{1,0:T(8,128)(2,1)S(1)}, bf16[384,256]{1,0:T(8,128)(2,1)S(1)}, u32[]{:S(2)}, u32[]{:S(2)}) collective-permute-start(bf16[384,256]{1,0:T(8,128)(2,1)S(1)} %get-tuple-element.39.refs_1_.refs_4_), channel_id=1, source_target_pairs={{0,3},{1,0},{2,1},{3,2},{4,7},{5,4},{6,5},{7,6},{8,11},{9,8},{10,9... | collective-permute-start | bytes 589832 | tf_op jit(solution)/shard_map/ppermute | solution.py:397
  10.2 1.6 %collective-permute-start.1 = (bf16[384,256]{1,0:T(8,128)(2,1)S(1)}, bf16[384,256]{1,0:T(8,128)(2,1)}, u32[]{:S(2)}, u32[]{:S(2)}) collective-permute-start(bf16[384,256]{1,0:T(8,128)(2,1)S(1)} %get-tuple-element.33.refs_1_.refs_3_), channel_id=1, source_target_pairs={{0,3},{1,0},{2,1},{3,2},{4,7},{5,4},{6,5},{7,6},{8,11},{9,8},{10,9... | collective-permute-start | bytes 589832 | tf_op jit(solution)/shard_map/ppermute | solution.py:397
  11.8 0.1 collective-permute-done.refs_2_
  12.0 0.5 collective-permute-start.2
  12.5 1.5 %collective-permute-start.3 = (bf16[384,256]{1,0:T(8,128)(2,1)S(1)}, bf16[384,256]{1,0:T(8,128)(2,1)}, u32[]{:S(2)}, u32[]{:S(2)}) collective-permute-start(bf16[384,256]{1,0:T(8,128)(2,1)S(1)} %get-tuple-element.39.refs_1_.refs_4_), channel_id=1, source_target_pairs={{0,1},{1,2},{2,3},{3,0},{4,5},{5,6},{6,7},{7,4},{8,9},{9,10},{10,1... | collective-permute-start | bytes 589832 | tf_op jit(solution)/shard_map/ppermute | solution.py:397
  13.9 2.4 %collective-permute-done.4.refs_3_ = bf16[384,256]{1,0:T(8,128)(2,1)S(1)} collective-permute-done((bf16[384,256]{1,0:T(8,128)(2,1)S(1)}, bf16[384,256]{1,0:T(8,128)(2,1)S(1)}, u32[]{:S(2)}, u32[]{:S(2)}) %collective-permute-start.4) | collective-permute-done | bytes 196640 | tf_op jit(solution)/shard_map/ppermute | solution.py:397
  16.4 2.9 %collective-permute-start.5 = (bf16[384,256]{1,0:T(8,128)(2,1)S(1)}, bf16[384,256]{1,0:T(8,128)(2,1)}, u32[]{:S(2)}, u32[]{:S(2)}) collective-permute-start(bf16[384,256]{1,0:T(8,128)(2,1)S(1)} %collective-permute-done.4.refs_3_), channel_id=1, source_target_pairs={{0,3},{1,0},{2,1},{3,2},{4,7},{5,4},{6,5},{7,6},{8,11},{9,8},{10,9... | collective-permute-start | bytes 589832 | tf_op jit(solution)/shard_map/ppermute | solution.py:397
  19.3 1.4 %collective-permute-done.1.refs_3_ = bf16[384,256]{1,0:T(8,128)(2,1)} collective-permute-done((bf16[384,256]{1,0:T(8,128)(2,1)S(1)}, bf16[384,256]{1,0:T(8,128)(2,1)}, u32[]{:S(2)}, u32[]{:S(2)}) %collective-permute-start.1) | collective-permute-done | bytes 196640 | tf_op jit(solution)/shard_map/ppermute | solution.py:397
  20.7 0.4 collective-permute-done.2.refs_4_
  21.1 3.7 %second_a.1 = (bf16[384,1024]{1,0:T(8,128)(2,1)S(1)}, bf16[384,1280]{1,0:T(8,128)(2,1)S(1)}, bf16[392,256]{1,0:T(8,128)(2,1)S(1)}, bf16[8,256]{1,0:T(8,128)(2,1)...) custom-call(s32[1]{0:T(128)} %bitcast.1.refs_0_, ...), custom_call_target="tpu_custom_call" | custom-call | flops 1258291200 | bytes 5984260 | tf_op jit(solution)/shard_map/second_a/pallas_call | solution.py:367
  24.8 3.4 %second_b.1 = (bf16[384,1024]{1,0:T(8,128)(2,1)S(1)}, bf16[384,1280]{1,0:T(8,128)(2,1)S(1)}, bf16[392,256]{1,0:T(8,128)(2,1)S(1)}, bf16[8,256]{1,0:T(8,128)(2,1)S(1)}) custom-call(s32[1]{0:T(128)} %bitcast.1.refs_0_, bf16[384,256]{1,0:T(8,128)(2,1)S(1)} %get-tuple-element.39.refs_1_.refs_4_, bf16[384,256]{1,0:T(8,128)(2,1)} %collective-permute-done.3.refs_2_, ...), custom_call_target="tpu_custom_call" | custom-call | flops 1258291200 | bytes 5386244 | tf_op jit(solution)/shard_map/second_b/pallas_call | solution.py:367
  28.3 2.6 %collective-permute-start.10 = (bf16[392,256]{1,0:T(8,128)(2,1)S(1)}, bf16[392,256]{1,0:T(8,128)(2,1)S(1)}, u32[]{:S(2)}, u32[]{:S(2)}) collective-permute-start(bf16[392,256]{1,0:T(8,128)(2,1)S(1)} %get-tuple-element.50), channel_id=1, source_target_pairs={{0,3},{1,0},{2,1},{3,2},{4,7},{5,4},{6,5},{7,6},{8,11},{9,8},{10,9... | collective-permute-start | bytes 602120 | tf_op jit(solution)/shard_map/ppermute | solution.py:397
  30.8 0.0 collective-permute-start.6
  30.8 1.0 %back_b.1 = (bf16[392,256]{1,0:T(8,128)(2,1)S(1)}, bf16[392,256]{1,0:T(8,128)(2,1)S(1)}, bf16[384,256]{1,0:T(8,128)(2,1)S(1)}) custom-call(s32[1]{0:T(128)} %bitcast.1.refs_0_, bf16[384,1280]{1,0:T(8,128)(2,1)S(1)} %get-tuple-element.43.refs_1_.refs_4_, bf16[5,1024,256]{2,1,0:T(8,128)(2,1)S(1)} %get-tuple-element.36.refs_5_.refs_2_, ...), custom_call_target="tpu_custom_call" | custom-call | flops 3019898880 | bytes 16826384 | tf_op jit(solution)/shard_map/back_b/pallas_call | solution.py:367
  31.8 0.7 collective-permute-start.8
  32.5 2.7 %collective-permute-start.9 = (bf16[392,256]{1,0:T(8,128)(2,1)S(1)}, bf16[392,256]{1,0:T(8,128)(2,1)S(1)}, u32[]{:S(2)}, u32[]{:S(2)}) collective-permute-start(bf16[392,256]{1,0:T(8,128)(2,1)S(1)} %get-tuple-element.48), channel_id=1, source_target_pairs={{0,3},{1,0},{2,1},{3,2},{4,7},{5,4},{6,5},{7,6},{8,11},{9,8},{10,9... | collective-permute-start | bytes 602120 | tf_op jit(solution)/shard_map/ppermute | solution.py:397
  35.2 1.0 %collective-permute-done.10.refs_1_.refs_12_ = bf16[392,256]{1,0:T(8,128)(2,1)S(1)} collective-permute-done((bf16[392,256]{1,0:T(8,128)(2,1)S(1)}, bf16[392,256]{1,0:T(8,128)(2,1)S(1)}, u32[]{:S(2)}, u32[]{:S(2)}) %collective-permute-start.10) | collective-permute-done | bytes 200736 | tf_op jit(solution)/shard_map/ppermute | solution.py:397
  36.3 3.8 %collective-permute-start.11 = (bf16[392,256]{1,0:T(8,128)(2,1)S(1)}, bf16[392,256]{1,0:T(8,128)(2,1)S(1)}, u32[]{:S(2)}, u32[]{:S(2)}) collective-permute-start(bf16[392,256]{1,0:T(8,128)(2,1)S(1)} %relay_b.1.refs_6_), channel_id=1, source_target_pairs={{0,3},{1,0},{2,1},{3,2},{4,7},{5,4},{6,5},{7,6},{8,11},{9,8},{10,9... | collective-permute-start | bytes 602120 | tf_op jit(solution)/shard_map/ppermute | solution.py:397
  40.1 0.3 collective-permute-start.7
  40.4 2.9 %weight_second.1 = (bf16[16,160,256]{2,1,0:T(8,128)(2,1)S(1)}, bf16[16,160,256]{2,1,0:T(8,128)(2,1)S(1)}) custom-call(s32[1]{0:T(128)} %bitcast.refs_0_, bf16[384,1024]{1,0:T(8,128)(2,1)S(1)} %get-tuple-element.53.refs_1_, bf16[384,1024]{1,0:T(8,128)(2,1)S(1)} %get-tuple-element.54.refs_2_, bf16[384,1280]{1,0:T(8,128)(2,1)S(1)} %get-tuple-element.55.refs_3_, ...), custom_call_target="tpu_custom_call" | custom-call | flops 8053063680 | bytes 24641552 | tf_op jit(solution)/shard_map/weight_second/pallas_call | solution.py:367
  43.3 0.1 collective-permute-start.13
  43.4 3.8 %collective-permute-done.7.refs_7_ = bf16[392,256]{1,0:T(8,128)(2,1)S(1)} collective-permute-done((bf16[392,256]{1,0:T(8,128)(2,1)S(1)}, bf16[392,256]{1,0:T(8,128)(2,1)S(1)}, u32[]{:S(2)}, u32[]{:S(2)}) %collective-permute-start.7) | collective-permute-done | bytes 200736 | tf_op jit(solution)/shard_map/ppermute | solution.py:397
  47.3 3.2 %weight_first.1 = (bf16[16,88,256]{2,1,0:T(8,128)(2,1)S(1)}, bf16[16,88,256]{2,1,0:T(8,128)(2,1)S(1)}) custom-call(s32[1]{0:T(128)} %bitcast.refs_0_, bf16[8,256]{1,0:T(8,128)(2,1)S(1)} %get-tuple-element.38.refs_1_, bf16[8,256]{1,0:T(8,128)(2,1)S(1)} %get-tuple-element.42.refs_3_.refs_2_, bf16[384,256]{1,0:T(8,128)(2,1)S(1)} %get-tuple-element.33.refs_1_.refs_3_, ...), custom_call_target="tpu_custom_call" | custom-call | flops 20132659200 | bytes 115998800 | tf_op jit(solution)/shard_map/weight_first/pallas_call | solution.py:367
  50.5 0.1 collective-permute-start.12
  50.6 1.4 %join_second.1.refs_2_ = bf16[16,248,256]{2,1,0:T(8,128)(2,1)} custom-call(bf16[16,160,256]{2,1,0:T(8,128)(2,1)S(1)} %get-tuple-element.56.refs_15_.refs_0_, bf16[16,160,256]{2,1,0:T(8,128)(2,1)S(1)} %collective-permute-done.13.refs_1_), custom_call_target="tpu_custom_call" | custom-call | bytes 4653056 | tf_op jit(solution)/shard_map/join_second/pallas_call | solution.py:367
  52.0 0.7 collective-permute-done.12.refs_1_
  52.8 1.1 %join_first.1 = bf16[16,248,256]{2,1,0:T(8,128)(2,1)} custom-call(bf16[16,88,256]{2,1,0:T(8,128)(2,1)S(1)} %get-tuple-element.57.refs_0_, bf16[16,88,256]{2,1,0:T(8,128)(2,1)S(1)} %collective-permute-done.12.refs_1_, bf16[16,248,256]{2,1,0:T(8,128)(2,1)} %join_second.1.refs_2_), custom_call_target="tpu_custom_call", output_to_operand_aliasing={{}: (2, {})} | custom-call | bytes 5505024 | tf_op jit(solution)/shard_map/join_first/pallas_call | solution.py:367
  53.8 36.1 %all_to_all.5.refs_0_ = bf16[16,248,256]{2,1,0:T(8,128)(2,1)S(1)} all-to-all(bf16[16,248,256]{2,1,0:T(8,128)(2,1)} %join_first.1), channel_id=1, replica_groups=mesh['dp_0'=4,'dp_1'=4,'dp_2'=2,'section'=4] {'dp_0','dp_1'}, dimensions={0} | all-to-all | bytes 4063232 | tf_op jit(solution)/shard_map/all_to_all | solution.py:562
  89.9 1.0 %total.1 = (f32[5,32,256]{2,1,0:T(8,128)}, f32[5,16,256]{2,1,0:T(8,128)}, f32[2]{0:T(128)}) custom-call(bf16[16,248,256]{2,1,0:T(8,128)(2,1)S(1)} %all_to_all.5.refs_0_), custom_call_target="tpu_custom_call" | custom-call | bytes 2277384 | tf_op jit(solution)/shard_map/total/pallas_call | solution.py:367
  (9 shorter events, 0.1 us)
Async XLA Ops:
  4.2 7.8 %collective-permute-start = (bf16[384,256]{1,0:T(8,128)(2,1)S(1)}, bf16[384,256]{1,0:T(8,128)(2,1)S(1)}, u32[]{:S(2)}, u32[]{:S(2)}) collective-permute-start(bf16[384,256]{1,0:T(8,128)(2,1)S(1)} %get-tuple-element.33.refs_1_.refs_3_), channel_id=1, source_target_pairs={{0,1},{1,2},{2,3},{3,0},{4,5},{5,6},{6,7},{7,4},{8,9},{9,10},{10,1... | collective-permute-start | bytes 589832 | tf_op jit(solution)/shard_map/ppermute | solution.py:397
  8.5 7.9 %collective-permute-start.4 = (bf16[384,256]{1,0:T(8,128)(2,1)S(1)}, bf16[384,256]{1,0:T(8,128)(2,1)S(1)}, u32[]{:S(2)}, u32[]{:S(2)}) collective-permute-start(bf16[384,256]{1,0:T(8,128)(2,1)S(1)} %get-tuple-element.39.refs_1_.refs_4_), channel_id=1, source_target_pairs={{0,3},{1,0},{2,1},{3,2},{4,7},{5,4},{6,5},{7,6},{8,11},{9,8},{10,9... | collective-permute-start | bytes 589832 | tf_op jit(solution)/shard_map/ppermute | solution.py:397
  10.2 10.5 %collective-permute-start.1 = (bf16[384,256]{1,0:T(8,128)(2,1)S(1)}, bf16[384,256]{1,0:T(8,128)(2,1)}, u32[]{:S(2)}, u32[]{:S(2)}) collective-permute-start(bf16[384,256]{1,0:T(8,128)(2,1)S(1)} %get-tuple-element.33.refs_1_.refs_3_), channel_id=1, source_target_pairs={{0,3},{1,0},{2,1},{3,2},{4,7},{5,4},{6,5},{7,6},{8,11},{9,8},{10,9... | collective-permute-start | bytes 589832 | tf_op jit(solution)/shard_map/ppermute | solution.py:397
  12.0 9.1 %collective-permute-start.2 = (bf16[384,256]{1,0:T(8,128)(2,1)S(1)}, bf16[384,256]{1,0:T(8,128)(2,1)}, u32[]{:S(2)}, u32[]{:S(2)}) collective-permute-start(bf16[384,256]{1,0:T(8,128)(2,1)S(1)} %collective-permute-done.refs_2_), channel_id=1, source_target_pairs={{0,1},{1,2},{2,3},{3,0},{4,5},{5,6},{6,7},{7,4},{8,9},{9,10},{10,1... | collective-permute-start | bytes 589832 | tf_op jit(solution)/shard_map/ppermute | solution.py:397
  12.5 12.3 %collective-permute-start.3 = (bf16[384,256]{1,0:T(8,128)(2,1)S(1)}, bf16[384,256]{1,0:T(8,128)(2,1)}, u32[]{:S(2)}, u32[]{:S(2)}) collective-permute-start(bf16[384,256]{1,0:T(8,128)(2,1)S(1)} %get-tuple-element.39.refs_1_.refs_4_), channel_id=1, source_target_pairs={{0,1},{1,2},{2,3},{3,0},{4,5},{5,6},{6,7},{7,4},{8,9},{9,10},{10,1... | collective-permute-start | bytes 589832 | tf_op jit(solution)/shard_map/ppermute | solution.py:397
  16.4 8.4 %collective-permute-start.5 = (bf16[384,256]{1,0:T(8,128)(2,1)S(1)}, bf16[384,256]{1,0:T(8,128)(2,1)}, u32[]{:S(2)}, u32[]{:S(2)}) collective-permute-start(bf16[384,256]{1,0:T(8,128)(2,1)S(1)} %collective-permute-done.4.refs_3_), channel_id=1, source_target_pairs={{0,3},{1,0},{2,1},{3,2},{4,7},{5,4},{6,5},{7,6},{8,11},{9,8},{10,9... | collective-permute-start | bytes 589832 | tf_op jit(solution)/shard_map/ppermute | solution.py:397
  28.3 8.0 %collective-permute-start.10 = (bf16[392,256]{1,0:T(8,128)(2,1)S(1)}, bf16[392,256]{1,0:T(8,128)(2,1)S(1)}, u32[]{:S(2)}, u32[]{:S(2)}) collective-permute-start(bf16[392,256]{1,0:T(8,128)(2,1)S(1)} %get-tuple-element.50), channel_id=1, source_target_pairs={{0,3},{1,0},{2,1},{3,2},{4,7},{5,4},{6,5},{7,6},{8,11},{9,8},{10,9... | collective-permute-start | bytes 602120 | tf_op jit(solution)/shard_map/ppermute | solution.py:397
  30.8 9.2 %collective-permute-start.6 = (bf16[392,256]{1,0:T(8,128)(2,1)S(1)}, bf16[392,256]{1,0:T(8,128)(2,1)S(1)}, u32[]{:S(2)}, u32[]{:S(2)}) collective-permute-start(bf16[392,256]{1,0:T(8,128)(2,1)S(1)} %get-tuple-element.46), channel_id=1, source_target_pairs={{0,1},{1,2},{2,3},{3,0},{4,5},{5,6},{6,7},{7,4},{8,9},{9,10},{10,1... | collective-permute-start | bytes 602120 | tf_op jit(solution)/shard_map/ppermute | solution.py:397
  31.8 11.6 %collective-permute-start.8 = (bf16[392,256]{1,0:T(8,128)(2,1)S(1)}, bf16[392,256]{1,0:T(8,128)(2,1)S(1)}, u32[]{:S(2)}, u32[]{:S(2)}) collective-permute-start(bf16[392,256]{1,0:T(8,128)(2,1)S(1)} %get-tuple-element.47), channel_id=1, source_target_pairs={{0,1},{1,2},{2,3},{3,0},{4,5},{5,6},{6,7},{7,4},{8,9},{9,10},{10,1... | collective-permute-start | bytes 602120 | tf_op jit(solution)/shard_map/ppermute | solution.py:397
  32.5 10.9 %collective-permute-start.9 = (bf16[392,256]{1,0:T(8,128)(2,1)S(1)}, bf16[392,256]{1,0:T(8,128)(2,1)S(1)}, u32[]{:S(2)}, u32[]{:S(2)}) collective-permute-start(bf16[392,256]{1,0:T(8,128)(2,1)S(1)} %get-tuple-element.48), channel_id=1, source_target_pairs={{0,3},{1,0},{2,1},{3,2},{4,7},{5,4},{6,5},{7,6},{8,11},{9,8},{10,9... | collective-permute-start | bytes 602120 | tf_op jit(solution)/shard_map/ppermute | solution.py:397
  36.3 7.1 %collective-permute-start.11 = (bf16[392,256]{1,0:T(8,128)(2,1)S(1)}, bf16[392,256]{1,0:T(8,128)(2,1)S(1)}, u32[]{:S(2)}, u32[]{:S(2)}) collective-permute-start(bf16[392,256]{1,0:T(8,128)(2,1)S(1)} %relay_b.1.refs_6_), channel_id=1, source_target_pairs={{0,3},{1,0},{2,1},{3,2},{4,7},{5,4},{6,5},{7,6},{8,11},{9,8},{10,9... | collective-permute-start | bytes 602120 | tf_op jit(solution)/shard_map/ppermute | solution.py:397
  40.1 7.2 %collective-permute-start.7 = (bf16[392,256]{1,0:T(8,128)(2,1)S(1)}, bf16[392,256]{1,0:T(8,128)(2,1)S(1)}, u32[]{:S(2)}, u32[]{:S(2)}) collective-permute-start(bf16[392,256]{1,0:T(8,128)(2,1)S(1)} %relay_a.1.refs_5_), channel_id=1, source_target_pairs={{0,1},{1,2},{2,3},{3,0},{4,5},{5,6},{6,7},{7,4},{8,9},{9,10},{10,1... | collective-permute-start | bytes 602120 | tf_op jit(solution)/shard_map/ppermute | solution.py:397
  43.3 7.3 %collective-permute-start.13 = (bf16[16,160,256]{2,1,0:T(8,128)(2,1)S(1)}, bf16[16,160,256]{2,1,0:T(8,128)(2,1)S(1)}, u32[]{:S(2)}, u32[]{:S(2)}) collective-permute-start(bf16[16,160,256]{2,1,0:T(8,128)(2,1)S(1)} %get-tuple-element.59), channel_id=1, source_target_pairs={{0,4},{4,0},{1,5},{5,1},{2,6},{6,2},{3,7},{7,3},{8,12},{12,8},{9,1... | collective-permute-start | bytes 3932168 | tf_op jit(solution)/shard_map/ppermute | solution.py:405
  50.5 2.3 %collective-permute-start.12 = (bf16[16,88,256]{2,1,0:T(8,128)(2,1)S(1)}, bf16[16,88,256]{2,1,0:T(8,128)(2,1)S(1)}, u32[]{:S(2)}, u32[]{:S(2)}) collective-permute-start(bf16[16,88,256]{2,1,0:T(8,128)(2,1)S(1)} %get-tuple-element.58), channel_id=1, source_target_pairs={{0,4},{4,0},{1,5},{5,1},{2,6},{6,2},{3,7},{7,3},{8,12},{12,8},{9,1... | collective-permute-start | bytes 2162696 | tf_op jit(solution)/shard_map/ppermute | solution.py:405

commit v5 on v4

--- a/solution.py
+++ b/solution.py
@@ -12,9 +12,9 @@
 ZY = ("dp_0", "dp_1")
 F32 = jnp.float32
 BF16 = jnp.bfloat16
-VMEM_LIMIT = 16 << 20
+VMEM_LIMIT = 51 << 20
 NEAR_PHASES = (False, False)
-NEAR_ALL = (True, True)
+NEAR_ALL = (False, True)
 NEAR_SMALL = True
 
 smooth_width = 0.1
@@ -323,6 +323,10 @@
         x[:, taps * own_rows :, :] = jnp.broadcast_to(lines[None], (groups, 8, width))
 
 
+def same_kernel(a, out):
+    out[...] = a[...]
+
+
 def join_kernel(at, a, b, joint, summed, sem):
     summed[...] = (a[...].astype(F32) + b[...].astype(F32)).astype(BF16)
     copy = pltpu.make_async_copy(summed, joint.at[:, at : at + summed.shape[1]], sem)
@@ -397,6 +401,10 @@
     return lax.ppermute(x, "section", [(i, (i + step) % count) for i in range(count)])
 
 
+def later(x, after, name):
+    return call(same_kernel, (x,), [like(x.shape)], after=after, name=name)[0]
+
+
 def added(a, b, name, after=()):
     return call(add_kernel, (a, b), [like(a.shape)], after=after, name=name)[0]
 
@@ -452,7 +460,7 @@
     far_a = turn(prev_a, 1)
     following_b = turn(h_b, -1)
     prev_b = turn(h_b, 1)
-    far_b = turn(following_b, -1)
+    far_b = turn(later(following_b, (following_a,), "ordered"), -1)
 
     second_outs = [like((rows, width_all)), like((rows, taps * width)), like((rows + 8, width)),
                    like((8, width))]
@@ -502,6 +510,7 @@
         hbm=() if NEAR_ALL[1] else (1,),
         cost=4,
         flops=2 * rows * taps * width * width * 3,
+        after=(relayed_a, from_following_a),
         name="back_b",
     )
     from_prev_b = turn(next_t, 1)

time: 91.4 us -> 96.9 us (1.060)
  Pallas kernels: 24 us -> 33.9 us
  starting transfers between devices: 20 us -> 17 us
  waiting for transfers between devices: 9.98 us -> 8.32 us
    pallas_call x12 -> x13, Pallas kernels: 24 us -> 33.9 us  [call(): pl.pallas_call(body, out_shape=[pltpu.HBM(x.shape, x.dtype) if at in hbm_...]
    ppermute x12, starting transfers between devices: 19.9 us -> 16.4 us  [turn(): lax.ppermute(x, 'section', [(i, (i + step) % count) for i in range(count)])]
    ppermute x12, waiting for transfers between devices: 9.23 us -> 7.76 us  [turn(): lax.ppermute(x, 'section', [(i, (i + step) % count) for i in range(count)])]
  transfers between devices with their start and end apart: 14 -> 14, of which waited for: 7 -> 4; matrix products, arithmetic and copies ran while one was open for 0% -> 0% of each run, Pallas kernels for 16% -> 29%
where the time goes in v5:
time: 96.9 us; the launch traced here: 96.6 us
  blocking collectives  36.4 us (38%)
  Pallas kernels  33.9 us (35%)
  starting transfers between devices  17 us (18%)
  waiting for transfers between devices  8.32 us (9%)
    all_to_all x1, blocking collectives, shards(): blocks = lax.all_to_all(joint, ZY, 0, 0)  36.4 us
    pallas_call x13, Pallas kernels, call(): pl.pallas_call(body, out_shape=[pltpu.HBM(x.shape, x.dtype) if at in hbm_...  33.9 us
    ppermute x12, starting transfers between devices, turn(): lax.ppermute(x, 'section', [(i, (i + step) % count) for i in range(count)])  16.4 us
    ppermute x12, waiting for transfers between devices, turn(): lax.ppermute(x, 'section', [(i, (i + step) % count) for i in range(count)])  7.76 us
  transfers between devices with their start and end apart: 14, of which 4 were waited for; matrix products, arithmetic and copies ran while one was open for 0% of the time, Pallas kernels for 29%

profile of v5, /device:TPU:0, one launch (start us, length us, event | category | flops | bytes accessed | tf_op | source)
XLA Modules:
  0.0 96.6 jit_solution(14636834979436496771)
XLA Ops:
  0.6 3.5 %first_a.1 = (bf16[384,256]{1,0:T(8,128)(2,1)S(1)}, bf16[3,384,512]{2,1,0:T(8,128)(2,1)}, f32[8,128]{1,0:T(8,128)S(1)}, bf16[5,512,256]{2,1,0:T(8,128)(2,1)S(1)}, bf16[8,144,512]{2,1,0:T(8,128)(2,1)S(1)}) custom-call(bf16[8,144,512]{2,1,0:T(8,128)(2,1)} %refs_0_.1, bf16[8,144,512]{2,1,0:T(8,128)(2,1)} %refs_1_.1, bf16[5,512,256]{2,1,0:T(8,128)(2,1)} %refs_2_.2), custom_call_target="tpu_custom_call" | custom-call | flops 503316480 | bytes 7540736 | tf_op jit(solution)/shard_map/first_a/pallas_call | solution.py:371
  4.1 1.6 %collective-permute-start = (bf16[384,256]{1,0:T(8,128)(2,1)S(1)}, bf16[384,256]{1,0:T(8,128)(2,1)S(1)}, u32[]{:S(2)}, u32[]{:S(2)}) collective-permute-start(bf16[384,256]{1,0:T(8,128)(2,1)S(1)} %get-tuple-element.33.refs_1_.refs_3_), channel_id=1, source_target_pairs={{0,1},{1,2},{2,3},{3,0},{4,5},{5,6},{6,7},{7,4},{8,9},{9,10},{10,1... | collective-permute-start | bytes 589832 | tf_op jit(solution)/shard_map/ppermute | solution.py:401
  5.8 1.7 %collective-permute-start.1 = (bf16[384,256]{1,0:T(8,128)(2,1)S(1)}, bf16[384,256]{1,0:T(8,128)(2,1)S(1)}, u32[]{:S(2)}, u32[]{:S(2)}) collective-permute-start(bf16[384,256]{1,0:T(8,128)(2,1)S(1)} %get-tuple-element.33.refs_1_.refs_3_), channel_id=1, source_target_pairs={{0,3},{1,0},{2,1},{3,2},{4,7},{5,4},{6,5},{7,6},{8,11},{9,8},{10,9... | collective-permute-start | bytes 589832 | tf_op jit(solution)/shard_map/ppermute | solution.py:401
  7.4 3.9 %first_b.1 = (bf16[384,256]{1,0:T(8,128)(2,1)S(1)}, bf16[3,384,512]{2,1,0:T(8,128)(2,1)}, f32[8,128]{1,0:T(8,128)S(1)}, bf16[5,1024,256]{2,1,0:T(8,128)(2,1)}) custom-call(bf16[8,144,512]{2,1,0:T(8,128)(2,1)S(1)} %get-tuple-element.34.refs_0_, bf16[5,512,256]{2,1,0:T(8,128)(2,1)S(1)} %get-tuple-element.35.refs_1_, bf16[5,1024,256]{2,1,0:T(8,128)(2,1)} %refs_2_.3), custom_call_target="tpu_custom_call" | custom-call | flops 503316480 | bytes 9113600 | tf_op jit(solution)/shard_map/first_b/pallas_call | solution.py:371
  11.3 1.7 %collective-permute-start.4 = (bf16[384,256]{1,0:T(8,128)(2,1)S(1)}, bf16[384,256]{1,0:T(8,128)(2,1)S(1)}, u32[]{:S(2)}, u32[]{:S(2)}) collective-permute-start(bf16[384,256]{1,0:T(8,128)(2,1)S(1)} %get-tuple-element.39.refs_1_.refs_4_), channel_id=1, source_target_pairs={{0,3},{1,0},{2,1},{3,2},{4,7},{5,4},{6,5},{7,6},{8,11},{9,8},{10,9... | collective-permute-start | bytes 589832 | tf_op jit(solution)/shard_map/ppermute | solution.py:401
  13.0 0.0 collective-permute-done.refs_2_
  13.0 0.4 collective-permute-start.2
  13.4 0.5 collective-permute-start.3
  13.9 3.5 %collective-permute-done.4.refs_0_.refs_3_ = bf16[384,256]{1,0:T(8,128)(2,1)S(1)} collective-permute-done((bf16[384,256]{1,0:T(8,128)(2,1)S(1)}, bf16[384,256]{1,0:T(8,128)(2,1)S(1)}, u32[]{:S(2)}, u32[]{:S(2)}) %collective-permute-start.4) | collective-permute-done | bytes 196640 | tf_op jit(solution)/shard_map/ppermute | solution.py:401
  17.5 2.9 %collective-permute-start.5 = (bf16[384,256]{1,0:T(8,128)(2,1)S(1)}, bf16[384,256]{1,0:T(8,128)(2,1)S(1)}, u32[]{:S(2)}, u32[]{:S(2)}) collective-permute-start(bf16[384,256]{1,0:T(8,128)(2,1)S(1)} %ordered.1), channel_id=1, source_target_pairs={{0,3},{1,0},{2,1},{3,2},{4,7},{5,4},{6,5},{7,6},{8,11},{9,8},{10,9... | collective-permute-start | bytes 589832 | tf_op jit(solution)/shard_map/ppermute | solution.py:401
  20.4 1.7 %collective-permute-done.2.refs_4_ = bf16[384,256]{1,0:T(8,128)(2,1)S(1)} collective-permute-done((bf16[384,256]{1,0:T(8,128)(2,1)S(1)}, bf16[384,256]{1,0:T(8,128)(2,1)S(1)}, u32[]{:S(2)}, u32[]{:S(2)}) %collective-permute-start.2) | collective-permute-done | bytes 196640 | tf_op jit(solution)/shard_map/ppermute | solution.py:401
  22.1 4.6 %second_a.1 = (bf16[384,1024]{1,0:T(8,128)(2,1)}, bf16[384,1280]{1,0:T(8,128)(2,1)}, bf16[392,256]{1,0:T(8,128)(2,1)S(1)}, bf16[8,256]{1,0:T(8,128)(2,1)S(1)}, b...) custom-call(s32[1]{0:T(128)} %bitcast.1.refs_0_, ...), custom_call_target="tpu_custom_call" | custom-call | flops 1258291200 | bytes 5984260 | tf_op jit(solution)/shard_map/second_a/pallas_call | solution.py:371
  26.7 0.1 collective-permute-start.6
  26.8 3.2 %collective-permute-start.7 = (bf16[392,256]{1,0:T(8,128)(2,1)S(1)}, bf16[392,256]{1,0:T(8,128)(2,1)S(1)}, u32[]{:S(2)}, u32[]{:S(2)}) collective-permute-start(bf16[392,256]{1,0:T(8,128)(2,1)S(1)} %get-tuple-element.46), channel_id=1, source_target_pairs={{0,3},{1,0},{2,1},{3,2},{4,7},{5,4},{6,5},{7,6},{8,11},{9,8},{10,9... | collective-permute-start | bytes 602120 | tf_op jit(solution)/shard_map/ppermute | solution.py:401
  30.0 4.2 %second_b.1 = (bf16[384,1024]{1,0:T(8,128)(2,1)S(1)}, bf16[384,1280]{1,0:T(8,128)(2,1)S(1)}, bf16[392,256]{1,0:T(8,128)(2,1)S(1)}, bf16[8,256]{1,0:T(8,128)(2,1)S(1)}) custom-call(s32[1]{0:T(128)} %bitcast.1.refs_0_, bf16[384,256]{1,0:T(8,128)(2,1)S(1)} %get-tuple-element.39.refs_1_.refs_4_, bf16[384,256]{1,0:T(8,128)(2,1)S(1)} %collective-permute-done.3.refs_2_, ...), custom_call_target="tpu_custom_call" | custom-call | flops 1258291200 | bytes 5386244 | tf_op jit(solution)/shard_map/second_b/pallas_call | solution.py:371
  34.3 0.1 collective-permute-start.10
  34.3 0.0 collective-permute-done.6.refs_1_.refs_11_
  34.3 0.1 relay_a.1.refs_4_.refs_5_
  34.4 2.1 %collective-permute-start.8 = (bf16[392,256]{1,0:T(8,128)(2,1)S(1)}, bf16[392,256]{1,0:T(8,128)(2,1)S(1)}, u32[]{:S(2)}, u32[]{:S(2)}) collective-permute-start(bf16[392,256]{1,0:T(8,128)(2,1)S(1)} %relay_a.1.refs_4_.refs_5_), channel_id=1, source_target_pairs={{0,1},{1,2},{2,3},{3,0},{4,5},{5,6},{6,7},{7,4},{8,9},{9,10},{10,1... | collective-permute-start | bytes 602120 | tf_op jit(solution)/shard_map/ppermute | solution.py:401
  36.5 2.7 %back_b.1 = (bf16[392,256]{1,0:T(8,128)(2,1)S(1)}, bf16[392,256]{1,0:T(8,128)(2,1)S(1)}, bf16[384,256]{1,0:T(8,128)(2,1)S(1)}) custom-call(s32[1]{0:T(128)} %bitcast.1.refs_0_, bf16[384,1280]{1,0:T(8,128)(2,1)S(1)} %get-tuple-element.43.refs_1_.refs_4_, bf16[5,1024,256]{2,1,0:T(8,128)(2,1)} %get-tuple-element.36.refs_5_.refs_2_, ...), custom_call_target="tpu_custom_call" | custom-call | flops 3019898880 | bytes 16826384 | tf_op jit(solution)/shard_map/back_b/pallas_call | solution.py:371
  39.2 2.5 %collective-permute-done.10.refs_1_.refs_12_ = bf16[392,256]{1,0:T(8,128)(2,1)S(1)} collective-permute-done((bf16[392,256]{1,0:T(8,128)(2,1)S(1)}, bf16[392,256]{1,0:T(8,128)(2,1)S(1)}, u32[]{:S(2)}, u32[]{:S(2)}) %collective-permute-start.10) | collective-permute-done | bytes 200736 | tf_op jit(solution)/shard_map/ppermute | solution.py:401
  41.8 0.1 collective-permute-start.11
  41.9 2.0 %collective-permute-start.9 = (bf16[392,256]{1,0:T(8,128)(2,1)S(1)}, bf16[392,256]{1,0:T(8,128)(2,1)S(1)}, u32[]{:S(2)}, u32[]{:S(2)}) collective-permute-start(bf16[392,256]{1,0:T(8,128)(2,1)S(1)} %get-tuple-element.48), channel_id=1, source_target_pairs={{0,1},{1,2},{2,3},{3,0},{4,5},{5,6},{6,7},{7,4},{8,9},{9,10},{10,1... | collective-permute-start | bytes 602120 | tf_op jit(solution)/shard_map/ppermute | solution.py:401
  43.9 7.1 %weight_second.1 = (bf16[16,160,256]{2,1,0:T(8,128)(2,1)}, bf16[16,160,256]{2,1,0:T(8,128)(2,1)}) custom-call(s32[1]{0:T(128)} %bitcast.refs_0_, bf16[384,1024]{1,0:T(8,128)(2,1)} %get-tuple-element.53.refs_1_, bf16[384,1024]{1,0:T(8,128)(2,1)S(1)} %get-tuple-element.54.refs_2_, bf16[384,1280]{1,0:T(8,128)(2,1)} %get-tuple-element.55.refs_3_, ...), custom_call_target="tpu_custom_call" | custom-call | flops 8053063680 | bytes 24641552 | tf_op jit(solution)/shard_map/weight_second/pallas_call | solution.py:371
  51.0 0.1 collective-permute-start.13
  51.1 4.2 %weight_first.1 = (bf16[16,88,256]{2,1,0:T(8,128)(2,1)S(1)}, bf16[16,88,256]{2,1,0:T(8,128)(2,1)}) custom-call(s32[1]{0:T(128)} %bitcast.refs_0_, bf16[8,256]{1,0:T(8,128)(2,1)S(1)} %get-tuple-element.38.refs_1_, bf16[8,256]{1,0:T(8,128)(2,1)S(1)} %get-tuple-element.42.refs_3_.refs_2_, bf16[384,256]{1,0:T(8,128)(2,1)S(1)} %get-tuple-element.33.refs_1_.refs_3_, ...), custom_call_target="tpu_custom_call" | custom-call | flops 20132659200 | bytes 115998800 | tf_op jit(solution)/shard_map/weight_first/pallas_call | solution.py:371
  55.3 0.6 collective-permute-start.12
  55.9 1.5 %join_second.1.refs_2_ = bf16[16,248,256]{2,1,0:T(8,128)(2,1)} custom-call(bf16[16,160,256]{2,1,0:T(8,128)(2,1)S(1)} %copy-done, bf16[16,160,256]{2,1,0:T(8,128)(2,1)S(1)} %collective-permute-done.13.refs_1_), custom_call_target="tpu_custom_call" | custom-call | bytes 4653056 | tf_op jit(solution)/shard_map/join_second/pallas_call | solution.py:371
  57.4 0.6 collective-permute-done.12.refs_1_
  57.9 1.1 %join_first.1 = bf16[16,248,256]{2,1,0:T(8,128)(2,1)} custom-call(bf16[16,88,256]{2,1,0:T(8,128)(2,1)S(1)} %get-tuple-element.57.refs_0_, bf16[16,88,256]{2,1,0:T(8,128)(2,1)S(1)} %collective-permute-done.12.refs_1_, bf16[16,248,256]{2,1,0:T(8,128)(2,1)} %join_second.1.refs_2_), custom_call_target="tpu_custom_call", output_to_operand_aliasing={{}: (2, {})} | custom-call | bytes 5505024 | tf_op jit(solution)/shard_map/join_first/pallas_call | solution.py:371
  59.0 36.4 %all_to_all.5.refs_0_ = bf16[16,248,256]{2,1,0:T(8,128)(2,1)S(1)} all-to-all(bf16[16,248,256]{2,1,0:T(8,128)(2,1)} %join_first.1), channel_id=1, replica_groups=mesh['dp_0'=4,'dp_1'=4,'dp_2'=2,'section'=4] {'dp_0','dp_1'}, dimensions={0} | all-to-all | bytes 4063232 | tf_op jit(solution)/shard_map/all_to_all | solution.py:571
  95.4 1.0 %total.1 = (f32[5,32,256]{2,1,0:T(8,128)}, f32[5,16,256]{2,1,0:T(8,128)}, f32[2]{0:T(128)}) custom-call(bf16[16,248,256]{2,1,0:T(8,128)(2,1)S(1)} %all_to_all.5.refs_0_), custom_call_target="tpu_custom_call" | custom-call | bytes 2277384 | tf_op jit(solution)/shard_map/total/pallas_call | solution.py:371
  (12 shorter events, 0.1 us)
Async XLA Ops:
  4.1 8.9 %collective-permute-start = (bf16[384,256]{1,0:T(8,128)(2,1)S(1)}, bf16[384,256]{1,0:T(8,128)(2,1)S(1)}, u32[]{:S(2)}, u32[]{:S(2)}) collective-permute-start(bf16[384,256]{1,0:T(8,128)(2,1)S(1)} %get-tuple-element.33.refs_1_.refs_3_), channel_id=1, source_target_pairs={{0,1},{1,2},{2,3},{3,0},{4,5},{5,6},{6,7},{7,4},{8,9},{9,10},{10,1... | collective-permute-start | bytes 589832 | tf_op jit(solution)/shard_map/ppermute | solution.py:401
  5.8 8.1 %collective-permute-start.1 = (bf16[384,256]{1,0:T(8,128)(2,1)S(1)}, bf16[384,256]{1,0:T(8,128)(2,1)S(1)}, u32[]{:S(2)}, u32[]{:S(2)}) collective-permute-start(bf16[384,256]{1,0:T(8,128)(2,1)S(1)} %get-tuple-element.33.refs_1_.refs_3_), channel_id=1, source_target_pairs={{0,3},{1,0},{2,1},{3,2},{4,7},{5,4},{6,5},{7,6},{8,11},{9,8},{10,9... | collective-permute-start | bytes 589832 | tf_op jit(solution)/shard_map/ppermute | solution.py:401
  11.3 6.1 %collective-permute-start.4 = (bf16[384,256]{1,0:T(8,128)(2,1)S(1)}, bf16[384,256]{1,0:T(8,128)(2,1)S(1)}, u32[]{:S(2)}, u32[]{:S(2)}) collective-permute-start(bf16[384,256]{1,0:T(8,128)(2,1)S(1)} %get-tuple-element.39.refs_1_.refs_4_), channel_id=1, source_target_pairs={{0,3},{1,0},{2,1},{3,2},{4,7},{5,4},{6,5},{7,6},{8,11},{9,8},{10,9... | collective-permute-start | bytes 589832 | tf_op jit(solution)/shard_map/ppermute | solution.py:401
  13.0 9.1 %collective-permute-start.2 = (bf16[384,256]{1,0:T(8,128)(2,1)S(1)}, bf16[384,256]{1,0:T(8,128)(2,1)S(1)}, u32[]{:S(2)}, u32[]{:S(2)}) collective-permute-start(bf16[384,256]{1,0:T(8,128)(2,1)S(1)} %collective-permute-done.refs_2_), channel_id=1, source_target_pairs={{0,1},{1,2},{2,3},{3,0},{4,5},{5,6},{6,7},{7,4},{8,9},{9,10},{10,1... | collective-permute-start | bytes 589832 | tf_op jit(solution)/shard_map/ppermute | solution.py:401
  13.4 16.6 %collective-permute-start.3 = (bf16[384,256]{1,0:T(8,128)(2,1)S(1)}, bf16[384,256]{1,0:T(8,128)(2,1)S(1)}, u32[]{:S(2)}, u32[]{:S(2)}) collective-permute-start(bf16[384,256]{1,0:T(8,128)(2,1)S(1)} %get-tuple-element.39.refs_1_.refs_4_), channel_id=1, source_target_pairs={{0,1},{1,2},{2,3},{3,0},{4,5},{5,6},{6,7},{7,4},{8,9},{9,10},{10,1... | collective-permute-start | bytes 589832 | tf_op jit(solution)/shard_map/ppermute | solution.py:401
  17.5 12.5 %collective-permute-start.5 = (bf16[384,256]{1,0:T(8,128)(2,1)S(1)}, bf16[384,256]{1,0:T(8,128)(2,1)S(1)}, u32[]{:S(2)}, u32[]{:S(2)}) collective-permute-start(bf16[384,256]{1,0:T(8,128)(2,1)S(1)} %ordered.1), channel_id=1, source_target_pairs={{0,3},{1,0},{2,1},{3,2},{4,7},{5,4},{6,5},{7,6},{8,11},{9,8},{10,9... | collective-permute-start | bytes 589832 | tf_op jit(solution)/shard_map/ppermute | solution.py:401
  26.7 7.7 %collective-permute-start.6 = (bf16[392,256]{1,0:T(8,128)(2,1)S(1)}, bf16[392,256]{1,0:T(8,128)(2,1)S(1)}, u32[]{:S(2)}, u32[]{:S(2)}) collective-permute-start(bf16[392,256]{1,0:T(8,128)(2,1)S(1)} %get-tuple-element.45), channel_id=1, source_target_pairs={{0,1},{1,2},{2,3},{3,0},{4,5},{5,6},{6,7},{7,4},{8,9},{9,10},{10,1... | collective-permute-start | bytes 602120 | tf_op jit(solution)/shard_map/ppermute | solution.py:401
  26.8 9.7 %collective-permute-start.7 = (bf16[392,256]{1,0:T(8,128)(2,1)S(1)}, bf16[392,256]{1,0:T(8,128)(2,1)S(1)}, u32[]{:S(2)}, u32[]{:S(2)}) collective-permute-start(bf16[392,256]{1,0:T(8,128)(2,1)S(1)} %get-tuple-element.46), channel_id=1, source_target_pairs={{0,3},{1,0},{2,1},{3,2},{4,7},{5,4},{6,5},{7,6},{8,11},{9,8},{10,9... | collective-permute-start | bytes 602120 | tf_op jit(solution)/shard_map/ppermute | solution.py:401
  34.3 7.5 %collective-permute-start.10 = (bf16[392,256]{1,0:T(8,128)(2,1)S(1)}, bf16[392,256]{1,0:T(8,128)(2,1)S(1)}, u32[]{:S(2)}, u32[]{:S(2)}) collective-permute-start(bf16[392,256]{1,0:T(8,128)(2,1)S(1)} %get-tuple-element.50), channel_id=1, source_target_pairs={{0,3},{1,0},{2,1},{3,2},{4,7},{5,4},{6,5},{7,6},{8,11},{9,8},{10,9... | collective-permute-start | bytes 602120 | tf_op jit(solution)/shard_map/ppermute | solution.py:401
  34.4 16.7 %collective-permute-start.8 = (bf16[392,256]{1,0:T(8,128)(2,1)S(1)}, bf16[392,256]{1,0:T(8,128)(2,1)S(1)}, u32[]{:S(2)}, u32[]{:S(2)}) collective-permute-start(bf16[392,256]{1,0:T(8,128)(2,1)S(1)} %relay_a.1.refs_4_.refs_5_), channel_id=1, source_target_pairs={{0,1},{1,2},{2,3},{3,0},{4,5},{5,6},{6,7},{7,4},{8,9},{9,10},{10,1... | collective-permute-start | bytes 602120 | tf_op jit(solution)/shard_map/ppermute | solution.py:401
  41.8 9.3 %collective-permute-start.11 = (bf16[392,256]{1,0:T(8,128)(2,1)S(1)}, bf16[392,256]{1,0:T(8,128)(2,1)S(1)}, u32[]{:S(2)}, u32[]{:S(2)}) collective-permute-start(bf16[392,256]{1,0:T(8,128)(2,1)S(1)} %relay_b.1.refs_6_), channel_id=1, source_target_pairs={{0,3},{1,0},{2,1},{3,2},{4,7},{5,4},{6,5},{7,6},{8,11},{9,8},{10,9... | collective-permute-start | bytes 602120 | tf_op jit(solution)/shard_map/ppermute | solution.py:401
  41.9 9.2 %collective-permute-start.9 = (bf16[392,256]{1,0:T(8,128)(2,1)S(1)}, bf16[392,256]{1,0:T(8,128)(2,1)S(1)}, u32[]{:S(2)}, u32[]{:S(2)}) collective-permute-start(bf16[392,256]{1,0:T(8,128)(2,1)S(1)} %get-tuple-element.48), channel_id=1, source_target_pairs={{0,1},{1,2},{2,3},{3,0},{4,5},{5,6},{6,7},{7,4},{8,9},{9,10},{10,1... | collective-permute-start | bytes 602120 | tf_op jit(solution)/shard_map/ppermute | solution.py:401
  51.0 4.9 %collective-permute-start.13 = (bf16[16,160,256]{2,1,0:T(8,128)(2,1)}, bf16[16,160,256]{2,1,0:T(8,128)(2,1)S(1)}, u32[]{:S(2)}, u32[]{:S(2)}) collective-permute-start(bf16[16,160,256]{2,1,0:T(8,128)(2,1)} %get-tuple-element.59), channel_id=1, source_target_pairs={{0,4},{4,0},{1,5},{5,1},{2,6},{6,2},{3,7},{7,3},{8,12},{12,8},{9,1... | collective-permute-start | bytes 3932168 | tf_op jit(solution)/shard_map/ppermute | solution.py:413
  51.1 4.8 %copy-start = (bf16[16,160,256]{2,1,0:T(8,128)(2,1)S(1)}, bf16[16,160,256]{2,1,0:T(8,128)(2,1)}, u32[]{:S(2)}) copy-start(bf16[16,160,256]{2,1,0:T(8,128)(2,1)} %get-tuple-element.56.refs_15_.refs_0_) | copy-start | bytes 3932164
  55.3 2.6 %collective-permute-start.12 = (bf16[16,88,256]{2,1,0:T(8,128)(2,1)}, bf16[16,88,256]{2,1,0:T(8,128)(2,1)S(1)}, u32[]{:S(2)}, u32[]{:S(2)}) collective-permute-start(bf16[16,88,256]{2,1,0:T(8,128)(2,1)} %get-tuple-element.58), channel_id=1, source_target_pairs={{0,4},{4,0},{1,5},{5,1},{2,6},{6,2},{3,7},{7,3},{8,12},{12,8},{9,1... | collective-permute-start | bytes 2162696 | tf_op jit(solution)/shard_map/ppermute | solution.py:413

commit v6 on v5

--- a/solution.py
+++ b/solution.py
@@ -12,7 +12,7 @@
 ZY = ("dp_0", "dp_1")
 F32 = jnp.float32
 BF16 = jnp.bfloat16
-VMEM_LIMIT = 51 << 20
+VMEM_LIMIT = 16 << 20
 NEAR_PHASES = (False, False)
 NEAR_ALL = (False, True)
 NEAR_SMALL = True
@@ -460,7 +460,7 @@
     far_a = turn(prev_a, 1)
     following_b = turn(h_b, -1)
     prev_b = turn(h_b, 1)
-    far_b = turn(later(following_b, (following_a,), "ordered"), -1)
+    far_b = turn(later(following_b, (following_a, h_a, prev_a, w_second), "ordered"), -1)
 
     second_outs = [like((rows, width_all)), like((rows, taps * width)), like((rows + 8, width)),
                    like((8, width))]
@@ -496,7 +496,7 @@
         loose=(1, 2, 3, 4),
         hbm_outs=() if NEAR_ALL[1] else (0, 1),
         cost=1,
-        after=(own_a,),
+        after=(loss_a,),
         flops=flops,
         name="second_b",
     )

time: 96.9 us -> 96.1 us (level)
  Pallas kernels: 33.9 us -> 30.4 us
  local copies, waits for them, and re-layouts: 0.01 us -> 1.6 us
    pallas_call x13, Pallas kernels: 33.9 us -> 30.4 us  [call(): pl.pallas_call(body, out_shape=[pltpu.HBM(x.shape, x.dtype) if at in hbm_...]
    unnamed x2 -> x8, local copies, waits for them, and re-layouts: 0.01 us -> 1.6 us
  transfers between devices with their start and end apart: 14 -> 14, of which waited for: 4 -> 5; matrix products, arithmetic and copies ran while one was open for 0% -> 0% of each run, Pallas kernels for 29% -> 26%
where the time goes in v6:
time: 96.1 us; the launch traced here: 95.8 us
  blocking collectives  36.4 us (38%)
  Pallas kernels  30.4 us (32%)
  starting transfers between devices  17.5 us (18%)
  waiting for transfers between devices  8.96 us (9%)
  local copies, waits for them, and re-layouts  1.6 us (2%)
    all_to_all x1, blocking collectives, shards(): blocks = lax.all_to_all(joint, ZY, 0, 0)  36.4 us
    pallas_call x13, Pallas kernels, call(): pl.pallas_call(body, out_shape=[pltpu.HBM(x.shape, x.dtype) if at in hbm_...  30.4 us
    ppermute x12, starting transfers between devices, turn(): lax.ppermute(x, 'section', [(i, (i + step) % count) for i in range(count)])  16.8 us
    ppermute x12, waiting for transfers between devices, turn(): lax.ppermute(x, 'section', [(i, (i + step) % count) for i in range(count)])  8.57 us
  transfers between devices with their start and end apart: 14, of which 5 were waited for; matrix products, arithmetic and copies ran while one was open for 0% of the time, Pallas kernels for 26%

profile of v6, /device:TPU:0, one launch (start us, length us, event | category | flops | bytes accessed | tf_op | source)
XLA Modules:
  0.0 95.8 jit_solution(4974017562299784367)
XLA Ops:
  0.6 3.5 %first_a.1 = (bf16[384,256]{1,0:T(8,128)(2,1)S(1)}, bf16[3,384,512]{2,1,0:T(8,128)(2,1)}, f32[8,128]{1,0:T(8,128)S(1)}, bf16[5,512,256]{2,1,0:T(8,128)(2,1)S(1)}, bf16[8,144,512]{2,1,0:T(8,128)(2,1)S(1)}) custom-call(bf16[8,144,512]{2,1,0:T(8,128)(2,1)} %refs_0_.1, bf16[8,144,512]{2,1,0:T(8,128)(2,1)} %refs_1_.1, bf16[5,512,256]{2,1,0:T(8,128)(2,1)} %refs_2_.2), custom_call_target="tpu_custom_call" | custom-call | flops 503316480 | bytes 7540736 | tf_op jit(solution)/shard_map/first_a/pallas_call | solution.py:371
  4.2 1.6 %collective-permute-start = (bf16[384,256]{1,0:T(8,128)(2,1)S(1)}, bf16[384,256]{1,0:T(8,128)(2,1)S(1)}, u32[]{:S(2)}, u32[]{:S(2)}) collective-permute-start(bf16[384,256]{1,0:T(8,128)(2,1)S(1)} %get-tuple-element.33.refs_1_.refs_2_.refs_3_), channel_id=1, source_target_pairs={{0,1},{1,2},{2,3},{3,0},{4,5},{5,6},{6,7},{7,4},{8,9},{9,10},{10,1... | collective-permute-start | bytes 589832 | tf_op jit(solution)/shard_map/ppermute | solution.py:401
  5.8 1.7 %collective-permute-start.1 = (bf16[384,256]{1,0:T(8,128)(2,1)S(1)}, bf16[384,256]{1,0:T(8,128)(2,1)S(1)}, u32[]{:S(2)}, u32[]{:S(2)}) collective-permute-start(bf16[384,256]{1,0:T(8,128)(2,1)S(1)} %get-tuple-element.33.refs_1_.refs_2_.refs_3_), channel_id=1, source_target_pairs={{0,3},{1,0},{2,1},{3,2},{4,7},{5,4},{6,5},{7,6},{8,11},{9,8},{10,9... | collective-permute-start | bytes 589832 | tf_op jit(solution)/shard_map/ppermute | solution.py:401
  7.5 3.0 %first_b.1 = (bf16[384,256]{1,0:T(8,128)(2,1)}, bf16[3,384,512]{2,1,0:T(8,128)(2,1)}, f32[8,128]{1,0:T(8,128)S(1)}, bf16[5,1024,256]{2,1,0:T(8,128)(2,1)S(1)}) custom-call(bf16[8,144,512]{2,1,0:T(8,128)(2,1)S(1)} %get-tuple-element.34.refs_0_, bf16[5,512,256]{2,1,0:T(8,128)(2,1)S(1)} %get-tuple-element.35.refs_1_, bf16[5,1024,256]{2,1,0:T(8,128)(2,1)} %refs_2_.3), custom_call_target="tpu_custom_call" | custom-call | flops 503316480 | bytes 9113600 | tf_op jit(solution)/shard_map/first_b/pallas_call | solution.py:371
  10.5 1.7 %collective-permute-start.4 = (bf16[384,256]{1,0:T(8,128)(2,1)}, bf16[384,256]{1,0:T(8,128)(2,1)S(1)}, u32[]{:S(2)}, u32[]{:S(2)}) collective-permute-start(bf16[384,256]{1,0:T(8,128)(2,1)} %get-tuple-element.39.refs_1_.refs_4_), channel_id=1, source_target_pairs={{0,3},{1,0},{2,1},{3,2},{4,7},{5,4},{6,5},{7,6},{8,11},{9,8},{10,9... | collective-permute-start | bytes 589832 | tf_op jit(solution)/shard_map/ppermute | solution.py:401
  12.2 0.4 collective-permute-start.2
  12.6 1.3 %collective-permute-start.3 = (bf16[384,256]{1,0:T(8,128)(2,1)}, bf16[384,256]{1,0:T(8,128)(2,1)}, u32[]{:S(2)}, u32[]{:S(2)}) collective-permute-start(bf16[384,256]{1,0:T(8,128)(2,1)} %get-tuple-element.39.refs_1_.refs_4_), channel_id=1, source_target_pairs={{0,1},{1,2},{2,3},{3,0},{4,5},{5,6},{6,7},{7,4},{8,9},{9,10},{10,1... | collective-permute-start | bytes 589832 | tf_op jit(solution)/shard_map/ppermute | solution.py:401
  14.0 2.9 %collective-permute-done.4.refs_0_.refs_3_ = bf16[384,256]{1,0:T(8,128)(2,1)S(1)} collective-permute-done((bf16[384,256]{1,0:T(8,128)(2,1)}, bf16[384,256]{1,0:T(8,128)(2,1)S(1)}, u32[]{:S(2)}, u32[]{:S(2)}) %collective-permute-start.4) | collective-permute-done | bytes 196640 | tf_op jit(solution)/shard_map/ppermute | solution.py:401
  16.9 0.7 ordered.1
  17.6 2.9 %collective-permute-start.5 = (bf16[384,256]{1,0:T(8,128)(2,1)}, bf16[384,256]{1,0:T(8,128)(2,1)}, u32[]{:S(2)}, u32[]{:S(2)}) collective-permute-start(bf16[384,256]{1,0:T(8,128)(2,1)} %ordered.1), channel_id=1, source_target_pairs={{0,3},{1,0},{2,1},{3,2},{4,7},{5,4},{6,5},{7,6},{8,11},{9,8},{10,9... | collective-permute-start | bytes 589832 | tf_op jit(solution)/shard_map/ppermute | solution.py:401
  20.4 0.9 collective-permute-done.2.refs_4_
  21.4 0.9 copy-done.1
  22.3 5.2 %second_a.1 = (bf16[384,1024]{1,0:T(8,128)(2,1)}, bf16[384,1280]{1,0:T(8,128)(2,1)}, bf16[392,256]{1,0:T(8,128)(2,1)}, bf16[8,256]{1,0:T(8,128)(2,1)S(1)}, bf16[...) custom-call(s32[1]{0:T(128)} %bitcast.1.refs_0_, ...), custom_call_target="tpu_custom_call" | custom-call | flops 1258291200 | bytes 5984260 | tf_op jit(solution)/shard_map/second_a/pallas_call | solution.py:371
  27.5 0.7 copy-done.2
  28.2 3.2 %collective-permute-start.7 = (bf16[392,256]{1,0:T(8,128)(2,1)}, bf16[392,256]{1,0:T(8,128)(2,1)}, u32[]{:S(2)}, u32[]{:S(2)}) collective-permute-start(bf16[392,256]{1,0:T(8,128)(2,1)} %get-tuple-element.46), channel_id=1, source_target_pairs={{0,3},{1,0},{2,1},{3,2},{4,7},{5,4},{6,5},{7,6},{8,11},{9,8},{10,9... | collective-permute-start | bytes 602120 | tf_op jit(solution)/shard_map/ppermute | solution.py:401
  31.4 3.5 %second_b.1 = (bf16[384,1024]{1,0:T(8,128)(2,1)S(1)}, bf16[384,1280]{1,0:T(8,128)(2,1)S(1)}, bf16[392,256]{1,0:T(8,128)(2,1)S(1)}, bf16[8,256]{1,0:T(8,128)(2,1)S(1)}) custom-call(s32[1]{0:T(128)} %bitcast.1.refs_0_, bf16[384,256]{1,0:T(8,128)(2,1)} %get-tuple-element.39.refs_1_.refs_4_, bf16[384,256]{1,0:T(8,128)(2,1)} %collective-permute-done.3.refs_2_, ...), custom_call_target="tpu_custom_call" | custom-call | flops 1258291200 | bytes 5386244 | tf_op jit(solution)/shard_map/second_b/pallas_call | solution.py:371
  35.0 0.1 collective-permute-start.10
  35.1 0.3 collective-permute-done.6.refs_1_.refs_11_
  35.4 1.8 %collective-permute-start.8 = (bf16[392,256]{1,0:T(8,128)(2,1)S(1)}, bf16[392,256]{1,0:T(8,128)(2,1)S(1)}, u32[]{:S(2)}, u32[]{:S(2)}) collective-permute-start(bf16[392,256]{1,0:T(8,128)(2,1)S(1)} %relay_a.1.refs_4_.refs_5_), channel_id=1, source_target_pairs={{0,1},{1,2},{2,3},{3,0},{4,5},{5,6},{6,7},{7,4},{8,9},{9,10},{10,1... | collective-permute-start | bytes 602120 | tf_op jit(solution)/shard_map/ppermute | solution.py:401
  37.2 1.0 %back_b.1 = (bf16[392,256]{1,0:T(8,128)(2,1)S(1)}, bf16[392,256]{1,0:T(8,128)(2,1)S(1)}, bf16[384,256]{1,0:T(8,128)(2,1)S(1)}) custom-call(s32[1]{0:T(128)} %bitcast.1.refs_0_, bf16[384,1280]{1,0:T(8,128)(2,1)S(1)} %get-tuple-element.43.refs_1_.refs_4_, bf16[5,1024,256]{2,1,0:T(8,128)(2,1)S(1)} %get-tuple-element.36.refs_5_.refs_4_.refs_2_, ...), custom_call_target="tpu_custom_call" | custom-call | flops 3019898880 | bytes 16826384 | tf_op jit(solution)/shard_map/back_b/pallas_call | solution.py:371
  38.2 4.4 %collective-permute-done.10.refs_1_.refs_12_ = bf16[392,256]{1,0:T(8,128)(2,1)S(1)} collective-permute-done((bf16[392,256]{1,0:T(8,128)(2,1)S(1)}, bf16[392,256]{1,0:T(8,128)(2,1)S(1)}, u32[]{:S(2)}, u32[]{:S(2)}) %collective-permute-start.10) | collective-permute-done | bytes 200736 | tf_op jit(solution)/shard_map/ppermute | solution.py:401
  42.7 0.1 collective-permute-start.11
  42.7 2.0 %collective-permute-start.9 = (bf16[392,256]{1,0:T(8,128)(2,1)S(1)}, bf16[392,256]{1,0:T(8,128)(2,1)S(1)}, u32[]{:S(2)}, u32[]{:S(2)}) collective-permute-start(bf16[392,256]{1,0:T(8,128)(2,1)S(1)} %get-tuple-element.48), channel_id=1, source_target_pairs={{0,1},{1,2},{2,3},{3,0},{4,5},{5,6},{6,7},{7,4},{8,9},{9,10},{10,1... | collective-permute-start | bytes 602120 | tf_op jit(solution)/shard_map/ppermute | solution.py:401
  44.8 5.6 %weight_second.1 = (bf16[16,160,256]{2,1,0:T(8,128)(2,1)S(1)}, bf16[16,160,256]{2,1,0:T(8,128)(2,1)S(1)}) custom-call(s32[1]{0:T(128)} %bitcast.refs_0_, bf16[384,1024]{1,0:T(8,128)(2,1)} %get-tuple-element.53.refs_1_, bf16[384,1024]{1,0:T(8,128)(2,1)S(1)} %get-tuple-element.54.refs_2_, bf16[384,1280]{1,0:T(8,128)(2,1)} %get-tuple-element.55.refs_3_, ...), custom_call_target="tpu_custom_call" | custom-call | flops 8053063680 | bytes 24641552 | tf_op jit(solution)/shard_map/weight_second/pallas_call | solution.py:371
  50.4 0.1 collective-permute-start.13
  50.5 4.2 %weight_first.1 = (bf16[16,88,256]{2,1,0:T(8,128)(2,1)S(1)}, bf16[16,88,256]{2,1,0:T(8,128)(2,1)S(1)}) custom-call(s32[1]{0:T(128)} %bitcast.refs_0_, bf16[8,256]{1,0:T(8,128)(2,1)S(1)} %get-tuple-element.38.refs_7_.refs_1_, bf16[8,256]{1,0:T(8,128)(2,1)S(1)} %get-tuple-element.41.refs_3_.refs_2_, ...), custom_call_target="tpu_custom_call" | custom-call | flops 20132659200 | bytes 115998800 | tf_op jit(solution)/shard_map/weight_first/pallas_call | solution.py:371
  54.8 0.6 collective-permute-start.12
  55.3 1.4 %join_second.1.refs_2_ = bf16[16,248,256]{2,1,0:T(8,128)(2,1)} custom-call(bf16[16,160,256]{2,1,0:T(8,128)(2,1)S(1)} %get-tuple-element.56.refs_15_.refs_0_, bf16[16,160,256]{2,1,0:T(8,128)(2,1)S(1)} %collective-permute-done.13.refs_1_), custom_call_target="tpu_custom_call" | custom-call | bytes 4653056 | tf_op jit(solution)/shard_map/join_second/pallas_call | solution.py:371
  56.8 0.4 collective-permute-done.12.refs_1_
  57.2 1.1 %join_first.1 = bf16[16,248,256]{2,1,0:T(8,128)(2,1)} custom-call(bf16[16,88,256]{2,1,0:T(8,128)(2,1)S(1)} %get-tuple-element.57.refs_0_, bf16[16,88,256]{2,1,0:T(8,128)(2,1)S(1)} %collective-permute-done.12.refs_1_, bf16[16,248,256]{2,1,0:T(8,128)(2,1)} %join_second.1.refs_2_), custom_call_target="tpu_custom_call", output_to_operand_aliasing={{}: (2, {})} | custom-call | bytes 5505024 | tf_op jit(solution)/shard_map/join_first/pallas_call | solution.py:371
  58.2 36.4 %all_to_all.5.refs_0_ = bf16[16,248,256]{2,1,0:T(8,128)(2,1)S(1)} all-to-all(bf16[16,248,256]{2,1,0:T(8,128)(2,1)} %join_first.1), channel_id=1, replica_groups=mesh['dp_0'=4,'dp_1'=4,'dp_2'=2,'section'=4] {'dp_0','dp_1'}, dimensions={0} | all-to-all | bytes 4063232 | tf_op jit(solution)/shard_map/all_to_all | solution.py:571
  94.6 1.0 %total.1 = (f32[5,32,256]{2,1,0:T(8,128)}, f32[5,16,256]{2,1,0:T(8,128)}, f32[2]{0:T(128)}) custom-call(bf16[16,248,256]{2,1,0:T(8,128)(2,1)S(1)} %all_to_all.5.refs_0_), custom_call_target="tpu_custom_call" | custom-call | bytes 2277384 | tf_op jit(solution)/shard_map/total/pallas_call | solution.py:371
  (18 shorter events, 0.1 us)
Async XLA Ops:
  4.2 8.1 %collective-permute-start = (bf16[384,256]{1,0:T(8,128)(2,1)S(1)}, bf16[384,256]{1,0:T(8,128)(2,1)S(1)}, u32[]{:S(2)}, u32[]{:S(2)}) collective-permute-start(bf16[384,256]{1,0:T(8,128)(2,1)S(1)} %get-tuple-element.33.refs_1_.refs_2_.refs_3_), channel_id=1, source_target_pairs={{0,1},{1,2},{2,3},{3,0},{4,5},{5,6},{6,7},{7,4},{8,9},{9,10},{10,1... | collective-permute-start | bytes 589832 | tf_op jit(solution)/shard_map/ppermute | solution.py:401
  5.8 8.1 %collective-permute-start.1 = (bf16[384,256]{1,0:T(8,128)(2,1)S(1)}, bf16[384,256]{1,0:T(8,128)(2,1)S(1)}, u32[]{:S(2)}, u32[]{:S(2)}) collective-permute-start(bf16[384,256]{1,0:T(8,128)(2,1)S(1)} %get-tuple-element.33.refs_1_.refs_2_.refs_3_), channel_id=1, source_target_pairs={{0,3},{1,0},{2,1},{3,2},{4,7},{5,4},{6,5},{7,6},{8,11},{9,8},{10,9... | collective-permute-start | bytes 589832 | tf_op jit(solution)/shard_map/ppermute | solution.py:401
  10.5 6.3 %collective-permute-start.4 = (bf16[384,256]{1,0:T(8,128)(2,1)}, bf16[384,256]{1,0:T(8,128)(2,1)S(1)}, u32[]{:S(2)}, u32[]{:S(2)}) collective-permute-start(bf16[384,256]{1,0:T(8,128)(2,1)} %get-tuple-element.39.refs_1_.refs_4_), channel_id=1, source_target_pairs={{0,3},{1,0},{2,1},{3,2},{4,7},{5,4},{6,5},{7,6},{8,11},{9,8},{10,9... | collective-permute-start | bytes 589832 | tf_op jit(solution)/shard_map/ppermute | solution.py:401
  12.2 9.2 %collective-permute-start.2 = (bf16[384,256]{1,0:T(8,128)(2,1)S(1)}, bf16[384,256]{1,0:T(8,128)(2,1)}, u32[]{:S(2)}, u32[]{:S(2)}) collective-permute-start(bf16[384,256]{1,0:T(8,128)(2,1)S(1)} %collective-permute-done.refs_2_.refs_3_), channel_id=1, source_target_pairs={{0,1},{1,2},{2,3},{3,0},{4,5},{5,6},{6,7},{7,4},{8,9},{9,10},{10,1... | collective-permute-start | bytes 589832 | tf_op jit(solution)/shard_map/ppermute | solution.py:401
  12.6 18.8 %collective-permute-start.3 = (bf16[384,256]{1,0:T(8,128)(2,1)}, bf16[384,256]{1,0:T(8,128)(2,1)}, u32[]{:S(2)}, u32[]{:S(2)}) collective-permute-start(bf16[384,256]{1,0:T(8,128)(2,1)} %get-tuple-element.39.refs_1_.refs_4_), channel_id=1, source_target_pairs={{0,1},{1,2},{2,3},{3,0},{4,5},{5,6},{6,7},{7,4},{8,9},{9,10},{10,1... | collective-permute-start | bytes 589832 | tf_op jit(solution)/shard_map/ppermute | solution.py:401
  13.9 3.6 %copy-start = (bf16[384,256]{1,0:T(8,128)(2,1)}, bf16[384,256]{1,0:T(8,128)(2,1)S(1)}, u32[]{:S(2)}) copy-start(bf16[384,256]{1,0:T(8,128)(2,1)S(1)} %collective-permute-done.1.refs_3_.refs_1_) | copy-start | bytes 589828
  17.6 13.9 %collective-permute-start.5 = (bf16[384,256]{1,0:T(8,128)(2,1)}, bf16[384,256]{1,0:T(8,128)(2,1)}, u32[]{:S(2)}, u32[]{:S(2)}) collective-permute-start(bf16[384,256]{1,0:T(8,128)(2,1)} %ordered.1), channel_id=1, source_target_pairs={{0,3},{1,0},{2,1},{3,2},{4,7},{5,4},{6,5},{7,6},{8,11},{9,8},{10,9... | collective-permute-start | bytes 589832 | tf_op jit(solution)/shard_map/ppermute | solution.py:401
  21.4 0.9 copy-start.1
  27.5 0.7 copy-start.2
  28.2 7.1 %collective-permute-start.6 = (bf16[392,256]{1,0:T(8,128)(2,1)}, bf16[392,256]{1,0:T(8,128)(2,1)S(1)}, u32[]{:S(2)}, u32[]{:S(2)}) collective-permute-start(bf16[392,256]{1,0:T(8,128)(2,1)} %get-tuple-element.45), channel_id=1, source_target_pairs={{0,1},{1,2},{2,3},{3,0},{4,5},{5,6},{6,7},{7,4},{8,9},{9,10},{10,1... | collective-permute-start | bytes 602120 | tf_op jit(solution)/shard_map/ppermute | solution.py:401
  28.2 9.0 %collective-permute-start.7 = (bf16[392,256]{1,0:T(8,128)(2,1)}, bf16[392,256]{1,0:T(8,128)(2,1)}, u32[]{:S(2)}, u32[]{:S(2)}) collective-permute-start(bf16[392,256]{1,0:T(8,128)(2,1)} %get-tuple-element.46), channel_id=1, source_target_pairs={{0,3},{1,0},{2,1},{3,2},{4,7},{5,4},{6,5},{7,6},{8,11},{9,8},{10,9... | collective-permute-start | bytes 602120 | tf_op jit(solution)/shard_map/ppermute | solution.py:401
  35.0 7.6 %collective-permute-start.10 = (bf16[392,256]{1,0:T(8,128)(2,1)S(1)}, bf16[392,256]{1,0:T(8,128)(2,1)S(1)}, u32[]{:S(2)}, u32[]{:S(2)}) collective-permute-start(bf16[392,256]{1,0:T(8,128)(2,1)S(1)} %get-tuple-element.50), channel_id=1, source_target_pairs={{0,3},{1,0},{2,1},{3,2},{4,7},{5,4},{6,5},{7,6},{8,11},{9,8},{10,9... | collective-permute-start | bytes 602120 | tf_op jit(solution)/shard_map/ppermute | solution.py:401
  35.4 15.1 %collective-permute-start.8 = (bf16[392,256]{1,0:T(8,128)(2,1)S(1)}, bf16[392,256]{1,0:T(8,128)(2,1)S(1)}, u32[]{:S(2)}, u32[]{:S(2)}) collective-permute-start(bf16[392,256]{1,0:T(8,128)(2,1)S(1)} %relay_a.1.refs_4_.refs_5_), channel_id=1, source_target_pairs={{0,1},{1,2},{2,3},{3,0},{4,5},{5,6},{6,7},{7,4},{8,9},{9,10},{10,1... | collective-permute-start | bytes 602120 | tf_op jit(solution)/shard_map/ppermute | solution.py:401
  42.7 7.8 %collective-permute-start.11 = (bf16[392,256]{1,0:T(8,128)(2,1)S(1)}, bf16[392,256]{1,0:T(8,128)(2,1)S(1)}, u32[]{:S(2)}, u32[]{:S(2)}) collective-permute-start(bf16[392,256]{1,0:T(8,128)(2,1)S(1)} %relay_b.1.refs_6_), channel_id=1, source_target_pairs={{0,3},{1,0},{2,1},{3,2},{4,7},{5,4},{6,5},{7,6},{8,11},{9,8},{10,9... | collective-permute-start | bytes 602120 | tf_op jit(solution)/shard_map/ppermute | solution.py:401
  42.7 7.8 %collective-permute-start.9 = (bf16[392,256]{1,0:T(8,128)(2,1)S(1)}, bf16[392,256]{1,0:T(8,128)(2,1)S(1)}, u32[]{:S(2)}, u32[]{:S(2)}) collective-permute-start(bf16[392,256]{1,0:T(8,128)(2,1)S(1)} %get-tuple-element.48), channel_id=1, source_target_pairs={{0,1},{1,2},{2,3},{3,0},{4,5},{5,6},{6,7},{7,4},{8,9},{9,10},{10,1... | collective-permute-start | bytes 602120 | tf_op jit(solution)/shard_map/ppermute | solution.py:401
  44.8 5.8 %copy-start.3 = (bf16[384,256]{1,0:T(8,128)(2,1)S(1)}, bf16[384,256]{1,0:T(8,128)(2,1)}, u32[]{:S(2)}) copy-start(bf16[384,256]{1,0:T(8,128)(2,1)} %copy-done.2) | copy-start | bytes 589828
  50.4 4.9 %collective-permute-start.13 = (bf16[16,160,256]{2,1,0:T(8,128)(2,1)S(1)}, bf16[16,160,256]{2,1,0:T(8,128)(2,1)S(1)}, u32[]{:S(2)}, u32[]{:S(2)}) collective-permute-start(bf16[16,160,256]{2,1,0:T(8,128)(2,1)S(1)} %get-tuple-element.59), channel_id=1, source_target_pairs={{0,4},{4,0},{1,5},{5,1},{2,6},{6,2},{3,7},{7,3},{8,12},{12,8},{9,1... | collective-permute-start | bytes 3932168 | tf_op jit(solution)/shard_map/ppermute | solution.py:413
  54.8 2.4 %collective-permute-start.12 = (bf16[16,88,256]{2,1,0:T(8,128)(2,1)S(1)}, bf16[16,88,256]{2,1,0:T(8,128)(2,1)S(1)}, u32[]{:S(2)}, u32[]{:S(2)}) collective-permute-start(bf16[16,88,256]{2,1,0:T(8,128)(2,1)S(1)} %get-tuple-element.58), channel_id=1, source_target_pairs={{0,4},{4,0},{1,5},{5,1},{2,6},{6,2},{3,7},{7,3},{8,12},{12,8},{9,1... | collective-permute-start | bytes 2162696 | tf_op jit(solution)/shard_map/ppermute | solution.py:413

commit v7 on v4

--- a/solution.py
+++ b/solution.py
@@ -32,8 +32,9 @@
 
 def difference_terms(real, fake):
     difference = real.astype(F32) - fake.astype(F32)
-    root = jnp.sqrt(difference * difference + smooth_width * smooth_width)
-    return difference, root
+    square = difference * difference + smooth_width * smooth_width
+    inverse = lax.rsqrt(square)
+    return difference * inverse, square * inverse
 
 
 def dot(a, b):
@@ -90,6 +91,13 @@
         copy_out.wait()
 
 
+def copies_of(source, target, sems):
+    return [
+        pltpu.make_async_copy(source.at[n], target.at[n], sems.at[n])
+        for n in range(source.shape[0])
+    ]
+
+
 def first_early_kernel(
     real, fake, w_hbm, h_out, phases_out, loss, w, rest,
     padded, held, held_sem, rest_sem, w_sem, *far_scratch,
@@ -99,20 +107,22 @@
     for n in range(2 * cols):
         source = real if n < cols else fake
         pltpu.make_async_copy(source.at[n % cols], held.at[n], held_sem.at[n]).start()
-    w_copy = pltpu.make_async_copy(w_hbm, w, w_sem)
-    w_copy.start()
+    w_copies = copies_of(w_hbm, w, w_sem)
+    for copy in w_copies:
+        copy.start()
     rest_copies = [
         pltpu.make_async_copy(x.at[cols:], rest.at[at * cols : (at + 1) * cols], rest_sem.at[at])
         for at, x in enumerate((real, fake))
     ]
-    for copy in rest_copies:
-        copy.start()
 
     def take(n):
         source = real if n < cols else fake
         pltpu.make_async_copy(source.at[n % cols], held.at[n], held_sem.at[n]).wait()
         if n == 2 * cols - 1:
-            w_copy.wait()
+            for copy in rest_copies:
+                copy.start()
+            for copy in w_copies:
+                copy.wait()
         return held[n]
 
     strided_conv(take, cols, span, w, h_out, phases_out, loss, padded, *far_scratch)
@@ -121,11 +131,13 @@
 
 
 def first_late_kernel(rest, w, w_next_hbm, h_out, phases_out, loss, w_next, padded, sem, *far):
-    copy = pltpu.make_async_copy(w_next_hbm, w_next, sem)
-    copy.start()
+    copies = copies_of(w_next_hbm, w_next, sem)
+    for copy in copies:
+        copy.start()
     cols, span = rest.shape[0] // 2, rest.shape[1]
     strided_conv(lambda n: rest[n], cols, span, w, h_out, phases_out, loss, padded, *far)
-    copy.wait()
+    for copy in copies:
+        copy.wait()
 
 
 def second_kernel(
@@ -162,10 +174,10 @@
         padded[:, 8 : 8 + frames, :] = dot(h_all[...], w[k]).reshape(-1, frames, width)
         pre = pre + padded[:, 6 + k : 6 + k + frames, :].reshape(rows, width)
     h = leaky(pre)
-    difference, root = difference_terms(h[:half], h[half:])
+    slope, root = difference_terms(h[:half], h[half:])
     loss_rows = losses_split(loss_first[...], fold_rows(root - smooth_width))
     loss[...] = loss_rows
-    slope = difference / root / normaliser
+    slope = slope * (1.0 / normaliser)
     for value, sign, at in ((h[:half], 1.0, 0), (h[half:], -1.0, half // frames)):
         gate = jnp.where(value.astype(F32) > 0, 1.0, leak_slope)
         delta = (sign * slope * gate).astype(BF16).astype(F32)
@@ -280,18 +292,18 @@
         if not near:
             held, sem = rest[:2]
             rest = rest[2:]
-            large.append(pltpu.make_async_copy(x, held, sem))
+            large.append(copies_of(x, held, sem))
             x = held
         phases.append(x)
-    for copy in small + large:
+    for copy in small + [copies[p] for p in range(3) for copies in large]:
         copy.start()
     for copy in small:
         copy.wait()
     padded[:, frames:, :] = jnp.zeros((padded.shape[0], 8, width), F32)
     for n in range(2):
         h, own, a, b = (sources[2 * at + n] for at in range(4))
-        difference, root = difference_terms(h[:half], h[half:rows])
-        slope = difference / root / normaliser
+        slope, _ = difference_terms(h[:half], h[half:rows])
+        slope = slope * (1.0 / normaliser)
         for at, sign in ((0, 1.0), (half, -1.0)):
             cut = slice(at, at + half)
             up = own[cut].astype(F32) + a[cut].astype(F32) + b[cut].astype(F32)
@@ -306,9 +318,9 @@
     groups = mine.shape[0]
     own_rows = (mine.shape[1] - 8) // taps
     outs = (mine, theirs)
-    for copy in large:
-        copy.wait()
     for p in range(3):
+        for copies in large:
+            copies[p].wait()
         lanes = width if p == 0 else 2 * width
         g = dot_rows(phases[0][p], moved[:rows, :lanes])
         g = g + dot_rows(phases[1][p], moved[rows:, :lanes])
@@ -323,11 +335,21 @@
         x[:, taps * own_rows :, :] = jnp.broadcast_to(lines[None], (groups, 8, width))
 
 
-def join_kernel(at, a, b, joint, summed, sem):
-    summed[...] = (a[...].astype(F32) + b[...].astype(F32)).astype(BF16)
-    copy = pltpu.make_async_copy(summed, joint.at[:, at : at + summed.shape[1]], sem)
-    copy.start()
-    copy.wait()
+def join_kernel(at, a, b, joint, summed, sems):
+    count = sems.shape[0]
+    step = a.shape[0] // count
+    copies = []
+    for n in range(count):
+        cut = slice(n * step, (n + 1) * step)
+        summed[cut] = (a[cut].astype(F32) + b[cut].astype(F32)).astype(BF16)
+        copies.append(
+            pltpu.make_async_copy(
+                summed.at[cut], joint.at[cut, at : at + summed.shape[1]], sems.at[n]
+            )
+        )
+        copies[-1].start()
+    for copy in copies:
+        copy.wait()
 
 
 def join_late_kernel(at, a, b, held, joint, summed, sem):
@@ -429,7 +451,7 @@
         (real_in, fake_in, kernel_first),
         chunk_outs + [like(kernel_first.shape), like((cols, span, in_width))],
         conv_scratch
-        + [pltpu.VMEM((cols, span, in_width), BF16), dma((cols,)), dma((2,)), dma]
+        + [pltpu.VMEM((cols, span, in_width), BF16), dma((cols,)), dma((2,)), dma((taps,))]
         + phases_far * (not NEAR_PHASES[0]),
         hbm=(0, 1, 2),
         hbm_outs=() if NEAR_PHASES[0] else (1,),
@@ -442,7 +464,7 @@
         first_late_kernel,
         (rest, w_first, kernel_second),
         chunk_outs + [like(kernel_second.shape)],
-        conv_scratch + [dma] + phases_far * (not NEAR_PHASES[1]),
+        conv_scratch + [dma((taps,))] + phases_far * (not NEAR_PHASES[1]),
         hbm=(2,),
         hbm_outs=() if NEAR_PHASES[1] else (1,),
         flops=flops,
@@ -528,7 +550,7 @@
         functools.partial(join_kernel, 0),
         (mine_second, other_core(theirs)),
         [joint_like],
-        [pltpu.VMEM((groups, size_second, width), BF16), dma],
+        [pltpu.VMEM((groups, size_second, width), BF16), dma((4,))],
         hbm_outs=(0,),
         name="join_second",
     )
@@ -540,7 +562,7 @@
         [like((groups, taps * first_rows + 8, width))] * 2,
         [pltpu.VMEM((2 * cols, frames + 8, width), F32), pltpu.VMEM((2 * rows, 2 * width), BF16)]
         + [pltpu.VMEM((10, rows + 8, width), BF16), dma((10,))] * (not NEAR_SMALL)
-        + phases_far * (2 - sum(NEAR_PHASES)),
+        + [phases_far[0], dma((3,))] * (2 - sum(NEAR_PHASES)),
         smem=1,
         hbm=tuple(at for at in (13, 14) if not NEAR_PHASES[at - 13]),
         loose=() if NEAR_SMALL else tuple(range(3, 13)),
@@ -553,7 +575,7 @@
         functools.partial(join_late_kernel, size_second),
         (mine_first, other_core(theirs), joint),
         [joint_like],
-        [pltpu.VMEM((groups, size_first, width), BF16), dma],
+        [pltpu.VMEM((groups, size_first, width), BF16), dma((4,))],
         hbm=(2,),
         hbm_outs=(0,),
         aliases={2: 0},

time: 91.4 us -> 92.3 us (level)
  transfers between devices with their start and end apart: 14 -> 14, of which waited for: 7 -> 7; matrix products, arithmetic and copies ran while one was open for 0% -> 0% of each run, Pallas kernels for 16% -> 17%
where the time goes in v7:
time: 92.3 us; the launch traced here: 92 us
  blocking collectives  36.1 us (39%)
  Pallas kernels  24.7 us (27%)
  starting transfers between devices  19.8 us (21%)
  waiting for transfers between devices  10.4 us (11%)
  between operations  0.95 us (1%)
    all_to_all x1, blocking collectives, shards(): blocks = lax.all_to_all(joint, ZY, 0, 0)  36.1 us
    pallas_call x12, Pallas kernels, call(): pl.pallas_call(body, out_shape=[pltpu.HBM(x.shape, x.dtype) if at in hbm_...  24.7 us
    ppermute x12, starting transfers between devices, turn(): lax.ppermute(x, 'section', [(i, (i + step) % count) for i in range(count)])  19.6 us
    ppermute x12, waiting for transfers between devices, turn(): lax.ppermute(x, 'section', [(i, (i + step) % count) for i in range(count)])  9.48 us
  transfers between devices with their start and end apart: 14, of which 7 were waited for; matrix products, arithmetic and copies ran while one was open for 0% of the time, Pallas kernels for 17%

profile of v7, /device:TPU:0, one launch (start us, length us, event | category | flops | bytes accessed | tf_op | source)
XLA Modules:
  0.0 92.0 jit_solution(17402933846164363759)
XLA Ops:
  0.6 3.9 %first_a.1 = (bf16[384,256]{1,0:T(8,128)(2,1)S(1)}, bf16[3,384,512]{2,1,0:T(8,128)(2,1)}, f32[8,128]{1,0:T(8,128)S(1)}, bf16[5,512,256]{2,1,0:T(8,128)(2,1)S(1)}, bf16[8,144,512]{2,1,0:T(8,128)(2,1)S(1)}) custom-call(bf16[8,144,512]{2,1,0:T(8,128)(2,1)} %refs_0_.1, bf16[8,144,512]{2,1,0:T(8,128)(2,1)} %refs_1_.1, bf16[5,512,256]{2,1,0:T(8,128)(2,1)} %refs_2_.2), custom_call_target="tpu_custom_call" | custom-call | flops 503316480 | bytes 7540736 | tf_op jit(solution)/shard_map/first_a/pallas_call | solution.py:389
  4.5 1.6 %collective-permute-start = (bf16[384,256]{1,0:T(8,128)(2,1)S(1)}, bf16[384,256]{1,0:T(8,128)(2,1)S(1)}, u32[]{:S(2)}, u32[]{:S(2)}) collective-permute-start(bf16[384,256]{1,0:T(8,128)(2,1)S(1)} %get-tuple-element.33.refs_1_.refs_3_), channel_id=1, source_target_pairs={{0,1},{1,2},{2,3},{3,0},{4,5},{5,6},{6,7},{7,4},{8,9},{9,10},{10,1... | collective-permute-start | bytes 589832 | tf_op jit(solution)/shard_map/ppermute | solution.py:419
  6.2 2.5 %first_b.1 = (bf16[384,256]{1,0:T(8,128)(2,1)S(1)}, bf16[3,384,512]{2,1,0:T(8,128)(2,1)}, f32[8,128]{1,0:T(8,128)S(1)}, bf16[5,1024,256]{2,1,0:T(8,128)(2,1)S(1)}) custom-call(bf16[8,144,512]{2,1,0:T(8,128)(2,1)S(1)} %get-tuple-element.34.refs_0_, bf16[5,512,256]{2,1,0:T(8,128)(2,1)S(1)} %get-tuple-element.35.refs_1_, bf16[5,1024,256]{2,1,0:T(8,128)(2,1)} %refs_2_.3), custom_call_target="tpu_custom_call" | custom-call | flops 503316480 | bytes 9113600 | tf_op jit(solution)/shard_map/first_b/pallas_call | solution.py:389
  8.7 1.7 %collective-permute-start.4 = (bf16[384,256]{1,0:T(8,128)(2,1)S(1)}, bf16[384,256]{1,0:T(8,128)(2,1)S(1)}, u32[]{:S(2)}, u32[]{:S(2)}) collective-permute-start(bf16[384,256]{1,0:T(8,128)(2,1)S(1)} %get-tuple-element.39.refs_1_.refs_4_), channel_id=1, source_target_pairs={{0,3},{1,0},{2,1},{3,2},{4,7},{5,4},{6,5},{7,6},{8,11},{9,8},{10,9... | collective-permute-start | bytes 589832 | tf_op jit(solution)/shard_map/ppermute | solution.py:419
  10.4 1.6 %collective-permute-start.1 = (bf16[384,256]{1,0:T(8,128)(2,1)S(1)}, bf16[384,256]{1,0:T(8,128)(2,1)}, u32[]{:S(2)}, u32[]{:S(2)}) collective-permute-start(bf16[384,256]{1,0:T(8,128)(2,1)S(1)} %get-tuple-element.33.refs_1_.refs_3_), channel_id=1, source_target_pairs={{0,3},{1,0},{2,1},{3,2},{4,7},{5,4},{6,5},{7,6},{8,11},{9,8},{10,9... | collective-permute-start | bytes 589832 | tf_op jit(solution)/shard_map/ppermute | solution.py:419
  12.0 0.3 collective-permute-done.refs_2_
  12.3 0.5 collective-permute-start.2
  12.8 1.5 %collective-permute-start.3 = (bf16[384,256]{1,0:T(8,128)(2,1)S(1)}, bf16[384,256]{1,0:T(8,128)(2,1)}, u32[]{:S(2)}, u32[]{:S(2)}) collective-permute-start(bf16[384,256]{1,0:T(8,128)(2,1)S(1)} %get-tuple-element.39.refs_1_.refs_4_), channel_id=1, source_target_pairs={{0,1},{1,2},{2,3},{3,0},{4,5},{5,6},{6,7},{7,4},{8,9},{9,10},{10,1... | collective-permute-start | bytes 589832 | tf_op jit(solution)/shard_map/ppermute | solution.py:419
  14.3 2.3 %collective-permute-done.4.refs_3_ = bf16[384,256]{1,0:T(8,128)(2,1)S(1)} collective-permute-done((bf16[384,256]{1,0:T(8,128)(2,1)S(1)}, bf16[384,256]{1,0:T(8,128)(2,1)S(1)}, u32[]{:S(2)}, u32[]{:S(2)}) %collective-permute-start.4) | collective-permute-done | bytes 196640 | tf_op jit(solution)/shard_map/ppermute | solution.py:419
  16.6 2.9 %collective-permute-start.5 = (bf16[384,256]{1,0:T(8,128)(2,1)S(1)}, bf16[384,256]{1,0:T(8,128)(2,1)}, u32[]{:S(2)}, u32[]{:S(2)}) collective-permute-start(bf16[384,256]{1,0:T(8,128)(2,1)S(1)} %collective-permute-done.4.refs_3_), channel_id=1, source_target_pairs={{0,3},{1,0},{2,1},{3,2},{4,7},{5,4},{6,5},{7,6},{8,11},{9,8},{10,9... | collective-permute-start | bytes 589832 | tf_op jit(solution)/shard_map/ppermute | solution.py:419
  19.5 1.4 %collective-permute-done.1.refs_3_ = bf16[384,256]{1,0:T(8,128)(2,1)} collective-permute-done((bf16[384,256]{1,0:T(8,128)(2,1)S(1)}, bf16[384,256]{1,0:T(8,128)(2,1)}, u32[]{:S(2)}, u32[]{:S(2)}) %collective-permute-start.1) | collective-permute-done | bytes 196640 | tf_op jit(solution)/shard_map/ppermute | solution.py:419
  20.9 0.5 collective-permute-done.2.refs_4_
  21.4 3.6 %second_a.1 = (bf16[384,1024]{1,0:T(8,128)(2,1)S(1)}, bf16[384,1280]{1,0:T(8,128)(2,1)S(1)}, bf16[392,256]{1,0:T(8,128)(2,1)S(1)}, bf16[8,256]{1,0:T(8,128)(2,1)...) custom-call(s32[1]{0:T(128)} %bitcast.1.refs_0_, ...), custom_call_target="tpu_custom_call" | custom-call | flops 1258291200 | bytes 5984260 | tf_op jit(solution)/shard_map/second_a/pallas_call | solution.py:389
  25.1 3.4 %second_b.1 = (bf16[384,1024]{1,0:T(8,128)(2,1)S(1)}, bf16[384,1280]{1,0:T(8,128)(2,1)S(1)}, bf16[392,256]{1,0:T(8,128)(2,1)S(1)}, bf16[8,256]{1,0:T(8,128)(2,1)S(1)}) custom-call(s32[1]{0:T(128)} %bitcast.1.refs_0_, bf16[384,256]{1,0:T(8,128)(2,1)S(1)} %get-tuple-element.39.refs_1_.refs_4_, bf16[384,256]{1,0:T(8,128)(2,1)} %collective-permute-done.3.refs_2_, ...), custom_call_target="tpu_custom_call" | custom-call | flops 1258291200 | bytes 5386244 | tf_op jit(solution)/shard_map/second_b/pallas_call | solution.py:389
  28.4 2.4 %collective-permute-start.10 = (bf16[392,256]{1,0:T(8,128)(2,1)S(1)}, bf16[392,256]{1,0:T(8,128)(2,1)S(1)}, u32[]{:S(2)}, u32[]{:S(2)}) collective-permute-start(bf16[392,256]{1,0:T(8,128)(2,1)S(1)} %get-tuple-element.50), channel_id=1, source_target_pairs={{0,3},{1,0},{2,1},{3,2},{4,7},{5,4},{6,5},{7,6},{8,11},{9,8},{10,9... | collective-permute-start | bytes 602120 | tf_op jit(solution)/shard_map/ppermute | solution.py:419
  30.9 0.0 collective-permute-start.6
  30.9 1.0 %back_b.1 = (bf16[392,256]{1,0:T(8,128)(2,1)S(1)}, bf16[392,256]{1,0:T(8,128)(2,1)S(1)}, bf16[384,256]{1,0:T(8,128)(2,1)S(1)}) custom-call(s32[1]{0:T(128)} %bitcast.1.refs_0_, bf16[384,1280]{1,0:T(8,128)(2,1)S(1)} %get-tuple-element.43.refs_1_.refs_4_, bf16[5,1024,256]{2,1,0:T(8,128)(2,1)S(1)} %get-tuple-element.36.refs_5_.refs_2_, ...), custom_call_target="tpu_custom_call" | custom-call | flops 3019898880 | bytes 16826384 | tf_op jit(solution)/shard_map/back_b/pallas_call | solution.py:389
  31.9 0.7 collective-permute-start.8
  32.6 2.7 %collective-permute-start.9 = (bf16[392,256]{1,0:T(8,128)(2,1)S(1)}, bf16[392,256]{1,0:T(8,128)(2,1)S(1)}, u32[]{:S(2)}, u32[]{:S(2)}) collective-permute-start(bf16[392,256]{1,0:T(8,128)(2,1)S(1)} %get-tuple-element.48), channel_id=1, source_target_pairs={{0,3},{1,0},{2,1},{3,2},{4,7},{5,4},{6,5},{7,6},{8,11},{9,8},{10,9... | collective-permute-start | bytes 602120 | tf_op jit(solution)/shard_map/ppermute | solution.py:419
  35.3 1.1 %collective-permute-done.10.refs_1_.refs_12_ = bf16[392,256]{1,0:T(8,128)(2,1)S(1)} collective-permute-done((bf16[392,256]{1,0:T(8,128)(2,1)S(1)}, bf16[392,256]{1,0:T(8,128)(2,1)S(1)}, u32[]{:S(2)}, u32[]{:S(2)}) %collective-permute-start.10) | collective-permute-done | bytes 200736 | tf_op jit(solution)/shard_map/ppermute | solution.py:419
  36.4 3.6 %collective-permute-start.11 = (bf16[392,256]{1,0:T(8,128)(2,1)S(1)}, bf16[392,256]{1,0:T(8,128)(2,1)S(1)}, u32[]{:S(2)}, u32[]{:S(2)}) collective-permute-start(bf16[392,256]{1,0:T(8,128)(2,1)S(1)} %relay_b.1.refs_6_), channel_id=1, source_target_pairs={{0,3},{1,0},{2,1},{3,2},{4,7},{5,4},{6,5},{7,6},{8,11},{9,8},{10,9... | collective-permute-start | bytes 602120 | tf_op jit(solution)/shard_map/ppermute | solution.py:419
  40.1 0.3 collective-permute-start.7
  40.4 2.9 %weight_second.1 = (bf16[16,160,256]{2,1,0:T(8,128)(2,1)S(1)}, bf16[16,160,256]{2,1,0:T(8,128)(2,1)S(1)}) custom-call(s32[1]{0:T(128)} %bitcast.refs_0_, bf16[384,1024]{1,0:T(8,128)(2,1)S(1)} %get-tuple-element.53.refs_1_, bf16[384,1024]{1,0:T(8,128)(2,1)S(1)} %get-tuple-element.54.refs_2_, bf16[384,1280]{1,0:T(8,128)(2,1)S(1)} %get-tuple-element.55.refs_3_, ...), custom_call_target="tpu_custom_call" | custom-call | flops 8053063680 | bytes 24641552 | tf_op jit(solution)/shard_map/weight_second/pallas_call | solution.py:389
  43.3 0.1 collective-permute-start.13
  43.5 3.8 %collective-permute-done.7.refs_7_ = bf16[392,256]{1,0:T(8,128)(2,1)S(1)} collective-permute-done((bf16[392,256]{1,0:T(8,128)(2,1)S(1)}, bf16[392,256]{1,0:T(8,128)(2,1)S(1)}, u32[]{:S(2)}, u32[]{:S(2)}) %collective-permute-start.7) | collective-permute-done | bytes 200736 | tf_op jit(solution)/shard_map/ppermute | solution.py:419
  47.3 4.2 %weight_first.1 = (bf16[16,88,256]{2,1,0:T(8,128)(2,1)S(1)}, bf16[16,88,256]{2,1,0:T(8,128)(2,1)S(1)}) custom-call(s32[1]{0:T(128)} %bitcast.refs_0_, bf16[8,256]{1,0:T(8,128)(2,1)S(1)} %get-tuple-element.38.refs_1_, bf16[8,256]{1,0:T(8,128)(2,1)S(1)} %get-tuple-element.42.refs_3_.refs_2_, bf16[384,256]{1,0:T(8,128)(2,1)S(1)} %get-tuple-element.33.refs_1_.refs_3_, ...), custom_call_target="tpu_custom_call" | custom-call | flops 20132659200 | bytes 115998800 | tf_op jit(solution)/shard_map/weight_first/pallas_call | solution.py:389
  51.5 0.1 collective-permute-start.12
  51.6 1.2 %join_second.1.refs_2_ = bf16[16,248,256]{2,1,0:T(8,128)(2,1)} custom-call(bf16[16,160,256]{2,1,0:T(8,128)(2,1)S(1)} %get-tuple-element.56.refs_15_.refs_0_, bf16[16,160,256]{2,1,0:T(8,128)(2,1)S(1)} %collective-permute-done.13.refs_1_), custom_call_target="tpu_custom_call" | custom-call | bytes 4653056 | tf_op jit(solution)/shard_map/join_second/pallas_call | solution.py:389
  52.8 0.9 %collective-permute-done.12.refs_1_ = bf16[16,88,256]{2,1,0:T(8,128)(2,1)S(1)} collective-permute-done((bf16[16,88,256]{2,1,0:T(8,128)(2,1)S(1)}, bf16[16,88,256]{2,1,0:T(8,128)(2,1)S(1)}, u32[]{:S(2)}, u32[]{:S(2)}) %collective-permute-start.12) | collective-permute-done | bytes 720928 | tf_op jit(solution)/shard_map/ppermute | solution.py:427
  53.7 1.0 %join_first.1 = bf16[16,248,256]{2,1,0:T(8,128)(2,1)} custom-call(bf16[16,88,256]{2,1,0:T(8,128)(2,1)S(1)} %get-tuple-element.57.refs_0_, bf16[16,88,256]{2,1,0:T(8,128)(2,1)S(1)} %collective-permute-done.12.refs_1_, bf16[16,248,256]{2,1,0:T(8,128)(2,1)} %join_second.1.refs_2_), custom_call_target="tpu_custom_call", output_to_operand_aliasing={{}: (2, {})} | custom-call | bytes 5505024 | tf_op jit(solution)/shard_map/join_first/pallas_call | solution.py:389
  54.7 36.1 %all_to_all.5.refs_0_ = bf16[16,248,256]{2,1,0:T(8,128)(2,1)S(1)} all-to-all(bf16[16,248,256]{2,1,0:T(8,128)(2,1)} %join_first.1), channel_id=1, replica_groups=mesh['dp_0'=4,'dp_1'=4,'dp_2'=2,'section'=4] {'dp_0','dp_1'}, dimensions={0} | all-to-all | bytes 4063232 | tf_op jit(solution)/shard_map/all_to_all | solution.py:584
  90.8 1.0 %total.1 = (f32[5,32,256]{2,1,0:T(8,128)}, f32[5,16,256]{2,1,0:T(8,128)}, f32[2]{0:T(128)}) custom-call(bf16[16,248,256]{2,1,0:T(8,128)(2,1)S(1)} %all_to_all.5.refs_0_), custom_call_target="tpu_custom_call" | custom-call | bytes 2277384 | tf_op jit(solution)/shard_map/total/pallas_call | solution.py:389
  (9 shorter events, 0.1 us)
Async XLA Ops:
  4.5 7.8 %collective-permute-start = (bf16[384,256]{1,0:T(8,128)(2,1)S(1)}, bf16[384,256]{1,0:T(8,128)(2,1)S(1)}, u32[]{:S(2)}, u32[]{:S(2)}) collective-permute-start(bf16[384,256]{1,0:T(8,128)(2,1)S(1)} %get-tuple-element.33.refs_1_.refs_3_), channel_id=1, source_target_pairs={{0,1},{1,2},{2,3},{3,0},{4,5},{5,6},{6,7},{7,4},{8,9},{9,10},{10,1... | collective-permute-start | bytes 589832 | tf_op jit(solution)/shard_map/ppermute | solution.py:419
  8.7 7.9 %collective-permute-start.4 = (bf16[384,256]{1,0:T(8,128)(2,1)S(1)}, bf16[384,256]{1,0:T(8,128)(2,1)S(1)}, u32[]{:S(2)}, u32[]{:S(2)}) collective-permute-start(bf16[384,256]{1,0:T(8,128)(2,1)S(1)} %get-tuple-element.39.refs_1_.refs_4_), channel_id=1, source_target_pairs={{0,3},{1,0},{2,1},{3,2},{4,7},{5,4},{6,5},{7,6},{8,11},{9,8},{10,9... | collective-permute-start | bytes 589832 | tf_op jit(solution)/shard_map/ppermute | solution.py:419
  10.4 10.5 %collective-permute-start.1 = (bf16[384,256]{1,0:T(8,128)(2,1)S(1)}, bf16[384,256]{1,0:T(8,128)(2,1)}, u32[]{:S(2)}, u32[]{:S(2)}) collective-permute-start(bf16[384,256]{1,0:T(8,128)(2,1)S(1)} %get-tuple-element.33.refs_1_.refs_3_), channel_id=1, source_target_pairs={{0,3},{1,0},{2,1},{3,2},{4,7},{5,4},{6,5},{7,6},{8,11},{9,8},{10,9... | collective-permute-start | bytes 589832 | tf_op jit(solution)/shard_map/ppermute | solution.py:419
  12.3 9.1 %collective-permute-start.2 = (bf16[384,256]{1,0:T(8,128)(2,1)S(1)}, bf16[384,256]{1,0:T(8,128)(2,1)}, u32[]{:S(2)}, u32[]{:S(2)}) collective-permute-start(bf16[384,256]{1,0:T(8,128)(2,1)S(1)} %collective-permute-done.refs_2_), channel_id=1, source_target_pairs={{0,1},{1,2},{2,3},{3,0},{4,5},{5,6},{6,7},{7,4},{8,9},{9,10},{10,1... | collective-permute-start | bytes 589832 | tf_op jit(solution)/shard_map/ppermute | solution.py:419
  12.8 12.2 %collective-permute-start.3 = (bf16[384,256]{1,0:T(8,128)(2,1)S(1)}, bf16[384,256]{1,0:T(8,128)(2,1)}, u32[]{:S(2)}, u32[]{:S(2)}) collective-permute-start(bf16[384,256]{1,0:T(8,128)(2,1)S(1)} %get-tuple-element.39.refs_1_.refs_4_), channel_id=1, source_target_pairs={{0,1},{1,2},{2,3},{3,0},{4,5},{5,6},{6,7},{7,4},{8,9},{9,10},{10,1... | collective-permute-start | bytes 589832 | tf_op jit(solution)/shard_map/ppermute | solution.py:419
  16.6 8.5 %collective-permute-start.5 = (bf16[384,256]{1,0:T(8,128)(2,1)S(1)}, bf16[384,256]{1,0:T(8,128)(2,1)}, u32[]{:S(2)}, u32[]{:S(2)}) collective-permute-start(bf16[384,256]{1,0:T(8,128)(2,1)S(1)} %collective-permute-done.4.refs_3_), channel_id=1, source_target_pairs={{0,3},{1,0},{2,1},{3,2},{4,7},{5,4},{6,5},{7,6},{8,11},{9,8},{10,9... | collective-permute-start | bytes 589832 | tf_op jit(solution)/shard_map/ppermute | solution.py:419
  28.4 7.9 %collective-permute-start.10 = (bf16[392,256]{1,0:T(8,128)(2,1)S(1)}, bf16[392,256]{1,0:T(8,128)(2,1)S(1)}, u32[]{:S(2)}, u32[]{:S(2)}) collective-permute-start(bf16[392,256]{1,0:T(8,128)(2,1)S(1)} %get-tuple-element.50), channel_id=1, source_target_pairs={{0,3},{1,0},{2,1},{3,2},{4,7},{5,4},{6,5},{7,6},{8,11},{9,8},{10,9... | collective-permute-start | bytes 602120 | tf_op jit(solution)/shard_map/ppermute | solution.py:419
  30.9 9.2 %collective-permute-start.6 = (bf16[392,256]{1,0:T(8,128)(2,1)S(1)}, bf16[392,256]{1,0:T(8,128)(2,1)S(1)}, u32[]{:S(2)}, u32[]{:S(2)}) collective-permute-start(bf16[392,256]{1,0:T(8,128)(2,1)S(1)} %get-tuple-element.46), channel_id=1, source_target_pairs={{0,1},{1,2},{2,3},{3,0},{4,5},{5,6},{6,7},{7,4},{8,9},{9,10},{10,1... | collective-permute-start | bytes 602120 | tf_op jit(solution)/shard_map/ppermute | solution.py:419
  31.9 11.6 %collective-permute-start.8 = (bf16[392,256]{1,0:T(8,128)(2,1)S(1)}, bf16[392,256]{1,0:T(8,128)(2,1)S(1)}, u32[]{:S(2)}, u32[]{:S(2)}) collective-permute-start(bf16[392,256]{1,0:T(8,128)(2,1)S(1)} %get-tuple-element.47), channel_id=1, source_target_pairs={{0,1},{1,2},{2,3},{3,0},{4,5},{5,6},{6,7},{7,4},{8,9},{9,10},{10,1... | collective-permute-start | bytes 602120 | tf_op jit(solution)/shard_map/ppermute | solution.py:419
  32.6 10.9 %collective-permute-start.9 = (bf16[392,256]{1,0:T(8,128)(2,1)S(1)}, bf16[392,256]{1,0:T(8,128)(2,1)S(1)}, u32[]{:S(2)}, u32[]{:S(2)}) collective-permute-start(bf16[392,256]{1,0:T(8,128)(2,1)S(1)} %get-tuple-element.48), channel_id=1, source_target_pairs={{0,3},{1,0},{2,1},{3,2},{4,7},{5,4},{6,5},{7,6},{8,11},{9,8},{10,9... | collective-permute-start | bytes 602120 | tf_op jit(solution)/shard_map/ppermute | solution.py:419
  36.4 7.0 %collective-permute-start.11 = (bf16[392,256]{1,0:T(8,128)(2,1)S(1)}, bf16[392,256]{1,0:T(8,128)(2,1)S(1)}, u32[]{:S(2)}, u32[]{:S(2)}) collective-permute-start(bf16[392,256]{1,0:T(8,128)(2,1)S(1)} %relay_b.1.refs_6_), channel_id=1, source_target_pairs={{0,3},{1,0},{2,1},{3,2},{4,7},{5,4},{6,5},{7,6},{8,11},{9,8},{10,9... | collective-permute-start | bytes 602120 | tf_op jit(solution)/shard_map/ppermute | solution.py:419
  40.1 7.2 %collective-permute-start.7 = (bf16[392,256]{1,0:T(8,128)(2,1)S(1)}, bf16[392,256]{1,0:T(8,128)(2,1)S(1)}, u32[]{:S(2)}, u32[]{:S(2)}) collective-permute-start(bf16[392,256]{1,0:T(8,128)(2,1)S(1)} %relay_a.1.refs_5_), channel_id=1, source_target_pairs={{0,1},{1,2},{2,3},{3,0},{4,5},{5,6},{6,7},{7,4},{8,9},{9,10},{10,1... | collective-permute-start | bytes 602120 | tf_op jit(solution)/shard_map/ppermute | solution.py:419
  43.3 8.2 %collective-permute-start.13 = (bf16[16,160,256]{2,1,0:T(8,128)(2,1)S(1)}, bf16[16,160,256]{2,1,0:T(8,128)(2,1)S(1)}, u32[]{:S(2)}, u32[]{:S(2)}) collective-permute-start(bf16[16,160,256]{2,1,0:T(8,128)(2,1)S(1)} %get-tuple-element.59), channel_id=1, source_target_pairs={{0,4},{4,0},{1,5},{5,1},{2,6},{6,2},{3,7},{7,3},{8,12},{12,8},{9,1... | collective-permute-start | bytes 3932168 | tf_op jit(solution)/shard_map/ppermute | solution.py:427
  51.5 2.3 %collective-permute-start.12 = (bf16[16,88,256]{2,1,0:T(8,128)(2,1)S(1)}, bf16[16,88,256]{2,1,0:T(8,128)(2,1)S(1)}, u32[]{:S(2)}, u32[]{:S(2)}) collective-permute-start(bf16[16,88,256]{2,1,0:T(8,128)(2,1)S(1)} %get-tuple-element.58), channel_id=1, source_target_pairs={{0,4},{4,0},{1,5},{5,1},{2,6},{6,2},{3,7},{7,3},{8,12},{12,8},{9,1... | collective-permute-start | bytes 2162696 | tf_op jit(solution)/shard_map/ppermute | solution.py:427

commit v8 on v7

--- a/solution.py
+++ b/solution.py
@@ -13,7 +13,7 @@
 F32 = jnp.float32
 BF16 = jnp.bfloat16
 VMEM_LIMIT = 16 << 20
-NEAR_PHASES = (False, False)
+NEAR_PHASES = (True, False)
 NEAR_ALL = (True, True)
 NEAR_SMALL = True
 
@@ -115,12 +115,13 @@
         for at, x in enumerate((real, fake))
     ]
 
+    for copy in rest_copies:
+        copy.start()
+
     def take(n):
         source = real if n < cols else fake
         pltpu.make_async_copy(source.at[n % cols], held.at[n], held_sem.at[n]).wait()
         if n == 2 * cols - 1:
-            for copy in rest_copies:
-                copy.start()
             for copy in w_copies:
                 copy.wait()
         return held[n]
@@ -292,10 +293,10 @@
         if not near:
             held, sem = rest[:2]
             rest = rest[2:]
-            large.append(copies_of(x, held, sem))
+            large.append(pltpu.make_async_copy(x, held, sem))
             x = held
         phases.append(x)
-    for copy in small + [copies[p] for p in range(3) for copies in large]:
+    for copy in small + large:
         copy.start()
     for copy in small:
         copy.wait()
@@ -318,9 +319,9 @@
     groups = mine.shape[0]
     own_rows = (mine.shape[1] - 8) // taps
     outs = (mine, theirs)
+    for copy in large:
+        copy.wait()
     for p in range(3):
-        for copies in large:
-            copies[p].wait()
         lanes = width if p == 0 else 2 * width
         g = dot_rows(phases[0][p], moved[:rows, :lanes])
         g = g + dot_rows(phases[1][p], moved[rows:, :lanes])
@@ -562,7 +563,7 @@
         [like((groups, taps * first_rows + 8, width))] * 2,
         [pltpu.VMEM((2 * cols, frames + 8, width), F32), pltpu.VMEM((2 * rows, 2 * width), BF16)]
         + [pltpu.VMEM((10, rows + 8, width), BF16), dma((10,))] * (not NEAR_SMALL)
-        + [phases_far[0], dma((3,))] * (2 - sum(NEAR_PHASES)),
+        + phases_far * (2 - sum(NEAR_PHASES)),
         smem=1,
         hbm=tuple(at for at in (13, 14) if not NEAR_PHASES[at - 13]),
         loose=() if NEAR_SMALL else tuple(range(3, 13)),

time: 92.3 us -> 90.2 us (0.977)
  Pallas kernels: 24.7 us -> 22.6 us
    pallas_call x12, Pallas kernels: 24.7 us -> 22.6 us  [call(): pl.pallas_call(body, out_shape=[pltpu.HBM(x.shape, x.dtype) if at in hbm_...]
  transfers between devices with their start and end apart: 14 -> 14, of which waited for: 7 -> 7; matrix products, arithmetic and copies ran while one was open for 0% -> 0% of each run, Pallas kernels for 17% -> 16%
where the time goes in v8:
time: 90.2 us; the launch traced here: 89.9 us
  blocking collectives  36.1 us (40%)
  Pallas kernels  22.6 us (25%)
  starting transfers between devices  19.8 us (22%)
  waiting for transfers between devices  10.4 us (12%)
  between operations  0.97 us (1%)
    all_to_all x1, blocking collectives, shards(): blocks = lax.all_to_all(joint, ZY, 0, 0)  36.1 us
    pallas_call x12, Pallas kernels, call(): pl.pallas_call(body, out_shape=[pltpu.HBM(x.shape, x.dtype) if at in hbm_...  22.6 us
    ppermute x12, starting transfers between devices, turn(): lax.ppermute(x, 'section', [(i, (i + step) % count) for i in range(count)])  19.6 us
    ppermute x12, waiting for transfers between devices, turn(): lax.ppermute(x, 'section', [(i, (i + step) % count) for i in range(count)])  9.45 us
  transfers between devices with their start and end apart: 14, of which 7 were waited for; matrix products, arithmetic and copies ran while one was open for 0% of the time, Pallas kernels for 16%

profile of v8, /device:TPU:0, one launch (start us, length us, event | category | flops | bytes accessed | tf_op | source)
XLA Modules:
  0.0 89.9 jit_solution(14794907719975358835)
XLA Ops:
  0.6 3.1 %first_a.1 = (bf16[384,256]{1,0:T(8,128)(2,1)S(1)}, bf16[3,384,512]{2,1,0:T(8,128)(2,1)S(1)}, f32[8,128]{1,0:T(8,128)S(1)}, bf16[5,512,256]{2,1,0:T(8,128)(2,1)S(1)}, bf16[8,144,512]{2,1,0:T(8,128)(2,1)S(1)}) custom-call(bf16[8,144,512]{2,1,0:T(8,128)(2,1)} %refs_0_.1, bf16[8,144,512]{2,1,0:T(8,128)(2,1)} %refs_1_.1, bf16[5,512,256]{2,1,0:T(8,128)(2,1)} %refs_2_.2), custom_call_target="tpu_custom_call" | custom-call | flops 503316480 | bytes 7540736 | tf_op jit(solution)/shard_map/first_a/pallas_call | solution.py:390
  3.7 1.6 %collective-permute-start = (bf16[384,256]{1,0:T(8,128)(2,1)S(1)}, bf16[384,256]{1,0:T(8,128)(2,1)S(1)}, u32[]{:S(2)}, u32[]{:S(2)}) collective-permute-start(bf16[384,256]{1,0:T(8,128)(2,1)S(1)} %get-tuple-element.33.refs_1_.refs_3_), channel_id=1, source_target_pairs={{0,1},{1,2},{2,3},{3,0},{4,5},{5,6},{6,7},{7,4},{8,9},{9,10},{10,1... | collective-permute-start | bytes 589832 | tf_op jit(solution)/shard_map/ppermute | solution.py:420
  5.4 2.5 %first_b.1 = (bf16[384,256]{1,0:T(8,128)(2,1)S(1)}, bf16[3,384,512]{2,1,0:T(8,128)(2,1)}, f32[8,128]{1,0:T(8,128)S(1)}, bf16[5,1024,256]{2,1,0:T(8,128)(2,1)S(1)}) custom-call(bf16[8,144,512]{2,1,0:T(8,128)(2,1)S(1)} %get-tuple-element.34.refs_0_, bf16[5,512,256]{2,1,0:T(8,128)(2,1)S(1)} %get-tuple-element.35.refs_1_, bf16[5,1024,256]{2,1,0:T(8,128)(2,1)} %refs_2_.3), custom_call_target="tpu_custom_call" | custom-call | flops 503316480 | bytes 9113600 | tf_op jit(solution)/shard_map/first_b/pallas_call | solution.py:390
  7.9 1.7 %collective-permute-start.4 = (bf16[384,256]{1,0:T(8,128)(2,1)S(1)}, bf16[384,256]{1,0:T(8,128)(2,1)S(1)}, u32[]{:S(2)}, u32[]{:S(2)}) collective-permute-start(bf16[384,256]{1,0:T(8,128)(2,1)S(1)} %get-tuple-element.39.refs_1_.refs_4_), channel_id=1, source_target_pairs={{0,3},{1,0},{2,1},{3,2},{4,7},{5,4},{6,5},{7,6},{8,11},{9,8},{10,9... | collective-permute-start | bytes 589832 | tf_op jit(solution)/shard_map/ppermute | solution.py:420
  9.6 1.6 %collective-permute-start.1 = (bf16[384,256]{1,0:T(8,128)(2,1)S(1)}, bf16[384,256]{1,0:T(8,128)(2,1)}, u32[]{:S(2)}, u32[]{:S(2)}) collective-permute-start(bf16[384,256]{1,0:T(8,128)(2,1)S(1)} %get-tuple-element.33.refs_1_.refs_3_), channel_id=1, source_target_pairs={{0,3},{1,0},{2,1},{3,2},{4,7},{5,4},{6,5},{7,6},{8,11},{9,8},{10,9... | collective-permute-start | bytes 589832 | tf_op jit(solution)/shard_map/ppermute | solution.py:420
  11.3 0.3 collective-permute-done.refs_2_
  11.6 0.5 collective-permute-start.2
  12.0 1.5 %collective-permute-start.3 = (bf16[384,256]{1,0:T(8,128)(2,1)S(1)}, bf16[384,256]{1,0:T(8,128)(2,1)}, u32[]{:S(2)}, u32[]{:S(2)}) collective-permute-start(bf16[384,256]{1,0:T(8,128)(2,1)S(1)} %get-tuple-element.39.refs_1_.refs_4_), channel_id=1, source_target_pairs={{0,1},{1,2},{2,3},{3,0},{4,5},{5,6},{6,7},{7,4},{8,9},{9,10},{10,1... | collective-permute-start | bytes 589832 | tf_op jit(solution)/shard_map/ppermute | solution.py:420
  13.5 2.3 %collective-permute-done.4.refs_3_ = bf16[384,256]{1,0:T(8,128)(2,1)S(1)} collective-permute-done((bf16[384,256]{1,0:T(8,128)(2,1)S(1)}, bf16[384,256]{1,0:T(8,128)(2,1)S(1)}, u32[]{:S(2)}, u32[]{:S(2)}) %collective-permute-start.4) | collective-permute-done | bytes 196640 | tf_op jit(solution)/shard_map/ppermute | solution.py:420
  15.8 2.9 %collective-permute-start.5 = (bf16[384,256]{1,0:T(8,128)(2,1)S(1)}, bf16[384,256]{1,0:T(8,128)(2,1)}, u32[]{:S(2)}, u32[]{:S(2)}) collective-permute-start(bf16[384,256]{1,0:T(8,128)(2,1)S(1)} %collective-permute-done.4.refs_3_), channel_id=1, source_target_pairs={{0,3},{1,0},{2,1},{3,2},{4,7},{5,4},{6,5},{7,6},{8,11},{9,8},{10,9... | collective-permute-start | bytes 589832 | tf_op jit(solution)/shard_map/ppermute | solution.py:420
  18.7 1.4 %collective-permute-done.1.refs_3_ = bf16[384,256]{1,0:T(8,128)(2,1)} collective-permute-done((bf16[384,256]{1,0:T(8,128)(2,1)S(1)}, bf16[384,256]{1,0:T(8,128)(2,1)}, u32[]{:S(2)}, u32[]{:S(2)}) %collective-permute-start.1) | collective-permute-done | bytes 196640 | tf_op jit(solution)/shard_map/ppermute | solution.py:420
  20.1 0.5 collective-permute-done.2.refs_4_
  20.6 3.7 %second_a.1 = (bf16[384,1024]{1,0:T(8,128)(2,1)S(1)}, bf16[384,1280]{1,0:T(8,128)(2,1)S(1)}, bf16[392,256]{1,0:T(8,128)(2,1)S(1)}, bf16[8,256]{1,0:T(8,128)(2,1)...) custom-call(s32[1]{0:T(128)} %bitcast.1.refs_0_, ...), custom_call_target="tpu_custom_call" | custom-call | flops 1258291200 | bytes 5984260 | tf_op jit(solution)/shard_map/second_a/pallas_call | solution.py:390
  24.3 0.0 collective-permute-done.5.refs_4_
  24.3 3.4 %second_b.1 = (bf16[384,1024]{1,0:T(8,128)(2,1)S(1)}, bf16[384,1280]{1,0:T(8,128)(2,1)S(1)}, bf16[392,256]{1,0:T(8,128)(2,1)S(1)}, bf16[8,256]{1,0:T(8,128)(2,1)S(1)}) custom-call(s32[1]{0:T(128)} %bitcast.1.refs_0_, bf16[384,256]{1,0:T(8,128)(2,1)S(1)} %get-tuple-element.39.refs_1_.refs_4_, bf16[384,256]{1,0:T(8,128)(2,1)} %collective-permute-done.3.refs_2_, ...), custom_call_target="tpu_custom_call" | custom-call | flops 1258291200 | bytes 5386244 | tf_op jit(solution)/shard_map/second_b/pallas_call | solution.py:390
  27.7 2.4 %collective-permute-start.10 = (bf16[392,256]{1,0:T(8,128)(2,1)S(1)}, bf16[392,256]{1,0:T(8,128)(2,1)S(1)}, u32[]{:S(2)}, u32[]{:S(2)}) collective-permute-start(bf16[392,256]{1,0:T(8,128)(2,1)S(1)} %get-tuple-element.50), channel_id=1, source_target_pairs={{0,3},{1,0},{2,1},{3,2},{4,7},{5,4},{6,5},{7,6},{8,11},{9,8},{10,9... | collective-permute-start | bytes 602120 | tf_op jit(solution)/shard_map/ppermute | solution.py:420
  30.1 1.0 %back_b.1 = (bf16[392,256]{1,0:T(8,128)(2,1)S(1)}, bf16[392,256]{1,0:T(8,128)(2,1)S(1)}, bf16[384,256]{1,0:T(8,128)(2,1)S(1)}) custom-call(s32[1]{0:T(128)} %bitcast.1.refs_0_, bf16[384,1280]{1,0:T(8,128)(2,1)S(1)} %get-tuple-element.43.refs_1_.refs_4_, bf16[5,1024,256]{2,1,0:T(8,128)(2,1)S(1)} %get-tuple-element.36.refs_5_.refs_2_, ...), custom_call_target="tpu_custom_call" | custom-call | flops 3019898880 | bytes 16826384 | tf_op jit(solution)/shard_map/back_b/pallas_call | solution.py:390
  31.1 0.7 collective-permute-start.8
  31.8 2.7 %collective-permute-start.9 = (bf16[392,256]{1,0:T(8,128)(2,1)S(1)}, bf16[392,256]{1,0:T(8,128)(2,1)S(1)}, u32[]{:S(2)}, u32[]{:S(2)}) collective-permute-start(bf16[392,256]{1,0:T(8,128)(2,1)S(1)} %get-tuple-element.48), channel_id=1, source_target_pairs={{0,3},{1,0},{2,1},{3,2},{4,7},{5,4},{6,5},{7,6},{8,11},{9,8},{10,9... | collective-permute-start | bytes 602120 | tf_op jit(solution)/shard_map/ppermute | solution.py:420
  34.5 1.1 %collective-permute-done.10.refs_1_.refs_12_ = bf16[392,256]{1,0:T(8,128)(2,1)S(1)} collective-permute-done((bf16[392,256]{1,0:T(8,128)(2,1)S(1)}, bf16[392,256]{1,0:T(8,128)(2,1)S(1)}, u32[]{:S(2)}, u32[]{:S(2)}) %collective-permute-start.10) | collective-permute-done | bytes 200736 | tf_op jit(solution)/shard_map/ppermute | solution.py:420
  35.7 3.7 %collective-permute-start.11 = (bf16[392,256]{1,0:T(8,128)(2,1)S(1)}, bf16[392,256]{1,0:T(8,128)(2,1)S(1)}, u32[]{:S(2)}, u32[]{:S(2)}) collective-permute-start(bf16[392,256]{1,0:T(8,128)(2,1)S(1)} %relay_b.1.refs_6_), channel_id=1, source_target_pairs={{0,3},{1,0},{2,1},{3,2},{4,7},{5,4},{6,5},{7,6},{8,11},{9,8},{10,9... | collective-permute-start | bytes 602120 | tf_op jit(solution)/shard_map/ppermute | solution.py:420
  39.4 0.3 collective-permute-start.7
  39.7 3.0 %weight_second.1 = (bf16[16,160,256]{2,1,0:T(8,128)(2,1)S(1)}, bf16[16,160,256]{2,1,0:T(8,128)(2,1)S(1)}) custom-call(s32[1]{0:T(128)} %bitcast.refs_0_, bf16[384,1024]{1,0:T(8,128)(2,1)S(1)} %get-tuple-element.53.refs_1_, bf16[384,1024]{1,0:T(8,128)(2,1)S(1)} %get-tuple-element.54.refs_2_, bf16[384,1280]{1,0:T(8,128)(2,1)S(1)} %get-tuple-element.55.refs_3_, ...), custom_call_target="tpu_custom_call" | custom-call | flops 8053063680 | bytes 24641552 | tf_op jit(solution)/shard_map/weight_second/pallas_call | solution.py:390
  42.6 0.1 collective-permute-start.13
  42.7 3.8 %collective-permute-done.7.refs_7_ = bf16[392,256]{1,0:T(8,128)(2,1)S(1)} collective-permute-done((bf16[392,256]{1,0:T(8,128)(2,1)S(1)}, bf16[392,256]{1,0:T(8,128)(2,1)S(1)}, u32[]{:S(2)}, u32[]{:S(2)}) %collective-permute-start.7) | collective-permute-done | bytes 200736 | tf_op jit(solution)/shard_map/ppermute | solution.py:420
  46.6 2.9 %weight_first.1 = (bf16[16,88,256]{2,1,0:T(8,128)(2,1)S(1)}, bf16[16,88,256]{2,1,0:T(8,128)(2,1)S(1)}) custom-call(s32[1]{0:T(128)} %bitcast.refs_0_, bf16[8,256]{1,0:T(8,128)(2,1)S(1)} %get-tuple-element.38.refs_1_, bf16[8,256]{1,0:T(8,128)(2,1)S(1)} %get-tuple-element.42.refs_3_.refs_2_, bf16[384,256]{1,0:T(8,128)(2,1)S(1)} %get-tuple-element.33.refs_1_.refs_3_, ...), custom_call_target="tpu_custom_call" | custom-call | flops 20132659200 | bytes 115998800 | tf_op jit(solution)/shard_map/weight_first/pallas_call | solution.py:390
  49.4 0.1 collective-permute-start.12
  49.5 1.2 %join_second.1.refs_2_ = bf16[16,248,256]{2,1,0:T(8,128)(2,1)} custom-call(bf16[16,160,256]{2,1,0:T(8,128)(2,1)S(1)} %get-tuple-element.56.refs_15_.refs_0_, bf16[16,160,256]{2,1,0:T(8,128)(2,1)S(1)} %collective-permute-done.13.refs_1_), custom_call_target="tpu_custom_call" | custom-call | bytes 4653056 | tf_op jit(solution)/shard_map/join_second/pallas_call | solution.py:390
  50.7 1.0 %collective-permute-done.12.refs_1_ = bf16[16,88,256]{2,1,0:T(8,128)(2,1)S(1)} collective-permute-done((bf16[16,88,256]{2,1,0:T(8,128)(2,1)S(1)}, bf16[16,88,256]{2,1,0:T(8,128)(2,1)S(1)}, u32[]{:S(2)}, u32[]{:S(2)}) %collective-permute-start.12) | collective-permute-done | bytes 720928 | tf_op jit(solution)/shard_map/ppermute | solution.py:428
  51.7 0.9 %join_first.1 = bf16[16,248,256]{2,1,0:T(8,128)(2,1)} custom-call(bf16[16,88,256]{2,1,0:T(8,128)(2,1)S(1)} %get-tuple-element.57.refs_0_, bf16[16,88,256]{2,1,0:T(8,128)(2,1)S(1)} %collective-permute-done.12.refs_1_, bf16[16,248,256]{2,1,0:T(8,128)(2,1)} %join_second.1.refs_2_), custom_call_target="tpu_custom_call", output_to_operand_aliasing={{}: (2, {})} | custom-call | bytes 5505024 | tf_op jit(solution)/shard_map/join_first/pallas_call | solution.py:390
  52.6 36.1 %all_to_all.5.refs_0_ = bf16[16,248,256]{2,1,0:T(8,128)(2,1)S(1)} all-to-all(bf16[16,248,256]{2,1,0:T(8,128)(2,1)} %join_first.1), channel_id=1, replica_groups=mesh['dp_0'=4,'dp_1'=4,'dp_2'=2,'section'=4] {'dp_0','dp_1'}, dimensions={0} | all-to-all | bytes 4063232 | tf_op jit(solution)/shard_map/all_to_all | solution.py:585
  88.7 1.0 %total.1 = (f32[5,32,256]{2,1,0:T(8,128)}, f32[5,16,256]{2,1,0:T(8,128)}, f32[2]{0:T(128)}) custom-call(bf16[16,248,256]{2,1,0:T(8,128)(2,1)S(1)} %all_to_all.5.refs_0_), custom_call_target="tpu_custom_call" | custom-call | bytes 2277384 | tf_op jit(solution)/shard_map/total/pallas_call | solution.py:390
  (13 shorter events, 0.1 us)
Async XLA Ops:
  3.7 4.2 %copy-start = (bf16[3,384,512]{2,1,0:T(8,128)(2,1)}, bf16[3,384,512]{2,1,0:T(8,128)(2,1)S(1)}, u32[]{:S(2)}) copy-start(bf16[3,384,512]{2,1,0:T(8,128)(2,1)S(1)} %get-tuple-element.51.refs_13_) | copy-start | bytes 3538948
  3.7 7.8 %collective-permute-start = (bf16[384,256]{1,0:T(8,128)(2,1)S(1)}, bf16[384,256]{1,0:T(8,128)(2,1)S(1)}, u32[]{:S(2)}, u32[]{:S(2)}) collective-permute-start(bf16[384,256]{1,0:T(8,128)(2,1)S(1)} %get-tuple-element.33.refs_1_.refs_3_), channel_id=1, source_target_pairs={{0,1},{1,2},{2,3},{3,0},{4,5},{5,6},{6,7},{7,4},{8,9},{9,10},{10,1... | collective-permute-start | bytes 589832 | tf_op jit(solution)/shard_map/ppermute | solution.py:420
  7.9 7.9 %collective-permute-start.4 = (bf16[384,256]{1,0:T(8,128)(2,1)S(1)}, bf16[384,256]{1,0:T(8,128)(2,1)S(1)}, u32[]{:S(2)}, u32[]{:S(2)}) collective-permute-start(bf16[384,256]{1,0:T(8,128)(2,1)S(1)} %get-tuple-element.39.refs_1_.refs_4_), channel_id=1, source_target_pairs={{0,3},{1,0},{2,1},{3,2},{4,7},{5,4},{6,5},{7,6},{8,11},{9,8},{10,9... | collective-permute-start | bytes 589832 | tf_op jit(solution)/shard_map/ppermute | solution.py:420
  9.6 10.5 %collective-permute-start.1 = (bf16[384,256]{1,0:T(8,128)(2,1)S(1)}, bf16[384,256]{1,0:T(8,128)(2,1)}, u32[]{:S(2)}, u32[]{:S(2)}) collective-permute-start(bf16[384,256]{1,0:T(8,128)(2,1)S(1)} %get-tuple-element.33.refs_1_.refs_3_), channel_id=1, source_target_pairs={{0,3},{1,0},{2,1},{3,2},{4,7},{5,4},{6,5},{7,6},{8,11},{9,8},{10,9... | collective-permute-start | bytes 589832 | tf_op jit(solution)/shard_map/ppermute | solution.py:420
  11.6 9.1 %collective-permute-start.2 = (bf16[384,256]{1,0:T(8,128)(2,1)S(1)}, bf16[384,256]{1,0:T(8,128)(2,1)}, u32[]{:S(2)}, u32[]{:S(2)}) collective-permute-start(bf16[384,256]{1,0:T(8,128)(2,1)S(1)} %collective-permute-done.refs_2_), channel_id=1, source_target_pairs={{0,1},{1,2},{2,3},{3,0},{4,5},{5,6},{6,7},{7,4},{8,9},{9,10},{10,1... | collective-permute-start | bytes 589832 | tf_op jit(solution)/shard_map/ppermute | solution.py:420
  12.0 12.3 %collective-permute-start.3 = (bf16[384,256]{1,0:T(8,128)(2,1)S(1)}, bf16[384,256]{1,0:T(8,128)(2,1)}, u32[]{:S(2)}, u32[]{:S(2)}) collective-permute-start(bf16[384,256]{1,0:T(8,128)(2,1)S(1)} %get-tuple-element.39.refs_1_.refs_4_), channel_id=1, source_target_pairs={{0,1},{1,2},{2,3},{3,0},{4,5},{5,6},{6,7},{7,4},{8,9},{9,10},{10,1... | collective-permute-start | bytes 589832 | tf_op jit(solution)/shard_map/ppermute | solution.py:420
  15.8 8.5 %collective-permute-start.5 = (bf16[384,256]{1,0:T(8,128)(2,1)S(1)}, bf16[384,256]{1,0:T(8,128)(2,1)}, u32[]{:S(2)}, u32[]{:S(2)}) collective-permute-start(bf16[384,256]{1,0:T(8,128)(2,1)S(1)} %collective-permute-done.4.refs_3_), channel_id=1, source_target_pairs={{0,3},{1,0},{2,1},{3,2},{4,7},{5,4},{6,5},{7,6},{8,11},{9,8},{10,9... | collective-permute-start | bytes 589832 | tf_op jit(solution)/shard_map/ppermute | solution.py:420
  27.7 7.9 %collective-permute-start.10 = (bf16[392,256]{1,0:T(8,128)(2,1)S(1)}, bf16[392,256]{1,0:T(8,128)(2,1)S(1)}, u32[]{:S(2)}, u32[]{:S(2)}) collective-permute-start(bf16[392,256]{1,0:T(8,128)(2,1)S(1)} %get-tuple-element.50), channel_id=1, source_target_pairs={{0,3},{1,0},{2,1},{3,2},{4,7},{5,4},{6,5},{7,6},{8,11},{9,8},{10,9... | collective-permute-start | bytes 602120 | tf_op jit(solution)/shard_map/ppermute | solution.py:420
  30.1 9.2 %collective-permute-start.6 = (bf16[392,256]{1,0:T(8,128)(2,1)S(1)}, bf16[392,256]{1,0:T(8,128)(2,1)S(1)}, u32[]{:S(2)}, u32[]{:S(2)}) collective-permute-start(bf16[392,256]{1,0:T(8,128)(2,1)S(1)} %get-tuple-element.46), channel_id=1, source_target_pairs={{0,1},{1,2},{2,3},{3,0},{4,5},{5,6},{6,7},{7,4},{8,9},{9,10},{10,1... | collective-permute-start | bytes 602120 | tf_op jit(solution)/shard_map/ppermute | solution.py:420
  31.1 11.6 %collective-permute-start.8 = (bf16[392,256]{1,0:T(8,128)(2,1)S(1)}, bf16[392,256]{1,0:T(8,128)(2,1)S(1)}, u32[]{:S(2)}, u32[]{:S(2)}) collective-permute-start(bf16[392,256]{1,0:T(8,128)(2,1)S(1)} %get-tuple-element.47), channel_id=1, source_target_pairs={{0,1},{1,2},{2,3},{3,0},{4,5},{5,6},{6,7},{7,4},{8,9},{9,10},{10,1... | collective-permute-start | bytes 602120 | tf_op jit(solution)/shard_map/ppermute | solution.py:420
  31.8 10.9 %collective-permute-start.9 = (bf16[392,256]{1,0:T(8,128)(2,1)S(1)}, bf16[392,256]{1,0:T(8,128)(2,1)S(1)}, u32[]{:S(2)}, u32[]{:S(2)}) collective-permute-start(bf16[392,256]{1,0:T(8,128)(2,1)S(1)} %get-tuple-element.48), channel_id=1, source_target_pairs={{0,3},{1,0},{2,1},{3,2},{4,7},{5,4},{6,5},{7,6},{8,11},{9,8},{10,9... | collective-permute-start | bytes 602120 | tf_op jit(solution)/shard_map/ppermute | solution.py:420
  35.7 7.1 %collective-permute-start.11 = (bf16[392,256]{1,0:T(8,128)(2,1)S(1)}, bf16[392,256]{1,0:T(8,128)(2,1)S(1)}, u32[]{:S(2)}, u32[]{:S(2)}) collective-permute-start(bf16[392,256]{1,0:T(8,128)(2,1)S(1)} %relay_b.1.refs_6_), channel_id=1, source_target_pairs={{0,3},{1,0},{2,1},{3,2},{4,7},{5,4},{6,5},{7,6},{8,11},{9,8},{10,9... | collective-permute-start | bytes 602120 | tf_op jit(solution)/shard_map/ppermute | solution.py:420
  39.4 7.2 %collective-permute-start.7 = (bf16[392,256]{1,0:T(8,128)(2,1)S(1)}, bf16[392,256]{1,0:T(8,128)(2,1)S(1)}, u32[]{:S(2)}, u32[]{:S(2)}) collective-permute-start(bf16[392,256]{1,0:T(8,128)(2,1)S(1)} %relay_a.1.refs_5_), channel_id=1, source_target_pairs={{0,1},{1,2},{2,3},{3,0},{4,5},{5,6},{6,7},{7,4},{8,9},{9,10},{10,1... | collective-permute-start | bytes 602120 | tf_op jit(solution)/shard_map/ppermute | solution.py:420
  39.6 6.9 %copy-start.1 = (bf16[3,384,512]{2,1,0:T(8,128)(2,1)S(1)}, bf16[3,384,512]{2,1,0:T(8,128)(2,1)}, u32[]{:S(2)}) copy-start(bf16[3,384,512]{2,1,0:T(8,128)(2,1)} %copy-done) | copy-start | bytes 3538948
  42.6 6.9 %collective-permute-start.13 = (bf16[16,160,256]{2,1,0:T(8,128)(2,1)S(1)}, bf16[16,160,256]{2,1,0:T(8,128)(2,1)S(1)}, u32[]{:S(2)}, u32[]{:S(2)}) collective-permute-start(bf16[16,160,256]{2,1,0:T(8,128)(2,1)S(1)} %get-tuple-element.59), channel_id=1, source_target_pairs={{0,4},{4,0},{1,5},{5,1},{2,6},{6,2},{3,7},{7,3},{8,12},{12,8},{9,1... | collective-permute-start | bytes 3932168 | tf_op jit(solution)/shard_map/ppermute | solution.py:428
  49.4 2.3 %collective-permute-start.12 = (bf16[16,88,256]{2,1,0:T(8,128)(2,1)S(1)}, bf16[16,88,256]{2,1,0:T(8,128)(2,1)S(1)}, u32[]{:S(2)}, u32[]{:S(2)}) collective-permute-start(bf16[16,88,256]{2,1,0:T(8,128)(2,1)S(1)} %get-tuple-element.58), channel_id=1, source_target_pairs={{0,4},{4,0},{1,5},{5,1},{2,6},{6,2},{3,7},{7,3},{8,12},{12,8},{9,1... | collective-permute-start | bytes 2162696 | tf_op jit(solution)/shard_map/ppermute | solution.py:428

commit v9 on v8

--- a/solution.py
+++ b/solution.py
@@ -142,7 +142,7 @@
 
 
 def second_kernel(
-    normaliser, whole, near, s_ref, own, prev, following, far, w, loss_first,
+    normaliser, whole, near, s_ref, own, prev, following, far_r, far_f, w, loss_first,
     all_out, shifted_out, far_t, loss, *rest,
 ):
     if near:
@@ -156,11 +156,12 @@
     frames = padded.shape[1] - 16
     s = s_ref[0]
     copies = []
-    for away, x in enumerate((own, following, far, prev)):
+    for x, away, top in (
+        (own, 0, 0), (following, 1, 0), (far_r, 2, 0), (far_f, 2, half), (prev, 3, 0)
+    ):
         at = pl.multiple_of(lax.rem(s + away, 4) * width, 256)
-        copies.append(
-            pltpu.make_async_copy(x, h_all.at[:, pl.ds(at, width)], in_sems.at[away])
-        )
+        target = h_all.at[top : top + x.shape[0], pl.ds(at, width)]
+        copies.append(pltpu.make_async_copy(x, target, in_sems.at[len(copies)]))
         copies[-1].start()
     for copy in copies:
         copy.wait()
@@ -472,26 +473,26 @@
         cost=1,
         name="first_b",
     )
-    far_a = turn(prev_a, 1)
+    far_a = (turn(prev_a[: rows // 2], 1), turn(following_a[rows // 2 :], -1))
     following_b = turn(h_b, -1)
     prev_b = turn(h_b, 1)
-    far_b = turn(following_b, -1)
+    far_b = (turn(prev_b[: rows // 2], 1), turn(following_b[rows // 2 :], -1))
 
     second_outs = [like((rows, width_all)), like((rows, taps * width)), like((rows + 8, width)),
                    like((8, width))]
     back_outs = [like((rows + 8, width)), like((rows + 8, width)), like((rows, width))]
     second_scratch = [
-        pltpu.VMEM((cols, frames + 16, width), F32), dma((4,)),
+        pltpu.VMEM((cols, frames + 16, width), F32), dma((5,)),
     ]
     copies = all_far + [dma, dma]
     flops = 2 * rows * taps * (width_all + width) * width
     all_a, shifted_a, far_t, loss_a, next_t, prev_t, own_a = call(
         functools.partial(second_kernel, normaliser, True, NEAR_ALL[0]),
-        (s, h_a, prev_a, following_a, far_a, w_second, loss_a),
+        (s, h_a, prev_a, following_a, *far_a, w_second, loss_a),
         second_outs + back_outs,
         second_scratch + copies * (not NEAR_ALL[0]),
         smem=1,
-        loose=(1, 2, 3, 4),
+        loose=(1, 2, 3, 4, 5),
         hbm_outs=() if NEAR_ALL[0] else (0, 1),
         cost=1,
         flops=flops,
@@ -504,11 +505,11 @@
 
     all_b, shifted_b, far_t, loss_b = call(
         functools.partial(second_kernel, normaliser, False, NEAR_ALL[1]),
-        (s, h_b, prev_b, following_b, far_b, w_second, loss_b),
+        (s, h_b, prev_b, following_b, *far_b, w_second, loss_b),
         second_outs,
         second_scratch + copies * (not NEAR_ALL[1]),
         smem=1,
-        loose=(1, 2, 3, 4),
+        loose=(1, 2, 3, 4, 5),
         hbm_outs=() if NEAR_ALL[1] else (0, 1),
         cost=1,
         after=(own_a,),

time: 90.2 us -> 94 us (1.042)
  starting transfers between devices: 19.8 us -> 24 us
  waiting for transfers between devices: 10.4 us -> 6.26 us
  local copies, waits for them, and re-layouts: 0.01 us -> 2.25 us
  Pallas kernels: 22.6 us -> 24 us
    ppermute x12 -> x14, starting transfers between devices: 19.6 us -> 23.9 us  [turn(): lax.ppermute(x, 'section', [(i, (i + step) % count) for i in range(count)])]
    ppermute x12 -> x14, waiting for transfers between devices: 9.45 us -> 5.33 us  [turn(): lax.ppermute(x, 'section', [(i, (i + step) % count) for i in range(count)])]
    pallas_call x12, Pallas kernels: 22.6 us -> 24 us  [call(): pl.pallas_call(body, out_shape=[pltpu.HBM(x.shape, x.dtype) if at in hbm_...]
    slice x0 -> x4, local copies, waits for them, and re-layouts: none -> 1.31 us  [the longest x2 1.29 us: shards(): far_a = (turn(prev_a[:rows // 2], 1), turn(following_a[rows // 2:], -1))]
  transfers between devices with their start and end apart: 14 -> 16, of which waited for: 7 -> 4; matrix products, arithmetic and copies ran while one was open for 0% -> 1% of each run, Pallas kernels for 16% -> 17%
where the time goes in v9:
time: 94 us; the launch traced here: 93.7 us
  blocking collectives  36.1 us (38%)
  Pallas kernels  24 us (26%)
  starting transfers between devices  24 us (26%)
  waiting for transfers between devices  6.26 us (7%)
  local copies, waits for them, and re-layouts  2.25 us (2%)
  between operations  1.04 us (1%)
    all_to_all x1, blocking collectives, shards(): blocks = lax.all_to_all(joint, ZY, 0, 0)  36.1 us
    pallas_call x12, Pallas kernels, call(): pl.pallas_call(body, out_shape=[pltpu.HBM(x.shape, x.dtype) if at in hbm_...  24 us
    ppermute x14, starting transfers between devices, turn(): lax.ppermute(x, 'section', [(i, (i + step) % count) for i in range(count)])  23.9 us
    ppermute x14, waiting for transfers between devices, turn(): lax.ppermute(x, 'section', [(i, (i + step) % count) for i in range(count)])  5.33 us
  transfers between devices with their start and end apart: 16, of which 4 were waited for; matrix products, arithmetic and copies ran while one was open for 1% of the time, Pallas kernels for 17%

profile of v9, /device:TPU:0, one launch (start us, length us, event | category | flops | bytes accessed | tf_op | source)
XLA Modules:
  0.0 93.7 jit_solution(2632912768180880490)
XLA Ops:
  0.6 3.1 %first_a.1 = (bf16[384,256]{1,0:T(8,128)(2,1)S(1)}, bf16[3,384,512]{2,1,0:T(8,128)(2,1)S(1)}, f32[8,128]{1,0:T(8,128)S(1)}, bf16[5,512,256]{2,1,0:T(8,128)(2,1)S(1)}, bf16[8,144,512]{2,1,0:T(8,128)(2,1)S(1)}) custom-call(bf16[8,144,512]{2,1,0:T(8,128)(2,1)} %refs_0_.1, bf16[8,144,512]{2,1,0:T(8,128)(2,1)} %refs_1_.1, bf16[5,512,256]{2,1,0:T(8,128)(2,1)} %refs_2_.2), custom_call_target="tpu_custom_call" | custom-call | flops 503316480 | bytes 7540736 | tf_op jit(solution)/shard_map/first_a/pallas_call | solution.py:391
  3.8 1.6 %collective-permute-start = (bf16[384,256]{1,0:T(8,128)(2,1)S(1)}, bf16[384,256]{1,0:T(8,128)(2,1)S(1)}, u32[]{:S(2)}, u32[]{:S(2)}) collective-permute-start(bf16[384,256]{1,0:T(8,128)(2,1)S(1)} %get-tuple-element.33.refs_1_.refs_3_), channel_id=1, source_target_pairs={{0,1},{1,2},{2,3},{3,0},{4,5},{5,6},{6,7},{7,4},{8,9},{9,10},{10,1... | collective-permute-start | bytes 589832 | tf_op jit(solution)/shard_map/ppermute | solution.py:421
  5.4 1.7 %collective-permute-start.1 = (bf16[384,256]{1,0:T(8,128)(2,1)S(1)}, bf16[384,256]{1,0:T(8,128)(2,1)S(1)}, u32[]{:S(2)}, u32[]{:S(2)}) collective-permute-start(bf16[384,256]{1,0:T(8,128)(2,1)S(1)} %get-tuple-element.33.refs_1_.refs_3_), channel_id=1, source_target_pairs={{0,3},{1,0},{2,1},{3,2},{4,7},{5,4},{6,5},{7,6},{8,11},{9,8},{10,9... | collective-permute-start | bytes 589832 | tf_op jit(solution)/shard_map/ppermute | solution.py:421
  7.1 3.0 %first_b.1 = (bf16[384,256]{1,0:T(8,128)(2,1)}, bf16[3,384,512]{2,1,0:T(8,128)(2,1)}, f32[8,128]{1,0:T(8,128)S(1)}, bf16[5,1024,256]{2,1,0:T(8,128)(2,1)S(1)}) custom-call(bf16[8,144,512]{2,1,0:T(8,128)(2,1)S(1)} %get-tuple-element.34.refs_0_, bf16[5,512,256]{2,1,0:T(8,128)(2,1)S(1)} %get-tuple-element.35.refs_1_, bf16[5,1024,256]{2,1,0:T(8,128)(2,1)} %refs_2_.3), custom_call_target="tpu_custom_call" | custom-call | flops 503316480 | bytes 9113600 | tf_op jit(solution)/shard_map/first_b/pallas_call | solution.py:391
  10.1 0.4 collective-permute-start.4
  10.5 2.9 %collective-permute-start.5 = (bf16[384,256]{1,0:T(8,128)(2,1)}, bf16[384,256]{1,0:T(8,128)(2,1)S(1)}, u32[]{:S(2)}, u32[]{:S(2)}) collective-permute-start(bf16[384,256]{1,0:T(8,128)(2,1)} %get-tuple-element.39.refs_1_.refs_4_), channel_id=1, source_target_pairs={{0,3},{1,0},{2,1},{3,2},{4,7},{5,4},{6,5},{7,6},{8,11},{9,8},{10,9... | collective-permute-start | bytes 589832 | tf_op jit(solution)/shard_map/ppermute | solution.py:421
  13.4 0.6 slice.16
  14.1 0.6 slice.17
  14.7 3.2 %collective-permute-start.3 = (bf16[192,256]{1,0:T(8,128)(2,1)}, bf16[192,256]{1,0:T(8,128)(2,1)}, u32[]{:S(2)}, u32[]{:S(2)}) collective-permute-start(bf16[192,256]{1,0:T(8,128)(2,1)} %slice.17), channel_id=1, source_target_pairs={{0,3},{1,0},{2,1},{3,2},{4,7},{5,4},{6,5},{7,6},{8,11},{9,8},{10,9... | collective-permute-start | bytes 294920 | tf_op jit(solution)/shard_map/ppermute | solution.py:421
  18.0 0.5 collective-permute-done.4.refs_2_
  18.5 0.1 collective-permute-start.6
  18.6 3.3 %collective-permute-start.7 = (bf16[192,256]{1,0:T(8,128)(2,1)S(1)}, bf16[192,256]{1,0:T(8,128)(2,1)S(1)}, u32[]{:S(2)}, u32[]{:S(2)}) collective-permute-start(bf16[192,256]{1,0:T(8,128)(2,1)S(1)} %slice.19), channel_id=1, source_target_pairs={{0,3},{1,0},{2,1},{3,2},{4,7},{5,4},{6,5},{7,6},{8,11},{9,8},{10,9... | collective-permute-start | bytes 294920 | tf_op jit(solution)/shard_map/ppermute | solution.py:421
  21.9 0.9 copy-done.3
  22.8 3.6 %second_a.1 = (bf16[384,1024]{1,0:T(8,128)(2,1)S(1)}, bf16[384,1280]{1,0:T(8,128)(2,1)S(1)}, bf16[392,256]{1,0:T(8,128)(2,1)S(1)}, bf16[8,256]{1,0:T(8,128)(2,1)...) custom-call(s32[1]{0:T(128)} %bitcast.1.refs_0_, ...), custom_call_target="tpu_custom_call" | custom-call | flops 1258291200 | bytes 5984260 | tf_op jit(solution)/shard_map/second_a/pallas_call | solution.py:391
  26.4 3.3 %second_b.1 = (bf16[384,1024]{1,0:T(8,128)(2,1)S(1)}, bf16[384,1280]{1,0:T(8,128)(2,1)S(1)}, bf16[392,256]{1,0:T(8,128)(2,1)S(1)}, bf16[8,256]{1,0:T(8,128)(2,1)S(1)}) custom-call(s32[1]{0:T(128)} %bitcast.1.refs_0_, bf16[384,256]{1,0:T(8,128)(2,1)} %get-tuple-element.39.refs_1_.refs_4_, bf16[384,256]{1,0:T(8,128)(2,1)S(1)} %collective-permute-done.4.refs_2_, ...), custom_call_target="tpu_custom_call" | custom-call | flops 1258291200 | bytes 5386244 | tf_op jit(solution)/shard_map/second_b/pallas_call | solution.py:391
  29.7 3.3 %collective-permute-start.12 = (bf16[392,256]{1,0:T(8,128)(2,1)S(1)}, bf16[392,256]{1,0:T(8,128)(2,1)S(1)}, u32[]{:S(2)}, u32[]{:S(2)}) collective-permute-start(bf16[392,256]{1,0:T(8,128)(2,1)S(1)} %get-tuple-element.50), channel_id=1, source_target_pairs={{0,3},{1,0},{2,1},{3,2},{4,7},{5,4},{6,5},{7,6},{8,11},{9,8},{10,9... | collective-permute-start | bytes 602120 | tf_op jit(solution)/shard_map/ppermute | solution.py:421
  33.0 1.0 %back_b.1 = (bf16[392,256]{1,0:T(8,128)(2,1)S(1)}, bf16[392,256]{1,0:T(8,128)(2,1)S(1)}, bf16[384,256]{1,0:T(8,128)(2,1)S(1)}) custom-call(s32[1]{0:T(128)} %bitcast.1.refs_0_, bf16[384,1280]{1,0:T(8,128)(2,1)S(1)} %get-tuple-element.43.refs_1_.refs_4_, bf16[5,1024,256]{2,1,0:T(8,128)(2,1)S(1)} %get-tuple-element.36.refs_6_.refs_2_, ...), custom_call_target="tpu_custom_call" | custom-call | flops 3019898880 | bytes 16826384 | tf_op jit(solution)/shard_map/back_b/pallas_call | solution.py:391
  33.9 0.1 collective-permute-start.10
  34.0 3.3 %collective-permute-start.11 = (bf16[392,256]{1,0:T(8,128)(2,1)S(1)}, bf16[392,256]{1,0:T(8,128)(2,1)S(1)}, u32[]{:S(2)}, u32[]{:S(2)}) collective-permute-start(bf16[392,256]{1,0:T(8,128)(2,1)S(1)} %get-tuple-element.48), channel_id=1, source_target_pairs={{0,3},{1,0},{2,1},{3,2},{4,7},{5,4},{6,5},{7,6},{8,11},{9,8},{10,9... | collective-permute-start | bytes 602120 | tf_op jit(solution)/shard_map/ppermute | solution.py:421
  37.3 1.0 %collective-permute-done.12.refs_1_.refs_12_ = bf16[392,256]{1,0:T(8,128)(2,1)S(1)} collective-permute-done((bf16[392,256]{1,0:T(8,128)(2,1)S(1)}, bf16[392,256]{1,0:T(8,128)(2,1)S(1)}, u32[]{:S(2)}, u32[]{:S(2)}) %collective-permute-start.12) | collective-permute-done | bytes 200736 | tf_op jit(solution)/shard_map/ppermute | solution.py:421
  38.3 3.8 %collective-permute-start.13 = (bf16[392,256]{1,0:T(8,128)(2,1)S(1)}, bf16[392,256]{1,0:T(8,128)(2,1)S(1)}, u32[]{:S(2)}, u32[]{:S(2)}) collective-permute-start(bf16[392,256]{1,0:T(8,128)(2,1)S(1)} %relay_b.1.refs_6_), channel_id=1, source_target_pairs={{0,3},{1,0},{2,1},{3,2},{4,7},{5,4},{6,5},{7,6},{8,11},{9,8},{10,9... | collective-permute-start | bytes 602120 | tf_op jit(solution)/shard_map/ppermute | solution.py:421
  42.2 0.3 collective-permute-start.9
  42.4 2.9 %weight_second.1 = (bf16[16,160,256]{2,1,0:T(8,128)(2,1)S(1)}, bf16[16,160,256]{2,1,0:T(8,128)(2,1)S(1)}) custom-call(s32[1]{0:T(128)} %bitcast.refs_0_, bf16[384,1024]{1,0:T(8,128)(2,1)S(1)} %get-tuple-element.53.refs_1_, bf16[384,1024]{1,0:T(8,128)(2,1)S(1)} %get-tuple-element.54.refs_2_, bf16[384,1280]{1,0:T(8,128)(2,1)S(1)} %get-tuple-element.55.refs_3_, ...), custom_call_target="tpu_custom_call" | custom-call | flops 8053063680 | bytes 24641552 | tf_op jit(solution)/shard_map/weight_second/pallas_call | solution.py:391
  45.4 0.1 collective-permute-start.15
  45.5 3.8 %collective-permute-done.9.refs_7_ = bf16[392,256]{1,0:T(8,128)(2,1)S(1)} collective-permute-done((bf16[392,256]{1,0:T(8,128)(2,1)S(1)}, bf16[392,256]{1,0:T(8,128)(2,1)S(1)}, u32[]{:S(2)}, u32[]{:S(2)}) %collective-permute-start.9) | collective-permute-done | bytes 200736 | tf_op jit(solution)/shard_map/ppermute | solution.py:421
  49.3 3.8 %weight_first.1 = (bf16[16,88,256]{2,1,0:T(8,128)(2,1)S(1)}, bf16[16,88,256]{2,1,0:T(8,128)(2,1)S(1)}) custom-call(s32[1]{0:T(128)} %bitcast.refs_0_, bf16[8,256]{1,0:T(8,128)(2,1)S(1)} %get-tuple-element.38.refs_1_, bf16[8,256]{1,0:T(8,128)(2,1)S(1)} %get-tuple-element.42.refs_3_.refs_2_, bf16[384,256]{1,0:T(8,128)(2,1)S(1)} %copy-done.4, ...), custom_call_target="tpu_custom_call" | custom-call | flops 20132659200 | bytes 115998800 | tf_op jit(solution)/shard_map/weight_first/pallas_call | solution.py:391
  53.1 0.1 collective-permute-start.14
  53.2 1.2 %join_second.1.refs_2_ = bf16[16,248,256]{2,1,0:T(8,128)(2,1)} custom-call(bf16[16,160,256]{2,1,0:T(8,128)(2,1)S(1)} %get-tuple-element.56.refs_15_.refs_0_, bf16[16,160,256]{2,1,0:T(8,128)(2,1)S(1)} %collective-permute-done.15.refs_1_), custom_call_target="tpu_custom_call" | custom-call | bytes 4653056 | tf_op jit(solution)/shard_map/join_second/pallas_call | solution.py:391
  54.5 0.9 collective-permute-done.14.refs_1_
  55.4 1.0 %join_first.1 = bf16[16,248,256]{2,1,0:T(8,128)(2,1)} custom-call(bf16[16,88,256]{2,1,0:T(8,128)(2,1)S(1)} %get-tuple-element.57.refs_0_, bf16[16,88,256]{2,1,0:T(8,128)(2,1)S(1)} %collective-permute-done.14.refs_1_, bf16[16,248,256]{2,1,0:T(8,128)(2,1)} %join_second.1.refs_2_), custom_call_target="tpu_custom_call", output_to_operand_aliasing={{}: (2, {})} | custom-call | bytes 5505024 | tf_op jit(solution)/shard_map/join_first/pallas_call | solution.py:391
  56.4 36.1 %all_to_all.5.refs_0_ = bf16[16,248,256]{2,1,0:T(8,128)(2,1)S(1)} all-to-all(bf16[16,248,256]{2,1,0:T(8,128)(2,1)} %join_first.1), channel_id=1, replica_groups=mesh['dp_0'=4,'dp_1'=4,'dp_2'=2,'section'=4] {'dp_0','dp_1'}, dimensions={0} | all-to-all | bytes 4063232 | tf_op jit(solution)/shard_map/all_to_all | solution.py:586
  92.5 1.0 %total.1 = (f32[5,32,256]{2,1,0:T(8,128)}, f32[5,16,256]{2,1,0:T(8,128)}, f32[2]{0:T(128)}) custom-call(bf16[16,248,256]{2,1,0:T(8,128)(2,1)S(1)} %all_to_all.5.refs_0_), custom_call_target="tpu_custom_call" | custom-call | bytes 2277384 | tf_op jit(solution)/shard_map/total/pallas_call | solution.py:391
  (27 shorter events, 0.2 us)
Async XLA Ops:
  3.7 6.4 %copy-start = (bf16[3,384,512]{2,1,0:T(8,128)(2,1)}, bf16[3,384,512]{2,1,0:T(8,128)(2,1)S(1)}, u32[]{:S(2)}) copy-start(bf16[3,384,512]{2,1,0:T(8,128)(2,1)S(1)} %get-tuple-element.51.refs_13_) | copy-start | bytes 3538948
  3.7 6.4 %copy-start.2 = (bf16[384,256]{1,0:T(8,128)(2,1)}, bf16[384,256]{1,0:T(8,128)(2,1)S(1)}, u32[]{:S(2)}) copy-start(bf16[384,256]{1,0:T(8,128)(2,1)S(1)} %get-tuple-element.33.refs_1_.refs_3_) | copy-start | bytes 589828
  3.8 9.7 %collective-permute-start = (bf16[384,256]{1,0:T(8,128)(2,1)S(1)}, bf16[384,256]{1,0:T(8,128)(2,1)S(1)}, u32[]{:S(2)}, u32[]{:S(2)}) collective-permute-start(bf16[384,256]{1,0:T(8,128)(2,1)S(1)} %get-tuple-element.33.refs_1_.refs_3_), channel_id=1, source_target_pairs={{0,1},{1,2},{2,3},{3,0},{4,5},{5,6},{6,7},{7,4},{8,9},{9,10},{10,1... | collective-permute-start | bytes 589832 | tf_op jit(solution)/shard_map/ppermute | solution.py:421
  5.4 8.7 %collective-permute-start.1 = (bf16[384,256]{1,0:T(8,128)(2,1)S(1)}, bf16[384,256]{1,0:T(8,128)(2,1)S(1)}, u32[]{:S(2)}, u32[]{:S(2)}) collective-permute-start(bf16[384,256]{1,0:T(8,128)(2,1)S(1)} %get-tuple-element.33.refs_1_.refs_3_), channel_id=1, source_target_pairs={{0,3},{1,0},{2,1},{3,2},{4,7},{5,4},{6,5},{7,6},{8,11},{9,8},{10,9... | collective-permute-start | bytes 589832 | tf_op jit(solution)/shard_map/ppermute | solution.py:421
  10.1 8.4 %collective-permute-start.4 = (bf16[384,256]{1,0:T(8,128)(2,1)}, bf16[384,256]{1,0:T(8,128)(2,1)S(1)}, u32[]{:S(2)}, u32[]{:S(2)}) collective-permute-start(bf16[384,256]{1,0:T(8,128)(2,1)} %get-tuple-element.39.refs_1_.refs_4_), channel_id=1, source_target_pairs={{0,1},{1,2},{2,3},{3,0},{4,5},{5,6},{6,7},{7,4},{8,9},{9,10},{10,1... | collective-permute-start | bytes 589832 | tf_op jit(solution)/shard_map/ppermute | solution.py:421
  10.5 8.0 %collective-permute-start.5 = (bf16[384,256]{1,0:T(8,128)(2,1)}, bf16[384,256]{1,0:T(8,128)(2,1)S(1)}, u32[]{:S(2)}, u32[]{:S(2)}) collective-permute-start(bf16[384,256]{1,0:T(8,128)(2,1)} %get-tuple-element.39.refs_1_.refs_4_), channel_id=1, source_target_pairs={{0,3},{1,0},{2,1},{3,2},{4,7},{5,4},{6,5},{7,6},{8,11},{9,8},{10,9... | collective-permute-start | bytes 589832 | tf_op jit(solution)/shard_map/ppermute | solution.py:421
  14.1 7.8 %collective-permute-start.2 = (bf16[192,256]{1,0:T(8,128)(2,1)}, bf16[192,256]{1,0:T(8,128)(2,1)S(1)}, u32[]{:S(2)}, u32[]{:S(2)}) collective-permute-start(bf16[192,256]{1,0:T(8,128)(2,1)} %slice.16), channel_id=1, source_target_pairs={{0,1},{1,2},{2,3},{3,0},{4,5},{5,6},{6,7},{7,4},{8,9},{9,10},{10,1... | collective-permute-start | bytes 294920 | tf_op jit(solution)/shard_map/ppermute | solution.py:421
  14.7 7.2 %collective-permute-start.3 = (bf16[192,256]{1,0:T(8,128)(2,1)}, bf16[192,256]{1,0:T(8,128)(2,1)}, u32[]{:S(2)}, u32[]{:S(2)}) collective-permute-start(bf16[192,256]{1,0:T(8,128)(2,1)} %slice.17), channel_id=1, source_target_pairs={{0,3},{1,0},{2,1},{3,2},{4,7},{5,4},{6,5},{7,6},{8,11},{9,8},{10,9... | collective-permute-start | bytes 294920 | tf_op jit(solution)/shard_map/ppermute | solution.py:421
  18.5 7.9 %collective-permute-start.6 = (bf16[192,256]{1,0:T(8,128)(2,1)S(1)}, bf16[192,256]{1,0:T(8,128)(2,1)S(1)}, u32[]{:S(2)}, u32[]{:S(2)}) collective-permute-start(bf16[192,256]{1,0:T(8,128)(2,1)S(1)} %slice.18), channel_id=1, source_target_pairs={{0,1},{1,2},{2,3},{3,0},{4,5},{5,6},{6,7},{7,4},{8,9},{9,10},{10,1... | collective-permute-start | bytes 294920 | tf_op jit(solution)/shard_map/ppermute | solution.py:421
  18.6 7.8 %collective-permute-start.7 = (bf16[192,256]{1,0:T(8,128)(2,1)S(1)}, bf16[192,256]{1,0:T(8,128)(2,1)S(1)}, u32[]{:S(2)}, u32[]{:S(2)}) collective-permute-start(bf16[192,256]{1,0:T(8,128)(2,1)S(1)} %slice.19), channel_id=1, source_target_pairs={{0,3},{1,0},{2,1},{3,2},{4,7},{5,4},{6,5},{7,6},{8,11},{9,8},{10,9... | collective-permute-start | bytes 294920 | tf_op jit(solution)/shard_map/ppermute | solution.py:421
  21.9 0.9 copy-start.3
  29.7 8.6 %collective-permute-start.12 = (bf16[392,256]{1,0:T(8,128)(2,1)S(1)}, bf16[392,256]{1,0:T(8,128)(2,1)S(1)}, u32[]{:S(2)}, u32[]{:S(2)}) collective-permute-start(bf16[392,256]{1,0:T(8,128)(2,1)S(1)} %get-tuple-element.50), channel_id=1, source_target_pairs={{0,3},{1,0},{2,1},{3,2},{4,7},{5,4},{6,5},{7,6},{8,11},{9,8},{10,9... | collective-permute-start | bytes 602120 | tf_op jit(solution)/shard_map/ppermute | solution.py:421
  33.0 9.1 %collective-permute-start.8 = (bf16[392,256]{1,0:T(8,128)(2,1)S(1)}, bf16[392,256]{1,0:T(8,128)(2,1)S(1)}, u32[]{:S(2)}, u32[]{:S(2)}) collective-permute-start(bf16[392,256]{1,0:T(8,128)(2,1)S(1)} %get-tuple-element.46), channel_id=1, source_target_pairs={{0,1},{1,2},{2,3},{3,0},{4,5},{5,6},{6,7},{7,4},{8,9},{9,10},{10,1... | collective-permute-start | bytes 602120 | tf_op jit(solution)/shard_map/ppermute | solution.py:421
  33.9 11.6 %collective-permute-start.10 = (bf16[392,256]{1,0:T(8,128)(2,1)S(1)}, bf16[392,256]{1,0:T(8,128)(2,1)S(1)}, u32[]{:S(2)}, u32[]{:S(2)}) collective-permute-start(bf16[392,256]{1,0:T(8,128)(2,1)S(1)} %get-tuple-element.47), channel_id=1, source_target_pairs={{0,1},{1,2},{2,3},{3,0},{4,5},{5,6},{6,7},{7,4},{8,9},{9,10},{10,1... | collective-permute-start | bytes 602120 | tf_op jit(solution)/shard_map/ppermute | solution.py:421
  34.0 11.5 %collective-permute-start.11 = (bf16[392,256]{1,0:T(8,128)(2,1)S(1)}, bf16[392,256]{1,0:T(8,128)(2,1)S(1)}, u32[]{:S(2)}, u32[]{:S(2)}) collective-permute-start(bf16[392,256]{1,0:T(8,128)(2,1)S(1)} %get-tuple-element.48), channel_id=1, source_target_pairs={{0,3},{1,0},{2,1},{3,2},{4,7},{5,4},{6,5},{7,6},{8,11},{9,8},{10,9... | collective-permute-start | bytes 602120 | tf_op jit(solution)/shard_map/ppermute | solution.py:421
  38.3 7.2 %collective-permute-start.13 = (bf16[392,256]{1,0:T(8,128)(2,1)S(1)}, bf16[392,256]{1,0:T(8,128)(2,1)S(1)}, u32[]{:S(2)}, u32[]{:S(2)}) collective-permute-start(bf16[392,256]{1,0:T(8,128)(2,1)S(1)} %relay_b.1.refs_6_), channel_id=1, source_target_pairs={{0,3},{1,0},{2,1},{3,2},{4,7},{5,4},{6,5},{7,6},{8,11},{9,8},{10,9... | collective-permute-start | bytes 602120 | tf_op jit(solution)/shard_map/ppermute | solution.py:421
  42.2 7.2 %collective-permute-start.9 = (bf16[392,256]{1,0:T(8,128)(2,1)S(1)}, bf16[392,256]{1,0:T(8,128)(2,1)S(1)}, u32[]{:S(2)}, u32[]{:S(2)}) collective-permute-start(bf16[392,256]{1,0:T(8,128)(2,1)S(1)} %relay_a.1.refs_5_), channel_id=1, source_target_pairs={{0,1},{1,2},{2,3},{3,0},{4,5},{5,6},{6,7},{7,4},{8,9},{9,10},{10,1... | collective-permute-start | bytes 602120 | tf_op jit(solution)/shard_map/ppermute | solution.py:421
  42.4 6.9 %copy-start.1 = (bf16[3,384,512]{2,1,0:T(8,128)(2,1)S(1)}, bf16[3,384,512]{2,1,0:T(8,128)(2,1)}, u32[]{:S(2)}) copy-start(bf16[3,384,512]{2,1,0:T(8,128)(2,1)} %copy-done) | copy-start | bytes 3538948
  42.4 6.9 %copy-start.4 = (bf16[384,256]{1,0:T(8,128)(2,1)S(1)}, bf16[384,256]{1,0:T(8,128)(2,1)}, u32[]{:S(2)}) copy-start(bf16[384,256]{1,0:T(8,128)(2,1)} %copy-done.2) | copy-start | bytes 589828
  45.4 7.8 %collective-permute-start.15 = (bf16[16,160,256]{2,1,0:T(8,128)(2,1)S(1)}, bf16[16,160,256]{2,1,0:T(8,128)(2,1)S(1)}, u32[]{:S(2)}, u32[]{:S(2)}) collective-permute-start(bf16[16,160,256]{2,1,0:T(8,128)(2,1)S(1)} %get-tuple-element.59), channel_id=1, source_target_pairs={{0,4},{4,0},{1,5},{5,1},{2,6},{6,2},{3,7},{7,3},{8,12},{12,8},{9,1... | collective-permute-start | bytes 3932168 | tf_op jit(solution)/shard_map/ppermute | solution.py:429
  53.1 2.3 %collective-permute-start.14 = (bf16[16,88,256]{2,1,0:T(8,128)(2,1)S(1)}, bf16[16,88,256]{2,1,0:T(8,128)(2,1)S(1)}, u32[]{:S(2)}, u32[]{:S(2)}) collective-permute-start(bf16[16,88,256]{2,1,0:T(8,128)(2,1)S(1)} %get-tuple-element.58), channel_id=1, source_target_pairs={{0,4},{4,0},{1,5},{5,1},{2,6},{6,2},{3,7},{7,3},{8,12},{12,8},{9,1... | collective-permute-start | bytes 2162696 | tf_op jit(solution)/shard_map/ppermute | solution.py:429

commit v10 on v8

--- a/solution.py
+++ b/solution.py
@@ -336,6 +336,10 @@
         x[:, taps * own_rows :, :] = jnp.broadcast_to(lines[None], (groups, 8, width))
 
 
+def same_kernel(a, out):
+    out[...] = a[...]
+
+
 def join_kernel(at, a, b, joint, summed, sems):
     count = sems.shape[0]
     step = a.shape[0] // count
@@ -420,6 +424,10 @@
     return lax.ppermute(x, "section", [(i, (i + step) % count) for i in range(count)])
 
 
+def later(x, after, name):
+    return call(same_kernel, (x,), [like(x.shape)], after=after, name=name)[0]
+
+
 def added(a, b, name, after=()):
     return call(add_kernel, (a, b), [like(a.shape)], after=after, name=name)[0]
 
@@ -474,7 +482,7 @@
     )
     far_a = turn(prev_a, 1)
     following_b = turn(h_b, -1)
-    prev_b = turn(h_b, 1)
+    prev_b = turn(later(h_b, (following_a,), "ordered"), 1)
     far_b = turn(following_b, -1)
 
     second_outs = [like((rows, width_all)), like((rows, taps * width)), like((rows + 8, width)),

time: 90.2 us -> 89.4 us (level)
    pallas_call x12 -> x13, Pallas kernels: 22.6 us -> 22.7 us  [call(): pl.pallas_call(body, out_shape=[pltpu.HBM(x.shape, x.dtype) if at in hbm_...]
  transfers between devices with their start and end apart: 14 -> 14, of which waited for: 7 -> 6; matrix products, arithmetic and copies ran while one was open for 0% -> 0% of each run, Pallas kernels for 16% -> 16%
where the time goes in v10:
time: 89.4 us; the launch traced here: 89.1 us
  blocking collectives  36.1 us (40%)
  Pallas kernels  22.7 us (25%)
  starting transfers between devices  19.1 us (21%)
  waiting for transfers between devices  10.2 us (11%)
  between operations  0.98 us (1%)
    all_to_all x1, blocking collectives, shards(): blocks = lax.all_to_all(joint, ZY, 0, 0)  36.1 us
    pallas_call x13, Pallas kernels, call(): pl.pallas_call(body, out_shape=[pltpu.HBM(x.shape, x.dtype) if at in hbm_...  22.7 us
    ppermute x12, starting transfers between devices, turn(): lax.ppermute(x, 'section', [(i, (i + step) % count) for i in range(count)])  18.9 us
    ppermute x12, waiting for transfers between devices, turn(): lax.ppermute(x, 'section', [(i, (i + step) % count) for i in range(count)])  9.25 us
  transfers between devices with their start and end apart: 14, of which 6 were waited for; matrix products, arithmetic and copies ran while one was open for 0% of the time, Pallas kernels for 16%

profile of v10, /device:TPU:0, one launch (start us, length us, event | category | flops | bytes accessed | tf_op | source)
XLA Modules:
  0.0 89.1 jit_solution(8663331047206341675)
XLA Ops:
  0.6 3.1 %first_a.1 = (bf16[384,256]{1,0:T(8,128)(2,1)S(1)}, bf16[3,384,512]{2,1,0:T(8,128)(2,1)S(1)}, f32[8,128]{1,0:T(8,128)S(1)}, bf16[5,512,256]{2,1,0:T(8,128)(2,1)S(1)}, bf16[8,144,512]{2,1,0:T(8,128)(2,1)S(1)}) custom-call(bf16[8,144,512]{2,1,0:T(8,128)(2,1)} %refs_0_.1, bf16[8,144,512]{2,1,0:T(8,128)(2,1)} %refs_1_.1, bf16[5,512,256]{2,1,0:T(8,128)(2,1)} %refs_2_.2), custom_call_target="tpu_custom_call" | custom-call | flops 503316480 | bytes 7540736 | tf_op jit(solution)/shard_map/first_a/pallas_call | solution.py:394
  3.7 1.6 %collective-permute-start = (bf16[384,256]{1,0:T(8,128)(2,1)S(1)}, bf16[384,256]{1,0:T(8,128)(2,1)}, u32[]{:S(2)}, u32[]{:S(2)}) collective-permute-start(bf16[384,256]{1,0:T(8,128)(2,1)S(1)} %get-tuple-element.33.refs_1_.refs_3_), channel_id=1, source_target_pairs={{0,1},{1,2},{2,3},{3,0},{4,5},{5,6},{6,7},{7,4},{8,9},{9,10},{10,1... | collective-permute-start | bytes 589832 | tf_op jit(solution)/shard_map/ppermute | solution.py:424
  5.4 1.7 %collective-permute-start.1 = (bf16[384,256]{1,0:T(8,128)(2,1)S(1)}, bf16[384,256]{1,0:T(8,128)(2,1)S(1)}, u32[]{:S(2)}, u32[]{:S(2)}) collective-permute-start(bf16[384,256]{1,0:T(8,128)(2,1)S(1)} %get-tuple-element.33.refs_1_.refs_3_), channel_id=1, source_target_pairs={{0,3},{1,0},{2,1},{3,2},{4,7},{5,4},{6,5},{7,6},{8,11},{9,8},{10,9... | collective-permute-start | bytes 589832 | tf_op jit(solution)/shard_map/ppermute | solution.py:424
  7.1 2.5 %first_b.1 = (bf16[384,256]{1,0:T(8,128)(2,1)S(1)}, bf16[3,384,512]{2,1,0:T(8,128)(2,1)}, f32[8,128]{1,0:T(8,128)S(1)}, bf16[5,1024,256]{2,1,0:T(8,128)(2,1)S(1)}) custom-call(bf16[8,144,512]{2,1,0:T(8,128)(2,1)S(1)} %get-tuple-element.34.refs_0_, bf16[5,512,256]{2,1,0:T(8,128)(2,1)S(1)} %get-tuple-element.35.refs_1_, bf16[5,1024,256]{2,1,0:T(8,128)(2,1)} %refs_2_.3), custom_call_target="tpu_custom_call" | custom-call | flops 503316480 | bytes 9113600 | tf_op jit(solution)/shard_map/first_b/pallas_call | solution.py:394
  9.6 1.7 %collective-permute-start.4 = (bf16[384,256]{1,0:T(8,128)(2,1)S(1)}, bf16[384,256]{1,0:T(8,128)(2,1)}, u32[]{:S(2)}, u32[]{:S(2)}) collective-permute-start(bf16[384,256]{1,0:T(8,128)(2,1)S(1)} %get-tuple-element.39.refs_0_.refs_1_.refs_4_), channel_id=1, source_target_pairs={{0,3},{1,0},{2,1},{3,2},{4,7},{5,4},{6,5},{7,6},{8,11},{9,8},{10,9... | collective-permute-start | bytes 589832 | tf_op jit(solution)/shard_map/ppermute | solution.py:424
  11.3 0.4 collective-permute-done.refs_2_
  11.7 0.5 collective-permute-start.2
  12.1 0.0 collective-permute-done.1.refs_3_.refs_1_
  12.2 2.5 %collective-permute-start.3 = (bf16[384,256]{1,0:T(8,128)(2,1)S(1)}, bf16[384,256]{1,0:T(8,128)(2,1)}, u32[]{:S(2)}, u32[]{:S(2)}) collective-permute-start(bf16[384,256]{1,0:T(8,128)(2,1)S(1)} %ordered.1), channel_id=1, source_target_pairs={{0,1},{1,2},{2,3},{3,0},{4,5},{5,6},{6,7},{7,4},{8,9},{9,10},{10,1... | collective-permute-start | bytes 589832 | tf_op jit(solution)/shard_map/ppermute | solution.py:424
  14.7 1.4 %collective-permute-done.4.refs_3_ = bf16[384,256]{1,0:T(8,128)(2,1)} collective-permute-done((bf16[384,256]{1,0:T(8,128)(2,1)S(1)}, bf16[384,256]{1,0:T(8,128)(2,1)}, u32[]{:S(2)}, u32[]{:S(2)}) %collective-permute-start.4) | collective-permute-done | bytes 196640 | tf_op jit(solution)/shard_map/ppermute | solution.py:424
  16.1 2.8 %collective-permute-start.5 = (bf16[384,256]{1,0:T(8,128)(2,1)}, bf16[384,256]{1,0:T(8,128)(2,1)}, u32[]{:S(2)}, u32[]{:S(2)}) collective-permute-start(bf16[384,256]{1,0:T(8,128)(2,1)} %collective-permute-done.4.refs_3_), channel_id=1, source_target_pairs={{0,3},{1,0},{2,1},{3,2},{4,7},{5,4},{6,5},{7,6},{8,11},{9,8},{10,9... | collective-permute-start | bytes 589832 | tf_op jit(solution)/shard_map/ppermute | solution.py:424
  18.9 2.0 %collective-permute-done.2.refs_4_ = bf16[384,256]{1,0:T(8,128)(2,1)} collective-permute-done((bf16[384,256]{1,0:T(8,128)(2,1)}, bf16[384,256]{1,0:T(8,128)(2,1)}, u32[]{:S(2)}, u32[]{:S(2)}) %collective-permute-start.2) | collective-permute-done | bytes 196640 | tf_op jit(solution)/shard_map/ppermute | solution.py:424
  20.9 3.7 %second_a.1 = (bf16[384,1024]{1,0:T(8,128)(2,1)S(1)}, bf16[384,1280]{1,0:T(8,128)(2,1)S(1)}, bf16[392,256]{1,0:T(8,128)(2,1)S(1)}, bf16[8,256]{1,0:T(8,128)(2,1)...) custom-call(s32[1]{0:T(128)} %bitcast.1.refs_0_, ...), custom_call_target="tpu_custom_call" | custom-call | flops 1258291200 | bytes 5984260 | tf_op jit(solution)/shard_map/second_a/pallas_call | solution.py:394
  24.6 3.4 %second_b.1 = (bf16[384,1024]{1,0:T(8,128)(2,1)S(1)}, bf16[384,1280]{1,0:T(8,128)(2,1)S(1)}, bf16[392,256]{1,0:T(8,128)(2,1)S(1)}, bf16[8,256]{1,0:T(8,128)(2,1)S(1)}) custom-call(s32[1]{0:T(128)} %bitcast.1.refs_0_, bf16[384,256]{1,0:T(8,128)(2,1)S(1)} %get-tuple-element.39.refs_0_.refs_1_.refs_4_, bf16[384,256]{1,0:T(8,128)(2,1)} %collective-permute-done.3.refs_2_, ...), custom_call_target="tpu_custom_call" | custom-call | flops 1258291200 | bytes 5386244 | tf_op jit(solution)/shard_map/second_b/pallas_call | solution.py:394
  28.1 1.5 %collective-permute-start.10 = (bf16[392,256]{1,0:T(8,128)(2,1)S(1)}, bf16[392,256]{1,0:T(8,128)(2,1)S(1)}, u32[]{:S(2)}, u32[]{:S(2)}) collective-permute-start(bf16[392,256]{1,0:T(8,128)(2,1)S(1)} %get-tuple-element.50), channel_id=1, source_target_pairs={{0,3},{1,0},{2,1},{3,2},{4,7},{5,4},{6,5},{7,6},{8,11},{9,8},{10,9... | collective-permute-start | bytes 602120 | tf_op jit(solution)/shard_map/ppermute | solution.py:424
  29.6 0.6 collective-permute-start.6
  30.2 1.0 %back_b.1 = (bf16[392,256]{1,0:T(8,128)(2,1)S(1)}, bf16[392,256]{1,0:T(8,128)(2,1)S(1)}, bf16[384,256]{1,0:T(8,128)(2,1)S(1)}) custom-call(s32[1]{0:T(128)} %bitcast.1.refs_0_, bf16[384,1280]{1,0:T(8,128)(2,1)S(1)} %get-tuple-element.43.refs_1_.refs_4_, bf16[5,1024,256]{2,1,0:T(8,128)(2,1)S(1)} %get-tuple-element.36.refs_5_.refs_2_, ...), custom_call_target="tpu_custom_call" | custom-call | flops 3019898880 | bytes 16826384 | tf_op jit(solution)/shard_map/back_b/pallas_call | solution.py:394
  31.2 0.1 collective-permute-start.8
  31.3 3.2 %collective-permute-start.9 = (bf16[392,256]{1,0:T(8,128)(2,1)S(1)}, bf16[392,256]{1,0:T(8,128)(2,1)S(1)}, u32[]{:S(2)}, u32[]{:S(2)}) collective-permute-start(bf16[392,256]{1,0:T(8,128)(2,1)S(1)} %get-tuple-element.48), channel_id=1, source_target_pairs={{0,3},{1,0},{2,1},{3,2},{4,7},{5,4},{6,5},{7,6},{8,11},{9,8},{10,9... | collective-permute-start | bytes 602120 | tf_op jit(solution)/shard_map/ppermute | solution.py:424
  34.5 1.6 %collective-permute-done.10.refs_1_.refs_12_ = bf16[392,256]{1,0:T(8,128)(2,1)S(1)} collective-permute-done((bf16[392,256]{1,0:T(8,128)(2,1)S(1)}, bf16[392,256]{1,0:T(8,128)(2,1)S(1)}, u32[]{:S(2)}, u32[]{:S(2)}) %collective-permute-start.10) | collective-permute-done | bytes 200736 | tf_op jit(solution)/shard_map/ppermute | solution.py:424
  36.1 2.4 %collective-permute-start.11 = (bf16[392,256]{1,0:T(8,128)(2,1)S(1)}, bf16[392,256]{1,0:T(8,128)(2,1)S(1)}, u32[]{:S(2)}, u32[]{:S(2)}) collective-permute-start(bf16[392,256]{1,0:T(8,128)(2,1)S(1)} %relay_b.1.refs_6_), channel_id=1, source_target_pairs={{0,3},{1,0},{2,1},{3,2},{4,7},{5,4},{6,5},{7,6},{8,11},{9,8},{10,9... | collective-permute-start | bytes 602120 | tf_op jit(solution)/shard_map/ppermute | solution.py:424
  38.6 0.3 collective-permute-start.7
  38.9 3.0 %weight_second.1 = (bf16[16,160,256]{2,1,0:T(8,128)(2,1)S(1)}, bf16[16,160,256]{2,1,0:T(8,128)(2,1)S(1)}) custom-call(s32[1]{0:T(128)} %bitcast.refs_0_, bf16[384,1024]{1,0:T(8,128)(2,1)S(1)} %get-tuple-element.53.refs_1_, bf16[384,1024]{1,0:T(8,128)(2,1)S(1)} %get-tuple-element.54.refs_2_, bf16[384,1280]{1,0:T(8,128)(2,1)S(1)} %get-tuple-element.55.refs_3_, ...), custom_call_target="tpu_custom_call" | custom-call | flops 8053063680 | bytes 24641552 | tf_op jit(solution)/shard_map/weight_second/pallas_call | solution.py:394
  41.8 0.1 collective-permute-start.13
  42.0 3.8 %collective-permute-done.7.refs_7_ = bf16[392,256]{1,0:T(8,128)(2,1)S(1)} collective-permute-done((bf16[392,256]{1,0:T(8,128)(2,1)S(1)}, bf16[392,256]{1,0:T(8,128)(2,1)S(1)}, u32[]{:S(2)}, u32[]{:S(2)}) %collective-permute-start.7) | collective-permute-done | bytes 200736 | tf_op jit(solution)/shard_map/ppermute | solution.py:424
  45.8 2.9 %weight_first.1 = (bf16[16,88,256]{2,1,0:T(8,128)(2,1)S(1)}, bf16[16,88,256]{2,1,0:T(8,128)(2,1)S(1)}) custom-call(s32[1]{0:T(128)} %bitcast.refs_0_, bf16[8,256]{1,0:T(8,128)(2,1)S(1)} %get-tuple-element.38.refs_1_, bf16[8,256]{1,0:T(8,128)(2,1)S(1)} %get-tuple-element.42.refs_3_.refs_2_, bf16[384,256]{1,0:T(8,128)(2,1)S(1)} %get-tuple-element.33.refs_1_.refs_3_, ...), custom_call_target="tpu_custom_call" | custom-call | flops 20132659200 | bytes 115998800 | tf_op jit(solution)/shard_map/weight_first/pallas_call | solution.py:394
  48.6 0.1 collective-permute-start.12
  48.7 1.2 %join_second.1.refs_2_ = bf16[16,248,256]{2,1,0:T(8,128)(2,1)} custom-call(bf16[16,160,256]{2,1,0:T(8,128)(2,1)S(1)} %get-tuple-element.56.refs_15_.refs_0_, bf16[16,160,256]{2,1,0:T(8,128)(2,1)S(1)} %collective-permute-done.13.refs_1_), custom_call_target="tpu_custom_call" | custom-call | bytes 4653056 | tf_op jit(solution)/shard_map/join_second/pallas_call | solution.py:394
  49.9 1.0 %collective-permute-done.12.refs_1_ = bf16[16,88,256]{2,1,0:T(8,128)(2,1)S(1)} collective-permute-done((bf16[16,88,256]{2,1,0:T(8,128)(2,1)S(1)}, bf16[16,88,256]{2,1,0:T(8,128)(2,1)S(1)}, u32[]{:S(2)}, u32[]{:S(2)}) %collective-permute-start.12) | collective-permute-done | bytes 720928 | tf_op jit(solution)/shard_map/ppermute | solution.py:436
  50.9 0.9 %join_first.1 = bf16[16,248,256]{2,1,0:T(8,128)(2,1)} custom-call(bf16[16,88,256]{2,1,0:T(8,128)(2,1)S(1)} %get-tuple-element.57.refs_0_, bf16[16,88,256]{2,1,0:T(8,128)(2,1)S(1)} %collective-permute-done.12.refs_1_, bf16[16,248,256]{2,1,0:T(8,128)(2,1)} %join_second.1.refs_2_), custom_call_target="tpu_custom_call", output_to_operand_aliasing={{}: (2, {})} | custom-call | bytes 5505024 | tf_op jit(solution)/shard_map/join_first/pallas_call | solution.py:394
  51.8 36.1 %all_to_all.5.refs_0_ = bf16[16,248,256]{2,1,0:T(8,128)(2,1)S(1)} all-to-all(bf16[16,248,256]{2,1,0:T(8,128)(2,1)} %join_first.1), channel_id=1, replica_groups=mesh['dp_0'=4,'dp_1'=4,'dp_2'=2,'section'=4] {'dp_0','dp_1'}, dimensions={0} | all-to-all | bytes 4063232 | tf_op jit(solution)/shard_map/all_to_all | solution.py:593
  88.0 1.0 %total.1 = (f32[5,32,256]{2,1,0:T(8,128)}, f32[5,16,256]{2,1,0:T(8,128)}, f32[2]{0:T(128)}) custom-call(bf16[16,248,256]{2,1,0:T(8,128)(2,1)S(1)} %all_to_all.5.refs_0_), custom_call_target="tpu_custom_call" | custom-call | bytes 2277384 | tf_op jit(solution)/shard_map/total/pallas_call | solution.py:394
  (14 shorter events, 0.1 us)
Async XLA Ops:
  3.7 5.8 %copy-start = (bf16[3,384,512]{2,1,0:T(8,128)(2,1)}, bf16[3,384,512]{2,1,0:T(8,128)(2,1)S(1)}, u32[]{:S(2)}) copy-start(bf16[3,384,512]{2,1,0:T(8,128)(2,1)S(1)} %get-tuple-element.51.refs_13_) | copy-start | bytes 3538948
  3.7 7.9 %collective-permute-start = (bf16[384,256]{1,0:T(8,128)(2,1)S(1)}, bf16[384,256]{1,0:T(8,128)(2,1)}, u32[]{:S(2)}, u32[]{:S(2)}) collective-permute-start(bf16[384,256]{1,0:T(8,128)(2,1)S(1)} %get-tuple-element.33.refs_1_.refs_3_), channel_id=1, source_target_pairs={{0,1},{1,2},{2,3},{3,0},{4,5},{5,6},{6,7},{7,4},{8,9},{9,10},{10,1... | collective-permute-start | bytes 589832 | tf_op jit(solution)/shard_map/ppermute | solution.py:424
  5.4 6.8 %collective-permute-start.1 = (bf16[384,256]{1,0:T(8,128)(2,1)S(1)}, bf16[384,256]{1,0:T(8,128)(2,1)S(1)}, u32[]{:S(2)}, u32[]{:S(2)}) collective-permute-start(bf16[384,256]{1,0:T(8,128)(2,1)S(1)} %get-tuple-element.33.refs_1_.refs_3_), channel_id=1, source_target_pairs={{0,3},{1,0},{2,1},{3,2},{4,7},{5,4},{6,5},{7,6},{8,11},{9,8},{10,9... | collective-permute-start | bytes 589832 | tf_op jit(solution)/shard_map/ppermute | solution.py:424
  9.6 6.5 %collective-permute-start.4 = (bf16[384,256]{1,0:T(8,128)(2,1)S(1)}, bf16[384,256]{1,0:T(8,128)(2,1)}, u32[]{:S(2)}, u32[]{:S(2)}) collective-permute-start(bf16[384,256]{1,0:T(8,128)(2,1)S(1)} %get-tuple-element.39.refs_0_.refs_1_.refs_4_), channel_id=1, source_target_pairs={{0,3},{1,0},{2,1},{3,2},{4,7},{5,4},{6,5},{7,6},{8,11},{9,8},{10,9... | collective-permute-start | bytes 589832 | tf_op jit(solution)/shard_map/ppermute | solution.py:424
  11.7 9.3 %collective-permute-start.2 = (bf16[384,256]{1,0:T(8,128)(2,1)}, bf16[384,256]{1,0:T(8,128)(2,1)}, u32[]{:S(2)}, u32[]{:S(2)}) collective-permute-start(bf16[384,256]{1,0:T(8,128)(2,1)} %collective-permute-done.refs_2_), channel_id=1, source_target_pairs={{0,1},{1,2},{2,3},{3,0},{4,5},{5,6},{6,7},{7,4},{8,9},{9,10},{10,1... | collective-permute-start | bytes 589832 | tf_op jit(solution)/shard_map/ppermute | solution.py:424
  12.2 12.5 %collective-permute-start.3 = (bf16[384,256]{1,0:T(8,128)(2,1)S(1)}, bf16[384,256]{1,0:T(8,128)(2,1)}, u32[]{:S(2)}, u32[]{:S(2)}) collective-permute-start(bf16[384,256]{1,0:T(8,128)(2,1)S(1)} %ordered.1), channel_id=1, source_target_pairs={{0,1},{1,2},{2,3},{3,0},{4,5},{5,6},{6,7},{7,4},{8,9},{9,10},{10,1... | collective-permute-start | bytes 589832 | tf_op jit(solution)/shard_map/ppermute | solution.py:424
  16.1 8.6 %collective-permute-start.5 = (bf16[384,256]{1,0:T(8,128)(2,1)}, bf16[384,256]{1,0:T(8,128)(2,1)}, u32[]{:S(2)}, u32[]{:S(2)}) collective-permute-start(bf16[384,256]{1,0:T(8,128)(2,1)} %collective-permute-done.4.refs_3_), channel_id=1, source_target_pairs={{0,3},{1,0},{2,1},{3,2},{4,7},{5,4},{6,5},{7,6},{8,11},{9,8},{10,9... | collective-permute-start | bytes 589832 | tf_op jit(solution)/shard_map/ppermute | solution.py:424
  28.1 8.0 %collective-permute-start.10 = (bf16[392,256]{1,0:T(8,128)(2,1)S(1)}, bf16[392,256]{1,0:T(8,128)(2,1)S(1)}, u32[]{:S(2)}, u32[]{:S(2)}) collective-permute-start(bf16[392,256]{1,0:T(8,128)(2,1)S(1)} %get-tuple-element.50), channel_id=1, source_target_pairs={{0,3},{1,0},{2,1},{3,2},{4,7},{5,4},{6,5},{7,6},{8,11},{9,8},{10,9... | collective-permute-start | bytes 602120 | tf_op jit(solution)/shard_map/ppermute | solution.py:424
  29.6 8.9 %collective-permute-start.6 = (bf16[392,256]{1,0:T(8,128)(2,1)S(1)}, bf16[392,256]{1,0:T(8,128)(2,1)S(1)}, u32[]{:S(2)}, u32[]{:S(2)}) collective-permute-start(bf16[392,256]{1,0:T(8,128)(2,1)S(1)} %get-tuple-element.46), channel_id=1, source_target_pairs={{0,1},{1,2},{2,3},{3,0},{4,5},{5,6},{6,7},{7,4},{8,9},{9,10},{10,1... | collective-permute-start | bytes 602120 | tf_op jit(solution)/shard_map/ppermute | solution.py:424
  31.2 10.8 %collective-permute-start.8 = (bf16[392,256]{1,0:T(8,128)(2,1)S(1)}, bf16[392,256]{1,0:T(8,128)(2,1)S(1)}, u32[]{:S(2)}, u32[]{:S(2)}) collective-permute-start(bf16[392,256]{1,0:T(8,128)(2,1)S(1)} %get-tuple-element.47), channel_id=1, source_target_pairs={{0,1},{1,2},{2,3},{3,0},{4,5},{5,6},{6,7},{7,4},{8,9},{9,10},{10,1... | collective-permute-start | bytes 602120 | tf_op jit(solution)/shard_map/ppermute | solution.py:424
  31.3 10.7 %collective-permute-start.9 = (bf16[392,256]{1,0:T(8,128)(2,1)S(1)}, bf16[392,256]{1,0:T(8,128)(2,1)S(1)}, u32[]{:S(2)}, u32[]{:S(2)}) collective-permute-start(bf16[392,256]{1,0:T(8,128)(2,1)S(1)} %get-tuple-element.48), channel_id=1, source_target_pairs={{0,3},{1,0},{2,1},{3,2},{4,7},{5,4},{6,5},{7,6},{8,11},{9,8},{10,9... | collective-permute-start | bytes 602120 | tf_op jit(solution)/shard_map/ppermute | solution.py:424
  36.1 5.8 %collective-permute-start.11 = (bf16[392,256]{1,0:T(8,128)(2,1)S(1)}, bf16[392,256]{1,0:T(8,128)(2,1)S(1)}, u32[]{:S(2)}, u32[]{:S(2)}) collective-permute-start(bf16[392,256]{1,0:T(8,128)(2,1)S(1)} %relay_b.1.refs_6_), channel_id=1, source_target_pairs={{0,3},{1,0},{2,1},{3,2},{4,7},{5,4},{6,5},{7,6},{8,11},{9,8},{10,9... | collective-permute-start | bytes 602120 | tf_op jit(solution)/shard_map/ppermute | solution.py:424
  38.6 7.2 %collective-permute-start.7 = (bf16[392,256]{1,0:T(8,128)(2,1)S(1)}, bf16[392,256]{1,0:T(8,128)(2,1)S(1)}, u32[]{:S(2)}, u32[]{:S(2)}) collective-permute-start(bf16[392,256]{1,0:T(8,128)(2,1)S(1)} %relay_a.1.refs_5_), channel_id=1, source_target_pairs={{0,1},{1,2},{2,3},{3,0},{4,5},{5,6},{6,7},{7,4},{8,9},{9,10},{10,1... | collective-permute-start | bytes 602120 | tf_op jit(solution)/shard_map/ppermute | solution.py:424
  38.9 6.9 %copy-start.1 = (bf16[3,384,512]{2,1,0:T(8,128)(2,1)S(1)}, bf16[3,384,512]{2,1,0:T(8,128)(2,1)}, u32[]{:S(2)}) copy-start(bf16[3,384,512]{2,1,0:T(8,128)(2,1)} %copy-done) | copy-start | bytes 3538948
  41.8 6.9 %collective-permute-start.13 = (bf16[16,160,256]{2,1,0:T(8,128)(2,1)S(1)}, bf16[16,160,256]{2,1,0:T(8,128)(2,1)S(1)}, u32[]{:S(2)}, u32[]{:S(2)}) collective-permute-start(bf16[16,160,256]{2,1,0:T(8,128)(2,1)S(1)} %get-tuple-element.59), channel_id=1, source_target_pairs={{0,4},{4,0},{1,5},{5,1},{2,6},{6,2},{3,7},{7,3},{8,12},{12,8},{9,1... | collective-permute-start | bytes 3932168 | tf_op jit(solution)/shard_map/ppermute | solution.py:436
  48.6 2.3 %collective-permute-start.12 = (bf16[16,88,256]{2,1,0:T(8,128)(2,1)S(1)}, bf16[16,88,256]{2,1,0:T(8,128)(2,1)S(1)}, u32[]{:S(2)}, u32[]{:S(2)}) collective-permute-start(bf16[16,88,256]{2,1,0:T(8,128)(2,1)S(1)} %get-tuple-element.58), channel_id=1, source_target_pairs={{0,4},{4,0},{1,5},{5,1},{2,6},{6,2},{3,7},{7,3},{8,12},{12,8},{9,1... | collective-permute-start | bytes 2162696 | tf_op jit(solution)/shard_map/ppermute | solution.py:436

commit v11 on v10

--- a/solution.py
+++ b/solution.py
@@ -147,23 +147,17 @@
 ):
     if near:
         h_all, shifted = all_out, shifted_out
-        *backs, padded, in_sems = rest
+        *backs, padded = rest
     else:
-        *backs, padded, in_sems, h_all, shifted, all_sem, shifted_sem = rest
+        *backs, padded, h_all, shifted, all_sem, shifted_sem = rest
     rows, width = own.shape
     half = rows // 2
     taps = w.shape[0]
     frames = padded.shape[1] - 16
     s = s_ref[0]
-    copies = []
     for away, x in enumerate((own, following, far, prev)):
         at = pl.multiple_of(lax.rem(s + away, 4) * width, 256)
-        copies.append(
-            pltpu.make_async_copy(x, h_all.at[:, pl.ds(at, width)], in_sems.at[away])
-        )
-        copies[-1].start()
-    for copy in copies:
-        copy.wait()
+        h_all[:, pl.ds(at, width)] = x[...]
     if not near:
         copy_all = pltpu.make_async_copy(h_all, all_out, all_sem)
         copy_all.start()
@@ -489,7 +483,7 @@
                    like((8, width))]
     back_outs = [like((rows + 8, width)), like((rows + 8, width)), like((rows, width))]
     second_scratch = [
-        pltpu.VMEM((cols, frames + 16, width), F32), dma((4,)),
+        pltpu.VMEM((cols, frames + 16, width), F32),
     ]
     copies = all_far + [dma, dma]
     flops = 2 * rows * taps * (width_all + width) * width
@@ -499,7 +493,6 @@
         second_outs + back_outs,
         second_scratch + copies * (not NEAR_ALL[0]),
         smem=1,
-        loose=(1, 2, 3, 4),
         hbm_outs=() if NEAR_ALL[0] else (0, 1),
         cost=1,
         flops=flops,
@@ -516,7 +509,6 @@
         second_outs,
         second_scratch + copies * (not NEAR_ALL[1]),
         smem=1,
-        loose=(1, 2, 3, 4),
         hbm_outs=() if NEAR_ALL[1] else (0, 1),
         cost=1,
         after=(own_a,),

time: 89.4 us -> 89.4 us (level)
  no operation moved by 1% of the time
where the time goes in v11:
time: 89.4 us; the launch traced here: 89.1 us
  blocking collectives  36.1 us (40%)
  Pallas kernels  22.7 us (25%)
  starting transfers between devices  19.1 us (21%)
  waiting for transfers between devices  10.2 us (11%)
  between operations  0.98 us (1%)
    all_to_all x1, blocking collectives, shards(): blocks = lax.all_to_all(joint, ZY, 0, 0)  36.1 us
    pallas_call x13, Pallas kernels, call(): pl.pallas_call(body, out_shape=[pltpu.HBM(x.shape, x.dtype) if at in hbm_...  22.7 us
    ppermute x12, starting transfers between devices, turn(): lax.ppermute(x, 'section', [(i, (i + step) % count) for i in range(count)])  18.9 us
    ppermute x12, waiting for transfers between devices, turn(): lax.ppermute(x, 'section', [(i, (i + step) % count) for i in range(count)])  9.25 us
  transfers between devices with their start and end apart: 14, of which 6 were waited for; matrix products, arithmetic and copies ran while one was open for 0% of the time, Pallas kernels for 16%

profile of v11, /device:TPU:0, one launch (start us, length us, event | category | flops | bytes accessed | tf_op | source)
XLA Modules:
  0.0 89.1 jit_solution(7337540735002866212)
XLA Ops:
  0.6 3.1 %first_a.1 = (bf16[384,256]{1,0:T(8,128)(2,1)S(1)}, bf16[3,384,512]{2,1,0:T(8,128)(2,1)S(1)}, f32[8,128]{1,0:T(8,128)S(1)}, bf16[5,512,256]{2,1,0:T(8,128)(2,1)S(1)}, bf16[8,144,512]{2,1,0:T(8,128)(2,1)S(1)}) custom-call(bf16[8,144,512]{2,1,0:T(8,128)(2,1)} %refs_0_.1, bf16[8,144,512]{2,1,0:T(8,128)(2,1)} %refs_1_.1, bf16[5,512,256]{2,1,0:T(8,128)(2,1)} %refs_2_.2), custom_call_target="tpu_custom_call" | custom-call | flops 503316480 | bytes 7540736 | tf_op jit(solution)/shard_map/first_a/pallas_call | solution.py:388
  3.7 1.6 %collective-permute-start = (bf16[384,256]{1,0:T(8,128)(2,1)S(1)}, bf16[384,256]{1,0:T(8,128)(2,1)}, u32[]{:S(2)}, u32[]{:S(2)}) collective-permute-start(bf16[384,256]{1,0:T(8,128)(2,1)S(1)} %get-tuple-element.33.refs_1_.refs_3_), channel_id=1, source_target_pairs={{0,1},{1,2},{2,3},{3,0},{4,5},{5,6},{6,7},{7,4},{8,9},{9,10},{10,1... | collective-permute-start | bytes 589832 | tf_op jit(solution)/shard_map/ppermute | solution.py:418
  5.4 1.7 %collective-permute-start.1 = (bf16[384,256]{1,0:T(8,128)(2,1)S(1)}, bf16[384,256]{1,0:T(8,128)(2,1)S(1)}, u32[]{:S(2)}, u32[]{:S(2)}) collective-permute-start(bf16[384,256]{1,0:T(8,128)(2,1)S(1)} %get-tuple-element.33.refs_1_.refs_3_), channel_id=1, source_target_pairs={{0,3},{1,0},{2,1},{3,2},{4,7},{5,4},{6,5},{7,6},{8,11},{9,8},{10,9... | collective-permute-start | bytes 589832 | tf_op jit(solution)/shard_map/ppermute | solution.py:418
  7.1 2.5 %first_b.1 = (bf16[384,256]{1,0:T(8,128)(2,1)S(1)}, bf16[3,384,512]{2,1,0:T(8,128)(2,1)}, f32[8,128]{1,0:T(8,128)S(1)}, bf16[5,1024,256]{2,1,0:T(8,128)(2,1)S(1)}) custom-call(bf16[8,144,512]{2,1,0:T(8,128)(2,1)S(1)} %get-tuple-element.34.refs_0_, bf16[5,512,256]{2,1,0:T(8,128)(2,1)S(1)} %get-tuple-element.35.refs_1_, bf16[5,1024,256]{2,1,0:T(8,128)(2,1)} %refs_2_.3), custom_call_target="tpu_custom_call" | custom-call | flops 503316480 | bytes 9113600 | tf_op jit(solution)/shard_map/first_b/pallas_call | solution.py:388
  9.6 1.7 %collective-permute-start.4 = (bf16[384,256]{1,0:T(8,128)(2,1)S(1)}, bf16[384,256]{1,0:T(8,128)(2,1)}, u32[]{:S(2)}, u32[]{:S(2)}) collective-permute-start(bf16[384,256]{1,0:T(8,128)(2,1)S(1)} %get-tuple-element.39.refs_0_.refs_1_.refs_4_), channel_id=1, source_target_pairs={{0,3},{1,0},{2,1},{3,2},{4,7},{5,4},{6,5},{7,6},{8,11},{9,8},{10,9... | collective-permute-start | bytes 589832 | tf_op jit(solution)/shard_map/ppermute | solution.py:418
  11.3 0.4 collective-permute-done.refs_2_
  11.7 0.5 collective-permute-start.2
  12.1 0.0 collective-permute-done.1.refs_3_.refs_1_
  12.2 2.5 %collective-permute-start.3 = (bf16[384,256]{1,0:T(8,128)(2,1)S(1)}, bf16[384,256]{1,0:T(8,128)(2,1)}, u32[]{:S(2)}, u32[]{:S(2)}) collective-permute-start(bf16[384,256]{1,0:T(8,128)(2,1)S(1)} %ordered.1), channel_id=1, source_target_pairs={{0,1},{1,2},{2,3},{3,0},{4,5},{5,6},{6,7},{7,4},{8,9},{9,10},{10,1... | collective-permute-start | bytes 589832 | tf_op jit(solution)/shard_map/ppermute | solution.py:418
  14.7 1.4 %collective-permute-done.4.refs_3_ = bf16[384,256]{1,0:T(8,128)(2,1)} collective-permute-done((bf16[384,256]{1,0:T(8,128)(2,1)S(1)}, bf16[384,256]{1,0:T(8,128)(2,1)}, u32[]{:S(2)}, u32[]{:S(2)}) %collective-permute-start.4) | collective-permute-done | bytes 196640 | tf_op jit(solution)/shard_map/ppermute | solution.py:418
  16.1 2.8 %collective-permute-start.5 = (bf16[384,256]{1,0:T(8,128)(2,1)}, bf16[384,256]{1,0:T(8,128)(2,1)}, u32[]{:S(2)}, u32[]{:S(2)}) collective-permute-start(bf16[384,256]{1,0:T(8,128)(2,1)} %collective-permute-done.4.refs_3_), channel_id=1, source_target_pairs={{0,3},{1,0},{2,1},{3,2},{4,7},{5,4},{6,5},{7,6},{8,11},{9,8},{10,9... | collective-permute-start | bytes 589832 | tf_op jit(solution)/shard_map/ppermute | solution.py:418
  18.9 2.0 %collective-permute-done.2.refs_4_ = bf16[384,256]{1,0:T(8,128)(2,1)} collective-permute-done((bf16[384,256]{1,0:T(8,128)(2,1)}, bf16[384,256]{1,0:T(8,128)(2,1)}, u32[]{:S(2)}, u32[]{:S(2)}) %collective-permute-start.2) | collective-permute-done | bytes 196640 | tf_op jit(solution)/shard_map/ppermute | solution.py:418
  20.9 3.6 %second_a.1 = (bf16[384,1024]{1,0:T(8,128)(2,1)S(1)}, bf16[384,1280]{1,0:T(8,128)(2,1)S(1)}, bf16[392,256]{1,0:T(8,128)(2,1)S(1)}, bf16[8,256]{1,0:T(8,128)(2,1)...) custom-call(s32[1]{0:T(128)} %bitcast.1.refs_0_, ...), custom_call_target="tpu_custom_call" | custom-call | flops 1258291200 | bytes 5984260 | tf_op jit(solution)/shard_map/second_a/pallas_call | solution.py:388
  24.6 3.4 %second_b.1 = (bf16[384,1024]{1,0:T(8,128)(2,1)S(1)}, bf16[384,1280]{1,0:T(8,128)(2,1)S(1)}, bf16[392,256]{1,0:T(8,128)(2,1)S(1)}, bf16[8,256]{1,0:T(8,128)(2,1)S(1)}) custom-call(s32[1]{0:T(128)} %bitcast.1.refs_0_, bf16[384,256]{1,0:T(8,128)(2,1)S(1)} %get-tuple-element.39.refs_0_.refs_1_.refs_4_, bf16[384,256]{1,0:T(8,128)(2,1)} %collective-permute-done.3.refs_2_, ...), custom_call_target="tpu_custom_call" | custom-call | flops 1258291200 | bytes 5386244 | tf_op jit(solution)/shard_map/second_b/pallas_call | solution.py:388
  28.0 1.6 %collective-permute-start.10 = (bf16[392,256]{1,0:T(8,128)(2,1)S(1)}, bf16[392,256]{1,0:T(8,128)(2,1)S(1)}, u32[]{:S(2)}, u32[]{:S(2)}) collective-permute-start(bf16[392,256]{1,0:T(8,128)(2,1)S(1)} %get-tuple-element.50), channel_id=1, source_target_pairs={{0,3},{1,0},{2,1},{3,2},{4,7},{5,4},{6,5},{7,6},{8,11},{9,8},{10,9... | collective-permute-start | bytes 602120 | tf_op jit(solution)/shard_map/ppermute | solution.py:418
  29.6 0.5 collective-permute-start.6
  30.1 1.0 %back_b.1 = (bf16[392,256]{1,0:T(8,128)(2,1)S(1)}, bf16[392,256]{1,0:T(8,128)(2,1)S(1)}, bf16[384,256]{1,0:T(8,128)(2,1)S(1)}) custom-call(s32[1]{0:T(128)} %bitcast.1.refs_0_, bf16[384,1280]{1,0:T(8,128)(2,1)S(1)} %get-tuple-element.43.refs_1_.refs_4_, bf16[5,1024,256]{2,1,0:T(8,128)(2,1)S(1)} %get-tuple-element.36.refs_5_.refs_2_, ...), custom_call_target="tpu_custom_call" | custom-call | flops 3019898880 | bytes 16826384 | tf_op jit(solution)/shard_map/back_b/pallas_call | solution.py:388
  31.1 0.1 collective-permute-start.8
  31.2 3.2 %collective-permute-start.9 = (bf16[392,256]{1,0:T(8,128)(2,1)S(1)}, bf16[392,256]{1,0:T(8,128)(2,1)S(1)}, u32[]{:S(2)}, u32[]{:S(2)}) collective-permute-start(bf16[392,256]{1,0:T(8,128)(2,1)S(1)} %get-tuple-element.48), channel_id=1, source_target_pairs={{0,3},{1,0},{2,1},{3,2},{4,7},{5,4},{6,5},{7,6},{8,11},{9,8},{10,9... | collective-permute-start | bytes 602120 | tf_op jit(solution)/shard_map/ppermute | solution.py:418
  34.4 1.6 %collective-permute-done.10.refs_1_.refs_12_ = bf16[392,256]{1,0:T(8,128)(2,1)S(1)} collective-permute-done((bf16[392,256]{1,0:T(8,128)(2,1)S(1)}, bf16[392,256]{1,0:T(8,128)(2,1)S(1)}, u32[]{:S(2)}, u32[]{:S(2)}) %collective-permute-start.10) | collective-permute-done | bytes 200736 | tf_op jit(solution)/shard_map/ppermute | solution.py:418
  36.0 2.5 %collective-permute-start.11 = (bf16[392,256]{1,0:T(8,128)(2,1)S(1)}, bf16[392,256]{1,0:T(8,128)(2,1)S(1)}, u32[]{:S(2)}, u32[]{:S(2)}) collective-permute-start(bf16[392,256]{1,0:T(8,128)(2,1)S(1)} %relay_b.1.refs_6_), channel_id=1, source_target_pairs={{0,3},{1,0},{2,1},{3,2},{4,7},{5,4},{6,5},{7,6},{8,11},{9,8},{10,9... | collective-permute-start | bytes 602120 | tf_op jit(solution)/shard_map/ppermute | solution.py:418
  38.6 0.3 collective-permute-start.7
  38.8 3.0 %weight_second.1 = (bf16[16,160,256]{2,1,0:T(8,128)(2,1)S(1)}, bf16[16,160,256]{2,1,0:T(8,128)(2,1)S(1)}) custom-call(s32[1]{0:T(128)} %bitcast.refs_0_, bf16[384,1024]{1,0:T(8,128)(2,1)S(1)} %get-tuple-element.53.refs_1_, bf16[384,1024]{1,0:T(8,128)(2,1)S(1)} %get-tuple-element.54.refs_2_, bf16[384,1280]{1,0:T(8,128)(2,1)S(1)} %get-tuple-element.55.refs_3_, ...), custom_call_target="tpu_custom_call" | custom-call | flops 8053063680 | bytes 24641552 | tf_op jit(solution)/shard_map/weight_second/pallas_call | solution.py:388
  41.8 0.1 collective-permute-start.13
  41.9 3.8 %collective-permute-done.7.refs_7_ = bf16[392,256]{1,0:T(8,128)(2,1)S(1)} collective-permute-done((bf16[392,256]{1,0:T(8,128)(2,1)S(1)}, bf16[392,256]{1,0:T(8,128)(2,1)S(1)}, u32[]{:S(2)}, u32[]{:S(2)}) %collective-permute-start.7) | collective-permute-done | bytes 200736 | tf_op jit(solution)/shard_map/ppermute | solution.py:418
  45.7 2.9 %weight_first.1 = (bf16[16,88,256]{2,1,0:T(8,128)(2,1)S(1)}, bf16[16,88,256]{2,1,0:T(8,128)(2,1)S(1)}) custom-call(s32[1]{0:T(128)} %bitcast.refs_0_, bf16[8,256]{1,0:T(8,128)(2,1)S(1)} %get-tuple-element.38.refs_1_, bf16[8,256]{1,0:T(8,128)(2,1)S(1)} %get-tuple-element.42.refs_3_.refs_2_, bf16[384,256]{1,0:T(8,128)(2,1)S(1)} %get-tuple-element.33.refs_1_.refs_3_, ...), custom_call_target="tpu_custom_call" | custom-call | flops 20132659200 | bytes 115998800 | tf_op jit(solution)/shard_map/weight_first/pallas_call | solution.py:388
  48.6 0.1 collective-permute-start.12
  48.7 1.2 %join_second.1.refs_2_ = bf16[16,248,256]{2,1,0:T(8,128)(2,1)} custom-call(bf16[16,160,256]{2,1,0:T(8,128)(2,1)S(1)} %get-tuple-element.56.refs_15_.refs_0_, bf16[16,160,256]{2,1,0:T(8,128)(2,1)S(1)} %collective-permute-done.13.refs_1_), custom_call_target="tpu_custom_call" | custom-call | bytes 4653056 | tf_op jit(solution)/shard_map/join_second/pallas_call | solution.py:388
  49.9 1.0 %collective-permute-done.12.refs_1_ = bf16[16,88,256]{2,1,0:T(8,128)(2,1)S(1)} collective-permute-done((bf16[16,88,256]{2,1,0:T(8,128)(2,1)S(1)}, bf16[16,88,256]{2,1,0:T(8,128)(2,1)S(1)}, u32[]{:S(2)}, u32[]{:S(2)}) %collective-permute-start.12) | collective-permute-done | bytes 720928 | tf_op jit(solution)/shard_map/ppermute | solution.py:430
  50.9 0.9 %join_first.1 = bf16[16,248,256]{2,1,0:T(8,128)(2,1)} custom-call(bf16[16,88,256]{2,1,0:T(8,128)(2,1)S(1)} %get-tuple-element.57.refs_0_, bf16[16,88,256]{2,1,0:T(8,128)(2,1)S(1)} %collective-permute-done.12.refs_1_, bf16[16,248,256]{2,1,0:T(8,128)(2,1)} %join_second.1.refs_2_), custom_call_target="tpu_custom_call", output_to_operand_aliasing={{}: (2, {})} | custom-call | bytes 5505024 | tf_op jit(solution)/shard_map/join_first/pallas_call | solution.py:388
  51.8 36.1 %all_to_all.5.refs_0_ = bf16[16,248,256]{2,1,0:T(8,128)(2,1)S(1)} all-to-all(bf16[16,248,256]{2,1,0:T(8,128)(2,1)} %join_first.1), channel_id=1, replica_groups=mesh['dp_0'=4,'dp_1'=4,'dp_2'=2,'section'=4] {'dp_0','dp_1'}, dimensions={0} | all-to-all | bytes 4063232 | tf_op jit(solution)/shard_map/all_to_all | solution.py:585
  88.0 1.0 %total.1 = (f32[5,32,256]{2,1,0:T(8,128)}, f32[5,16,256]{2,1,0:T(8,128)}, f32[2]{0:T(128)}) custom-call(bf16[16,248,256]{2,1,0:T(8,128)(2,1)S(1)} %all_to_all.5.refs_0_), custom_call_target="tpu_custom_call" | custom-call | bytes 2277384 | tf_op jit(solution)/shard_map/total/pallas_call | solution.py:388
  (14 shorter events, 0.1 us)
Async XLA Ops:
  3.7 5.8 %copy-start = (bf16[3,384,512]{2,1,0:T(8,128)(2,1)}, bf16[3,384,512]{2,1,0:T(8,128)(2,1)S(1)}, u32[]{:S(2)}) copy-start(bf16[3,384,512]{2,1,0:T(8,128)(2,1)S(1)} %get-tuple-element.51.refs_13_) | copy-start | bytes 3538948
  3.7 7.9 %collective-permute-start = (bf16[384,256]{1,0:T(8,128)(2,1)S(1)}, bf16[384,256]{1,0:T(8,128)(2,1)}, u32[]{:S(2)}, u32[]{:S(2)}) collective-permute-start(bf16[384,256]{1,0:T(8,128)(2,1)S(1)} %get-tuple-element.33.refs_1_.refs_3_), channel_id=1, source_target_pairs={{0,1},{1,2},{2,3},{3,0},{4,5},{5,6},{6,7},{7,4},{8,9},{9,10},{10,1... | collective-permute-start | bytes 589832 | tf_op jit(solution)/shard_map/ppermute | solution.py:418
  5.4 6.8 %collective-permute-start.1 = (bf16[384,256]{1,0:T(8,128)(2,1)S(1)}, bf16[384,256]{1,0:T(8,128)(2,1)S(1)}, u32[]{:S(2)}, u32[]{:S(2)}) collective-permute-start(bf16[384,256]{1,0:T(8,128)(2,1)S(1)} %get-tuple-element.33.refs_1_.refs_3_), channel_id=1, source_target_pairs={{0,3},{1,0},{2,1},{3,2},{4,7},{5,4},{6,5},{7,6},{8,11},{9,8},{10,9... | collective-permute-start | bytes 589832 | tf_op jit(solution)/shard_map/ppermute | solution.py:418
  9.6 6.5 %collective-permute-start.4 = (bf16[384,256]{1,0:T(8,128)(2,1)S(1)}, bf16[384,256]{1,0:T(8,128)(2,1)}, u32[]{:S(2)}, u32[]{:S(2)}) collective-permute-start(bf16[384,256]{1,0:T(8,128)(2,1)S(1)} %get-tuple-element.39.refs_0_.refs_1_.refs_4_), channel_id=1, source_target_pairs={{0,3},{1,0},{2,1},{3,2},{4,7},{5,4},{6,5},{7,6},{8,11},{9,8},{10,9... | collective-permute-start | bytes 589832 | tf_op jit(solution)/shard_map/ppermute | solution.py:418
  11.7 9.3 %collective-permute-start.2 = (bf16[384,256]{1,0:T(8,128)(2,1)}, bf16[384,256]{1,0:T(8,128)(2,1)}, u32[]{:S(2)}, u32[]{:S(2)}) collective-permute-start(bf16[384,256]{1,0:T(8,128)(2,1)} %collective-permute-done.refs_2_), channel_id=1, source_target_pairs={{0,1},{1,2},{2,3},{3,0},{4,5},{5,6},{6,7},{7,4},{8,9},{9,10},{10,1... | collective-permute-start | bytes 589832 | tf_op jit(solution)/shard_map/ppermute | solution.py:418
  12.2 12.4 %collective-permute-start.3 = (bf16[384,256]{1,0:T(8,128)(2,1)S(1)}, bf16[384,256]{1,0:T(8,128)(2,1)}, u32[]{:S(2)}, u32[]{:S(2)}) collective-permute-start(bf16[384,256]{1,0:T(8,128)(2,1)S(1)} %ordered.1), channel_id=1, source_target_pairs={{0,1},{1,2},{2,3},{3,0},{4,5},{5,6},{6,7},{7,4},{8,9},{9,10},{10,1... | collective-permute-start | bytes 589832 | tf_op jit(solution)/shard_map/ppermute | solution.py:418
  16.1 8.5 %collective-permute-start.5 = (bf16[384,256]{1,0:T(8,128)(2,1)}, bf16[384,256]{1,0:T(8,128)(2,1)}, u32[]{:S(2)}, u32[]{:S(2)}) collective-permute-start(bf16[384,256]{1,0:T(8,128)(2,1)} %collective-permute-done.4.refs_3_), channel_id=1, source_target_pairs={{0,3},{1,0},{2,1},{3,2},{4,7},{5,4},{6,5},{7,6},{8,11},{9,8},{10,9... | collective-permute-start | bytes 589832 | tf_op jit(solution)/shard_map/ppermute | solution.py:418
  28.0 8.0 %collective-permute-start.10 = (bf16[392,256]{1,0:T(8,128)(2,1)S(1)}, bf16[392,256]{1,0:T(8,128)(2,1)S(1)}, u32[]{:S(2)}, u32[]{:S(2)}) collective-permute-start(bf16[392,256]{1,0:T(8,128)(2,1)S(1)} %get-tuple-element.50), channel_id=1, source_target_pairs={{0,3},{1,0},{2,1},{3,2},{4,7},{5,4},{6,5},{7,6},{8,11},{9,8},{10,9... | collective-permute-start | bytes 602120 | tf_op jit(solution)/shard_map/ppermute | solution.py:418
  29.6 8.9 %collective-permute-start.6 = (bf16[392,256]{1,0:T(8,128)(2,1)S(1)}, bf16[392,256]{1,0:T(8,128)(2,1)S(1)}, u32[]{:S(2)}, u32[]{:S(2)}) collective-permute-start(bf16[392,256]{1,0:T(8,128)(2,1)S(1)} %get-tuple-element.46), channel_id=1, source_target_pairs={{0,1},{1,2},{2,3},{3,0},{4,5},{5,6},{6,7},{7,4},{8,9},{9,10},{10,1... | collective-permute-start | bytes 602120 | tf_op jit(solution)/shard_map/ppermute | solution.py:418
  31.1 10.8 %collective-permute-start.8 = (bf16[392,256]{1,0:T(8,128)(2,1)S(1)}, bf16[392,256]{1,0:T(8,128)(2,1)S(1)}, u32[]{:S(2)}, u32[]{:S(2)}) collective-permute-start(bf16[392,256]{1,0:T(8,128)(2,1)S(1)} %get-tuple-element.47), channel_id=1, source_target_pairs={{0,1},{1,2},{2,3},{3,0},{4,5},{5,6},{6,7},{7,4},{8,9},{9,10},{10,1... | collective-permute-start | bytes 602120 | tf_op jit(solution)/shard_map/ppermute | solution.py:418
  31.2 10.7 %collective-permute-start.9 = (bf16[392,256]{1,0:T(8,128)(2,1)S(1)}, bf16[392,256]{1,0:T(8,128)(2,1)S(1)}, u32[]{:S(2)}, u32[]{:S(2)}) collective-permute-start(bf16[392,256]{1,0:T(8,128)(2,1)S(1)} %get-tuple-element.48), channel_id=1, source_target_pairs={{0,3},{1,0},{2,1},{3,2},{4,7},{5,4},{6,5},{7,6},{8,11},{9,8},{10,9... | collective-permute-start | bytes 602120 | tf_op jit(solution)/shard_map/ppermute | solution.py:418
  36.0 5.9 %collective-permute-start.11 = (bf16[392,256]{1,0:T(8,128)(2,1)S(1)}, bf16[392,256]{1,0:T(8,128)(2,1)S(1)}, u32[]{:S(2)}, u32[]{:S(2)}) collective-permute-start(bf16[392,256]{1,0:T(8,128)(2,1)S(1)} %relay_b.1.refs_6_), channel_id=1, source_target_pairs={{0,3},{1,0},{2,1},{3,2},{4,7},{5,4},{6,5},{7,6},{8,11},{9,8},{10,9... | collective-permute-start | bytes 602120 | tf_op jit(solution)/shard_map/ppermute | solution.py:418
  38.6 7.2 %collective-permute-start.7 = (bf16[392,256]{1,0:T(8,128)(2,1)S(1)}, bf16[392,256]{1,0:T(8,128)(2,1)S(1)}, u32[]{:S(2)}, u32[]{:S(2)}) collective-permute-start(bf16[392,256]{1,0:T(8,128)(2,1)S(1)} %relay_a.1.refs_5_), channel_id=1, source_target_pairs={{0,1},{1,2},{2,3},{3,0},{4,5},{5,6},{6,7},{7,4},{8,9},{9,10},{10,1... | collective-permute-start | bytes 602120 | tf_op jit(solution)/shard_map/ppermute | solution.py:418
  38.8 6.9 %copy-start.1 = (bf16[3,384,512]{2,1,0:T(8,128)(2,1)S(1)}, bf16[3,384,512]{2,1,0:T(8,128)(2,1)}, u32[]{:S(2)}) copy-start(bf16[3,384,512]{2,1,0:T(8,128)(2,1)} %copy-done) | copy-start | bytes 3538948
  41.8 6.9 %collective-permute-start.13 = (bf16[16,160,256]{2,1,0:T(8,128)(2,1)S(1)}, bf16[16,160,256]{2,1,0:T(8,128)(2,1)S(1)}, u32[]{:S(2)}, u32[]{:S(2)}) collective-permute-start(bf16[16,160,256]{2,1,0:T(8,128)(2,1)S(1)} %get-tuple-element.59), channel_id=1, source_target_pairs={{0,4},{4,0},{1,5},{5,1},{2,6},{6,2},{3,7},{7,3},{8,12},{12,8},{9,1... | collective-permute-start | bytes 3932168 | tf_op jit(solution)/shard_map/ppermute | solution.py:430
  48.6 2.3 %collective-permute-start.12 = (bf16[16,88,256]{2,1,0:T(8,128)(2,1)S(1)}, bf16[16,88,256]{2,1,0:T(8,128)(2,1)S(1)}, u32[]{:S(2)}, u32[]{:S(2)}) collective-permute-start(bf16[16,88,256]{2,1,0:T(8,128)(2,1)S(1)} %get-tuple-element.58), channel_id=1, source_target_pairs={{0,4},{4,0},{1,5},{5,1},{2,6},{6,2},{3,7},{7,3},{8,12},{12,8},{9,1... | collective-permute-start | bytes 2162696 | tf_op jit(solution)/shard_map/ppermute | solution.py:430

commit v12 on v10

--- a/solution.py
+++ b/solution.py
@@ -507,7 +507,7 @@
     )
     pass_a = turn(far_t, 1)
     from_following_a = turn(prev_t, -1)
-    relayed_a = added(next_t, pass_a, "relay_a")
+    relayed_a = added(next_t, pass_a, "relay_a", after=(from_following_a,))
     from_prev_a = turn(relayed_a, 1)
 
     all_b, shifted_b, far_t, loss_b = call(

time: 89.4 us -> 90 us (level)
  transfers between devices with their start and end apart: 14 -> 14, of which waited for: 6 -> 8; matrix products, arithmetic and copies ran while one was open for 0% -> 0% of each run, Pallas kernels for 16% -> 16%
where the time goes in v12:
time: 90 us; the launch traced here: 89.7 us
  blocking collectives  36.3 us (40%)
  Pallas kernels  22.7 us (25%)
  starting transfers between devices  19.8 us (22%)
  waiting for transfers between devices  9.87 us (11%)
  between operations  0.96 us (1%)
    all_to_all x1, blocking collectives, shards(): blocks = lax.all_to_all(joint, ZY, 0, 0)  36.3 us
    pallas_call x13, Pallas kernels, call(): pl.pallas_call(body, out_shape=[pltpu.HBM(x.shape, x.dtype) if at in hbm_...  22.7 us
    ppermute x12, starting transfers between devices, turn(): lax.ppermute(x, 'section', [(i, (i + step) % count) for i in range(count)])  19.7 us
    ppermute x12, waiting for transfers between devices, turn(): lax.ppermute(x, 'section', [(i, (i + step) % count) for i in range(count)])  8.91 us
  transfers between devices with their start and end apart: 14, of which 8 were waited for; matrix products, arithmetic and copies ran while one was open for 0% of the time, Pallas kernels for 16%

profile of v12, /device:TPU:0, one launch (start us, length us, event | category | flops | bytes accessed | tf_op | source)
XLA Modules:
  0.0 89.7 jit_solution(8424420148291598083)
XLA Ops:
  0.6 3.1 %first_a.1 = (bf16[384,256]{1,0:T(8,128)(2,1)S(1)}, bf16[3,384,512]{2,1,0:T(8,128)(2,1)S(1)}, f32[8,128]{1,0:T(8,128)S(1)}, bf16[5,512,256]{2,1,0:T(8,128)(2,1)S(1)}, bf16[8,144,512]{2,1,0:T(8,128)(2,1)S(1)}) custom-call(bf16[8,144,512]{2,1,0:T(8,128)(2,1)} %refs_0_.1, bf16[8,144,512]{2,1,0:T(8,128)(2,1)} %refs_1_.1, bf16[5,512,256]{2,1,0:T(8,128)(2,1)} %refs_2_.2), custom_call_target="tpu_custom_call" | custom-call | flops 503316480 | bytes 7540736 | tf_op jit(solution)/shard_map/first_a/pallas_call | solution.py:394
  3.7 1.6 %collective-permute-start = (bf16[384,256]{1,0:T(8,128)(2,1)S(1)}, bf16[384,256]{1,0:T(8,128)(2,1)}, u32[]{:S(2)}, u32[]{:S(2)}) collective-permute-start(bf16[384,256]{1,0:T(8,128)(2,1)S(1)} %get-tuple-element.33.refs_1_.refs_3_), channel_id=1, source_target_pairs={{0,1},{1,2},{2,3},{3,0},{4,5},{5,6},{6,7},{7,4},{8,9},{9,10},{10,1... | collective-permute-start | bytes 589832 | tf_op jit(solution)/shard_map/ppermute | solution.py:424
  5.4 1.7 %collective-permute-start.1 = (bf16[384,256]{1,0:T(8,128)(2,1)S(1)}, bf16[384,256]{1,0:T(8,128)(2,1)S(1)}, u32[]{:S(2)}, u32[]{:S(2)}) collective-permute-start(bf16[384,256]{1,0:T(8,128)(2,1)S(1)} %get-tuple-element.33.refs_1_.refs_3_), channel_id=1, source_target_pairs={{0,3},{1,0},{2,1},{3,2},{4,7},{5,4},{6,5},{7,6},{8,11},{9,8},{10,9... | collective-permute-start | bytes 589832 | tf_op jit(solution)/shard_map/ppermute | solution.py:424
  7.1 2.5 %first_b.1 = (bf16[384,256]{1,0:T(8,128)(2,1)S(1)}, bf16[3,384,512]{2,1,0:T(8,128)(2,1)}, f32[8,128]{1,0:T(8,128)S(1)}, bf16[5,1024,256]{2,1,0:T(8,128)(2,1)S(1)}) custom-call(bf16[8,144,512]{2,1,0:T(8,128)(2,1)S(1)} %get-tuple-element.34.refs_0_, bf16[5,512,256]{2,1,0:T(8,128)(2,1)S(1)} %get-tuple-element.35.refs_1_, bf16[5,1024,256]{2,1,0:T(8,128)(2,1)} %refs_2_.3), custom_call_target="tpu_custom_call" | custom-call | flops 503316480 | bytes 9113600 | tf_op jit(solution)/shard_map/first_b/pallas_call | solution.py:394
  9.6 1.7 %collective-permute-start.4 = (bf16[384,256]{1,0:T(8,128)(2,1)S(1)}, bf16[384,256]{1,0:T(8,128)(2,1)}, u32[]{:S(2)}, u32[]{:S(2)}) collective-permute-start(bf16[384,256]{1,0:T(8,128)(2,1)S(1)} %get-tuple-element.39.refs_0_.refs_1_.refs_4_), channel_id=1, source_target_pairs={{0,3},{1,0},{2,1},{3,2},{4,7},{5,4},{6,5},{7,6},{8,11},{9,8},{10,9... | collective-permute-start | bytes 589832 | tf_op jit(solution)/shard_map/ppermute | solution.py:424
  11.3 0.4 collective-permute-done.refs_2_
  11.7 0.5 collective-permute-start.2
  12.2 2.5 %collective-permute-start.3 = (bf16[384,256]{1,0:T(8,128)(2,1)S(1)}, bf16[384,256]{1,0:T(8,128)(2,1)}, u32[]{:S(2)}, u32[]{:S(2)}) collective-permute-start(bf16[384,256]{1,0:T(8,128)(2,1)S(1)} %ordered.1), channel_id=1, source_target_pairs={{0,1},{1,2},{2,3},{3,0},{4,5},{5,6},{6,7},{7,4},{8,9},{9,10},{10,1... | collective-permute-start | bytes 589832 | tf_op jit(solution)/shard_map/ppermute | solution.py:424
  14.7 1.4 %collective-permute-done.4.refs_3_ = bf16[384,256]{1,0:T(8,128)(2,1)} collective-permute-done((bf16[384,256]{1,0:T(8,128)(2,1)S(1)}, bf16[384,256]{1,0:T(8,128)(2,1)}, u32[]{:S(2)}, u32[]{:S(2)}) %collective-permute-start.4) | collective-permute-done | bytes 196640 | tf_op jit(solution)/shard_map/ppermute | solution.py:424
  16.1 2.8 %collective-permute-start.5 = (bf16[384,256]{1,0:T(8,128)(2,1)}, bf16[384,256]{1,0:T(8,128)(2,1)}, u32[]{:S(2)}, u32[]{:S(2)}) collective-permute-start(bf16[384,256]{1,0:T(8,128)(2,1)} %collective-permute-done.4.refs_3_), channel_id=1, source_target_pairs={{0,3},{1,0},{2,1},{3,2},{4,7},{5,4},{6,5},{7,6},{8,11},{9,8},{10,9... | collective-permute-start | bytes 589832 | tf_op jit(solution)/shard_map/ppermute | solution.py:424
  18.9 2.0 %collective-permute-done.2.refs_4_ = bf16[384,256]{1,0:T(8,128)(2,1)} collective-permute-done((bf16[384,256]{1,0:T(8,128)(2,1)}, bf16[384,256]{1,0:T(8,128)(2,1)}, u32[]{:S(2)}, u32[]{:S(2)}) %collective-permute-start.2) | collective-permute-done | bytes 196640 | tf_op jit(solution)/shard_map/ppermute | solution.py:424
  20.9 3.7 %second_a.1 = (bf16[384,1024]{1,0:T(8,128)(2,1)S(1)}, bf16[384,1280]{1,0:T(8,128)(2,1)S(1)}, bf16[392,256]{1,0:T(8,128)(2,1)S(1)}, bf16[8,256]{1,0:T(8,128)(2,1)...) custom-call(s32[1]{0:T(128)} %bitcast.1.refs_0_, ...), custom_call_target="tpu_custom_call" | custom-call | flops 1258291200 | bytes 5984260 | tf_op jit(solution)/shard_map/second_a/pallas_call | solution.py:394
  24.6 3.4 %second_b.1 = (bf16[384,1024]{1,0:T(8,128)(2,1)S(1)}, bf16[384,1280]{1,0:T(8,128)(2,1)S(1)}, bf16[392,256]{1,0:T(8,128)(2,1)S(1)}, bf16[8,256]{1,0:T(8,128)(2,1)S(1)}) custom-call(s32[1]{0:T(128)} %bitcast.1.refs_0_, bf16[384,256]{1,0:T(8,128)(2,1)S(1)} %get-tuple-element.39.refs_0_.refs_1_.refs_4_, bf16[384,256]{1,0:T(8,128)(2,1)} %collective-permute-done.3.refs_2_, ...), custom_call_target="tpu_custom_call" | custom-call | flops 1258291200 | bytes 5386244 | tf_op jit(solution)/shard_map/second_b/pallas_call | solution.py:394
  28.1 1.5 %collective-permute-start.10 = (bf16[392,256]{1,0:T(8,128)(2,1)S(1)}, bf16[392,256]{1,0:T(8,128)(2,1)S(1)}, u32[]{:S(2)}, u32[]{:S(2)}) collective-permute-start(bf16[392,256]{1,0:T(8,128)(2,1)S(1)} %get-tuple-element.50), channel_id=1, source_target_pairs={{0,3},{1,0},{2,1},{3,2},{4,7},{5,4},{6,5},{7,6},{8,11},{9,8},{10,9... | collective-permute-start | bytes 602120 | tf_op jit(solution)/shard_map/ppermute | solution.py:424
  29.6 0.6 collective-permute-start.6
  30.2 2.7 %collective-permute-start.7 = (bf16[392,256]{1,0:T(8,128)(2,1)S(1)}, bf16[392,256]{1,0:T(8,128)(2,1)S(1)}, u32[]{:S(2)}, u32[]{:S(2)}) collective-permute-start(bf16[392,256]{1,0:T(8,128)(2,1)S(1)} %get-tuple-element.47), channel_id=1, source_target_pairs={{0,3},{1,0},{2,1},{3,2},{4,7},{5,4},{6,5},{7,6},{8,11},{9,8},{10,9... | collective-permute-start | bytes 602120 | tf_op jit(solution)/shard_map/ppermute | solution.py:424
  32.9 1.0 %back_b.1 = (bf16[392,256]{1,0:T(8,128)(2,1)S(1)}, bf16[392,256]{1,0:T(8,128)(2,1)S(1)}, bf16[384,256]{1,0:T(8,128)(2,1)S(1)}) custom-call(s32[1]{0:T(128)} %bitcast.1.refs_0_, bf16[384,1280]{1,0:T(8,128)(2,1)S(1)} %get-tuple-element.43.refs_1_.refs_4_, bf16[5,1024,256]{2,1,0:T(8,128)(2,1)S(1)} %get-tuple-element.36.refs_5_.refs_2_, ...), custom_call_target="tpu_custom_call" | custom-call | flops 3019898880 | bytes 16826384 | tf_op jit(solution)/shard_map/back_b/pallas_call | solution.py:394
  33.9 0.6 collective-permute-done.10.refs_1_.refs_12_
  34.6 3.8 %collective-permute-start.11 = (bf16[392,256]{1,0:T(8,128)(2,1)S(1)}, bf16[392,256]{1,0:T(8,128)(2,1)S(1)}, u32[]{:S(2)}, u32[]{:S(2)}) collective-permute-start(bf16[392,256]{1,0:T(8,128)(2,1)S(1)} %relay_b.1.refs_6_), channel_id=1, source_target_pairs={{0,3},{1,0},{2,1},{3,2},{4,7},{5,4},{6,5},{7,6},{8,11},{9,8},{10,9... | collective-permute-start | bytes 602120 | tf_op jit(solution)/shard_map/ppermute | solution.py:424
  38.4 0.3 collective-permute-done.6.refs_1_.refs_11_
  38.8 0.3 collective-permute-start.8
  39.0 2.9 %weight_second.1 = (bf16[16,160,256]{2,1,0:T(8,128)(2,1)S(1)}, bf16[16,160,256]{2,1,0:T(8,128)(2,1)S(1)}) custom-call(s32[1]{0:T(128)} %bitcast.refs_0_, bf16[384,1024]{1,0:T(8,128)(2,1)S(1)} %get-tuple-element.53.refs_1_, bf16[384,1024]{1,0:T(8,128)(2,1)S(1)} %get-tuple-element.54.refs_2_, bf16[384,1280]{1,0:T(8,128)(2,1)S(1)} %get-tuple-element.55.refs_3_, ...), custom_call_target="tpu_custom_call" | custom-call | flops 8053063680 | bytes 24641552 | tf_op jit(solution)/shard_map/weight_second/pallas_call | solution.py:394
  42.0 0.1 collective-permute-start.13
  42.1 0.9 collective-permute-done.9.refs_8_
  42.9 3.2 %collective-permute-done.8.refs_7_ = bf16[392,256]{1,0:T(8,128)(2,1)S(1)} collective-permute-done((bf16[392,256]{1,0:T(8,128)(2,1)S(1)}, bf16[392,256]{1,0:T(8,128)(2,1)S(1)}, u32[]{:S(2)}, u32[]{:S(2)}) %collective-permute-start.8) | collective-permute-done | bytes 200736 | tf_op jit(solution)/shard_map/ppermute | solution.py:424
  46.2 2.9 %weight_first.1 = (bf16[16,88,256]{2,1,0:T(8,128)(2,1)S(1)}, bf16[16,88,256]{2,1,0:T(8,128)(2,1)S(1)}) custom-call(s32[1]{0:T(128)} %bitcast.refs_0_, bf16[8,256]{1,0:T(8,128)(2,1)S(1)} %get-tuple-element.38.refs_1_, bf16[8,256]{1,0:T(8,128)(2,1)S(1)} %get-tuple-element.42.refs_3_.refs_2_, bf16[384,256]{1,0:T(8,128)(2,1)S(1)} %get-tuple-element.33.refs_1_.refs_3_, ...), custom_call_target="tpu_custom_call" | custom-call | flops 20132659200 | bytes 115998800 | tf_op jit(solution)/shard_map/weight_first/pallas_call | solution.py:394
  49.0 0.1 collective-permute-start.12
  49.1 1.2 %join_second.1.refs_2_ = bf16[16,248,256]{2,1,0:T(8,128)(2,1)} custom-call(bf16[16,160,256]{2,1,0:T(8,128)(2,1)S(1)} %get-tuple-element.56.refs_15_.refs_0_, bf16[16,160,256]{2,1,0:T(8,128)(2,1)S(1)} %collective-permute-done.13.refs_1_), custom_call_target="tpu_custom_call" | custom-call | bytes 4653056 | tf_op jit(solution)/shard_map/join_second/pallas_call | solution.py:394
  50.3 1.0 %collective-permute-done.12.refs_1_ = bf16[16,88,256]{2,1,0:T(8,128)(2,1)S(1)} collective-permute-done((bf16[16,88,256]{2,1,0:T(8,128)(2,1)S(1)}, bf16[16,88,256]{2,1,0:T(8,128)(2,1)S(1)}, u32[]{:S(2)}, u32[]{:S(2)}) %collective-permute-start.12) | collective-permute-done | bytes 720928 | tf_op jit(solution)/shard_map/ppermute | solution.py:436
  51.3 0.9 %join_first.1 = bf16[16,248,256]{2,1,0:T(8,128)(2,1)} custom-call(bf16[16,88,256]{2,1,0:T(8,128)(2,1)S(1)} %get-tuple-element.57.refs_0_, bf16[16,88,256]{2,1,0:T(8,128)(2,1)S(1)} %collective-permute-done.12.refs_1_, bf16[16,248,256]{2,1,0:T(8,128)(2,1)} %join_second.1.refs_2_), custom_call_target="tpu_custom_call", output_to_operand_aliasing={{}: (2, {})} | custom-call | bytes 5505024 | tf_op jit(solution)/shard_map/join_first/pallas_call | solution.py:394
  52.2 36.3 %all_to_all.5.refs_0_ = bf16[16,248,256]{2,1,0:T(8,128)(2,1)S(1)} all-to-all(bf16[16,248,256]{2,1,0:T(8,128)(2,1)} %join_first.1), channel_id=1, replica_groups=mesh['dp_0'=4,'dp_1'=4,'dp_2'=2,'section'=4] {'dp_0','dp_1'}, dimensions={0} | all-to-all | bytes 4063232 | tf_op jit(solution)/shard_map/all_to_all | solution.py:593
  88.5 1.0 %total.1 = (f32[5,32,256]{2,1,0:T(8,128)}, f32[5,16,256]{2,1,0:T(8,128)}, f32[2]{0:T(128)}) custom-call(bf16[16,248,256]{2,1,0:T(8,128)(2,1)S(1)} %all_to_all.5.refs_0_), custom_call_target="tpu_custom_call" | custom-call | bytes 2277384 | tf_op jit(solution)/shard_map/total/pallas_call | solution.py:394
  (14 shorter events, 0.2 us)
Async XLA Ops:
  3.7 5.8 %copy-start = (bf16[3,384,512]{2,1,0:T(8,128)(2,1)}, bf16[3,384,512]{2,1,0:T(8,128)(2,1)S(1)}, u32[]{:S(2)}) copy-start(bf16[3,384,512]{2,1,0:T(8,128)(2,1)S(1)} %get-tuple-element.51.refs_13_) | copy-start | bytes 3538948
  3.7 7.9 %collective-permute-start = (bf16[384,256]{1,0:T(8,128)(2,1)S(1)}, bf16[384,256]{1,0:T(8,128)(2,1)}, u32[]{:S(2)}, u32[]{:S(2)}) collective-permute-start(bf16[384,256]{1,0:T(8,128)(2,1)S(1)} %get-tuple-element.33.refs_1_.refs_3_), channel_id=1, source_target_pairs={{0,1},{1,2},{2,3},{3,0},{4,5},{5,6},{6,7},{7,4},{8,9},{9,10},{10,1... | collective-permute-start | bytes 589832 | tf_op jit(solution)/shard_map/ppermute | solution.py:424
  5.4 6.8 %collective-permute-start.1 = (bf16[384,256]{1,0:T(8,128)(2,1)S(1)}, bf16[384,256]{1,0:T(8,128)(2,1)S(1)}, u32[]{:S(2)}, u32[]{:S(2)}) collective-permute-start(bf16[384,256]{1,0:T(8,128)(2,1)S(1)} %get-tuple-element.33.refs_1_.refs_3_), channel_id=1, source_target_pairs={{0,3},{1,0},{2,1},{3,2},{4,7},{5,4},{6,5},{7,6},{8,11},{9,8},{10,9... | collective-permute-start | bytes 589832 | tf_op jit(solution)/shard_map/ppermute | solution.py:424
  9.6 6.5 %collective-permute-start.4 = (bf16[384,256]{1,0:T(8,128)(2,1)S(1)}, bf16[384,256]{1,0:T(8,128)(2,1)}, u32[]{:S(2)}, u32[]{:S(2)}) collective-permute-start(bf16[384,256]{1,0:T(8,128)(2,1)S(1)} %get-tuple-element.39.refs_0_.refs_1_.refs_4_), channel_id=1, source_target_pairs={{0,3},{1,0},{2,1},{3,2},{4,7},{5,4},{6,5},{7,6},{8,11},{9,8},{10,9... | collective-permute-start | bytes 589832 | tf_op jit(solution)/shard_map/ppermute | solution.py:424
  11.7 9.3 %collective-permute-start.2 = (bf16[384,256]{1,0:T(8,128)(2,1)}, bf16[384,256]{1,0:T(8,128)(2,1)}, u32[]{:S(2)}, u32[]{:S(2)}) collective-permute-start(bf16[384,256]{1,0:T(8,128)(2,1)} %collective-permute-done.refs_2_), channel_id=1, source_target_pairs={{0,1},{1,2},{2,3},{3,0},{4,5},{5,6},{6,7},{7,4},{8,9},{9,10},{10,1... | collective-permute-start | bytes 589832 | tf_op jit(solution)/shard_map/ppermute | solution.py:424
  12.2 12.5 %collective-permute-start.3 = (bf16[384,256]{1,0:T(8,128)(2,1)S(1)}, bf16[384,256]{1,0:T(8,128)(2,1)}, u32[]{:S(2)}, u32[]{:S(2)}) collective-permute-start(bf16[384,256]{1,0:T(8,128)(2,1)S(1)} %ordered.1), channel_id=1, source_target_pairs={{0,1},{1,2},{2,3},{3,0},{4,5},{5,6},{6,7},{7,4},{8,9},{9,10},{10,1... | collective-permute-start | bytes 589832 | tf_op jit(solution)/shard_map/ppermute | solution.py:424
  16.1 8.6 %collective-permute-start.5 = (bf16[384,256]{1,0:T(8,128)(2,1)}, bf16[384,256]{1,0:T(8,128)(2,1)}, u32[]{:S(2)}, u32[]{:S(2)}) collective-permute-start(bf16[384,256]{1,0:T(8,128)(2,1)} %collective-permute-done.4.refs_3_), channel_id=1, source_target_pairs={{0,3},{1,0},{2,1},{3,2},{4,7},{5,4},{6,5},{7,6},{8,11},{9,8},{10,9... | collective-permute-start | bytes 589832 | tf_op jit(solution)/shard_map/ppermute | solution.py:424
  28.1 6.5 %collective-permute-start.10 = (bf16[392,256]{1,0:T(8,128)(2,1)S(1)}, bf16[392,256]{1,0:T(8,128)(2,1)S(1)}, u32[]{:S(2)}, u32[]{:S(2)}) collective-permute-start(bf16[392,256]{1,0:T(8,128)(2,1)S(1)} %get-tuple-element.50), channel_id=1, source_target_pairs={{0,3},{1,0},{2,1},{3,2},{4,7},{5,4},{6,5},{7,6},{8,11},{9,8},{10,9... | collective-permute-start | bytes 602120 | tf_op jit(solution)/shard_map/ppermute | solution.py:424
  29.6 9.1 %collective-permute-start.6 = (bf16[392,256]{1,0:T(8,128)(2,1)S(1)}, bf16[392,256]{1,0:T(8,128)(2,1)S(1)}, u32[]{:S(2)}, u32[]{:S(2)}) collective-permute-start(bf16[392,256]{1,0:T(8,128)(2,1)S(1)} %get-tuple-element.46), channel_id=1, source_target_pairs={{0,1},{1,2},{2,3},{3,0},{4,5},{5,6},{6,7},{7,4},{8,9},{9,10},{10,1... | collective-permute-start | bytes 602120 | tf_op jit(solution)/shard_map/ppermute | solution.py:424
  30.2 8.5 %collective-permute-start.7 = (bf16[392,256]{1,0:T(8,128)(2,1)S(1)}, bf16[392,256]{1,0:T(8,128)(2,1)S(1)}, u32[]{:S(2)}, u32[]{:S(2)}) collective-permute-start(bf16[392,256]{1,0:T(8,128)(2,1)S(1)} %get-tuple-element.47), channel_id=1, source_target_pairs={{0,3},{1,0},{2,1},{3,2},{4,7},{5,4},{6,5},{7,6},{8,11},{9,8},{10,9... | collective-permute-start | bytes 602120 | tf_op jit(solution)/shard_map/ppermute | solution.py:424
  33.8 9.1 %collective-permute-start.9 = (bf16[392,256]{1,0:T(8,128)(2,1)S(1)}, bf16[392,256]{1,0:T(8,128)(2,1)S(1)}, u32[]{:S(2)}, u32[]{:S(2)}) collective-permute-start(bf16[392,256]{1,0:T(8,128)(2,1)S(1)} %get-tuple-element.48), channel_id=1, source_target_pairs={{0,1},{1,2},{2,3},{3,0},{4,5},{5,6},{6,7},{7,4},{8,9},{9,10},{10,1... | collective-permute-start | bytes 602120 | tf_op jit(solution)/shard_map/ppermute | solution.py:424
  34.6 8.3 %collective-permute-start.11 = (bf16[392,256]{1,0:T(8,128)(2,1)S(1)}, bf16[392,256]{1,0:T(8,128)(2,1)S(1)}, u32[]{:S(2)}, u32[]{:S(2)}) collective-permute-start(bf16[392,256]{1,0:T(8,128)(2,1)S(1)} %relay_b.1.refs_6_), channel_id=1, source_target_pairs={{0,3},{1,0},{2,1},{3,2},{4,7},{5,4},{6,5},{7,6},{8,11},{9,8},{10,9... | collective-permute-start | bytes 602120 | tf_op jit(solution)/shard_map/ppermute | solution.py:424
  38.8 7.4 %collective-permute-start.8 = (bf16[392,256]{1,0:T(8,128)(2,1)S(1)}, bf16[392,256]{1,0:T(8,128)(2,1)S(1)}, u32[]{:S(2)}, u32[]{:S(2)}) collective-permute-start(bf16[392,256]{1,0:T(8,128)(2,1)S(1)} %relay_a.1.refs_5_), channel_id=1, source_target_pairs={{0,1},{1,2},{2,3},{3,0},{4,5},{5,6},{6,7},{7,4},{8,9},{9,10},{10,1... | collective-permute-start | bytes 602120 | tf_op jit(solution)/shard_map/ppermute | solution.py:424
  39.0 7.1 %copy-start.1 = (bf16[3,384,512]{2,1,0:T(8,128)(2,1)S(1)}, bf16[3,384,512]{2,1,0:T(8,128)(2,1)}, u32[]{:S(2)}) copy-start(bf16[3,384,512]{2,1,0:T(8,128)(2,1)} %copy-done) | copy-start | bytes 3538948
  42.0 7.1 %collective-permute-start.13 = (bf16[16,160,256]{2,1,0:T(8,128)(2,1)S(1)}, bf16[16,160,256]{2,1,0:T(8,128)(2,1)S(1)}, u32[]{:S(2)}, u32[]{:S(2)}) collective-permute-start(bf16[16,160,256]{2,1,0:T(8,128)(2,1)S(1)} %get-tuple-element.59), channel_id=1, source_target_pairs={{0,4},{4,0},{1,5},{5,1},{2,6},{6,2},{3,7},{7,3},{8,12},{12,8},{9,1... | collective-permute-start | bytes 3932168 | tf_op jit(solution)/shard_map/ppermute | solution.py:436
  49.0 2.3 %collective-permute-start.12 = (bf16[16,88,256]{2,1,0:T(8,128)(2,1)S(1)}, bf16[16,88,256]{2,1,0:T(8,128)(2,1)S(1)}, u32[]{:S(2)}, u32[]{:S(2)}) collective-permute-start(bf16[16,88,256]{2,1,0:T(8,128)(2,1)S(1)} %get-tuple-element.58), channel_id=1, source_target_pairs={{0,4},{4,0},{1,5},{5,1},{2,6},{6,2},{3,7},{7,3},{8,12},{12,8},{9,1... | collective-permute-start | bytes 2162696 | tf_op jit(solution)/shard_map/ppermute | solution.py:436

commit v13 on v10

--- a/solution.py
+++ b/solution.py
@@ -519,7 +519,7 @@
         loose=(1, 2, 3, 4),
         hbm_outs=() if NEAR_ALL[1] else (0, 1),
         cost=1,
-        after=(own_a,),
+        after=(loss_a,),
         flops=flops,
         name="second_b",
     )
@@ -536,7 +536,7 @@
         name="back_b",
     )
     from_prev_b = turn(next_t, 1)
-    relayed_b = added(prev_t, pass_b, "relay_b")
+    relayed_b = added(prev_t, pass_b, "relay_b", after=(from_following_a,))
     from_following_b = turn(relayed_b, -1)
 
     own_rows = width_all // replicas

time: 89.4 us -> 90.7 us (1.015)
  waiting for transfers between devices: 10.2 us -> 12.4 us
  starting transfers between devices: 19.1 us -> 18 us
    ppermute x12, waiting for transfers between devices: 9.25 us -> 11.4 us  [turn(): lax.ppermute(x, 'section', [(i, (i + step) % count) for i in range(count)])]
    ppermute x12, starting transfers between devices: 18.9 us -> 17.9 us  [turn(): lax.ppermute(x, 'section', [(i, (i + step) % count) for i in range(count)])]
  transfers between devices with their start and end apart: 14 -> 14, of which waited for: 6 -> 7; matrix products, arithmetic and copies ran while one was open for 0% -> 0% of each run, Pallas kernels for 16% -> 16%
where the time goes in v13:
time: 90.7 us; the launch traced here: 90.4 us
  blocking collectives  36.3 us (40%)
  Pallas kernels  22.7 us (25%)
  starting transfers between devices  18 us (20%)
  waiting for transfers between devices  12.4 us (14%)
  between operations  0.97 us (1%)
    all_to_all x1, blocking collectives, shards(): blocks = lax.all_to_all(joint, ZY, 0, 0)  36.3 us
    pallas_call x13, Pallas kernels, call(): pl.pallas_call(body, out_shape=[pltpu.HBM(x.shape, x.dtype) if at in hbm_...  22.7 us
    ppermute x12, starting transfers between devices, turn(): lax.ppermute(x, 'section', [(i, (i + step) % count) for i in range(count)])  17.9 us
    ppermute x12, waiting for transfers between devices, turn(): lax.ppermute(x, 'section', [(i, (i + step) % count) for i in range(count)])  11.4 us
  transfers between devices with their start and end apart: 14, of which 7 were waited for; matrix products, arithmetic and copies ran while one was open for 0% of the time, Pallas kernels for 16%

profile of v13, /device:TPU:0, one launch (start us, length us, event | category | flops | bytes accessed | tf_op | source)
XLA Modules:
  0.0 90.4 jit_solution(15999651066544665088)
XLA Ops:
  0.6 3.1 %first_a.1 = (bf16[384,256]{1,0:T(8,128)(2,1)S(1)}, bf16[3,384,512]{2,1,0:T(8,128)(2,1)S(1)}, f32[8,128]{1,0:T(8,128)S(1)}, bf16[5,512,256]{2,1,0:T(8,128)(2,1)S(1)}, bf16[8,144,512]{2,1,0:T(8,128)(2,1)S(1)}) custom-call(bf16[8,144,512]{2,1,0:T(8,128)(2,1)} %refs_0_.1, bf16[8,144,512]{2,1,0:T(8,128)(2,1)} %refs_1_.1, bf16[5,512,256]{2,1,0:T(8,128)(2,1)} %refs_2_.2), custom_call_target="tpu_custom_call" | custom-call | flops 503316480 | bytes 7540736 | tf_op jit(solution)/shard_map/first_a/pallas_call | solution.py:394
  3.7 1.6 %collective-permute-start = (bf16[384,256]{1,0:T(8,128)(2,1)S(1)}, bf16[384,256]{1,0:T(8,128)(2,1)}, u32[]{:S(2)}, u32[]{:S(2)}) collective-permute-start(bf16[384,256]{1,0:T(8,128)(2,1)S(1)} %get-tuple-element.33.refs_1_.refs_3_), channel_id=1, source_target_pairs={{0,1},{1,2},{2,3},{3,0},{4,5},{5,6},{6,7},{7,4},{8,9},{9,10},{10,1... | collective-permute-start | bytes 589832 | tf_op jit(solution)/shard_map/ppermute | solution.py:424
  5.4 1.7 %collective-permute-start.1 = (bf16[384,256]{1,0:T(8,128)(2,1)S(1)}, bf16[384,256]{1,0:T(8,128)(2,1)S(1)}, u32[]{:S(2)}, u32[]{:S(2)}) collective-permute-start(bf16[384,256]{1,0:T(8,128)(2,1)S(1)} %get-tuple-element.33.refs_1_.refs_3_), channel_id=1, source_target_pairs={{0,3},{1,0},{2,1},{3,2},{4,7},{5,4},{6,5},{7,6},{8,11},{9,8},{10,9... | collective-permute-start | bytes 589832 | tf_op jit(solution)/shard_map/ppermute | solution.py:424
  7.1 2.5 %first_b.1 = (bf16[384,256]{1,0:T(8,128)(2,1)S(1)}, bf16[3,384,512]{2,1,0:T(8,128)(2,1)}, f32[8,128]{1,0:T(8,128)S(1)}, bf16[5,1024,256]{2,1,0:T(8,128)(2,1)S(1)}) custom-call(bf16[8,144,512]{2,1,0:T(8,128)(2,1)S(1)} %get-tuple-element.34.refs_0_, bf16[5,512,256]{2,1,0:T(8,128)(2,1)S(1)} %get-tuple-element.35.refs_1_, bf16[5,1024,256]{2,1,0:T(8,128)(2,1)} %refs_2_.3), custom_call_target="tpu_custom_call" | custom-call | flops 503316480 | bytes 9113600 | tf_op jit(solution)/shard_map/first_b/pallas_call | solution.py:394
  9.6 1.7 %collective-permute-start.4 = (bf16[384,256]{1,0:T(8,128)(2,1)S(1)}, bf16[384,256]{1,0:T(8,128)(2,1)}, u32[]{:S(2)}, u32[]{:S(2)}) collective-permute-start(bf16[384,256]{1,0:T(8,128)(2,1)S(1)} %get-tuple-element.39.refs_0_.refs_1_.refs_4_), channel_id=1, source_target_pairs={{0,3},{1,0},{2,1},{3,2},{4,7},{5,4},{6,5},{7,6},{8,11},{9,8},{10,9... | collective-permute-start | bytes 589832 | tf_op jit(solution)/shard_map/ppermute | solution.py:424
  11.3 0.4 collective-permute-done.refs_2_
  11.7 0.5 collective-permute-start.2
  12.2 2.5 %collective-permute-start.3 = (bf16[384,256]{1,0:T(8,128)(2,1)S(1)}, bf16[384,256]{1,0:T(8,128)(2,1)}, u32[]{:S(2)}, u32[]{:S(2)}) collective-permute-start(bf16[384,256]{1,0:T(8,128)(2,1)S(1)} %ordered.1), channel_id=1, source_target_pairs={{0,1},{1,2},{2,3},{3,0},{4,5},{5,6},{6,7},{7,4},{8,9},{9,10},{10,1... | collective-permute-start | bytes 589832 | tf_op jit(solution)/shard_map/ppermute | solution.py:424
  14.7 1.4 %collective-permute-done.4.refs_3_ = bf16[384,256]{1,0:T(8,128)(2,1)} collective-permute-done((bf16[384,256]{1,0:T(8,128)(2,1)S(1)}, bf16[384,256]{1,0:T(8,128)(2,1)}, u32[]{:S(2)}, u32[]{:S(2)}) %collective-permute-start.4) | collective-permute-done | bytes 196640 | tf_op jit(solution)/shard_map/ppermute | solution.py:424
  16.1 2.8 %collective-permute-start.5 = (bf16[384,256]{1,0:T(8,128)(2,1)}, bf16[384,256]{1,0:T(8,128)(2,1)}, u32[]{:S(2)}, u32[]{:S(2)}) collective-permute-start(bf16[384,256]{1,0:T(8,128)(2,1)} %collective-permute-done.4.refs_3_), channel_id=1, source_target_pairs={{0,3},{1,0},{2,1},{3,2},{4,7},{5,4},{6,5},{7,6},{8,11},{9,8},{10,9... | collective-permute-start | bytes 589832 | tf_op jit(solution)/shard_map/ppermute | solution.py:424
  18.9 2.0 %collective-permute-done.2.refs_4_ = bf16[384,256]{1,0:T(8,128)(2,1)} collective-permute-done((bf16[384,256]{1,0:T(8,128)(2,1)}, bf16[384,256]{1,0:T(8,128)(2,1)}, u32[]{:S(2)}, u32[]{:S(2)}) %collective-permute-start.2) | collective-permute-done | bytes 196640 | tf_op jit(solution)/shard_map/ppermute | solution.py:424
  20.9 3.7 %second_a.1 = (bf16[384,1024]{1,0:T(8,128)(2,1)S(1)}, bf16[384,1280]{1,0:T(8,128)(2,1)S(1)}, bf16[392,256]{1,0:T(8,128)(2,1)S(1)}, bf16[8,256]{1,0:T(8,128)(2,1)...) custom-call(s32[1]{0:T(128)} %bitcast.1.refs_0_, ...), custom_call_target="tpu_custom_call" | custom-call | flops 1258291200 | bytes 5984260 | tf_op jit(solution)/shard_map/second_a/pallas_call | solution.py:394
  24.6 3.4 %second_b.1 = (bf16[384,1024]{1,0:T(8,128)(2,1)S(1)}, bf16[384,1280]{1,0:T(8,128)(2,1)S(1)}, bf16[392,256]{1,0:T(8,128)(2,1)S(1)}, bf16[8,256]{1,0:T(8,128)(2,1)S(1)}) custom-call(s32[1]{0:T(128)} %bitcast.1.refs_0_, bf16[384,256]{1,0:T(8,128)(2,1)S(1)} %get-tuple-element.39.refs_0_.refs_1_.refs_4_, bf16[384,256]{1,0:T(8,128)(2,1)} %collective-permute-done.3.refs_2_, ...), custom_call_target="tpu_custom_call" | custom-call | flops 1258291200 | bytes 5386244 | tf_op jit(solution)/shard_map/second_b/pallas_call | solution.py:394
  28.1 1.5 %collective-permute-start.10 = (bf16[392,256]{1,0:T(8,128)(2,1)S(1)}, bf16[392,256]{1,0:T(8,128)(2,1)S(1)}, u32[]{:S(2)}, u32[]{:S(2)}) collective-permute-start(bf16[392,256]{1,0:T(8,128)(2,1)S(1)} %get-tuple-element.50), channel_id=1, source_target_pairs={{0,3},{1,0},{2,1},{3,2},{4,7},{5,4},{6,5},{7,6},{8,11},{9,8},{10,9... | collective-permute-start | bytes 602120 | tf_op jit(solution)/shard_map/ppermute | solution.py:424
  29.6 0.1 collective-permute-start.9
  29.7 1.9 %collective-permute-start.6 = (bf16[392,256]{1,0:T(8,128)(2,1)S(1)}, bf16[392,256]{1,0:T(8,128)(2,1)S(1)}, u32[]{:S(2)}, u32[]{:S(2)}) collective-permute-start(bf16[392,256]{1,0:T(8,128)(2,1)S(1)} %get-tuple-element.46), channel_id=1, source_target_pairs={{0,1},{1,2},{2,3},{3,0},{4,5},{5,6},{6,7},{7,4},{8,9},{9,10},{10,1... | collective-permute-start | bytes 602120 | tf_op jit(solution)/shard_map/ppermute | solution.py:424
  31.7 1.0 %back_b.1 = (bf16[392,256]{1,0:T(8,128)(2,1)S(1)}, bf16[392,256]{1,0:T(8,128)(2,1)S(1)}, bf16[384,256]{1,0:T(8,128)(2,1)S(1)}) custom-call(s32[1]{0:T(128)} %bitcast.1.refs_0_, bf16[384,1280]{1,0:T(8,128)(2,1)S(1)} %get-tuple-element.43.refs_1_.refs_4_, bf16[5,1024,256]{2,1,0:T(8,128)(2,1)S(1)} %get-tuple-element.36.refs_5_.refs_2_, ...), custom_call_target="tpu_custom_call" | custom-call | flops 3019898880 | bytes 16826384 | tf_op jit(solution)/shard_map/back_b/pallas_call | solution.py:394
  32.6 0.6 collective-permute-start.8
  33.3 0.6 collective-permute-done.10.refs_1_.refs_12_
  33.9 3.1 %collective-permute-done.9.refs_2_.refs_9_ = bf16[392,256]{1,0:T(8,128)(2,1)S(1)} collective-permute-done((bf16[392,256]{1,0:T(8,128)(2,1)S(1)}, bf16[392,256]{1,0:T(8,128)(2,1)S(1)}, u32[]{:S(2)}, u32[]{:S(2)}) %collective-permute-start.9) | collective-permute-done | bytes 200736 | tf_op jit(solution)/shard_map/ppermute | solution.py:424
  37.0 2.6 %collective-permute-start.11 = (bf16[392,256]{1,0:T(8,128)(2,1)S(1)}, bf16[392,256]{1,0:T(8,128)(2,1)S(1)}, u32[]{:S(2)}, u32[]{:S(2)}) collective-permute-start(bf16[392,256]{1,0:T(8,128)(2,1)S(1)} %relay_b.1.refs_6_), channel_id=1, source_target_pairs={{0,3},{1,0},{2,1},{3,2},{4,7},{5,4},{6,5},{7,6},{8,11},{9,8},{10,9... | collective-permute-start | bytes 602120 | tf_op jit(solution)/shard_map/ppermute | solution.py:424
  39.7 0.3 collective-permute-start.7
  39.9 2.9 %weight_second.1 = (bf16[16,160,256]{2,1,0:T(8,128)(2,1)S(1)}, bf16[16,160,256]{2,1,0:T(8,128)(2,1)S(1)}) custom-call(s32[1]{0:T(128)} %bitcast.refs_0_, bf16[384,1024]{1,0:T(8,128)(2,1)S(1)} %get-tuple-element.53.refs_1_, bf16[384,1024]{1,0:T(8,128)(2,1)S(1)} %get-tuple-element.54.refs_2_, bf16[384,1280]{1,0:T(8,128)(2,1)S(1)} %get-tuple-element.55.refs_3_, ...), custom_call_target="tpu_custom_call" | custom-call | flops 8053063680 | bytes 24641552 | tf_op jit(solution)/shard_map/weight_second/pallas_call | solution.py:394
  42.9 0.1 collective-permute-start.13
  43.0 3.8 %collective-permute-done.7.refs_7_ = bf16[392,256]{1,0:T(8,128)(2,1)S(1)} collective-permute-done((bf16[392,256]{1,0:T(8,128)(2,1)S(1)}, bf16[392,256]{1,0:T(8,128)(2,1)S(1)}, u32[]{:S(2)}, u32[]{:S(2)}) %collective-permute-start.7) | collective-permute-done | bytes 200736 | tf_op jit(solution)/shard_map/ppermute | solution.py:424
  46.8 2.9 %weight_first.1 = (bf16[16,88,256]{2,1,0:T(8,128)(2,1)S(1)}, bf16[16,88,256]{2,1,0:T(8,128)(2,1)S(1)}) custom-call(s32[1]{0:T(128)} %bitcast.refs_0_, bf16[8,256]{1,0:T(8,128)(2,1)S(1)} %get-tuple-element.38.refs_7_.refs_1_, bf16[8,256]{1,0:T(8,128)(2,1)S(1)} %get-tuple-element.41.refs_3_.refs_2_, bf16[384,256]{1,0:T(8,128)(2,1)S(1)} %get-tuple-element.33.refs_1_.refs_3_, ...), custom_call_target="tpu_custom_call" | custom-call | flops 20132659200 | bytes 115998800 | tf_op jit(solution)/shard_map/weight_first/pallas_call | solution.py:394
  49.7 0.1 collective-permute-start.12
  49.8 1.2 %join_second.1.refs_2_ = bf16[16,248,256]{2,1,0:T(8,128)(2,1)} custom-call(bf16[16,160,256]{2,1,0:T(8,128)(2,1)S(1)} %get-tuple-element.56.refs_15_.refs_0_, bf16[16,160,256]{2,1,0:T(8,128)(2,1)S(1)} %collective-permute-done.13.refs_1_), custom_call_target="tpu_custom_call" | custom-call | bytes 4653056 | tf_op jit(solution)/shard_map/join_second/pallas_call | solution.py:394
  51.0 1.0 %collective-permute-done.12.refs_1_ = bf16[16,88,256]{2,1,0:T(8,128)(2,1)S(1)} collective-permute-done((bf16[16,88,256]{2,1,0:T(8,128)(2,1)S(1)}, bf16[16,88,256]{2,1,0:T(8,128)(2,1)S(1)}, u32[]{:S(2)}, u32[]{:S(2)}) %collective-permute-start.12) | collective-permute-done | bytes 720928 | tf_op jit(solution)/shard_map/ppermute | solution.py:436
  52.0 0.9 %join_first.1 = bf16[16,248,256]{2,1,0:T(8,128)(2,1)} custom-call(bf16[16,88,256]{2,1,0:T(8,128)(2,1)S(1)} %get-tuple-element.57.refs_0_, bf16[16,88,256]{2,1,0:T(8,128)(2,1)S(1)} %collective-permute-done.12.refs_1_, bf16[16,248,256]{2,1,0:T(8,128)(2,1)} %join_second.1.refs_2_), custom_call_target="tpu_custom_call", output_to_operand_aliasing={{}: (2, {})} | custom-call | bytes 5505024 | tf_op jit(solution)/shard_map/join_first/pallas_call | solution.py:394
  52.9 36.3 %all_to_all.5.refs_0_ = bf16[16,248,256]{2,1,0:T(8,128)(2,1)S(1)} all-to-all(bf16[16,248,256]{2,1,0:T(8,128)(2,1)} %join_first.1), channel_id=1, replica_groups=mesh['dp_0'=4,'dp_1'=4,'dp_2'=2,'section'=4] {'dp_0','dp_1'}, dimensions={0} | all-to-all | bytes 4063232 | tf_op jit(solution)/shard_map/all_to_all | solution.py:593
  89.2 1.0 %total.1 = (f32[5,32,256]{2,1,0:T(8,128)}, f32[5,16,256]{2,1,0:T(8,128)}, f32[2]{0:T(128)}) custom-call(bf16[16,248,256]{2,1,0:T(8,128)(2,1)S(1)} %all_to_all.5.refs_0_), custom_call_target="tpu_custom_call" | custom-call | bytes 2277384 | tf_op jit(solution)/shard_map/total/pallas_call | solution.py:394
  (14 shorter events, 0.1 us)
Async XLA Ops:
  3.7 5.8 %copy-start = (bf16[3,384,512]{2,1,0:T(8,128)(2,1)}, bf16[3,384,512]{2,1,0:T(8,128)(2,1)S(1)}, u32[]{:S(2)}) copy-start(bf16[3,384,512]{2,1,0:T(8,128)(2,1)S(1)} %get-tuple-element.51.refs_13_) | copy-start | bytes 3538948
  3.7 7.9 %collective-permute-start = (bf16[384,256]{1,0:T(8,128)(2,1)S(1)}, bf16[384,256]{1,0:T(8,128)(2,1)}, u32[]{:S(2)}, u32[]{:S(2)}) collective-permute-start(bf16[384,256]{1,0:T(8,128)(2,1)S(1)} %get-tuple-element.33.refs_1_.refs_3_), channel_id=1, source_target_pairs={{0,1},{1,2},{2,3},{3,0},{4,5},{5,6},{6,7},{7,4},{8,9},{9,10},{10,1... | collective-permute-start | bytes 589832 | tf_op jit(solution)/shard_map/ppermute | solution.py:424
  5.4 6.8 %collective-permute-start.1 = (bf16[384,256]{1,0:T(8,128)(2,1)S(1)}, bf16[384,256]{1,0:T(8,128)(2,1)S(1)}, u32[]{:S(2)}, u32[]{:S(2)}) collective-permute-start(bf16[384,256]{1,0:T(8,128)(2,1)S(1)} %get-tuple-element.33.refs_1_.refs_3_), channel_id=1, source_target_pairs={{0,3},{1,0},{2,1},{3,2},{4,7},{5,4},{6,5},{7,6},{8,11},{9,8},{10,9... | collective-permute-start | bytes 589832 | tf_op jit(solution)/shard_map/ppermute | solution.py:424
  9.6 6.5 %collective-permute-start.4 = (bf16[384,256]{1,0:T(8,128)(2,1)S(1)}, bf16[384,256]{1,0:T(8,128)(2,1)}, u32[]{:S(2)}, u32[]{:S(2)}) collective-permute-start(bf16[384,256]{1,0:T(8,128)(2,1)S(1)} %get-tuple-element.39.refs_0_.refs_1_.refs_4_), channel_id=1, source_target_pairs={{0,3},{1,0},{2,1},{3,2},{4,7},{5,4},{6,5},{7,6},{8,11},{9,8},{10,9... | collective-permute-start | bytes 589832 | tf_op jit(solution)/shard_map/ppermute | solution.py:424
  11.7 9.3 %collective-permute-start.2 = (bf16[384,256]{1,0:T(8,128)(2,1)}, bf16[384,256]{1,0:T(8,128)(2,1)}, u32[]{:S(2)}, u32[]{:S(2)}) collective-permute-start(bf16[384,256]{1,0:T(8,128)(2,1)} %collective-permute-done.refs_2_), channel_id=1, source_target_pairs={{0,1},{1,2},{2,3},{3,0},{4,5},{5,6},{6,7},{7,4},{8,9},{9,10},{10,1... | collective-permute-start | bytes 589832 | tf_op jit(solution)/shard_map/ppermute | solution.py:424
  12.2 12.5 %collective-permute-start.3 = (bf16[384,256]{1,0:T(8,128)(2,1)S(1)}, bf16[384,256]{1,0:T(8,128)(2,1)}, u32[]{:S(2)}, u32[]{:S(2)}) collective-permute-start(bf16[384,256]{1,0:T(8,128)(2,1)S(1)} %ordered.1), channel_id=1, source_target_pairs={{0,1},{1,2},{2,3},{3,0},{4,5},{5,6},{6,7},{7,4},{8,9},{9,10},{10,1... | collective-permute-start | bytes 589832 | tf_op jit(solution)/shard_map/ppermute | solution.py:424
  16.1 8.6 %collective-permute-start.5 = (bf16[384,256]{1,0:T(8,128)(2,1)}, bf16[384,256]{1,0:T(8,128)(2,1)}, u32[]{:S(2)}, u32[]{:S(2)}) collective-permute-start(bf16[384,256]{1,0:T(8,128)(2,1)} %collective-permute-done.4.refs_3_), channel_id=1, source_target_pairs={{0,3},{1,0},{2,1},{3,2},{4,7},{5,4},{6,5},{7,6},{8,11},{9,8},{10,9... | collective-permute-start | bytes 589832 | tf_op jit(solution)/shard_map/ppermute | solution.py:424
  28.1 5.8 %collective-permute-start.10 = (bf16[392,256]{1,0:T(8,128)(2,1)S(1)}, bf16[392,256]{1,0:T(8,128)(2,1)S(1)}, u32[]{:S(2)}, u32[]{:S(2)}) collective-permute-start(bf16[392,256]{1,0:T(8,128)(2,1)S(1)} %get-tuple-element.50), channel_id=1, source_target_pairs={{0,3},{1,0},{2,1},{3,2},{4,7},{5,4},{6,5},{7,6},{8,11},{9,8},{10,9... | collective-permute-start | bytes 602120 | tf_op jit(solution)/shard_map/ppermute | solution.py:424
  29.6 7.3 %collective-permute-start.9 = (bf16[392,256]{1,0:T(8,128)(2,1)S(1)}, bf16[392,256]{1,0:T(8,128)(2,1)S(1)}, u32[]{:S(2)}, u32[]{:S(2)}) collective-permute-start(bf16[392,256]{1,0:T(8,128)(2,1)S(1)} %get-tuple-element.48), channel_id=1, source_target_pairs={{0,3},{1,0},{2,1},{3,2},{4,7},{5,4},{6,5},{7,6},{8,11},{9,8},{10,9... | collective-permute-start | bytes 602120 | tf_op jit(solution)/shard_map/ppermute | solution.py:424
  29.7 9.9 %collective-permute-start.6 = (bf16[392,256]{1,0:T(8,128)(2,1)S(1)}, bf16[392,256]{1,0:T(8,128)(2,1)S(1)}, u32[]{:S(2)}, u32[]{:S(2)}) collective-permute-start(bf16[392,256]{1,0:T(8,128)(2,1)S(1)} %get-tuple-element.46), channel_id=1, source_target_pairs={{0,1},{1,2},{2,3},{3,0},{4,5},{5,6},{6,7},{7,4},{8,9},{9,10},{10,1... | collective-permute-start | bytes 602120 | tf_op jit(solution)/shard_map/ppermute | solution.py:424
  32.6 10.3 %collective-permute-start.8 = (bf16[392,256]{1,0:T(8,128)(2,1)S(1)}, bf16[392,256]{1,0:T(8,128)(2,1)S(1)}, u32[]{:S(2)}, u32[]{:S(2)}) collective-permute-start(bf16[392,256]{1,0:T(8,128)(2,1)S(1)} %get-tuple-element.47), channel_id=1, source_target_pairs={{0,1},{1,2},{2,3},{3,0},{4,5},{5,6},{6,7},{7,4},{8,9},{9,10},{10,1... | collective-permute-start | bytes 602120 | tf_op jit(solution)/shard_map/ppermute | solution.py:424
  37.0 6.0 %collective-permute-start.11 = (bf16[392,256]{1,0:T(8,128)(2,1)S(1)}, bf16[392,256]{1,0:T(8,128)(2,1)S(1)}, u32[]{:S(2)}, u32[]{:S(2)}) collective-permute-start(bf16[392,256]{1,0:T(8,128)(2,1)S(1)} %relay_b.1.refs_6_), channel_id=1, source_target_pairs={{0,3},{1,0},{2,1},{3,2},{4,7},{5,4},{6,5},{7,6},{8,11},{9,8},{10,9... | collective-permute-start | bytes 602120 | tf_op jit(solution)/shard_map/ppermute | solution.py:424
  39.7 7.2 %collective-permute-start.7 = (bf16[392,256]{1,0:T(8,128)(2,1)S(1)}, bf16[392,256]{1,0:T(8,128)(2,1)S(1)}, u32[]{:S(2)}, u32[]{:S(2)}) collective-permute-start(bf16[392,256]{1,0:T(8,128)(2,1)S(1)} %relay_a.1.refs_5_), channel_id=1, source_target_pairs={{0,1},{1,2},{2,3},{3,0},{4,5},{5,6},{6,7},{7,4},{8,9},{9,10},{10,1... | collective-permute-start | bytes 602120 | tf_op jit(solution)/shard_map/ppermute | solution.py:424
  39.9 6.9 %copy-start.1 = (bf16[3,384,512]{2,1,0:T(8,128)(2,1)S(1)}, bf16[3,384,512]{2,1,0:T(8,128)(2,1)}, u32[]{:S(2)}) copy-start(bf16[3,384,512]{2,1,0:T(8,128)(2,1)} %copy-done) | copy-start | bytes 3538948
  42.9 6.9 %collective-permute-start.13 = (bf16[16,160,256]{2,1,0:T(8,128)(2,1)S(1)}, bf16[16,160,256]{2,1,0:T(8,128)(2,1)S(1)}, u32[]{:S(2)}, u32[]{:S(2)}) collective-permute-start(bf16[16,160,256]{2,1,0:T(8,128)(2,1)S(1)} %get-tuple-element.59), channel_id=1, source_target_pairs={{0,4},{4,0},{1,5},{5,1},{2,6},{6,2},{3,7},{7,3},{8,12},{12,8},{9,1... | collective-permute-start | bytes 3932168 | tf_op jit(solution)/shard_map/ppermute | solution.py:436
  49.7 2.3 %collective-permute-start.12 = (bf16[16,88,256]{2,1,0:T(8,128)(2,1)S(1)}, bf16[16,88,256]{2,1,0:T(8,128)(2,1)S(1)}, u32[]{:S(2)}, u32[]{:S(2)}) collective-permute-start(bf16[16,88,256]{2,1,0:T(8,128)(2,1)S(1)} %get-tuple-element.58), channel_id=1, source_target_pairs={{0,4},{4,0},{1,5},{5,1},{2,6},{6,2},{3,7},{7,3},{8,12},{12,8},{9,1... | collective-permute-start | bytes 2162696 | tf_op jit(solution)/shard_map/ppermute | solution.py:436

commit v14 on v10

--- a/solution.py
+++ b/solution.py
@@ -111,8 +111,9 @@
     for copy in w_copies:
         copy.start()
     rest_copies = [
-        pltpu.make_async_copy(x.at[cols:], rest.at[at * cols : (at + 1) * cols], rest_sem.at[at])
+        pltpu.make_async_copy(x.at[cols + n], rest.at[at * cols + n], rest_sem.at[at * cols + n])
         for at, x in enumerate((real, fake))
+        for n in range(cols)
     ]
 
     for copy in rest_copies:
@@ -460,7 +461,7 @@
         (real_in, fake_in, kernel_first),
         chunk_outs + [like(kernel_first.shape), like((cols, span, in_width))],
         conv_scratch
-        + [pltpu.VMEM((cols, span, in_width), BF16), dma((cols,)), dma((2,)), dma((taps,))]
+        + [pltpu.VMEM((cols, span, in_width), BF16), dma((cols,)), dma((cols,)), dma((taps,))]
         + phases_far * (not NEAR_PHASES[0]),
         hbm=(0, 1, 2),
         hbm_outs=() if NEAR_PHASES[0] else (1,),

time: 89.4 us -> 89.5 us (level)
  no operation moved by 1% of the time
where the time goes in v14:
time: 89.5 us; the launch traced here: 89.2 us
  blocking collectives  36.1 us (40%)
  Pallas kernels  22.8 us (25%)
  starting transfers between devices  19.1 us (21%)
  waiting for transfers between devices  10.2 us (11%)
  between operations  0.99 us (1%)
    all_to_all x1, blocking collectives, shards(): blocks = lax.all_to_all(joint, ZY, 0, 0)  36.1 us
    pallas_call x13, Pallas kernels, call(): pl.pallas_call(body, out_shape=[pltpu.HBM(x.shape, x.dtype) if at in hbm_...  22.8 us
    ppermute x12, starting transfers between devices, turn(): lax.ppermute(x, 'section', [(i, (i + step) % count) for i in range(count)])  18.9 us
    ppermute x12, waiting for transfers between devices, turn(): lax.ppermute(x, 'section', [(i, (i + step) % count) for i in range(count)])  9.25 us
  transfers between devices with their start and end apart: 14, of which 6 were waited for; matrix products, arithmetic and copies ran while one was open for 0% of the time, Pallas kernels for 16%

profile of v14, /device:TPU:0, one launch (start us, length us, event | category | flops | bytes accessed | tf_op | source)
XLA Modules:
  0.0 89.2 jit_solution(16746656260592032796)
XLA Ops:
  0.6 3.2 %first_a.1 = (bf16[384,256]{1,0:T(8,128)(2,1)S(1)}, bf16[3,384,512]{2,1,0:T(8,128)(2,1)S(1)}, f32[8,128]{1,0:T(8,128)S(1)}, bf16[5,512,256]{2,1,0:T(8,128)(2,1)S(1)}, bf16[8,144,512]{2,1,0:T(8,128)(2,1)S(1)}) custom-call(bf16[8,144,512]{2,1,0:T(8,128)(2,1)} %refs_0_.1, bf16[8,144,512]{2,1,0:T(8,128)(2,1)} %refs_1_.1, bf16[5,512,256]{2,1,0:T(8,128)(2,1)} %refs_2_.2), custom_call_target="tpu_custom_call" | custom-call | flops 503316480 | bytes 7540736 | tf_op jit(solution)/shard_map/first_a/pallas_call | solution.py:395
  3.8 1.6 %collective-permute-start = (bf16[384,256]{1,0:T(8,128)(2,1)S(1)}, bf16[384,256]{1,0:T(8,128)(2,1)}, u32[]{:S(2)}, u32[]{:S(2)}) collective-permute-start(bf16[384,256]{1,0:T(8,128)(2,1)S(1)} %get-tuple-element.33.refs_1_.refs_3_), channel_id=1, source_target_pairs={{0,1},{1,2},{2,3},{3,0},{4,5},{5,6},{6,7},{7,4},{8,9},{9,10},{10,1... | collective-permute-start | bytes 589832 | tf_op jit(solution)/shard_map/ppermute | solution.py:425
  5.5 1.7 %collective-permute-start.1 = (bf16[384,256]{1,0:T(8,128)(2,1)S(1)}, bf16[384,256]{1,0:T(8,128)(2,1)S(1)}, u32[]{:S(2)}, u32[]{:S(2)}) collective-permute-start(bf16[384,256]{1,0:T(8,128)(2,1)S(1)} %get-tuple-element.33.refs_1_.refs_3_), channel_id=1, source_target_pairs={{0,3},{1,0},{2,1},{3,2},{4,7},{5,4},{6,5},{7,6},{8,11},{9,8},{10,9... | collective-permute-start | bytes 589832 | tf_op jit(solution)/shard_map/ppermute | solution.py:425
  7.1 2.5 %first_b.1 = (bf16[384,256]{1,0:T(8,128)(2,1)S(1)}, bf16[3,384,512]{2,1,0:T(8,128)(2,1)}, f32[8,128]{1,0:T(8,128)S(1)}, bf16[5,1024,256]{2,1,0:T(8,128)(2,1)S(1)}) custom-call(bf16[8,144,512]{2,1,0:T(8,128)(2,1)S(1)} %get-tuple-element.34.refs_0_, bf16[5,512,256]{2,1,0:T(8,128)(2,1)S(1)} %get-tuple-element.35.refs_1_, bf16[5,1024,256]{2,1,0:T(8,128)(2,1)} %refs_2_.3), custom_call_target="tpu_custom_call" | custom-call | flops 503316480 | bytes 9113600 | tf_op jit(solution)/shard_map/first_b/pallas_call | solution.py:395
  9.6 1.7 %collective-permute-start.4 = (bf16[384,256]{1,0:T(8,128)(2,1)S(1)}, bf16[384,256]{1,0:T(8,128)(2,1)}, u32[]{:S(2)}, u32[]{:S(2)}) collective-permute-start(bf16[384,256]{1,0:T(8,128)(2,1)S(1)} %get-tuple-element.39.refs_0_.refs_1_.refs_4_), channel_id=1, source_target_pairs={{0,3},{1,0},{2,1},{3,2},{4,7},{5,4},{6,5},{7,6},{8,11},{9,8},{10,9... | collective-permute-start | bytes 589832 | tf_op jit(solution)/shard_map/ppermute | solution.py:425
  11.3 0.4 collective-permute-done.refs_2_
  11.7 0.5 collective-permute-start.2
  12.2 0.0 collective-permute-done.1.refs_3_.refs_1_
  12.2 2.5 %collective-permute-start.3 = (bf16[384,256]{1,0:T(8,128)(2,1)S(1)}, bf16[384,256]{1,0:T(8,128)(2,1)}, u32[]{:S(2)}, u32[]{:S(2)}) collective-permute-start(bf16[384,256]{1,0:T(8,128)(2,1)S(1)} %ordered.1), channel_id=1, source_target_pairs={{0,1},{1,2},{2,3},{3,0},{4,5},{5,6},{6,7},{7,4},{8,9},{9,10},{10,1... | collective-permute-start | bytes 589832 | tf_op jit(solution)/shard_map/ppermute | solution.py:425
  14.7 1.4 %collective-permute-done.4.refs_3_ = bf16[384,256]{1,0:T(8,128)(2,1)} collective-permute-done((bf16[384,256]{1,0:T(8,128)(2,1)S(1)}, bf16[384,256]{1,0:T(8,128)(2,1)}, u32[]{:S(2)}, u32[]{:S(2)}) %collective-permute-start.4) | collective-permute-done | bytes 196640 | tf_op jit(solution)/shard_map/ppermute | solution.py:425
  16.1 2.8 %collective-permute-start.5 = (bf16[384,256]{1,0:T(8,128)(2,1)}, bf16[384,256]{1,0:T(8,128)(2,1)}, u32[]{:S(2)}, u32[]{:S(2)}) collective-permute-start(bf16[384,256]{1,0:T(8,128)(2,1)} %collective-permute-done.4.refs_3_), channel_id=1, source_target_pairs={{0,3},{1,0},{2,1},{3,2},{4,7},{5,4},{6,5},{7,6},{8,11},{9,8},{10,9... | collective-permute-start | bytes 589832 | tf_op jit(solution)/shard_map/ppermute | solution.py:425
  19.0 2.0 %collective-permute-done.2.refs_4_ = bf16[384,256]{1,0:T(8,128)(2,1)} collective-permute-done((bf16[384,256]{1,0:T(8,128)(2,1)}, bf16[384,256]{1,0:T(8,128)(2,1)}, u32[]{:S(2)}, u32[]{:S(2)}) %collective-permute-start.2) | collective-permute-done | bytes 196640 | tf_op jit(solution)/shard_map/ppermute | solution.py:425
  21.0 3.7 %second_a.1 = (bf16[384,1024]{1,0:T(8,128)(2,1)S(1)}, bf16[384,1280]{1,0:T(8,128)(2,1)S(1)}, bf16[392,256]{1,0:T(8,128)(2,1)S(1)}, bf16[8,256]{1,0:T(8,128)(2,1)...) custom-call(s32[1]{0:T(128)} %bitcast.1.refs_0_, ...), custom_call_target="tpu_custom_call" | custom-call | flops 1258291200 | bytes 5984260 | tf_op jit(solution)/shard_map/second_a/pallas_call | solution.py:395
  24.7 3.4 %second_b.1 = (bf16[384,1024]{1,0:T(8,128)(2,1)S(1)}, bf16[384,1280]{1,0:T(8,128)(2,1)S(1)}, bf16[392,256]{1,0:T(8,128)(2,1)S(1)}, bf16[8,256]{1,0:T(8,128)(2,1)S(1)}) custom-call(s32[1]{0:T(128)} %bitcast.1.refs_0_, bf16[384,256]{1,0:T(8,128)(2,1)S(1)} %get-tuple-element.39.refs_0_.refs_1_.refs_4_, bf16[384,256]{1,0:T(8,128)(2,1)} %collective-permute-done.3.refs_2_, ...), custom_call_target="tpu_custom_call" | custom-call | flops 1258291200 | bytes 5386244 | tf_op jit(solution)/shard_map/second_b/pallas_call | solution.py:395
  28.2 1.5 %collective-permute-start.10 = (bf16[392,256]{1,0:T(8,128)(2,1)S(1)}, bf16[392,256]{1,0:T(8,128)(2,1)S(1)}, u32[]{:S(2)}, u32[]{:S(2)}) collective-permute-start(bf16[392,256]{1,0:T(8,128)(2,1)S(1)} %get-tuple-element.50), channel_id=1, source_target_pairs={{0,3},{1,0},{2,1},{3,2},{4,7},{5,4},{6,5},{7,6},{8,11},{9,8},{10,9... | collective-permute-start | bytes 602120 | tf_op jit(solution)/shard_map/ppermute | solution.py:425
  29.7 0.6 collective-permute-start.6
  30.3 1.0 %back_b.1 = (bf16[392,256]{1,0:T(8,128)(2,1)S(1)}, bf16[392,256]{1,0:T(8,128)(2,1)S(1)}, bf16[384,256]{1,0:T(8,128)(2,1)S(1)}) custom-call(s32[1]{0:T(128)} %bitcast.1.refs_0_, bf16[384,1280]{1,0:T(8,128)(2,1)S(1)} %get-tuple-element.43.refs_1_.refs_4_, bf16[5,1024,256]{2,1,0:T(8,128)(2,1)S(1)} %get-tuple-element.36.refs_5_.refs_2_, ...), custom_call_target="tpu_custom_call" | custom-call | flops 3019898880 | bytes 16826384 | tf_op jit(solution)/shard_map/back_b/pallas_call | solution.py:395
  31.2 0.1 collective-permute-start.8
  31.3 3.2 %collective-permute-start.9 = (bf16[392,256]{1,0:T(8,128)(2,1)S(1)}, bf16[392,256]{1,0:T(8,128)(2,1)S(1)}, u32[]{:S(2)}, u32[]{:S(2)}) collective-permute-start(bf16[392,256]{1,0:T(8,128)(2,1)S(1)} %get-tuple-element.48), channel_id=1, source_target_pairs={{0,3},{1,0},{2,1},{3,2},{4,7},{5,4},{6,5},{7,6},{8,11},{9,8},{10,9... | collective-permute-start | bytes 602120 | tf_op jit(solution)/shard_map/ppermute | solution.py:425
  34.5 1.6 %collective-permute-done.10.refs_1_.refs_12_ = bf16[392,256]{1,0:T(8,128)(2,1)S(1)} collective-permute-done((bf16[392,256]{1,0:T(8,128)(2,1)S(1)}, bf16[392,256]{1,0:T(8,128)(2,1)S(1)}, u32[]{:S(2)}, u32[]{:S(2)}) %collective-permute-start.10) | collective-permute-done | bytes 200736 | tf_op jit(solution)/shard_map/ppermute | solution.py:425
  36.2 2.4 %collective-permute-start.11 = (bf16[392,256]{1,0:T(8,128)(2,1)S(1)}, bf16[392,256]{1,0:T(8,128)(2,1)S(1)}, u32[]{:S(2)}, u32[]{:S(2)}) collective-permute-start(bf16[392,256]{1,0:T(8,128)(2,1)S(1)} %relay_b.1.refs_6_), channel_id=1, source_target_pairs={{0,3},{1,0},{2,1},{3,2},{4,7},{5,4},{6,5},{7,6},{8,11},{9,8},{10,9... | collective-permute-start | bytes 602120 | tf_op jit(solution)/shard_map/ppermute | solution.py:425
  38.7 0.3 collective-permute-start.7
  38.9 3.0 %weight_second.1 = (bf16[16,160,256]{2,1,0:T(8,128)(2,1)S(1)}, bf16[16,160,256]{2,1,0:T(8,128)(2,1)S(1)}) custom-call(s32[1]{0:T(128)} %bitcast.refs_0_, bf16[384,1024]{1,0:T(8,128)(2,1)S(1)} %get-tuple-element.53.refs_1_, bf16[384,1024]{1,0:T(8,128)(2,1)S(1)} %get-tuple-element.54.refs_2_, bf16[384,1280]{1,0:T(8,128)(2,1)S(1)} %get-tuple-element.55.refs_3_, ...), custom_call_target="tpu_custom_call" | custom-call | flops 8053063680 | bytes 24641552 | tf_op jit(solution)/shard_map/weight_second/pallas_call | solution.py:395
  41.9 0.1 collective-permute-start.13
  42.0 3.8 %collective-permute-done.7.refs_7_ = bf16[392,256]{1,0:T(8,128)(2,1)S(1)} collective-permute-done((bf16[392,256]{1,0:T(8,128)(2,1)S(1)}, bf16[392,256]{1,0:T(8,128)(2,1)S(1)}, u32[]{:S(2)}, u32[]{:S(2)}) %collective-permute-start.7) | collective-permute-done | bytes 200736 | tf_op jit(solution)/shard_map/ppermute | solution.py:425
  45.8 2.9 %weight_first.1 = (bf16[16,88,256]{2,1,0:T(8,128)(2,1)S(1)}, bf16[16,88,256]{2,1,0:T(8,128)(2,1)S(1)}) custom-call(s32[1]{0:T(128)} %bitcast.refs_0_, bf16[8,256]{1,0:T(8,128)(2,1)S(1)} %get-tuple-element.38.refs_1_, bf16[8,256]{1,0:T(8,128)(2,1)S(1)} %get-tuple-element.42.refs_3_.refs_2_, bf16[384,256]{1,0:T(8,128)(2,1)S(1)} %get-tuple-element.33.refs_1_.refs_3_, ...), custom_call_target="tpu_custom_call" | custom-call | flops 20132659200 | bytes 115998800 | tf_op jit(solution)/shard_map/weight_first/pallas_call | solution.py:395
  48.7 0.1 collective-permute-start.12
  48.8 1.2 %join_second.1.refs_2_ = bf16[16,248,256]{2,1,0:T(8,128)(2,1)} custom-call(bf16[16,160,256]{2,1,0:T(8,128)(2,1)S(1)} %get-tuple-element.56.refs_15_.refs_0_, bf16[16,160,256]{2,1,0:T(8,128)(2,1)S(1)} %collective-permute-done.13.refs_1_), custom_call_target="tpu_custom_call" | custom-call | bytes 4653056 | tf_op jit(solution)/shard_map/join_second/pallas_call | solution.py:395
  50.0 1.0 %collective-permute-done.12.refs_1_ = bf16[16,88,256]{2,1,0:T(8,128)(2,1)S(1)} collective-permute-done((bf16[16,88,256]{2,1,0:T(8,128)(2,1)S(1)}, bf16[16,88,256]{2,1,0:T(8,128)(2,1)S(1)}, u32[]{:S(2)}, u32[]{:S(2)}) %collective-permute-start.12) | collective-permute-done | bytes 720928 | tf_op jit(solution)/shard_map/ppermute | solution.py:437
  51.0 0.9 %join_first.1 = bf16[16,248,256]{2,1,0:T(8,128)(2,1)} custom-call(bf16[16,88,256]{2,1,0:T(8,128)(2,1)S(1)} %get-tuple-element.57.refs_0_, bf16[16,88,256]{2,1,0:T(8,128)(2,1)S(1)} %collective-permute-done.12.refs_1_, bf16[16,248,256]{2,1,0:T(8,128)(2,1)} %join_second.1.refs_2_), custom_call_target="tpu_custom_call", output_to_operand_aliasing={{}: (2, {})} | custom-call | bytes 5505024 | tf_op jit(solution)/shard_map/join_first/pallas_call | solution.py:395
  51.9 36.1 %all_to_all.5.refs_0_ = bf16[16,248,256]{2,1,0:T(8,128)(2,1)S(1)} all-to-all(bf16[16,248,256]{2,1,0:T(8,128)(2,1)} %join_first.1), channel_id=1, replica_groups=mesh['dp_0'=4,'dp_1'=4,'dp_2'=2,'section'=4] {'dp_0','dp_1'}, dimensions={0} | all-to-all | bytes 4063232 | tf_op jit(solution)/shard_map/all_to_all | solution.py:594
  88.0 1.0 %total.1 = (f32[5,32,256]{2,1,0:T(8,128)}, f32[5,16,256]{2,1,0:T(8,128)}, f32[2]{0:T(128)}) custom-call(bf16[16,248,256]{2,1,0:T(8,128)(2,1)S(1)} %all_to_all.5.refs_0_), custom_call_target="tpu_custom_call" | custom-call | bytes 2277384 | tf_op jit(solution)/shard_map/total/pallas_call | solution.py:395
  (14 shorter events, 0.1 us)
Async XLA Ops:
  3.8 5.8 %copy-start = (bf16[3,384,512]{2,1,0:T(8,128)(2,1)}, bf16[3,384,512]{2,1,0:T(8,128)(2,1)S(1)}, u32[]{:S(2)}) copy-start(bf16[3,384,512]{2,1,0:T(8,128)(2,1)S(1)} %get-tuple-element.51.refs_13_) | copy-start | bytes 3538948
  3.8 7.9 %collective-permute-start = (bf16[384,256]{1,0:T(8,128)(2,1)S(1)}, bf16[384,256]{1,0:T(8,128)(2,1)}, u32[]{:S(2)}, u32[]{:S(2)}) collective-permute-start(bf16[384,256]{1,0:T(8,128)(2,1)S(1)} %get-tuple-element.33.refs_1_.refs_3_), channel_id=1, source_target_pairs={{0,1},{1,2},{2,3},{3,0},{4,5},{5,6},{6,7},{7,4},{8,9},{9,10},{10,1... | collective-permute-start | bytes 589832 | tf_op jit(solution)/shard_map/ppermute | solution.py:425
  5.5 6.8 %collective-permute-start.1 = (bf16[384,256]{1,0:T(8,128)(2,1)S(1)}, bf16[384,256]{1,0:T(8,128)(2,1)S(1)}, u32[]{:S(2)}, u32[]{:S(2)}) collective-permute-start(bf16[384,256]{1,0:T(8,128)(2,1)S(1)} %get-tuple-element.33.refs_1_.refs_3_), channel_id=1, source_target_pairs={{0,3},{1,0},{2,1},{3,2},{4,7},{5,4},{6,5},{7,6},{8,11},{9,8},{10,9... | collective-permute-start | bytes 589832 | tf_op jit(solution)/shard_map/ppermute | solution.py:425
  9.6 6.5 %collective-permute-start.4 = (bf16[384,256]{1,0:T(8,128)(2,1)S(1)}, bf16[384,256]{1,0:T(8,128)(2,1)}, u32[]{:S(2)}, u32[]{:S(2)}) collective-permute-start(bf16[384,256]{1,0:T(8,128)(2,1)S(1)} %get-tuple-element.39.refs_0_.refs_1_.refs_4_), channel_id=1, source_target_pairs={{0,3},{1,0},{2,1},{3,2},{4,7},{5,4},{6,5},{7,6},{8,11},{9,8},{10,9... | collective-permute-start | bytes 589832 | tf_op jit(solution)/shard_map/ppermute | solution.py:425
  11.7 9.3 %collective-permute-start.2 = (bf16[384,256]{1,0:T(8,128)(2,1)}, bf16[384,256]{1,0:T(8,128)(2,1)}, u32[]{:S(2)}, u32[]{:S(2)}) collective-permute-start(bf16[384,256]{1,0:T(8,128)(2,1)} %collective-permute-done.refs_2_), channel_id=1, source_target_pairs={{0,1},{1,2},{2,3},{3,0},{4,5},{5,6},{6,7},{7,4},{8,9},{9,10},{10,1... | collective-permute-start | bytes 589832 | tf_op jit(solution)/shard_map/ppermute | solution.py:425
  12.2 12.5 %collective-permute-start.3 = (bf16[384,256]{1,0:T(8,128)(2,1)S(1)}, bf16[384,256]{1,0:T(8,128)(2,1)}, u32[]{:S(2)}, u32[]{:S(2)}) collective-permute-start(bf16[384,256]{1,0:T(8,128)(2,1)S(1)} %ordered.1), channel_id=1, source_target_pairs={{0,1},{1,2},{2,3},{3,0},{4,5},{5,6},{6,7},{7,4},{8,9},{9,10},{10,1... | collective-permute-start | bytes 589832 | tf_op jit(solution)/shard_map/ppermute | solution.py:425
  16.1 8.6 %collective-permute-start.5 = (bf16[384,256]{1,0:T(8,128)(2,1)}, bf16[384,256]{1,0:T(8,128)(2,1)}, u32[]{:S(2)}, u32[]{:S(2)}) collective-permute-start(bf16[384,256]{1,0:T(8,128)(2,1)} %collective-permute-done.4.refs_3_), channel_id=1, source_target_pairs={{0,3},{1,0},{2,1},{3,2},{4,7},{5,4},{6,5},{7,6},{8,11},{9,8},{10,9... | collective-permute-start | bytes 589832 | tf_op jit(solution)/shard_map/ppermute | solution.py:425
  28.2 8.0 %collective-permute-start.10 = (bf16[392,256]{1,0:T(8,128)(2,1)S(1)}, bf16[392,256]{1,0:T(8,128)(2,1)S(1)}, u32[]{:S(2)}, u32[]{:S(2)}) collective-permute-start(bf16[392,256]{1,0:T(8,128)(2,1)S(1)} %get-tuple-element.50), channel_id=1, source_target_pairs={{0,3},{1,0},{2,1},{3,2},{4,7},{5,4},{6,5},{7,6},{8,11},{9,8},{10,9... | collective-permute-start | bytes 602120 | tf_op jit(solution)/shard_map/ppermute | solution.py:425
  29.7 8.9 %collective-permute-start.6 = (bf16[392,256]{1,0:T(8,128)(2,1)S(1)}, bf16[392,256]{1,0:T(8,128)(2,1)S(1)}, u32[]{:S(2)}, u32[]{:S(2)}) collective-permute-start(bf16[392,256]{1,0:T(8,128)(2,1)S(1)} %get-tuple-element.46), channel_id=1, source_target_pairs={{0,1},{1,2},{2,3},{3,0},{4,5},{5,6},{6,7},{7,4},{8,9},{9,10},{10,1... | collective-permute-start | bytes 602120 | tf_op jit(solution)/shard_map/ppermute | solution.py:425
  31.2 10.8 %collective-permute-start.8 = (bf16[392,256]{1,0:T(8,128)(2,1)S(1)}, bf16[392,256]{1,0:T(8,128)(2,1)S(1)}, u32[]{:S(2)}, u32[]{:S(2)}) collective-permute-start(bf16[392,256]{1,0:T(8,128)(2,1)S(1)} %get-tuple-element.47), channel_id=1, source_target_pairs={{0,1},{1,2},{2,3},{3,0},{4,5},{5,6},{6,7},{7,4},{8,9},{9,10},{10,1... | collective-permute-start | bytes 602120 | tf_op jit(solution)/shard_map/ppermute | solution.py:425
  31.3 10.7 %collective-permute-start.9 = (bf16[392,256]{1,0:T(8,128)(2,1)S(1)}, bf16[392,256]{1,0:T(8,128)(2,1)S(1)}, u32[]{:S(2)}, u32[]{:S(2)}) collective-permute-start(bf16[392,256]{1,0:T(8,128)(2,1)S(1)} %get-tuple-element.48), channel_id=1, source_target_pairs={{0,3},{1,0},{2,1},{3,2},{4,7},{5,4},{6,5},{7,6},{8,11},{9,8},{10,9... | collective-permute-start | bytes 602120 | tf_op jit(solution)/shard_map/ppermute | solution.py:425
  36.2 5.8 %collective-permute-start.11 = (bf16[392,256]{1,0:T(8,128)(2,1)S(1)}, bf16[392,256]{1,0:T(8,128)(2,1)S(1)}, u32[]{:S(2)}, u32[]{:S(2)}) collective-permute-start(bf16[392,256]{1,0:T(8,128)(2,1)S(1)} %relay_b.1.refs_6_), channel_id=1, source_target_pairs={{0,3},{1,0},{2,1},{3,2},{4,7},{5,4},{6,5},{7,6},{8,11},{9,8},{10,9... | collective-permute-start | bytes 602120 | tf_op jit(solution)/shard_map/ppermute | solution.py:425
  38.7 7.2 %collective-permute-start.7 = (bf16[392,256]{1,0:T(8,128)(2,1)S(1)}, bf16[392,256]{1,0:T(8,128)(2,1)S(1)}, u32[]{:S(2)}, u32[]{:S(2)}) collective-permute-start(bf16[392,256]{1,0:T(8,128)(2,1)S(1)} %relay_a.1.refs_5_), channel_id=1, source_target_pairs={{0,1},{1,2},{2,3},{3,0},{4,5},{5,6},{6,7},{7,4},{8,9},{9,10},{10,1... | collective-permute-start | bytes 602120 | tf_op jit(solution)/shard_map/ppermute | solution.py:425
  38.9 6.9 %copy-start.1 = (bf16[3,384,512]{2,1,0:T(8,128)(2,1)S(1)}, bf16[3,384,512]{2,1,0:T(8,128)(2,1)}, u32[]{:S(2)}) copy-start(bf16[3,384,512]{2,1,0:T(8,128)(2,1)} %copy-done) | copy-start | bytes 3538948
  41.9 6.9 %collective-permute-start.13 = (bf16[16,160,256]{2,1,0:T(8,128)(2,1)S(1)}, bf16[16,160,256]{2,1,0:T(8,128)(2,1)S(1)}, u32[]{:S(2)}, u32[]{:S(2)}) collective-permute-start(bf16[16,160,256]{2,1,0:T(8,128)(2,1)S(1)} %get-tuple-element.59), channel_id=1, source_target_pairs={{0,4},{4,0},{1,5},{5,1},{2,6},{6,2},{3,7},{7,3},{8,12},{12,8},{9,1... | collective-permute-start | bytes 3932168 | tf_op jit(solution)/shard_map/ppermute | solution.py:437
  48.7 2.3 %collective-permute-start.12 = (bf16[16,88,256]{2,1,0:T(8,128)(2,1)S(1)}, bf16[16,88,256]{2,1,0:T(8,128)(2,1)S(1)}, u32[]{:S(2)}, u32[]{:S(2)}) collective-permute-start(bf16[16,88,256]{2,1,0:T(8,128)(2,1)S(1)} %get-tuple-element.58), channel_id=1, source_target_pairs={{0,4},{4,0},{1,5},{5,1},{2,6},{6,2},{3,7},{7,3},{8,12},{12,8},{9,1... | collective-permute-start | bytes 2162696 | tf_op jit(solution)/shard_map/ppermute | solution.py:437
